TPU v7x, 32 devices: a whole 2x2x4 slice. The times are simulated.
32 devices in a mesh: gx: 4 (over y, x), gy: 2 (over core), gz: 4 (over z).
Axes of the slice: x: 2, y: 2, z: 4, core: 2. Of those that a mesh axis runs over, the one named last changes fastest.
Arguments:
- fields: float32 [16, 48, 16, 512], P(None, 'gx', 'gy', 'gz'), may hold values from -6 to 6
- speeds: float32 [3, 16], replicated, may hold values from -1.5 to 1.5
- kinetics: float32 [16, 16], replicated, may hold values from -2 to 0.75
- block_rank: int32 [48], P('gx'), may hold values from 0 to 47, each once
- x_factor: float32 [48, 96], replicated, may hold values from -0.875 to 0.875
- y_factor: float32 [16, 64], P('gy'), may hold values from -1.5 to 1.5
- z_factor: float32 [512, 54], P('gz'), may hold values from -0.25 to 0.25
Outputs:
- fields_next: float32 [16, 48, 16, 512], P(None, 'gx', 'gy', 'gz')
- core: float32 [16, 96, 64, 54], P('gz', 'gx', 'gy')
Inputs may be any that keep to these rules, and one draw needn't show every extreme that they name: block_rank is a permutation of the 48 x planes.
All inputs are finite; a program needn't handle non-finite values.
Results may differ from a plain program's by a relative error of at most 0.000098.
Values sent between devices are 32-bit elements; how exact they have to be, the bound alone decides.
No kernel may reach another device: no remote copies, remote signals or barrier semaphores. Data moves between devices by JAX's collectives and lax.ppermute only.
A program may use at most 128 MiB of HBM per device.

v0:
```python
import jax
import jax.numpy as jnp
from jax import lax
from jax.sharding import PartitionSpec as P

COEFFS = (0.8, -0.2, 4.0 / 105.0, -1.0 / 280.0)
TIME_STEP = 0.45


def with_halo(cells, sides, width):
    for axis, dim in sides:
        count = lax.axis_size(axis)
        ends = count - 1
        head = lax.slice_in_dim(cells, 0, width, axis=dim)
        tail = lax.slice_in_dim(cells, cells.shape[dim] - width, cells.shape[dim], axis=dim)
        cells = jnp.concatenate(
            [
                lax.ppermute(tail, axis, [(i, (i + 1) % count) for i in range(ends)]),
                cells,
                lax.ppermute(head, axis, [((i + 1) % count, i) for i in range(ends)]),
            ],
            axis=dim,
        )
    return cells


def tendency(padded, speeds, kinetics):
    extent = [padded.shape[1] - 8, padded.shape[2] - 8, padded.shape[3] - 8]

    def window(direction, offset):
        starts = [4, 4, 4]
        starts[direction] = starts[direction] + offset
        return padded[
            :,
            starts[0] : starts[0] + extent[0],
            starts[1] : starts[1] + extent[1],
            starts[2] : starts[2] + extent[2],
        ]

    center = window(0, 0)
    result = jnp.einsum("vw,wxyz->vxyz", kinetics, center, precision=lax.Precision.HIGHEST)
    for direction in range(3):
        gradient = COEFFS[0] * (window(direction, 1) - window(direction, -1))
        for offset in range(2, 5):
            gradient = gradient + COEFFS[offset - 1] * (
                window(direction, offset) - window(direction, -offset)
            )
        result = result - speeds[direction][:, None, None, None] * gradient
    return result


def shallow_rim(values):
    return with_halo(values, (("gx", 1), ("gy", 2), ("gz", 3)), 4)


def local(fields, speeds, kinetics, block_rank, x_factor, y_factor, z_factor):
    section = fields + TIME_STEP * tendency(shallow_rim(fields), speeds, kinetics)
    fields_next = 0.5 * (
        fields + section + TIME_STEP * tendency(shallow_rim(section), speeds, kinetics)
    )
    hp = lax.Precision.HIGHEST
    plane_ids = jnp.arange(x_factor.shape[0], dtype=jnp.int32)
    selector = (block_rank[:, None] == plane_ids[None, :]).astype(jnp.float32)
    x_rows = jnp.dot(selector, x_factor, precision=hp, preferred_element_type=jnp.float32)
    partial_z = jnp.einsum("vxyz,zc->vxyc", fields_next, z_factor, precision=hp)
    summed_z = lax.psum_scatter(partial_z, "gz", scatter_dimension=0, tiled=True)
    partial_x = jnp.einsum("vxyc,xa->vayc", summed_z, x_rows, precision=hp)
    summed_x = lax.psum_scatter(partial_x, "gx", scatter_dimension=1, tiled=True)
    partial_y = jnp.einsum("vayc,yb->vabc", summed_x, y_factor, precision=hp)
    core = lax.psum_scatter(partial_y, "gy", scatter_dimension=2, tiled=True)
    return (fields_next, core)


def solution(mesh):
    placed = (P(None, "gx", "gy", "gz"), P(), P(), P("gx"), P(), P("gy", None), P("gz", None))
    return jax.shard_map(
        local,
        mesh=mesh,
        in_specs=placed,
        out_specs=(P(None, "gx", "gy", "gz"), P("gz", "gx", "gy", None)),
        check_vma=False,
    )
```

profile of v0, /device:TPU:0, one launch (start us, length us, event | category | flops | bytes accessed | tf_op | source)
XLA Modules:
  0.0 261.3 jit_solution(5531175885518728344)
XLA Ops:
  7.2 1.1 fusion.96
  8.5 4.9 %collective-permute-start.1 = (f32[16,4,8,128]{3,0,2,1:T(8,128)S(1)}, f32[16,4,8,128]{3,0,2,1:T(8,128)S(1)}, u32[]{:S(2)}, u32[]{:S(2)}) collective-permute-start(f32[16,4,8,128]{3,0,2,1:T(8,128)S(1)} %copy.54), channel_id=1, source_target_pairs={{0,8},{8,16},{16,24},{1,9},{9,17},{17,25},{2,10},{10,18},{18,26},{... | collective-permute-start | bytes 786440 | tf_op jit(solution)/shard_map/ppermute | solution.py:18
  13.6 1.3 collective-permute-start
  14.9 4.1 %collective-permute-done.1 = f32[16,4,8,128]{3,0,2,1:T(8,128)S(1)} collective-permute-done((f32[16,4,8,128]{3,0,2,1:T(8,128)S(1)}, f32[16,4,8,128]{3,0,2,1:T(8,128)S(1)}, u32[]{:S(2)}, u32[]{:S(2)}) %collective-permute-start.1) | collective-permute-done | bytes 262176 | tf_op jit(solution)/shard_map/ppermute | solution.py:18
  19.5 7.0 %collective-permute-done = f32[16,4,8,128]{3,0,2,1:T(8,128)S(1)} collective-permute-done((f32[16,4,8,128]{3,0,2,1:T(8,128)S(1)}, f32[16,4,8,128]{3,0,2,1:T(8,128)S(1)}, u32[]{:S(2)}, u32[]{:S(2)}) %collective-permute-start) | collective-permute-done | bytes 262176 | tf_op jit(solution)/shard_map/ppermute | solution.py:20
  26.6 1.0 copy-done.16
  27.6 1.3 collective-permute-start.3
  29.0 1.3 collective-permute-start.2
  30.6 2.3 collective-permute-done.2
  33.0 0.9 copy-done.15
  34.1 2.4 fusion.92
  36.5 4.5 %copy.27 = f32[16,20,16,4]{1,2,3,0:T(8,128)} copy(f32[16,20,16,4]{3,0,2,1:T(8,128)} %get-tuple-element.9) | data formatting | bytes 163840 | tf_op jit(solution)/shard_map/slice | solution.py:15
  41.0 4.4 %collective-permute-start.5 = (f32[16,20,16,4]{1,2,3,0:T(8,128)}, f32[16,20,16,4]{1,2,3,0:T(8,128)}, u32[]{:S(2)}, u32[]{:S(2)}) collective-permute-start(f32[16,20,16,4]{1,2,3,0:T(8,128)} %copy.27), channel_id=1, source_target_pairs={{0,1},{1,2},{2,3},{4,5},{5,6},{6,7},{8,9},{9,10},{10,11},{12,13},{... | collective-permute-start | bytes 245768 | tf_op jit(solution)/shard_map/ppermute | solution.py:18
  45.4 3.1 %copy.25 = f32[16,20,16,4]{1,2,3,0:T(8,128)} copy(f32[16,20,16,4]{3,0,2,1:T(8,128)S(1)} %get-tuple-element.8) | data formatting | bytes 163840 | tf_op jit(solution)/shard_map/slice | solution.py:14
  48.5 1.5 collective-permute-start.4
  50.0 6.4 %collective-permute-done.5 = f32[16,20,16,4]{1,2,3,0:T(8,128)} collective-permute-done((f32[16,20,16,4]{1,2,3,0:T(8,128)}, f32[16,20,16,4]{1,2,3,0:T(8,128)}, u32[]{:S(2)}, u32[]{:S(2)}) %collective-permute-start.5) | collective-permute-done | bytes 81952 | tf_op jit(solution)/shard_map/ppermute | solution.py:18
  56.4 5.0 %copy.28 = f32[16,20,16,4]{3,0,2,1:T(8,128)} copy(f32[16,20,16,4]{1,2,3,0:T(8,128)} %collective-permute-done.5) | data formatting | bytes 163840 | tf_op jit(solution)/shard_map/ppermute | solution.py:18
  61.4 2.9 %collective-permute-done.4 = f32[16,20,16,4]{1,2,3,0:T(8,128)S(1)} collective-permute-done((f32[16,20,16,4]{1,2,3,0:T(8,128)}, f32[16,20,16,4]{1,2,3,0:T(8,128)S(1)}, u32[]{:S(2)}, u32[]{:S(2)}) %collective-permute-start.4) | collective-permute-done | bytes 81952 | tf_op jit(solution)/shard_map/ppermute | solution.py:20
  64.3 4.0 %copy.26 = f32[16,20,16,4]{3,0,2,1:T(8,128)} copy(f32[16,20,16,4]{1,2,3,0:T(8,128)S(1)} %collective-permute-done.4) | data formatting | bytes 163840 | tf_op jit(solution)/shard_map/ppermute | solution.py:20
  68.3 9.1 %fusion.9 = f32[16,12,8,128]{3,0,2,1:T(8,128)S(1)} fusion(f32[16,20,8,128]{3,0,2,1:T(8,128)S(1)} %copy-done.2, f32[16,20,4,128]{3,0,2,1:T(8,128)} %copy-done.14, f32[16,20,4,128]{3,0,2,1:T(8,128)} %copy-done.15, f32[16,20,16,4]{3,0,2,1:T(8,128)} %copy.28, f32[16,20,16,4]{3,0,2,1:T(8,128)} %copy.26, f32[16,16,8,128]{3,0,2,1:T(8,128)} %copy-done.17, ...), kind=kOutput, calls=%fused_computation.35 | convolution fusion | flops 52101120 | bytes 11445760 | tf_op jit(solution)/shard_map/vw,wxyz->vxyz/dot_general | solution.py:41
  77.5 3.4 %collective-permute-start.7 = (f32[16,4,8,128]{3,0,2,1:T(8,128)S(1)}, f32[16,4,8,128]{3,0,2,1:T(8,128)S(1)}, u32[]{:S(2)}, u32[]{:S(2)}) collective-permute-start(f32[16,4,8,128]{3,0,2,1:T(8,128)S(1)} %get-tuple-element.17), channel_id=1, source_target_pairs={{0,8},{8,16},{16,24},{1,9},{9,17},{17,25},{2,10},{10,18},{18,26},{... | collective-permute-start | bytes 786440 | tf_op jit(solution)/shard_map/ppermute | solution.py:18
  80.9 1.3 collective-permute-start.6
  82.2 3.4 %collective-permute-done.7 = f32[16,4,8,128]{3,0,2,1:T(8,128)S(1)} collective-permute-done((f32[16,4,8,128]{3,0,2,1:T(8,128)S(1)}, f32[16,4,8,128]{3,0,2,1:T(8,128)S(1)}, u32[]{:S(2)}, u32[]{:S(2)}) %collective-permute-start.7) | collective-permute-done | bytes 262176 | tf_op jit(solution)/shard_map/ppermute | solution.py:18
  85.6 6.4 %collective-permute-done.6 = f32[16,4,8,128]{3,0,2,1:T(8,128)S(1)} collective-permute-done((f32[16,4,8,128]{3,0,2,1:T(8,128)S(1)}, f32[16,4,8,128]{3,0,2,1:T(8,128)S(1)}, u32[]{:S(2)}, u32[]{:S(2)}) %collective-permute-start.6) | collective-permute-done | bytes 262176 | tf_op jit(solution)/shard_map/ppermute | solution.py:20
  92.1 1.3 collective-permute-start.8
  93.4 3.1 %collective-permute-start.9 = (f32[16,20,4,128]{3,0,2,1:T(8,128)S(1)}, f32[16,20,4,128]{3,0,2,1:T(8,128)S(1)}, u32[]{:S(2)}, u32[]{:S(2)}) collective-permute-start(f32[16,20,4,128]{3,0,2,1:T(8,128)S(1)} %get-tuple-element.12), channel_id=1, source_target_pairs={{0,4},{1,5},{2,6},{3,7},{8,12},{9,13},{10,14},{11,15},{16,20},{17,... | collective-permute-start | bytes 1966088 | tf_op jit(solution)/shard_map/ppermute | solution.py:18
  96.6 1.6 collective-permute-done.9
  99.3 2.4 fusion.91
  101.7 4.5 %copy.33 = f32[16,20,16,4]{1,2,3,0:T(8,128)} copy(f32[16,20,16,4]{3,0,2,1:T(8,128)} %get-tuple-element.7) | data formatting | bytes 163840 | tf_op jit(solution)/shard_map/slice | solution.py:15
  106.2 3.5 %collective-permute-start.11 = (f32[16,20,16,4]{1,2,3,0:T(8,128)}, f32[16,20,16,4]{1,2,3,0:T(8,128)}, u32[]{:S(2)}, u32[]{:S(2)}) collective-permute-start(f32[16,20,16,4]{1,2,3,0:T(8,128)} %copy.33), channel_id=1, source_target_pairs={{0,1},{1,2},{2,3},{4,5},{5,6},{6,7},{8,9},{9,10},{10,11},{12,13},{... | collective-permute-start | bytes 245768 | tf_op jit(solution)/shard_map/ppermute | solution.py:18
  109.7 3.1 %copy.31 = f32[16,20,16,4]{1,2,3,0:T(8,128)} copy(f32[16,20,16,4]{3,0,2,1:T(8,128)S(1)} %get-tuple-element.6) | data formatting | bytes 163840 | tf_op jit(solution)/shard_map/slice | solution.py:14
  112.8 1.5 collective-permute-start.10
  114.3 4.1 %pad_maximum_fusion.2 = (f32[16,20,12,128]{3,0,2,1:T(8,128)}, f32[16,20,12,128]{3,0,2,1:T(8,128)}) fusion(f32[16,20,4,128]{3,0,2,1:T(8,128)} %copy-done.4, f32[16,4,8,128]{3,0,2,1:T(8,128)} %copy-done.10, f32[16,12,8,128]{3,0,2,1:T(8,128)S(1)} %fusion.9, f32[16,4,8,128]{3,0,2,1:T(8,128)} %copy-done.8, f32[16,20,4,128]{3,0,2,1:T(8,128)} %copy-done.6), kind=kLoop, calls=%fused_computation.14 | loop fusion | flops 2949120 | bytes 6553600 | tf_op jit(solution)/shard_map/concatenate | solution.py:16
  118.4 2.6 collective-permute-done.11
  120.9 5.0 %copy.34 = f32[16,20,16,4]{3,0,2,1:T(8,128)} copy(f32[16,20,16,4]{1,2,3,0:T(8,128)} %collective-permute-done.11) | data formatting | bytes 163840 | tf_op jit(solution)/shard_map/ppermute | solution.py:18
  125.9 3.0 %collective-permute-done.10 = f32[16,20,16,4]{1,2,3,0:T(8,128)} collective-permute-done((f32[16,20,16,4]{1,2,3,0:T(8,128)}, f32[16,20,16,4]{1,2,3,0:T(8,128)}, u32[]{:S(2)}, u32[]{:S(2)}) %collective-permute-start.10) | collective-permute-done | bytes 81952 | tf_op jit(solution)/shard_map/ppermute | solution.py:20
  128.9 5.0 %copy.32 = f32[16,20,16,4]{3,0,2,1:T(8,128)} copy(f32[16,20,16,4]{1,2,3,0:T(8,128)} %collective-permute-done.10) | data formatting | bytes 163840 | tf_op jit(solution)/shard_map/ppermute | solution.py:20
  133.9 10.1 %fusion.5 = f32[16,12,8,128]{3,0,2,1:T(8,128)S(1)} fusion(f32[16,12,8,128]{3,0,2,1:T(8,128)S(1)} %fusion.9, f32[16,4,8,128]{3,0,2,1:T(8,128)S(1)} %copy-done.9, f32[16,4,8,128]{3,0,2,1:T(8,128)S(1)} %copy-done.11, f32[16,20,16,4]{3,0,2,1:T(8,128)} %copy.34, f32[16,20,4,128]{3,0,2,1:T(8,128)S(1)} %copy-done.5, f32[16,20,4,128]{3,0,2,1:T(8,128)S(1)} %copy-done.7, ...), kind=kOutput, calls=%fused_computation.31 | convolution fusion | flops 55640064 | bytes 11445760 | tf_op jit(solution)/shard_map/vw,wxyz->vxyz/dot_general | solution.py:41
  144.3 0.9 copy-done.3
  145.2 1.6 fusion.83
  147.1 19.9 %reduce-scatter.4.cloned.1.call-done = f32[4,12,8,54]{3,2,1,0:T(8,128)} async-done(((f32[16,12,8,54]{3,2,1,0:T(8,128)}), f32[4,12,8,54]{3,2,1,0:T(8,128)}) %reduce-scatter.4.cloned.1.call-update) | async-done | bytes 82960 | tf_op jit(solution)/shard_map/reduce_scatter | solution.py:66
  167.0 2.6 fusion.81
  169.6 1.7 copy.42
  172.7 59.0 %all-reduce.3.cloned.1.call-done = f32[4,96,8,54]{3,2,1,0:T(8,128)} async-done(((f32[4,96,8,54]{3,2,1,0:T(8,128)}), f32[4,96,8,54]{3,2,1,0:T(8,128)}) %all-reduce.3.cloned.1.call-update) | async-done | bytes 663568
  231.7 5.5 %convolution_bitcast_fusion = f32[4,24,64,54]{2,3,1,0:T(8,128)S(1)} fusion(f32[4,96,8,54]{3,2,1,0:T(8,128)} %all-reduce.3.cloned.1.call-done, u32[]{:T(128)S(6)} %multiply.1, f32[8,64]{1,0:T(8,128)S(1)} %copy-done.18), kind=kOutput, calls=%fused_computation.16 | convolution fusion | flops 31850496 | bytes 1722372 | tf_op jit(solution)/shard_map/vayc,yb->vabc/dot_general | solution.py:69
  237.2 2.7 %copy.35 = f32[4,24,64,54]{3,1,0,2:T(8,128)} copy(f32[4,24,64,54]{2,3,1,0:T(8,128)S(1)} %convolution_bitcast_fusion) | data formatting | bytes 2654208 | tf_op jit(solution)/shard_map/vayc,yb->vabc/transpose | solution.py:69
  240.0 11.3 %reduce-scatter.6.cloned.1.call-done = f32[4,24,32,54]{3,1,0,2:T(8,128)} async-done(((f32[4,24,64,54]{3,1,0,2:T(8,128)}), f32[4,24,32,54]{3,1,0,2:T(8,128)}) %reduce-scatter.6.cloned.1.call-update) | async-done | bytes 663568 | tf_op jit(solution)/shard_map/reduce_scatter | solution.py:70
  251.3 3.5 %copy.37 = f32[4,24,32,54]{3,2,1,0:T(8,128)} copy(f32[4,24,32,54]{3,1,0,2:T(8,128)} %reduce-scatter.6.cloned.1.call-done) | data formatting | bytes 1327104
  (68 shorter events, 4.4 us)
Async XLA Ops:
  7.2 138.0 %copy-start = (f32[128,54]{0,1:T(8,128)S(1)}, f32[128,54]{0,1:T(8,128)}, u32[]{:S(2)}) copy-start(f32[128,54]{0,1:T(8,128)} %param.13) | copy-start | bytes 82948
  7.2 11.8 %copy-start.12 = (f32[16,12,8,128]{3,2,1,0:T(8,128)S(1)}, f32[16,12,8,128]{3,2,1,0:T(8,128)}, u32[]{:S(2)}) copy-start(f32[16,12,8,128]{3,2,1,0:T(8,128)} %param.7) | copy-start | bytes 2359300
  7.2 159.8 %reduce-scatter.4.cloned.1.call-start = ((), (), s32[]{:S(2)}) async-start(), calls=%async_computation.2 | async-start | bytes 983040 | tf_op jit(solution)/shard_map/reduce_scatter | solution.py:66
  8.5 10.4 %collective-permute-start.1 = (f32[16,4,8,128]{3,0,2,1:T(8,128)S(1)}, f32[16,4,8,128]{3,0,2,1:T(8,128)S(1)}, u32[]{:S(2)}, u32[]{:S(2)}) collective-permute-start(f32[16,4,8,128]{3,0,2,1:T(8,128)S(1)} %copy.54), channel_id=1, source_target_pairs={{0,8},{8,16},{16,24},{1,9},{9,17},{17,25},{2,10},{10,18},{18,26},{... | collective-permute-start | bytes 786440 | tf_op jit(solution)/shard_map/ppermute | solution.py:18
  13.6 12.9 %collective-permute-start = (f32[16,4,8,128]{3,0,2,1:T(8,128)S(1)}, f32[16,4,8,128]{3,0,2,1:T(8,128)S(1)}, u32[]{:S(2)}, u32[]{:S(2)}) collective-permute-start(f32[16,4,8,128]{3,0,2,1:T(8,128)S(1)} %copy.55), channel_id=1, source_target_pairs={{8,0},{16,8},{24,16},{9,1},{17,9},{25,17},{10,2},{18,10},{26,18},{... | collective-permute-start | bytes 786440 | tf_op jit(solution)/shard_map/ppermute | solution.py:20
  19.5 11.1 %copy-start.17 = (f32[16,16,8,128]{3,0,2,1:T(8,128)}, f32[16,16,8,128]{3,0,2,1:T(8,128)S(1)}, u32[]{:S(2)}) copy-start(f32[16,16,8,128]{3,0,2,1:T(8,128)S(1)} %get-tuple-element.20) | copy-start | bytes 3145732
  26.6 1.0 copy-start.16
  27.5 5.4 %copy-start.1 = (f32[16,20,8,128]{3,0,2,1:T(8,128)}, f32[16,20,8,128]{3,0,2,1:T(8,128)S(1)}, u32[]{:S(2)}) copy-start(f32[16,20,8,128]{3,0,2,1:T(8,128)S(1)} %get-tuple-element.24) | copy-start | bytes 3932164
  27.6 3.0 %collective-permute-start.3 = (f32[16,20,4,128]{3,0,2,1:T(8,128)S(1)}, f32[16,20,4,128]{3,0,2,1:T(8,128)S(1)}, u32[]{:S(2)}, u32[]{:S(2)}) collective-permute-start(f32[16,20,4,128]{3,0,2,1:T(8,128)S(1)} %get-tuple-element.15), channel_id=1, source_target_pairs={{0,4},{1,5},{2,6},{3,7},{8,12},{9,13},{10,14},{11,15},{16,20},{17,... | collective-permute-start | bytes 1966088 | tf_op jit(solution)/shard_map/ppermute | solution.py:18
  29.0 4.0 %collective-permute-start.2 = (f32[16,20,4,128]{3,0,2,1:T(8,128)S(1)}, f32[16,20,4,128]{3,0,2,1:T(8,128)S(1)}, u32[]{:S(2)}, u32[]{:S(2)}) collective-permute-start(f32[16,20,4,128]{3,0,2,1:T(8,128)S(1)} %get-tuple-element.14), channel_id=1, source_target_pairs={{4,0},{5,1},{6,2},{7,3},{12,8},{13,9},{14,10},{15,11},{20,16},{21,... | collective-permute-start | bytes 1966088 | tf_op jit(solution)/shard_map/ppermute | solution.py:20
  30.6 2.3 copy-start.14
  33.0 0.9 copy-start.15
  41.0 9.0 %copy-start.19 = (f32[3,16]{1,0:T(4,128)S(1)}, f32[3,16]{1,0:T(4,128)}, u32[]{:S(2)}) copy-start(f32[3,16]{1,0:T(4,128)} %param.8) | copy-start | bytes 580
  41.0 15.4 %collective-permute-start.5 = (f32[16,20,16,4]{1,2,3,0:T(8,128)}, f32[16,20,16,4]{1,2,3,0:T(8,128)}, u32[]{:S(2)}, u32[]{:S(2)}) collective-permute-start(f32[16,20,16,4]{1,2,3,0:T(8,128)} %copy.27), channel_id=1, source_target_pairs={{0,1},{1,2},{2,3},{4,5},{5,6},{6,7},{8,9},{9,10},{10,11},{12,13},{... | collective-permute-start | bytes 245768 | tf_op jit(solution)/shard_map/ppermute | solution.py:18
  48.5 15.8 %collective-permute-start.4 = (f32[16,20,16,4]{1,2,3,0:T(8,128)}, f32[16,20,16,4]{1,2,3,0:T(8,128)S(1)}, u32[]{:S(2)}, u32[]{:S(2)}) collective-permute-start(f32[16,20,16,4]{1,2,3,0:T(8,128)} %copy.25), channel_id=1, source_target_pairs={{1,0},{2,1},{3,2},{5,4},{6,5},{7,6},{9,8},{10,9},{11,10},{13,12},{... | collective-permute-start | bytes 245768 | tf_op jit(solution)/shard_map/ppermute | solution.py:20
  61.4 6.9 %copy-start.2 = (f32[16,20,8,128]{3,0,2,1:T(8,128)S(1)}, f32[16,20,8,128]{3,0,2,1:T(8,128)}, u32[]{:S(2)}) copy-start(f32[16,20,8,128]{3,0,2,1:T(8,128)} %copy-done.1) | copy-start | bytes 3932164
  61.4 6.9 %copy-start.21 = (f32[16,16]{1,0:T(8,128)S(1)}, f32[16,16]{1,0:T(8,128)}, u32[]{:S(2)}) copy-start(f32[16,16]{1,0:T(8,128)} %param.9) | copy-start | bytes 3076
  77.5 8.1 %collective-permute-start.7 = (f32[16,4,8,128]{3,0,2,1:T(8,128)S(1)}, f32[16,4,8,128]{3,0,2,1:T(8,128)S(1)}, u32[]{:S(2)}, u32[]{:S(2)}) collective-permute-start(f32[16,4,8,128]{3,0,2,1:T(8,128)S(1)} %get-tuple-element.17), channel_id=1, source_target_pairs={{0,8},{8,16},{16,24},{1,9},{9,17},{17,25},{2,10},{10,18},{18,26},{... | collective-permute-start | bytes 786440 | tf_op jit(solution)/shard_map/ppermute | solution.py:18
  80.9 11.1 %collective-permute-start.6 = (f32[16,4,8,128]{3,0,2,1:T(8,128)S(1)}, f32[16,4,8,128]{3,0,2,1:T(8,128)S(1)}, u32[]{:S(2)}, u32[]{:S(2)}) collective-permute-start(f32[16,4,8,128]{3,0,2,1:T(8,128)S(1)} %get-tuple-element.16), channel_id=1, source_target_pairs={{8,0},{16,8},{24,16},{9,1},{17,9},{25,17},{10,2},{18,10},{26,18},{... | collective-permute-start | bytes 786440 | tf_op jit(solution)/shard_map/ppermute | solution.py:20
  85.6 12.7 %copy-start.8 = (f32[16,4,8,128]{3,0,2,1:T(8,128)}, f32[16,4,8,128]{3,0,2,1:T(8,128)S(1)}, u32[]{:S(2)}) copy-start(f32[16,4,8,128]{3,0,2,1:T(8,128)S(1)} %collective-permute-done.7) | copy-start | bytes 786436
  91.9 6.3 %copy-start.10 = (f32[16,4,8,128]{3,0,2,1:T(8,128)}, f32[16,4,8,128]{3,0,2,1:T(8,128)S(1)}, u32[]{:S(2)}) copy-start(f32[16,4,8,128]{3,0,2,1:T(8,128)S(1)} %collective-permute-done.6) | copy-start | bytes 786436
  92.1 4.4 %collective-permute-start.8 = (f32[16,20,4,128]{3,0,2,1:T(8,128)S(1)}, f32[16,20,4,128]{3,0,2,1:T(8,128)S(1)}, u32[]{:S(2)}, u32[]{:S(2)}) collective-permute-start(f32[16,20,4,128]{3,0,2,1:T(8,128)S(1)} %get-tuple-element.13), channel_id=1, source_target_pairs={{4,0},{5,1},{6,2},{7,3},{12,8},{13,9},{14,10},{15,11},{20,16},{21,... | collective-permute-start | bytes 1966088 | tf_op jit(solution)/shard_map/ppermute | solution.py:20
  93.4 4.8 %collective-permute-start.9 = (f32[16,20,4,128]{3,0,2,1:T(8,128)S(1)}, f32[16,20,4,128]{3,0,2,1:T(8,128)S(1)}, u32[]{:S(2)}, u32[]{:S(2)}) collective-permute-start(f32[16,20,4,128]{3,0,2,1:T(8,128)S(1)} %get-tuple-element.12), channel_id=1, source_target_pairs={{0,4},{1,5},{2,6},{3,7},{8,12},{9,13},{10,14},{11,15},{16,20},{17,... | collective-permute-start | bytes 1966088 | tf_op jit(solution)/shard_map/ppermute | solution.py:18
  96.6 1.7 copy-start.4
  98.2 0.8 copy-start.6
  106.2 14.7 %collective-permute-start.11 = (f32[16,20,16,4]{1,2,3,0:T(8,128)}, f32[16,20,16,4]{1,2,3,0:T(8,128)}, u32[]{:S(2)}, u32[]{:S(2)}) collective-permute-start(f32[16,20,16,4]{1,2,3,0:T(8,128)} %copy.33), channel_id=1, source_target_pairs={{0,1},{1,2},{2,3},{4,5},{5,6},{6,7},{8,9},{9,10},{10,11},{12,13},{... | collective-permute-start | bytes 245768 | tf_op jit(solution)/shard_map/ppermute | solution.py:18
  112.8 16.1 %collective-permute-start.10 = (f32[16,20,16,4]{1,2,3,0:T(8,128)}, f32[16,20,16,4]{1,2,3,0:T(8,128)}, u32[]{:S(2)}, u32[]{:S(2)}) collective-permute-start(f32[16,20,16,4]{1,2,3,0:T(8,128)} %copy.31), channel_id=1, source_target_pairs={{1,0},{2,1},{3,2},{5,4},{6,5},{7,6},{9,8},{10,9},{11,10},{13,12},{... | collective-permute-start | bytes 245768 | tf_op jit(solution)/shard_map/ppermute | solution.py:20
  125.9 8.0 %copy-start.5 = (f32[16,20,4,128]{3,0,2,1:T(8,128)S(1)}, f32[16,20,4,128]{3,0,2,1:T(8,128)}, u32[]{:S(2)}) copy-start(f32[16,20,4,128]{3,0,2,1:T(8,128)} %copy-done.4) | copy-start | bytes 1966084
  125.9 8.0 %copy-start.7 = (f32[16,20,4,128]{3,0,2,1:T(8,128)S(1)}, f32[16,20,4,128]{3,0,2,1:T(8,128)}, u32[]{:S(2)}) copy-start(f32[16,20,4,128]{3,0,2,1:T(8,128)} %copy-done.6) | copy-start | bytes 1966084
  125.9 8.0 %copy-start.9 = (f32[16,4,8,128]{3,0,2,1:T(8,128)S(1)}, f32[16,4,8,128]{3,0,2,1:T(8,128)}, u32[]{:S(2)}) copy-start(f32[16,4,8,128]{3,0,2,1:T(8,128)} %copy-done.8) | copy-start | bytes 786436
  125.9 8.0 %copy-start.11 = (f32[16,4,8,128]{3,0,2,1:T(8,128)S(1)}, f32[16,4,8,128]{3,0,2,1:T(8,128)}, u32[]{:S(2)}) copy-start(f32[16,4,8,128]{3,0,2,1:T(8,128)} %copy-done.10) | copy-start | bytes 786436
  125.9 8.0 %copy-start.13 = (f32[16,12,8,128]{3,2,1,0:T(8,128)S(1)}, f32[16,12,8,128]{3,2,1,0:T(8,128)}, u32[]{:S(2)}) copy-start(f32[16,12,8,128]{3,2,1,0:T(8,128)} %param.7) | copy-start | bytes 2359300
  144.0 2.9 %copy-start.20 = (f32[48,96]{1,0:T(8,128)S(1)}, f32[48,96]{1,0:T(8,128)}, u32[]{:S(2)}) copy-start(f32[48,96]{1,0:T(8,128)} %param.11) | copy-start | bytes 55300
  144.0 2.9 %copy-start.22 = (s32[12]{0:T(128)S(1)}, s32[12]{0:T(128)}, u32[]{:S(2)}) copy-start(s32[12]{0:T(128)} %param.10) | copy-start | bytes 148
  144.3 0.9 copy-start.3
  146.8 84.8 %all-reduce.3.cloned.1.call-start = ((), (), s32[]{:S(2)}) async-start(), calls=%async_computation.4 | async-start | bytes 3145728
  169.6 2.0 copy-start.23
  169.6 62.1 %copy-start.18 = (f32[8,64]{1,0:T(8,128)S(1)}, f32[8,64]{1,0:T(8,128)}, u32[]{:S(2)}) copy-start(f32[8,64]{1,0:T(8,128)} %param.12) | copy-start | bytes 6148
  171.3 80.0 %reduce-scatter.6.cloned.1.call-start = ((), (), s32[]{:S(2)}) async-start(), calls=%async_computation.3 | async-start | bytes 4718592 | tf_op jit(solution)/shard_map/reduce_scatter | solution.py:70
Sparse Core Ops, SparseCore 0:
  147.0 19.9 reduce-scatter.3
  171.4 60.2 all-reduce.2
  240.1 11.1 reduce-scatter.5
where the time goes:
time: 262 us; the launch traced here: 261 us
  waiting for transfers between devices  130 us (50%)
  local copies, waits for them, and re-layouts  53.5 us (20%)
  starting transfers between devices  29.1 us (11%)
  matrix products  29.1 us (11%)
  between operations  14.7 us (6%)
  other arithmetic  4.66 us (2%)
    unnamed x4, waiting for transfers between devices  59 us
    ppermute x6, waiting for transfers between devices, with_halo(): lax.ppermute(head, axis, [((i + 1) % count, i) for i in range(ends)])  21.6 us
    ppermute x6, starting transfers between devices, with_halo(): lax.ppermute(tail, axis, [(i, (i + 1) % count) for i in range(ends)])  20.6 us
    reduce_scatter x1, waiting for transfers between devices, local(): lax.psum_scatter(partial_z, 'gz', scatter_dimension=0, tiled=True)  19.9 us
    dot_general x2, matrix products, tendency(): jnp.einsum('vw,wxyz->vxyz', kinetics, center, precision=lax.Precision.HIG...  19.2 us
    ppermute x6, waiting for transfers between devices, with_halo(): lax.ppermute(tail, axis, [(i, (i + 1) % count) for i in range(ends)])  18.4 us
    slice x7, local copies, waits for them, and re-layouts, with_halo(): head = lax.slice_in_dim(cells, 0, width, axis=dim)  12.2 us
    reduce_scatter x1, waiting for transfers between devices, local(): core = lax.psum_scatter(partial_y, 'gy', scatter_dimension=2, tiled=True)  11.3 us
  transfers between devices with their start and end apart: 15, of which 14 were waited for; matrix products, arithmetic and copies ran while one was open for 8% of the time, Pallas kernels for 0%

commit v1 on v0

v1 whole, which is shorter than its diff:
```python
import functools

import jax
import jax.numpy as jnp
import numpy as np
from jax import lax
from jax.experimental import pallas as pl
from jax.experimental.pallas import tpu as pltpu
from jax.sharding import PartitionSpec as P

COEFFS = (0.8, -0.2, 4.0 / 105.0, -1.0 / 280.0)
TIME_STEP = 0.45
REACH = len(COEFFS)
HALF = 64
HIGHEST = lax.Precision.HIGHEST
VMEM = pl.BlockSpec(memory_space=pltpu.VMEM)
SMEM = pl.BlockSpec(memory_space=pltpu.SMEM)


def call(kernel, out_shapes, in_specs, args, scratch=()):
    return pl.pallas_call(
        kernel,
        out_shape=tuple(jax.ShapeDtypeStruct(s, d) for s, d in out_shapes),
        in_specs=in_specs,
        out_specs=tuple(VMEM for _ in out_shapes),
        scratch_shapes=list(scratch),
        compiler_params=pltpu.CompilerParams(vmem_limit_bytes=56 * 2**20),
    )(*args)


def pack_z(v, values, rim_ref):
    lane = lax.broadcasted_iota(jnp.int32, values.shape, 2)
    width = values.shape[2]
    last = pltpu.roll(values, REACH * v + REACH, 2)
    first = pltpu.roll(values, width // 2 + REACH * v, 2)
    rim = rim_ref[...]
    rim = jnp.where(lane // REACH == v, last, rim)
    rim = jnp.where(lane // REACH == v + width // 2 // REACH, first, rim)
    rim_ref[...] = rim


def split_rims(v, values, low_ref, high_ref, rim_ref):
    low_ref[v] = values[:REACH]
    high_ref[v] = values[values.shape[0] - REACH :]
    pack_z(v, values, rim_ref)


def pack_kernel(f_ref, low_ref, high_ref, rim_ref):
    rim_ref[...] = jnp.zeros_like(rim_ref)

    def step(v, carry):
        split_rims(v, f_ref[v], low_ref, high_ref, rim_ref)
        return carry

    lax.fori_loop(0, f_ref.shape[0], step, 0)


def tendency_of(v, q_ref, xl_ref, xh_ref, yl_ref, yh_ref, rim_ref, dz_ref, kin_ref, speed_ref, edge_ref):
    nvars, nx, ny, nz = q_ref.shape
    q = q_ref[v]
    total = kin_ref[v, 0] * q_ref[0]
    for w in range(1, nvars):
        total = total + kin_ref[v, w] * q_ref[w]
    tall = jnp.concatenate([xl_ref[v], q, xh_ref[v]], axis=0)
    below = yl_ref[v] * edge_ref[0]
    above = yh_ref[v] * edge_ref[1]
    row = lax.broadcasted_iota(jnp.int32, q.shape, 1)
    for k in range(1, REACH + 1):
        sx = speed_ref[0, v] * COEFFS[k - 1]
        total = total - sx * (tall[REACH + k : REACH + k + nx] - tall[REACH - k : REACH - k + nx])
        ahead = pltpu.roll(jnp.where(row < k, above, q), ny - k, 1)
        behind = pltpu.roll(jnp.where(row >= ny - k, below, q), k, 1)
        total = total - (speed_ref[1, v] * COEFFS[k - 1]) * (ahead - behind)
    rims = pltpu.roll(rim_ref[...].reshape(nx * ny, nz), lax.rem(nz - REACH * v, nz), 1)
    pair = jnp.concatenate([q.reshape(nx * ny, nz), rims], axis=1)
    gz = jnp.dot(pair, dz_ref[...], precision=HIGHEST, preferred_element_type=jnp.float32)
    return total - speed_ref[2, v] * gz.reshape(nx, ny, nz)


def join_rims(zl_ref, zh_ref, rim_ref):
    lane = lax.broadcasted_iota(jnp.int32, rim_ref.shape, 2)
    rim_ref[...] = jnp.where(lane < rim_ref.shape[2] // 2, zl_ref[...], zh_ref[...])


def section_kernel(
    f_ref, xl_ref, xh_ref, yl_ref, yh_ref, zl_ref, zh_ref, dz_ref, kin_ref, speed_ref, edge_ref,
    s_ref, low_ref, high_ref, out_rim_ref, rim_ref,
):
    join_rims(zl_ref, zh_ref, rim_ref)
    out_rim_ref[...] = jnp.zeros_like(out_rim_ref)

    def step(v, carry):
        rate = tendency_of(v, f_ref, xl_ref, xh_ref, yl_ref, yh_ref, rim_ref, dz_ref, kin_ref, speed_ref, edge_ref)
        s = f_ref[v] + TIME_STEP * rate
        s_ref[v] = s
        split_rims(v, s, low_ref, high_ref, out_rim_ref)
        return carry

    lax.fori_loop(0, f_ref.shape[0], step, 0)


def next_kernel(
    f_ref, s_ref, xl_ref, xh_ref, yl_ref, yh_ref, zl_ref, zh_ref, dz_ref, zf_ref, kin_ref, speed_ref, edge_ref,
    next_ref, proj_ref, rim_ref,
):
    nvars, nx, ny, nz = f_ref.shape
    join_rims(zl_ref, zh_ref, rim_ref)

    def step(p, carry):
        both = []
        for v in (2 * p, 2 * p + 1):
            rate = tendency_of(v, s_ref, xl_ref, xh_ref, yl_ref, yh_ref, rim_ref, dz_ref, kin_ref, speed_ref, edge_ref)
            new = 0.5 * (f_ref[v] + s_ref[v] + TIME_STEP * rate)
            next_ref[v] = new
            both.append(new.reshape(nx * ny, nz))
        pair = jnp.concatenate(both, axis=1)
        proj_ref[p] = jnp.dot(pair, zf_ref[...], precision=HIGHEST, preferred_element_type=jnp.float32)
        return carry

    lax.fori_loop(0, nvars // 2, step, 0)


def split_bf16(x):
    high = x.astype(jnp.bfloat16)
    return high, (x - high.astype(jnp.float32)).astype(jnp.bfloat16)


def factor_kernel(rank_ref, row_ref, xf_ref, yf_ref, high_ref, low_ref, xt_ref):
    width = rank_ref.shape[1]
    pick = lax.broadcasted_iota(jnp.int32, (xf_ref.shape[1], width), 0) == rank_ref[...]
    xt_ref[...] = jnp.dot(xf_ref[...], pick.astype(jnp.float32), precision=HIGHEST, preferred_element_type=jnp.float32)
    pick = lax.broadcasted_iota(jnp.int32, (yf_ref.shape[1], width), 0) == row_ref[...]
    yt = jnp.dot(yf_ref[...], pick.astype(jnp.float32), precision=HIGHEST, preferred_element_type=jnp.float32)
    ny = yt.shape[0]
    for a in range(xt_ref.shape[0]):
        high, low = split_bf16(xt_ref[a : a + 1, :] * yt)
        high_ref[a * ny : (a + 1) * ny, :] = high
        low_ref[a * ny : (a + 1) * ny, :] = low


def core_kernel(high_ref, low_ref, *refs):
    out_ref = refs[-1]
    pairs = refs[0].shape[0]
    rank = out_ref.shape[2]
    columns = [jnp.concatenate([r[p] for r in refs[:-1]], axis=0) for p in range(pairs)]
    high, low = split_bf16(jnp.concatenate(columns, axis=1))
    dot = functools.partial(jnp.dot, preferred_element_type=jnp.float32)
    result = dot(high_ref[...], high) + (dot(high_ref[...], low) + dot(low_ref[...], high))
    for v in range(2 * pairs):
        out_ref[v] = result[:, v * HALF : v * HALF + rank]


def shifted(x, axis, count, k):
    return lax.ppermute(x, axis, [(i, (i + k) % count) for i in range(count)])


def gathered(x, axis):
    count = lax.axis_size(axis)
    if count <= 4:
        return [x] + [shifted(x, axis, count, k) for k in range(1, count)]
    blocks = lax.all_gather(x, axis)
    return [blocks[k] for k in range(count)]


def both_ways(low, high, axis):
    ends = lax.axis_size(axis) - 1
    from_low = lax.ppermute(high, axis, [(i, i + 1) for i in range(ends)])
    from_high = lax.ppermute(low, axis, [(i + 1, i) for i in range(ends)])
    return from_low, from_high


def beside(block, axis):
    if lax.axis_size(axis) == 2:
        other = lax.ppermute(block, axis, [(0, 1), (1, 0)])
        return other, other
    return both_ways(block, block, axis)


def derivative_matrix(nz):
    matrix = np.zeros((2 * nz, nz), np.float32)
    for k in range(1, REACH + 1):
        for z in range(nz):
            for source, sign in ((z + k, 1.0), (z - k, -1.0)):
                if source >= nz:
                    source = nz + nz // 2 + source - nz
                elif source < 0:
                    source = nz + REACH + source
                matrix[source, z] += sign * COEFFS[k - 1]
    return matrix


def local(fields, speeds, kinetics, block_rank, x_factor, y_factor, z_factor):
    nvars, nx, ny, nz = fields.shape
    rank = z_factor.shape[1]
    gz = lax.axis_size("gz")
    f32, bf16 = jnp.float32, jnp.bfloat16
    rim = (nvars, REACH, ny, nz)
    plane = (nx, ny, nz)
    dz = jnp.asarray(derivative_matrix(nz))
    iy = lax.axis_index("gy")
    edges = jnp.stack([iy > 0, iy < lax.axis_size("gy") - 1]).astype(f32)

    low, high, packed = call(pack_kernel, [(rim, f32), (rim, f32), (plane, f32)], [VMEM], (fields,))
    yl, yh = beside(fields, "gy")
    xl, xh = both_ways(low, high, "gx")
    zl, zh = both_ways(packed, packed, "gz")
    section, low, high, packed = call(
        section_kernel,
        [(fields.shape, f32), (rim, f32), (rim, f32), (plane, f32)],
        [VMEM] * 8 + [SMEM] * 3,
        (fields, xl, xh, yl, yh, zl, zh, dz, kinetics, speeds, edges),
        [pltpu.VMEM(plane, f32)],
    )
    yl, yh = beside(section, "gy")
    xl, xh = both_ways(low, high, "gx")
    zl, zh = both_ways(packed, packed, "gz")
    zero = jnp.zeros((nz, HALF), f32)
    wide = jnp.pad(z_factor, ((0, 0), (0, HALF - rank)))
    zf = jnp.concatenate([jnp.concatenate([wide, zero], 1), jnp.concatenate([zero, wide], 1)], 0)
    fields_next, proj = call(
        next_kernel,
        [(fields.shape, f32), ((nvars // 2, nx * ny, 2 * HALF), f32)],
        [VMEM] * 10 + [SMEM] * 3,
        (fields, section, xl, xh, yl, yh, zl, zh, dz, zf, kinetics, speeds, edges),
        [pltpu.VMEM(plane, f32)],
    )

    ranks = jnp.stack(gathered(block_rank, "gx"))
    y_rows = jnp.concatenate(gathered(y_factor, "gy"), axis=0)
    blocks_y = lax.axis_size("gy")
    shape = (ranks.shape[0], blocks_y, nx, ny)
    rank_of = jnp.broadcast_to(ranks[:, None, :, None], shape).reshape(1, -1)
    row_ids = jnp.arange(blocks_y * ny, dtype=jnp.int32).reshape(1, blocks_y, 1, ny)
    row_of = jnp.broadcast_to(row_ids, shape).reshape(1, -1)
    a_count = x_factor.shape[1] // lax.axis_size("gx")
    b_count = y_factor.shape[1] // blocks_y
    xf = lax.dynamic_slice_in_dim(x_factor, lax.axis_index("gx") * a_count, a_count, 1).T
    yf = lax.dynamic_slice_in_dim(y_rows, iy * b_count, b_count, 1).T
    cells = rank_of.shape[1]
    q_high, q_low = call(
        factor_kernel,
        [((a_count * b_count, cells), bf16)] * 2,
        [VMEM] * 4,
        (rank_of, row_of, xf, yf),
        [pltpu.VMEM((a_count, cells), f32)],
    )

    pairs = nvars // 2 // gz
    chunks = proj.reshape(gz, pairs, nx * ny, 2 * HALF)
    iz = lax.axis_index("gz")
    own = lax.dynamic_index_in_dim(chunks, iz, 0, keepdims=False)
    for k in range(1, gz):
        piece = lax.dynamic_index_in_dim(chunks, lax.rem(iz + k, gz), 0, keepdims=False)
        own = own + shifted(piece, "gz", gz, k)
    parts = []
    for block in gathered(own, "gx"):
        parts += gathered(block, "gy")
    (core,) = call(
        core_kernel,
        [((2 * pairs, a_count * b_count, rank), f32)],
        [VMEM] * (2 + len(parts)),
        (q_high, q_low, *parts),
    )
    return fields_next, core.reshape(2 * pairs, a_count, b_count, rank)


def solution(mesh):
    placed = (P(None, "gx", "gy", "gz"), P(), P(), P("gx"), P(), P("gy", None), P("gz", None))
    return jax.shard_map(
        local,
        mesh=mesh,
        in_specs=placed,
        out_specs=(P(None, "gx", "gy", "gz"), P("gz", "gx", "gy", None)),
        check_vma=False,
    )
```

time: 262 us -> 91.6 us (0.35)
  waiting for transfers between devices: 130 us -> 15.3 us
  local copies, waits for them, and re-layouts: 53.5 us -> 7.81 us
  matrix products: 29.1 us -> 0 us
  Pallas kernels: 0 us -> 28.9 us
  between operations: 14.7 us -> 0.92 us
  starting transfers between devices: 29.1 us -> 35.8 us
    unnamed x4 -> x0, waiting for transfers between devices: 59 us -> none
    reduce_scatter x2 -> x0, waiting for transfers between devices: 31.2 us -> none  [the longest x1 19.9 us: local(): lax.psum_scatter(partial_z, 'gz', scatter_dimension=0, tiled=True)]
    dot_general x6 -> x0, matrix products: 29.1 us -> none  [the longest x2 19.2 us: tendency(): jnp.einsum('vw,wxyz->vxyz', kinetics, center, precision=lax.Precision.HIG...]
    pallas_call x0 -> x5, Pallas kernels: none -> 28.9 us  [call(): pl.pallas_call(kernel, out_shape=tuple((jax.ShapeDtypeStruct(s, d) for s,...]
    ppermute x12 -> x24, waiting for transfers between devices: 40 us -> 15.3 us  [the longest x14 8.1 us: shifted(): return lax.ppermute(x, axis, [(i, (i + k) % count) for i in range(count)])]
    slice x10 -> x0, local copies, waits for them, and re-layouts: 21.3 us -> none  [the longest x7 12.2 us: with_halo(): head = lax.slice_in_dim(cells, 0, width, axis=dim)]
    ppermute x4 -> x0, local copies, waits for them, and re-layouts: 18.9 us -> none  [the longest x2 9.92 us: with_halo(): lax.ppermute(tail, axis, [(i, (i + 1) % count) for i in range(ends)])]
    ppermute x12 -> x24, starting transfers between devices: 28.8 us -> 35.8 us  [the longest x4 16.9 us: both_ways(): from_low = lax.ppermute(high, axis, [(i, i + 1) for i in range(ends)])]
  transfers between devices with their start and end apart: 15 -> 24, of which waited for: 14 -> 8; matrix products, arithmetic and copies ran while one was open for 8% -> 7% of each run, Pallas kernels for 0% -> 17%
where the time goes in v1:
time: 91.6 us; the launch traced here: 91.1 us
  starting transfers between devices  35.8 us (39%)
  Pallas kernels  28.9 us (32%)
  waiting for transfers between devices  15.3 us (17%)
  local copies, waits for them, and re-layouts  7.81 us (9%)
  other arithmetic  2.35 us (3%)
  between operations  0.92 us (1%)
    pallas_call x5, Pallas kernels, call(): pl.pallas_call(kernel, out_shape=tuple((jax.ShapeDtypeStruct(s, d) for s,...  28.9 us
    ppermute x4, starting transfers between devices, both_ways(): from_low = lax.ppermute(high, axis, [(i, i + 1) for i in range(ends)])  16.9 us
    ppermute x14, starting transfers between devices, shifted(): return lax.ppermute(x, axis, [(i, (i + k) % count) for i in range(count)])  13.2 us
    ppermute x14, waiting for transfers between devices, shifted(): return lax.ppermute(x, axis, [(i, (i + k) % count) for i in range(count)])  8.1 us
    ppermute x4, waiting for transfers between devices, both_ways(): from_high = lax.ppermute(low, axis, [(i + 1, i) for i in range(ends)])  5.75 us
    unnamed x47, local copies, waits for them, and re-layouts  5.29 us
    ppermute x4, starting transfers between devices, both_ways(): from_high = lax.ppermute(low, axis, [(i + 1, i) for i in range(ends)])  5.16 us
  transfers between devices with their start and end apart: 24, of which 8 were waited for; matrix products, arithmetic and copies ran while one was open for 7% of the time, Pallas kernels for 17%

profile of v1, /device:TPU:0, one launch (start us, length us, event | category | flops | bytes accessed | tf_op | source)
XLA Modules:
  0.0 91.1 jit_solution(8126065345538935023)
XLA Ops:
  0.6 0.6 collective-permute-start.2
  1.2 3.3 %shard_map.95 = (f32[16,4,8,128]{3,2,1,0:T(8,128)}, f32[16,4,8,128]{3,2,1,0:T(8,128)}, f32[12,8,128]{2,1,0:T(8,128)}) custom-call(f32[16,12,8,128]{3,2,1,0:T(8,128)} %f_ref.5), custom_call_target="tpu_custom_call" | custom-call | tf_op jit(solution)/shard_map/pallas_call | solution.py:21
  4.5 4.4 %collective-permute-start = (f32[16,4,8,128]{3,2,1,0:T(8,128)}, f32[16,4,8,128]{3,2,1,0:T(8,128)S(1)}, u32[]{:S(2)}, u32[]{:S(2)}) collective-permute-start(f32[16,4,8,128]{3,2,1,0:T(8,128)} %get-tuple-element.13), channel_id=1, source_target_pairs={{0,8},{8,16},{16,24},{1,9},{9,17},{17,25},{2,10},{10,18},{18,26},{... | collective-permute-start | bytes 786440 | tf_op jit(solution)/shard_map/ppermute | solution.py:167
  8.9 1.3 %collective-permute-start.1 = (f32[16,4,8,128]{3,2,1,0:T(8,128)}, f32[16,4,8,128]{3,2,1,0:T(8,128)S(1)}, u32[]{:S(2)}, u32[]{:S(2)}) collective-permute-start(f32[16,4,8,128]{3,2,1,0:T(8,128)} %get-tuple-element.14), channel_id=1, source_target_pairs={{8,0},{16,8},{24,16},{9,1},{17,9},{25,17},{10,2},{18,10},{26,18},{... | collective-permute-start | bytes 786440 | tf_op jit(solution)/shard_map/ppermute | solution.py:168
  10.2 1.3 %collective-permute-start.4 = (f32[12,8,128]{2,1,0:T(8,128)}, f32[12,8,128]{2,1,0:T(8,128)S(1)}, u32[]{:S(2)}, u32[]{:S(2)}) collective-permute-start(f32[12,8,128]{2,1,0:T(8,128)} %get-tuple-element.15), channel_id=1, source_target_pairs={{1,0},{2,1},{3,2},{5,4},{6,5},{7,6},{9,8},{10,9},{11,10},{13,12},{... | collective-permute-start | bytes 147464 | tf_op jit(solution)/shard_map/ppermute | solution.py:168
  11.5 4.5 %collective-permute-start.3 = (f32[12,8,128]{2,1,0:T(8,128)}, f32[12,8,128]{2,1,0:T(8,128)S(1)}, u32[]{:S(2)}, u32[]{:S(2)}) collective-permute-start(f32[12,8,128]{2,1,0:T(8,128)} %get-tuple-element.15), channel_id=1, source_target_pairs={{0,1},{1,2},{2,3},{4,5},{5,6},{6,7},{8,9},{9,10},{10,11},{12,13},{... | collective-permute-start | bytes 147464 | tf_op jit(solution)/shard_map/ppermute | solution.py:167
  16.1 0.6 add_convert_fusion.edge_ref
  16.7 1.4 %collective-permute-done.3.zl_ref = f32[12,8,128]{2,1,0:T(8,128)S(1)} collective-permute-done((f32[12,8,128]{2,1,0:T(8,128)}, f32[12,8,128]{2,1,0:T(8,128)S(1)}, u32[]{:S(2)}, u32[]{:S(2)}) %collective-permute-start.3) | collective-permute-done | bytes 49184 | tf_op jit(solution)/shard_map/ppermute | solution.py:167
  18.2 4.8 %collective-permute-done.1.xh_ref = f32[16,4,8,128]{3,2,1,0:T(8,128)S(1)} collective-permute-done((f32[16,4,8,128]{3,2,1,0:T(8,128)}, f32[16,4,8,128]{3,2,1,0:T(8,128)S(1)}, u32[]{:S(2)}, u32[]{:S(2)}) %collective-permute-start.1) | collective-permute-done | bytes 262176 | tf_op jit(solution)/shard_map/ppermute | solution.py:168
  22.9 0.7 copy-done.5
  23.6 0.9 copy-done.1
  24.5 9.4 %shard_map.96 = (f32[16,12,8,128]{3,2,1,0:T(8,128)}, f32[16,4,8,128]{3,2,1,0:T(8,128)}, f32[16,4,8,128]{3,2,1,0:T(8,128)}, f32[12,8,128]{2,1,0:T(8,128)}) custom-call(f32[16,12,8,128]{3,2,1,0:T(8,128)} %f_ref.5, f32[16,4,8,128]{3,2,1,0:T(8,128)} %copy-done.4, f32[16,4,8,128]{3,2,1,0:T(8,128)} %copy-done.5, f32[16,12,8,128]{3,2,1,0:T(8,128)} %copy-done.1, ...), custom_call_target="tpu_custom_call" | custom-call | tf_op jit(solution)/shard_map/pallas_call | solution.py:21
  33.9 3.4 %collective-permute-start.5 = (f32[16,4,8,128]{3,2,1,0:T(8,128)}, f32[16,4,8,128]{3,2,1,0:T(8,128)S(1)}, u32[]{:S(2)}, u32[]{:S(2)}) collective-permute-start(f32[16,4,8,128]{3,2,1,0:T(8,128)} %get-tuple-element.17), channel_id=1, source_target_pairs={{0,8},{8,16},{16,24},{1,9},{9,17},{17,25},{2,10},{10,18},{18,26},{... | collective-permute-start | bytes 786440 | tf_op jit(solution)/shard_map/ppermute | solution.py:167
  37.3 1.3 %collective-permute-start.6 = (f32[16,4,8,128]{3,2,1,0:T(8,128)}, f32[16,4,8,128]{3,2,1,0:T(8,128)S(1)}, u32[]{:S(2)}, u32[]{:S(2)}) collective-permute-start(f32[16,4,8,128]{3,2,1,0:T(8,128)} %get-tuple-element.18), channel_id=1, source_target_pairs={{8,0},{16,8},{24,16},{9,1},{17,9},{25,17},{10,2},{18,10},{26,18},{... | collective-permute-start | bytes 786440 | tf_op jit(solution)/shard_map/ppermute | solution.py:168
  38.6 0.1 copy.18
  38.7 0.7 select_maximum_fusion.zf_ref
  39.5 1.3 %collective-permute-start.9 = (f32[12,8,128]{2,1,0:T(8,128)}, f32[12,8,128]{2,1,0:T(8,128)S(1)}, u32[]{:S(2)}, u32[]{:S(2)}) collective-permute-start(f32[12,8,128]{2,1,0:T(8,128)} %get-tuple-element.19), channel_id=1, source_target_pairs={{1,0},{2,1},{3,2},{5,4},{6,5},{7,6},{9,8},{10,9},{11,10},{13,12},{... | collective-permute-start | bytes 147464 | tf_op jit(solution)/shard_map/ppermute | solution.py:168
  40.8 4.5 %collective-permute-start.8 = (f32[12,8,128]{2,1,0:T(8,128)}, f32[12,8,128]{2,1,0:T(8,128)S(1)}, u32[]{:S(2)}, u32[]{:S(2)}) collective-permute-start(f32[12,8,128]{2,1,0:T(8,128)} %get-tuple-element.19), channel_id=1, source_target_pairs={{0,1},{1,2},{2,3},{4,5},{5,6},{6,7},{8,9},{9,10},{10,11},{12,13},{... | collective-permute-start | bytes 147464 | tf_op jit(solution)/shard_map/ppermute | solution.py:167
  45.3 0.1 constant_dynamic-slice_fusion
  45.4 0.7 copy.21
  46.1 2.7 %collective-permute-start.10 = (s32[12]{0:T(128)S(1)}, s32[12]{0:T(128)S(1)}, u32[]{:S(2)}, u32[]{:S(2)}) collective-permute-start(s32[12]{0:T(128)S(1)} %copy-done.21), channel_id=1, source_target_pairs={{0,8},{8,16},{16,24},{24,0},{1,9},{9,17},{17,25},{25,1},{2,10},{10... | collective-permute-start | bytes 152 | tf_op jit(solution)/shard_map/ppermute | solution.py:154
  48.8 0.3 collective-permute-start.12
  49.1 1.0 %collective-permute-done.6.xh_ref = f32[16,4,8,128]{3,2,1,0:T(8,128)S(1)} collective-permute-done((f32[16,4,8,128]{3,2,1,0:T(8,128)}, f32[16,4,8,128]{3,2,1,0:T(8,128)S(1)}, u32[]{:S(2)}, u32[]{:S(2)}) %collective-permute-start.6) | collective-permute-done | bytes 262176 | tf_op jit(solution)/shard_map/ppermute | solution.py:168
  50.1 0.7 copy-done.7
  50.8 0.9 copy-done.2
  51.7 9.2 %shard_map.97 = (f32[16,12,8,128]{3,2,1,0:T(8,128)}, f32[8,96,128]{2,1,0:T(8,128)}) custom-call(f32[16,12,8,128]{3,2,1,0:T(8,128)} %f_ref.5, f32[16,12,8,128]{3,2,1,0:T(8,128)} %get-tuple-element.16.s_ref, f32[16,4,8,128]{3,2,1,0:T(8,128)} %copy-done.6, f32[16,4,8,128]{3,2,1,0:T(8,128)} %copy-done.7, f32[16,12,8,128]{3,2,1,0:T(8,128)} %copy-done.2, ...), custom_call_target="tpu_custom_call" | custom-call | tf_op jit(solution)/shard_map/pallas_call | solution.py:21
  60.9 1.0 %dynamic-slice_bitcast_fusion.2 = (f32[2,96,128]{2,1,0:T(8,128)S(1)}, f32[2,96,128]{2,1,0:T(8,128)S(1)}, f32[2,96,128]{2,1,0:T(8,128)S(1)}) fusion(f32[4,2,96,128]{3,2,1,0:T(8,128)} %bitcast.23, s32[]{:T(128)S(6)} %select_n.22, s32[]{:T(128)S(6)} %select_n.24, s32[]{:T(128)S(6)} %select_n.23), kind=kLoop, calls=%fused_computation.8 | loop fusion | bytes 589836 | tf_op jit(solution)/shard_map/jit(dynamic_index_in_dim)/squeeze | solution.py:253
  61.9 1.6 %collective-permute-start.14 = (f32[2,96,128]{2,1,0:T(8,128)S(1)}, f32[2,96,128]{2,1,0:T(8,128)S(1)}, u32[]{:S(2)}, u32[]{:S(2)}) collective-permute-start(f32[2,96,128]{2,1,0:T(8,128)S(1)} %get-tuple-element.24), channel_id=1, source_target_pairs={{0,1},{1,2},{2,3},{3,0},{4,5},{5,6},{6,7},{7,4},{8,9},{9,10},{10,1... | collective-permute-start | bytes 294920 | tf_op jit(solution)/shard_map/ppermute | solution.py:154
  63.5 2.2 %collective-permute-start.16 = (f32[2,96,128]{2,1,0:T(8,128)S(1)}, f32[2,96,128]{2,1,0:T(8,128)S(1)}, u32[]{:S(2)}, u32[]{:S(2)}) collective-permute-start(f32[2,96,128]{2,1,0:T(8,128)S(1)} %get-tuple-element.25), channel_id=1, source_target_pairs={{0,3},{1,0},{2,1},{3,2},{4,7},{5,4},{6,5},{7,6},{8,11},{9,8},{10,9... | collective-permute-start | bytes 294920 | tf_op jit(solution)/shard_map/ppermute | solution.py:154
  65.8 0.8 collective-permute-start.15
  66.6 0.7 reshape.41.row_ref
  67.2 1.8 %collective-permute-done.14 = f32[2,96,128]{2,1,0:T(8,128)S(1)} collective-permute-done((f32[2,96,128]{2,1,0:T(8,128)S(1)}, f32[2,96,128]{2,1,0:T(8,128)S(1)}, u32[]{:S(2)}, u32[]{:S(2)}) %collective-permute-start.14) | collective-permute-done | bytes 98336 | tf_op jit(solution)/shard_map/ppermute | solution.py:154
  69.0 2.4 %collective-permute-start.11 = (s32[12]{0:T(128)S(1)}, s32[12]{0:T(128)S(1)}, u32[]{:S(2)}, u32[]{:S(2)}) collective-permute-start(s32[12]{0:T(128)S(1)} %copy-done.21), channel_id=1, source_target_pairs={{0,16},{8,24},{16,0},{24,8},{1,17},{9,25},{17,1},{25,9},{2,18},{10... | collective-permute-start | bytes 152 | tf_op jit(solution)/shard_map/ppermute | solution.py:154
  71.4 3.3 %collective-permute-done.15 = f32[2,96,128]{2,1,0:T(8,128)S(1)} collective-permute-done((f32[2,96,128]{2,1,0:T(8,128)S(1)}, f32[2,96,128]{2,1,0:T(8,128)S(1)}, u32[]{:S(2)}, u32[]{:S(2)}) %collective-permute-start.15) | collective-permute-done | bytes 98336 | tf_op jit(solution)/shard_map/ppermute | solution.py:154
  74.7 0.9 %fusion.1.refs_0_ = f32[2,96,128]{2,1,0:T(8,128)S(1)} fusion(f32[2,96,128]{2,1,0:T(8,128)S(1)} %collective-permute-done.16, f32[2,96,128]{2,1,0:T(8,128)S(1)} %collective-permute-done.15, f32[2,96,128]{2,1,0:T(8,128)S(1)} %collective-permute-done.14, f32[4,2,96,128]{3,2,1,0:T(8,128)} %bitcast.24, s32[]{:T(128)S(6)} %select_n.21), kind=kLoop, calls=%fused_computation.5 | loop fusion | flops 73728 | bytes 491524 | tf_op jit(solution)/shard_map/add | solution.py:254
  75.6 0.4 collective-permute-start.22
  76.1 0.9 %collective-permute-start.20 = (f32[2,96,128]{2,1,0:T(8,128)S(1)}, f32[2,96,128]{2,1,0:T(8,128)S(1)}, u32[]{:S(2)}, u32[]{:S(2)}) collective-permute-start(f32[2,96,128]{2,1,0:T(8,128)S(1)} %fusion.1.refs_0_), channel_id=1, source_target_pairs={{0,16},{8,24},{16,0},{24,8},{1,17},{9,25},{17,1},{25,9},{2,18},{10... | collective-permute-start | bytes 294920 | tf_op jit(solution)/shard_map/ppermute | solution.py:154
  77.0 1.7 %collective-permute-start.18 = (f32[2,96,128]{2,1,0:T(8,128)S(1)}, f32[2,96,128]{2,1,0:T(8,128)S(1)}, u32[]{:S(2)}, u32[]{:S(2)}) collective-permute-start(f32[2,96,128]{2,1,0:T(8,128)S(1)} %fusion.1.refs_0_), channel_id=1, source_target_pairs={{0,8},{8,16},{16,24},{24,0},{1,9},{9,17},{17,25},{25,1},{2,10},{10... | collective-permute-start | bytes 294920 | tf_op jit(solution)/shard_map/ppermute | solution.py:154
  78.8 0.7 reshape.37.rank_ref
  79.5 1.7 %collective-permute-done.22.refs_6_ = f32[2,96,128]{2,1,0:T(8,128)S(1)} collective-permute-done((f32[2,96,128]{2,1,0:T(8,128)S(1)}, f32[2,96,128]{2,1,0:T(8,128)S(1)}, u32[]{:S(2)}, u32[]{:S(2)}) %collective-permute-start.22) | collective-permute-done | bytes 98336 | tf_op jit(solution)/shard_map/ppermute | solution.py:154
  81.2 0.4 collective-permute-done.20.refs_4_
  81.5 0.2 collective-permute-start.21
  81.7 0.9 collective-permute-done.18.refs_2_
  82.6 0.1 dynamic-slice_maximum_fusion
  82.7 0.7 copy.22
  83.4 2.9 %shard_map.98 = (bf16[768,768]{1,0:T(8,128)(2,1)}, bf16[768,768]{1,0:T(8,128)(2,1)}) custom-call(s32[1,768]{1,0:T(1,128)} %reshape.37.rank_ref, s32[1,768]{1,0:T(1,128)} %reshape.41.row_ref, f32[24,48]{1,0:T(8,128)} %bitcast.26, f32[32,16]{1,0:T(8,128)} %bitcast.25), custom_call_target="tpu_custom_call" | custom-call | tf_op jit(solution)/shard_map/pallas_call | solution.py:21
  86.3 0.5 copy-done.11
  87.0 4.1 %shard_map.99 = f32[4,768,54]{2,1,0:T(8,128)} custom-call(bf16[768,768]{1,0:T(8,128)(2,1)} %get-tuple-element.21.high_ref, bf16[768,768]{1,0:T(8,128)(2,1)} %get-tuple-element.22.low_ref, f32[2,96,128]{2,1,0:T(8,128)} %copy-done.3, f32[2,96,128]{2,1,0:T(8,128)} %copy-done.11, f32[2,96,128]{2,1,0:T(8,128)} %copy-done.10, f32[2,96,128]{2,1,0:T(8,128)} %copy-done.14, ...), custom_call_target="tpu_custom_call" | custom-call | tf_op jit(solution)/shard_map/pallas_call | solution.py:21
  (65 shorter events, 0.3 us)
Async XLA Ops:
  0.6 44.7 %copy-start = (f32[48,96]{1,0:T(8,128)S(1)}, f32[48,96]{1,0:T(8,128)}, u32[]{:S(2)}) copy-start(f32[48,96]{1,0:T(8,128)} %param.12) | copy-start | bytes 55300
  0.6 22.3 %collective-permute-start.2 = (f32[16,12,8,128]{3,2,1,0:T(8,128)}, f32[16,12,8,128]{3,2,1,0:T(8,128)S(1)}, u32[]{:S(2)}, u32[]{:S(2)}) collective-permute-start(f32[16,12,8,128]{3,2,1,0:T(8,128)} %f_ref.5), channel_id=1, source_target_pairs={{0,4},{4,0},{1,5},{5,1},{2,6},{6,2},{3,7},{7,3},{8,12},{12,8},{9,1... | collective-permute-start | bytes 2359304 | tf_op jit(solution)/shard_map/ppermute | solution.py:174
  4.5 13.6 %collective-permute-start = (f32[16,4,8,128]{3,2,1,0:T(8,128)}, f32[16,4,8,128]{3,2,1,0:T(8,128)S(1)}, u32[]{:S(2)}, u32[]{:S(2)}) collective-permute-start(f32[16,4,8,128]{3,2,1,0:T(8,128)} %get-tuple-element.13), channel_id=1, source_target_pairs={{0,8},{8,16},{16,24},{1,9},{9,17},{17,25},{2,10},{10,18},{18,26},{... | collective-permute-start | bytes 786440 | tf_op jit(solution)/shard_map/ppermute | solution.py:167
  8.9 14.0 %collective-permute-start.1 = (f32[16,4,8,128]{3,2,1,0:T(8,128)}, f32[16,4,8,128]{3,2,1,0:T(8,128)S(1)}, u32[]{:S(2)}, u32[]{:S(2)}) collective-permute-start(f32[16,4,8,128]{3,2,1,0:T(8,128)} %get-tuple-element.14), channel_id=1, source_target_pairs={{8,0},{16,8},{24,16},{9,1},{17,9},{25,17},{10,2},{18,10},{26,18},{... | collective-permute-start | bytes 786440 | tf_op jit(solution)/shard_map/ppermute | solution.py:168
  10.2 6.5 %collective-permute-start.4 = (f32[12,8,128]{2,1,0:T(8,128)}, f32[12,8,128]{2,1,0:T(8,128)S(1)}, u32[]{:S(2)}, u32[]{:S(2)}) collective-permute-start(f32[12,8,128]{2,1,0:T(8,128)} %get-tuple-element.15), channel_id=1, source_target_pairs={{1,0},{2,1},{3,2},{5,4},{6,5},{7,6},{9,8},{10,9},{11,10},{13,12},{... | collective-permute-start | bytes 147464 | tf_op jit(solution)/shard_map/ppermute | solution.py:168
  11.5 6.6 %collective-permute-start.3 = (f32[12,8,128]{2,1,0:T(8,128)}, f32[12,8,128]{2,1,0:T(8,128)S(1)}, u32[]{:S(2)}, u32[]{:S(2)}) collective-permute-start(f32[12,8,128]{2,1,0:T(8,128)} %get-tuple-element.15), channel_id=1, source_target_pairs={{0,1},{1,2},{2,3},{4,5},{5,6},{6,7},{8,9},{9,10},{10,11},{12,13},{... | collective-permute-start | bytes 147464 | tf_op jit(solution)/shard_map/ppermute | solution.py:167
  16.7 21.9 %copy-start.19 = (f32[128,54]{0,1:T(8,128)S(1)}, f32[128,54]{0,1:T(8,128)}, u32[]{:S(2)}) copy-start(f32[128,54]{0,1:T(8,128)} %param.14) | copy-start | bytes 82948
  16.7 29.4 %copy-start.21 = (s32[12]{0:T(128)S(1)}, s32[12]{0:T(128)}, u32[]{:S(2)}) copy-start(s32[12]{0:T(128)} %param.11) | copy-start | bytes 148
  16.7 6.2 %copy-start.17 = (f32[12,8,128]{2,1,0:T(8,128)}, f32[12,8,128]{2,1,0:T(8,128)S(1)}, u32[]{:S(2)}) copy-start(f32[12,8,128]{2,1,0:T(8,128)S(1)} %collective-permute-done.4.zh_ref) | copy-start | bytes 147460
  18.2 4.8 %copy-start.18 = (f32[12,8,128]{2,1,0:T(8,128)}, f32[12,8,128]{2,1,0:T(8,128)S(1)}, u32[]{:S(2)}) copy-start(f32[12,8,128]{2,1,0:T(8,128)S(1)} %collective-permute-done.3.zl_ref) | copy-start | bytes 147460
  18.2 4.8 %copy-start.4 = (f32[16,4,8,128]{3,2,1,0:T(8,128)}, f32[16,4,8,128]{3,2,1,0:T(8,128)S(1)}, u32[]{:S(2)}) copy-start(f32[16,4,8,128]{3,2,1,0:T(8,128)S(1)} %collective-permute-done.xl_ref) | copy-start | bytes 786436
  22.9 0.7 copy-start.5
  23.6 0.9 copy-start.1
  33.9 16.2 %collective-permute-start.7 = (f32[16,12,8,128]{3,2,1,0:T(8,128)}, f32[16,12,8,128]{3,2,1,0:T(8,128)S(1)}, u32[]{:S(2)}, u32[]{:S(2)}) collective-permute-start(f32[16,12,8,128]{3,2,1,0:T(8,128)} %get-tuple-element.16.s_ref), channel_id=1, source_target_pairs={{0,4},{4,0},{1,5},{5,1},{2,6},{6,2},{3,7},{7,3},{8,12},{12,8},{9,1... | collective-permute-start | bytes 2359304 | tf_op jit(solution)/shard_map/ppermute | solution.py:174
  33.9 15.2 %collective-permute-start.5 = (f32[16,4,8,128]{3,2,1,0:T(8,128)}, f32[16,4,8,128]{3,2,1,0:T(8,128)S(1)}, u32[]{:S(2)}, u32[]{:S(2)}) collective-permute-start(f32[16,4,8,128]{3,2,1,0:T(8,128)} %get-tuple-element.17), channel_id=1, source_target_pairs={{0,8},{8,16},{16,24},{1,9},{9,17},{17,25},{2,10},{10,18},{18,26},{... | collective-permute-start | bytes 786440 | tf_op jit(solution)/shard_map/ppermute | solution.py:167
  37.3 12.8 %collective-permute-start.6 = (f32[16,4,8,128]{3,2,1,0:T(8,128)}, f32[16,4,8,128]{3,2,1,0:T(8,128)S(1)}, u32[]{:S(2)}, u32[]{:S(2)}) collective-permute-start(f32[16,4,8,128]{3,2,1,0:T(8,128)} %get-tuple-element.18), channel_id=1, source_target_pairs={{8,0},{16,8},{24,16},{9,1},{17,9},{25,17},{10,2},{18,10},{26,18},{... | collective-permute-start | bytes 786440 | tf_op jit(solution)/shard_map/ppermute | solution.py:168
  39.5 6.6 %collective-permute-start.9 = (f32[12,8,128]{2,1,0:T(8,128)}, f32[12,8,128]{2,1,0:T(8,128)S(1)}, u32[]{:S(2)}, u32[]{:S(2)}) collective-permute-start(f32[12,8,128]{2,1,0:T(8,128)} %get-tuple-element.19), channel_id=1, source_target_pairs={{1,0},{2,1},{3,2},{5,4},{6,5},{7,6},{9,8},{10,9},{11,10},{13,12},{... | collective-permute-start | bytes 147464 | tf_op jit(solution)/shard_map/ppermute | solution.py:168
  40.8 8.0 %collective-permute-start.8 = (f32[12,8,128]{2,1,0:T(8,128)}, f32[12,8,128]{2,1,0:T(8,128)S(1)}, u32[]{:S(2)}, u32[]{:S(2)}) collective-permute-start(f32[12,8,128]{2,1,0:T(8,128)} %get-tuple-element.19), channel_id=1, source_target_pairs={{0,1},{1,2},{2,3},{4,5},{5,6},{6,7},{8,9},{9,10},{10,11},{12,13},{... | collective-permute-start | bytes 147464 | tf_op jit(solution)/shard_map/ppermute | solution.py:167
  46.1 25.3 %copy-start.20 = (f32[8,64]{1,0:T(8,128)S(1)}, f32[8,64]{1,0:T(8,128)}, u32[]{:S(2)}) copy-start(f32[8,64]{1,0:T(8,128)} %param.13) | copy-start | bytes 6148
  46.1 4.0 %copy-start.15 = (f32[12,8,128]{2,1,0:T(8,128)}, f32[12,8,128]{2,1,0:T(8,128)S(1)}, u32[]{:S(2)}) copy-start(f32[12,8,128]{2,1,0:T(8,128)S(1)} %collective-permute-done.9.zh_ref) | copy-start | bytes 147460
  46.1 30.0 %collective-permute-start.10 = (s32[12]{0:T(128)S(1)}, s32[12]{0:T(128)S(1)}, u32[]{:S(2)}, u32[]{:S(2)}) collective-permute-start(s32[12]{0:T(128)S(1)} %copy-done.21), channel_id=1, source_target_pairs={{0,8},{8,16},{16,24},{24,0},{1,9},{9,17},{17,25},{25,1},{2,10},{10... | collective-permute-start | bytes 152 | tf_op jit(solution)/shard_map/ppermute | solution.py:154
  48.8 1.3 %copy-start.16 = (f32[12,8,128]{2,1,0:T(8,128)}, f32[12,8,128]{2,1,0:T(8,128)S(1)}, u32[]{:S(2)}) copy-start(f32[12,8,128]{2,1,0:T(8,128)S(1)} %collective-permute-done.8.zl_ref) | copy-start | bytes 147460
  48.8 28.2 %collective-permute-start.12 = (s32[12]{0:T(128)S(1)}, s32[12]{0:T(128)S(1)}, u32[]{:S(2)}, u32[]{:S(2)}) collective-permute-start(s32[12]{0:T(128)S(1)} %copy-done.21), channel_id=1, source_target_pairs={{0,24},{8,0},{16,8},{24,16},{1,25},{9,1},{17,9},{25,17},{2,26},{10... | collective-permute-start | bytes 152 | tf_op jit(solution)/shard_map/ppermute | solution.py:154
  49.1 1.0 %copy-start.6 = (f32[16,4,8,128]{3,2,1,0:T(8,128)}, f32[16,4,8,128]{3,2,1,0:T(8,128)S(1)}, u32[]{:S(2)}) copy-start(f32[16,4,8,128]{3,2,1,0:T(8,128)S(1)} %collective-permute-done.5.xl_ref) | copy-start | bytes 786436
  50.1 0.7 copy-start.7
  50.8 0.9 copy-start.2
  61.9 7.2 %collective-permute-start.14 = (f32[2,96,128]{2,1,0:T(8,128)S(1)}, f32[2,96,128]{2,1,0:T(8,128)S(1)}, u32[]{:S(2)}, u32[]{:S(2)}) collective-permute-start(f32[2,96,128]{2,1,0:T(8,128)S(1)} %get-tuple-element.24), channel_id=1, source_target_pairs={{0,1},{1,2},{2,3},{3,0},{4,5},{5,6},{6,7},{7,4},{8,9},{9,10},{10,1... | collective-permute-start | bytes 294920 | tf_op jit(solution)/shard_map/ppermute | solution.py:154
  63.5 7.9 %collective-permute-start.16 = (f32[2,96,128]{2,1,0:T(8,128)S(1)}, f32[2,96,128]{2,1,0:T(8,128)S(1)}, u32[]{:S(2)}, u32[]{:S(2)}) collective-permute-start(f32[2,96,128]{2,1,0:T(8,128)S(1)} %get-tuple-element.25), channel_id=1, source_target_pairs={{0,3},{1,0},{2,1},{3,2},{4,7},{5,4},{6,5},{7,6},{8,11},{9,8},{10,9... | collective-permute-start | bytes 294920 | tf_op jit(solution)/shard_map/ppermute | solution.py:154
  65.8 9.0 %collective-permute-start.15 = (f32[2,96,128]{2,1,0:T(8,128)S(1)}, f32[2,96,128]{2,1,0:T(8,128)S(1)}, u32[]{:S(2)}, u32[]{:S(2)}) collective-permute-start(f32[2,96,128]{2,1,0:T(8,128)S(1)} %get-tuple-element.26), channel_id=1, source_target_pairs={{0,2},{1,3},{2,0},{3,1},{4,6},{5,7},{6,4},{7,5},{8,10},{9,11},{10,... | collective-permute-start | bytes 294920 | tf_op jit(solution)/shard_map/ppermute | solution.py:154
  69.0 9.6 %collective-permute-start.11 = (s32[12]{0:T(128)S(1)}, s32[12]{0:T(128)S(1)}, u32[]{:S(2)}, u32[]{:S(2)}) collective-permute-start(s32[12]{0:T(128)S(1)} %copy-done.21), channel_id=1, source_target_pairs={{0,16},{8,24},{16,0},{24,8},{1,17},{9,25},{17,1},{25,9},{2,18},{10... | collective-permute-start | bytes 152 | tf_op jit(solution)/shard_map/ppermute | solution.py:154
  71.4 11.2 %collective-permute-start.13 = (f32[8,64]{1,0:T(8,128)S(1)}, f32[8,64]{1,0:T(8,128)S(1)}, u32[]{:S(2)}, u32[]{:S(2)}) collective-permute-start(f32[8,64]{1,0:T(8,128)S(1)} %copy-done.20), channel_id=1, source_target_pairs={{0,4},{4,0},{1,5},{5,1},{2,6},{6,2},{3,7},{7,3},{8,12},{12,8},{9,1... | collective-permute-start | bytes 6152 | tf_op jit(solution)/shard_map/ppermute | solution.py:154
  75.6 10.7 %copy-start.3 = (f32[2,96,128]{2,1,0:T(8,128)}, f32[2,96,128]{2,1,0:T(8,128)S(1)}, u32[]{:S(2)}) copy-start(f32[2,96,128]{2,1,0:T(8,128)S(1)} %fusion.1.refs_0_) | copy-start | bytes 294916
  75.6 5.5 %collective-permute-start.22 = (f32[2,96,128]{2,1,0:T(8,128)S(1)}, f32[2,96,128]{2,1,0:T(8,128)S(1)}, u32[]{:S(2)}, u32[]{:S(2)}) collective-permute-start(f32[2,96,128]{2,1,0:T(8,128)S(1)} %fusion.1.refs_0_), channel_id=1, source_target_pairs={{0,24},{8,0},{16,8},{24,16},{1,25},{9,1},{17,9},{25,17},{2,26},{10... | collective-permute-start | bytes 294920 | tf_op jit(solution)/shard_map/ppermute | solution.py:154
  76.1 5.5 %collective-permute-start.20 = (f32[2,96,128]{2,1,0:T(8,128)S(1)}, f32[2,96,128]{2,1,0:T(8,128)S(1)}, u32[]{:S(2)}, u32[]{:S(2)}) collective-permute-start(f32[2,96,128]{2,1,0:T(8,128)S(1)} %fusion.1.refs_0_), channel_id=1, source_target_pairs={{0,16},{8,24},{16,0},{24,8},{1,17},{9,25},{17,1},{25,9},{2,18},{10... | collective-permute-start | bytes 294920 | tf_op jit(solution)/shard_map/ppermute | solution.py:154
  77.0 5.6 %collective-permute-start.18 = (f32[2,96,128]{2,1,0:T(8,128)S(1)}, f32[2,96,128]{2,1,0:T(8,128)S(1)}, u32[]{:S(2)}, u32[]{:S(2)}) collective-permute-start(f32[2,96,128]{2,1,0:T(8,128)S(1)} %fusion.1.refs_0_), channel_id=1, source_target_pairs={{0,8},{8,16},{16,24},{24,0},{1,9},{9,17},{17,25},{25,1},{2,10},{10... | collective-permute-start | bytes 294920 | tf_op jit(solution)/shard_map/ppermute | solution.py:154
  79.5 6.8 %collective-permute-start.17 = (f32[2,96,128]{2,1,0:T(8,128)S(1)}, f32[2,96,128]{2,1,0:T(8,128)S(1)}, u32[]{:S(2)}, u32[]{:S(2)}) collective-permute-start(f32[2,96,128]{2,1,0:T(8,128)S(1)} %fusion.1.refs_0_), channel_id=1, source_target_pairs={{0,4},{4,0},{1,5},{5,1},{2,6},{6,2},{3,7},{7,3},{8,12},{12,8},{9,1... | collective-permute-start | bytes 294920 | tf_op jit(solution)/shard_map/ppermute | solution.py:154
  81.2 5.1 %copy-start.8 = (f32[2,96,128]{2,1,0:T(8,128)}, f32[2,96,128]{2,1,0:T(8,128)S(1)}, u32[]{:S(2)}) copy-start(f32[2,96,128]{2,1,0:T(8,128)S(1)} %collective-permute-done.22.refs_6_) | copy-start | bytes 294916
  81.2 5.1 %collective-permute-start.23 = (f32[2,96,128]{2,1,0:T(8,128)S(1)}, f32[2,96,128]{2,1,0:T(8,128)S(1)}, u32[]{:S(2)}, u32[]{:S(2)}) collective-permute-start(f32[2,96,128]{2,1,0:T(8,128)S(1)} %collective-permute-done.22.refs_6_), channel_id=1, source_target_pairs={{0,4},{4,0},{1,5},{5,1},{2,6},{6,2},{3,7},{7,3},{8,12},{12,8},{9,1... | collective-permute-start | bytes 294920 | tf_op jit(solution)/shard_map/ppermute | solution.py:154
  81.5 4.8 %copy-start.9 = (f32[2,96,128]{2,1,0:T(8,128)}, f32[2,96,128]{2,1,0:T(8,128)S(1)}, u32[]{:S(2)}) copy-start(f32[2,96,128]{2,1,0:T(8,128)S(1)} %collective-permute-done.20.refs_4_) | copy-start | bytes 294916
  81.5 4.7 %collective-permute-start.21 = (f32[2,96,128]{2,1,0:T(8,128)S(1)}, f32[2,96,128]{2,1,0:T(8,128)S(1)}, u32[]{:S(2)}, u32[]{:S(2)}) collective-permute-start(f32[2,96,128]{2,1,0:T(8,128)S(1)} %collective-permute-done.20.refs_4_), channel_id=1, source_target_pairs={{0,4},{4,0},{1,5},{5,1},{2,6},{6,2},{3,7},{7,3},{8,12},{12,8},{9,1... | collective-permute-start | bytes 294920 | tf_op jit(solution)/shard_map/ppermute | solution.py:154
  82.6 3.7 %copy-start.10 = (f32[2,96,128]{2,1,0:T(8,128)}, f32[2,96,128]{2,1,0:T(8,128)S(1)}, u32[]{:S(2)}) copy-start(f32[2,96,128]{2,1,0:T(8,128)S(1)} %collective-permute-done.18.refs_2_) | copy-start | bytes 294916
  82.6 3.7 %collective-permute-start.19 = (f32[2,96,128]{2,1,0:T(8,128)S(1)}, f32[2,96,128]{2,1,0:T(8,128)S(1)}, u32[]{:S(2)}, u32[]{:S(2)}) collective-permute-start(f32[2,96,128]{2,1,0:T(8,128)S(1)} %collective-permute-done.18.refs_2_), channel_id=1, source_target_pairs={{0,4},{4,0},{1,5},{5,1},{2,6},{6,2},{3,7},{7,3},{8,12},{12,8},{9,1... | collective-permute-start | bytes 294920 | tf_op jit(solution)/shard_map/ppermute | solution.py:154
  86.2 0.6 copy-start.11
  86.2 0.7 copy-start.12
  86.3 0.7 copy-start.13
  86.3 0.7 copy-start.14

commit v2 on v1

v2 whole, which is shorter than its diff:
```python
import functools

import jax
import jax.numpy as jnp
import numpy as np
from jax import lax
from jax.experimental import pallas as pl
from jax.experimental.pallas import tpu as pltpu
from jax.sharding import PartitionSpec as P

COEFFS = (0.8, -0.2, 4.0 / 105.0, -1.0 / 280.0)
SCALE = 840.0
WHOLE = (672.0, -168.0, 32.0, -3.0)
TIME_STEP = 0.45
REACH = len(COEFFS)
HALF = 64
F32, BF16 = jnp.float32, jnp.bfloat16
HIGHEST = lax.Precision.HIGHEST
VMEM = pl.BlockSpec(memory_space=pltpu.VMEM)
SMEM = pl.BlockSpec(memory_space=pltpu.SMEM)


def call(kernel, out_shapes, in_specs, args, scratch=(), room=16):
    return pl.pallas_call(
        kernel,
        out_shape=tuple(jax.ShapeDtypeStruct(s, d) for s, d in out_shapes),
        in_specs=in_specs,
        out_specs=tuple(VMEM for _ in out_shapes),
        scratch_shapes=list(scratch),
        compiler_params=pltpu.CompilerParams(vmem_limit_bytes=room * 2**20),
    )(*args)


def dot(a, b):
    return jnp.dot(a, b, preferred_element_type=F32)


def exact(a, b, dims=((1,), (0,))):
    return lax.dot_general(a, b, (dims, ((), ())), precision=HIGHEST, preferred_element_type=F32)


def split(x):
    high = x.astype(BF16)
    return high, (x - high.astype(F32)).astype(BF16)


def split_rims(v, values, low_ref, high_ref, rim_ref):
    low_ref[v] = values[:REACH]
    high_ref[v] = values[values.shape[0] - REACH :]
    width = values.shape[2]
    group = lax.shift_right_logical(lax.broadcasted_iota(jnp.int32, values.shape, 2), 2)
    last = pltpu.roll(values, REACH * v + REACH, 2)
    first = pltpu.roll(values, width // 2 + REACH * v, 2)
    rim = jnp.where(group == v, last, rim_ref[...])
    rim_ref[...] = jnp.where(group == v + width // 2 // REACH, first, rim)


def pack_kernel(f_ref, low_ref, high_ref, rim_ref):
    rim_ref[...] = jnp.zeros_like(rim_ref)

    def step(v, carry):
        split_rims(v, f_ref[v], low_ref, high_ref, rim_ref)
        return carry

    lax.fori_loop(0, f_ref.shape[0], step, 0)


def weight_kernel(kin_ref, speed_ref, edge_ref, unit_ref, shift_ref, zf_ref, w_ref, zf_out_ref, wide_ref):
    nvars = kin_ref.shape[0]
    rows, columns = unit_ref.shape
    row_v = lax.broadcasted_iota(jnp.int32, (rows, nvars), 0) // (rows // nvars)
    spread = (row_v == lax.broadcasted_iota(jnp.int32, (rows, nvars), 1)).astype(F32)
    column_v = lax.broadcasted_iota(jnp.int32, (nvars, columns), 1) // (columns // nvars)
    gather = (column_v == lax.broadcasted_iota(jnp.int32, (nvars, columns), 0)).astype(F32)
    rates = exact(exact(spread, kin_ref[...]), gather)
    speed = exact(spread, speed_ref[...], ((1,), (1,)))[:, 1:2]
    shifts = shift_ref[0] + edge_ref[0] * shift_ref[1] + edge_ref[1] * shift_ref[2]
    high, low = split(TIME_STEP * (rates * unit_ref[...] - speed * shifts))
    w_ref[0:rows] = high
    w_ref[rows:] = low
    depth = zf_ref.shape[0]
    wide_ref[...] = jnp.zeros_like(wide_ref)
    wide_ref[:, 0 : zf_ref.shape[1]] = zf_ref[...]
    high, low = split(wide_ref[...])
    zf_out_ref[0:depth, 0 : 2 * HALF] = high
    zf_out_ref[0:depth, 2 * HALF :] = low
    high, low = split(pltpu.roll(wide_ref[...], HALF, 1))
    zf_out_ref[depth:, 0 : 2 * HALF] = high
    zf_out_ref[depth:, 2 * HALF :] = low


def mix_planes(q_ref, beside_ref, w_ref, rate_ref):
    nvars, nx, ny, nz = q_ref.shape
    rows = nvars * ny

    def step(i, carry):
        high, low = [], []
        for p in (2 * i, 2 * i + 1):
            cells = jnp.concatenate([q_ref[:, p], beside_ref[:, p]], axis=1)
            h, l = split(cells.reshape(2 * rows, nz))
            high.append(h)
            low.append(l)
        both = dot(w_ref[...], jnp.concatenate(high, axis=1))
        total = both[:rows] + both[rows:] + dot(w_ref[0:rows], jnp.concatenate(low, axis=1))
        for j in range(2):
            rate_ref[:, 2 * i + j] = total[:, j * nz : (j + 1) * nz].reshape(nvars, ny, nz)
        return carry

    lax.fori_loop(0, nx // 2, step, 0)


def join_rims(zl_ref, zh_ref, shift_ref, rim_ref):
    nx, ny, nz = rim_ref.shape
    lane = lax.broadcasted_iota(jnp.int32, rim_ref.shape, 2)
    rim = jnp.where(lane < nz // 2, zl_ref[...], zh_ref[...]).reshape(nx * ny, nz)
    high, low = split(rim)
    rim_ref[...] = (dot(high, shift_ref[...]) + dot(low, shift_ref[...])).reshape(rim_ref.shape)


def step_of(v, q_ref, xl_ref, xh_ref, dz_ref, rate_ref, rim_ref, speed_ref):
    nvars, nx, ny, nz = q_ref.shape
    q = q_ref[v]
    tall = jnp.concatenate([xl_ref[v], q, xh_ref[v]], axis=0)
    gx = None
    for k in range(1, REACH + 1):
        part = COEFFS[k - 1] * (tall[REACH + k : REACH + k + nx] - tall[REACH - k : REACH - k + nx])
        gx = part if gx is None else gx + part
    high, low = split(q.reshape(nx * ny, nz))
    gz = dot(jnp.concatenate([high, low], axis=1), dz_ref[...]).reshape(nx, ny, nz)
    lane = lax.broadcasted_iota(jnp.int32, q.shape, 2)
    rim = rim_ref[...]
    first = pltpu.roll(rim, lax.rem(nz - REACH * v, nz), 2)
    last = pltpu.roll(rim, nz // 2 - REACH - REACH * v, 2)
    gz = gz + jnp.where(lane < REACH, first, jnp.where(lane >= nz - REACH, last, 0.0))
    return rate_ref[v] - (TIME_STEP * speed_ref[0, v]) * gx - (TIME_STEP / SCALE * speed_ref[2, v]) * gz


def section_kernel(
    f_ref, xl_ref, xh_ref, beside_ref, zl_ref, zh_ref, w_ref, dz_ref, shift_ref, speed_ref,
    s_ref, low_ref, high_ref, out_rim_ref, rate_ref, rim_ref,
):
    mix_planes(f_ref, beside_ref, w_ref, rate_ref)
    join_rims(zl_ref, zh_ref, shift_ref, rim_ref)
    out_rim_ref[...] = jnp.zeros_like(out_rim_ref)

    def step(v, carry):
        s = f_ref[v] + step_of(v, f_ref, xl_ref, xh_ref, dz_ref, rate_ref, rim_ref, speed_ref)
        s_ref[v] = s
        split_rims(v, s, low_ref, high_ref, out_rim_ref)
        return carry

    lax.fori_loop(0, f_ref.shape[0], step, 0)


def next_kernel(
    f_ref, s_ref, xl_ref, xh_ref, beside_ref, zl_ref, zh_ref, w_ref, dz_ref, shift_ref, zf_ref, speed_ref,
    next_ref, proj_ref, rate_ref, rim_ref,
):
    nvars, nx, ny, nz = f_ref.shape
    mix_planes(s_ref, beside_ref, w_ref, rate_ref)
    join_rims(zl_ref, zh_ref, shift_ref, rim_ref)

    def step(p, carry):
        both = []
        for v in (2 * p, 2 * p + 1):
            rate = step_of(v, s_ref, xl_ref, xh_ref, dz_ref, rate_ref, rim_ref, speed_ref)
            new = 0.5 * (f_ref[v] + s_ref[v] + rate)
            next_ref[v] = new
            both.append(new.reshape(nx * ny, nz))
        high, low = split(jnp.concatenate(both, axis=1))
        wide = dot(high, zf_ref[...])
        proj_ref[p] = wide[:, : 2 * HALF] + wide[:, 2 * HALF :] + dot(low, zf_ref[:, : 2 * HALF])
        return carry

    lax.fori_loop(0, nvars // 2, step, 0)


def factor_kernel(rank_ref, place_ref, xf_ref, *refs):
    y_refs, (out_ref, xt_ref) = refs[:-2], refs[-2:]
    planes, a_count = rank_ref.shape[1], xt_ref.shape[0]
    ny = y_refs[0].shape[0]
    width = planes * ny
    b_count = out_ref.shape[1] // a_count

    def own(count, total, place):
        column = lax.broadcasted_iota(jnp.int32, (count, total), 1)
        return (column == lax.broadcasted_iota(jnp.int32, (count, total), 0) + place * count).astype(F32)

    mine = exact(own(a_count, xf_ref.shape[1], place_ref[0]), xf_ref[...], ((1,), (1,)))
    pick = lax.broadcasted_iota(jnp.int32, (xf_ref.shape[0], planes), 0) == rank_ref[...]
    mine = exact(mine, pick.astype(F32))
    column = lax.broadcasted_iota(jnp.int32, (planes, width), 1)
    spread = lax.broadcasted_iota(jnp.int32, (planes, width), 0) == column // ny
    xt_ref[...] = exact(mine, spread.astype(F32))
    column = lax.broadcasted_iota(jnp.int32, (ny, width), 1)
    spread = lax.broadcasted_iota(jnp.int32, (ny, width), 0) == lax.rem(column, ny)
    for i, y_ref in enumerate(y_refs):
        rows = exact(own(b_count, y_ref.shape[1], place_ref[1]), y_ref[...], ((1,), (1,)))
        yt = exact(rows, spread.astype(F32))
        for a in range(a_count):
            high, low = split(xt_ref[a : a + 1, :] * yt)
            out_ref[0, a * b_count : (a + 1) * b_count, i * width : (i + 1) * width] = high
            out_ref[1, a * b_count : (a + 1) * b_count, i * width : (i + 1) * width] = low


def core_kernel(q_ref, *refs):
    out_ref = refs[-1]
    pairs = refs[0].shape[0]
    rank = out_ref.shape[2]
    columns = [jnp.concatenate([r[p] for r in refs[:-1]], axis=0) for p in range(pairs)]
    high, low = split(jnp.concatenate(columns, axis=1))
    result = dot(q_ref[0], high) + (dot(q_ref[0], low) + dot(q_ref[1], high))
    for v in range(2 * pairs):
        out_ref[v] = result[:, v * HALF : v * HALF + rank]


def shifted(x, axis, count, k):
    return lax.ppermute(x, axis, [(i, (i + k) % count) for i in range(count)])


def gathered(x, axis):
    count = lax.axis_size(axis)
    if count <= 4:
        return [x] + [shifted(x, axis, count, k) for k in range(1, count)]
    blocks = lax.all_gather(x, axis)
    return [blocks[k] for k in range(count)]


def both_ways(low, high, axis):
    ends = lax.axis_size(axis) - 1
    from_low = lax.ppermute(high, axis, [(i, i + 1) for i in range(ends)])
    from_high = lax.ppermute(low, axis, [(i + 1, i) for i in range(ends)])
    return from_low, from_high


def beside(block, axis):
    if lax.axis_size(axis) == 2:
        return lax.ppermute(block, axis, [(0, 1), (1, 0)])
    from_low, from_high = both_ways(block, block, axis)
    row = lax.broadcasted_iota(jnp.int32, block.shape, 2)
    return jnp.where(row < REACH, from_high, from_low)


def derivative_matrix(nz):
    matrix = np.zeros((nz, nz), np.float32)
    for k in range(1, REACH + 1):
        for z in range(nz):
            if z + k < nz:
                matrix[z + k, z] += WHOLE[k - 1]
            if z - k >= 0:
                matrix[z - k, z] -= WHOLE[k - 1]
    return np.concatenate([matrix, matrix], axis=0)


def rim_matrix(nvars, nz):
    matrix = np.zeros((nz, nz), np.float32)
    for v in range(nvars):
        for source in range(REACH):
            for target in range(REACH):
                left, right = target + REACH - source, source + REACH - target
                first, last = REACH * v, nz // 2 + REACH * v
                if left <= REACH:
                    matrix[first + source, first + target] -= WHOLE[left - 1]
                if right <= REACH:
                    matrix[last + source, last + target] += WHOLE[right - 1]
    return matrix


def y_matrices(nvars, ny):
    unit = np.zeros((nvars, ny, nvars, 2, ny), np.float32)
    shifts = np.zeros((3, nvars, ny, nvars, 2, ny), np.float32)
    for y in range(ny):
        unit[:, y, :, 0, y] = 1.0
        for k in range(1, REACH + 1):
            for source, sign in ((y + k, 1.0), (y - k, -1.0)):
                for v in range(nvars):
                    if source >= ny:
                        shifts[2, v, y, v, 1, source - ny] += sign * COEFFS[k - 1]
                    elif source < 0:
                        shifts[1, v, y, v, 1, source + ny] += sign * COEFFS[k - 1]
                    else:
                        shifts[0, v, y, v, 0, source] += sign * COEFFS[k - 1]
    return unit.reshape(nvars * ny, -1), shifts.reshape(3, nvars * ny, -1)


def local(fields, speeds, kinetics, block_rank, x_factor, y_factor, z_factor):
    nvars, nx, ny, nz = fields.shape
    rank = z_factor.shape[1]
    gx, gy, gz = (lax.axis_size(axis) for axis in ("gx", "gy", "gz"))
    ix, iy, iz = (lax.axis_index(axis) for axis in ("gx", "gy", "gz"))
    rim = (nvars, REACH, ny, nz)
    plane = (nx, ny, nz)
    dz = jnp.asarray(derivative_matrix(nz), BF16)
    rim_shift = jnp.asarray(rim_matrix(nvars, nz), BF16)
    unit, shifts = y_matrices(nvars, ny)
    edges = jnp.stack([iy > 0, iy < gy - 1]).astype(F32)
    places = jnp.stack([ix, iy]).astype(jnp.int32)
    scratch = [pltpu.VMEM(fields.shape, F32), pltpu.VMEM(plane, F32)]

    low, high, packed = call(pack_kernel, [(rim, F32), (rim, F32), (plane, F32)], [VMEM], (fields,))
    xl, xh = both_ways(low, high, "gx")
    zl, zh = both_ways(packed, packed, "gz")
    other = beside(fields, "gy")
    weights, zf = call(
        weight_kernel,
        [((2 * nvars * ny, 2 * nvars * ny), BF16), ((2 * nz, 4 * HALF), BF16)],
        [VMEM, VMEM, SMEM, VMEM, VMEM, VMEM],
        (kinetics, speeds, edges, unit, shifts, z_factor),
        [pltpu.VMEM((nz, 2 * HALF), F32)],
    )
    section, low, high, packed = call(
        section_kernel,
        [(fields.shape, F32), (rim, F32), (rim, F32), (plane, F32)],
        [VMEM] * 9 + [SMEM],
        (fields, xl, xh, other, zl, zh, weights, dz, rim_shift, speeds),
        scratch,
    )
    xl, xh = both_ways(low, high, "gx")
    zl, zh = both_ways(packed, packed, "gz")
    other = beside(section, "gy")
    fields_next, proj = call(
        next_kernel,
        [(fields.shape, F32), ((nvars // 2, nx * ny, 2 * HALF), F32)],
        [VMEM] * 11 + [SMEM],
        (fields, section, xl, xh, other, zl, zh, weights, dz, rim_shift, zf, speeds),
        scratch,
    )

    ranks = jnp.concatenate(gathered(block_rank.reshape(1, nx), "gx"), axis=1)
    y_rows = gathered(y_factor, "gy")
    a_count, b_count = x_factor.shape[1] // gx, y_factor.shape[1] // gy
    cells = gx * nx * gy * ny
    (factor,) = call(
        factor_kernel,
        [((2, a_count * b_count, cells), BF16)],
        [VMEM, SMEM, VMEM] + [VMEM] * gy,
        (ranks, places, x_factor, *y_rows),
        [pltpu.VMEM((a_count, gx * nx * ny), F32)],
    )

    pairs = nvars // 2 // gz
    chunks = proj.reshape(gz, pairs, nx * ny, 2 * HALF)
    own = lax.dynamic_index_in_dim(chunks, iz, 0, keepdims=False)
    for k in range(1, gz):
        piece = lax.dynamic_index_in_dim(chunks, lax.rem(iz + k, gz), 0, keepdims=False)
        own = own + shifted(piece, "gz", gz, k)
    blocks = [gathered(block, "gy") for block in gathered(own, "gx")]
    parts = [blocks[i][j] for j in range(gy) for i in range(gx)]
    (core,) = call(
        core_kernel,
        [((2 * pairs, a_count * b_count, rank), F32)],
        [VMEM] * (1 + len(parts)),
        (factor, *parts),
        room=16 if cells <= 1024 else 50,
    )
    return fields_next, core.reshape(2 * pairs, a_count, b_count, rank)


def solution(mesh):
    placed = (P(None, "gx", "gy", "gz"), P(), P(), P("gx"), P(), P("gy", None), P("gz", None))
    return jax.shard_map(
        local,
        mesh=mesh,
        in_specs=placed,
        out_specs=(P(None, "gx", "gy", "gz"), P("gz", "gx", "gy", None)),
        check_vma=False,
    )
```

time: 91.6 us -> 87.6 us (0.956)
  Pallas kernels: 28.9 us -> 19.1 us
  local copies, waits for them, and re-layouts: 7.81 us -> 13.8 us
  waiting for transfers between devices: 15.3 us -> 17.8 us
  starting transfers between devices: 35.8 us -> 34.3 us
  other arithmetic: 2.35 us -> 0.9 us
    pallas_call x5 -> x6, Pallas kernels: 28.9 us -> 19.1 us  [call(): pl.pallas_call(kernel, out_shape=tuple((jax.ShapeDtypeStruct(s, d) for s,...]
    unnamed x47 -> x39, local copies, waits for them, and re-layouts: 5.29 us -> 13.7 us
    ppermute x14, starting transfers between devices: 13.2 us -> 11.4 us  [shifted(): return lax.ppermute(x, axis, [(i, (i + k) % count) for i in range(count)])]
    ppermute x14, waiting for transfers between devices: 8.1 us -> 9.83 us  [shifted(): return lax.ppermute(x, axis, [(i, (i + k) % count) for i in range(count)])]
    reshape x2 -> x0, local copies, waits for them, and re-layouts: 1.35 us -> none  [the longest x1 0.68 us: local(): rank_of = jnp.broadcast_to(ranks[:, None, :, None], shape).reshape(1, -1)]
    squeeze x1, local copies, waits for them, and re-layouts: 1.01 us -> 0.02 us  [local(): lax.dynamic_index_in_dim(chunks, lax.rem(iz + k, gz), 0, keepdims=False)]
  transfers between devices with their start and end apart: 24 -> 24, of which waited for: 8 -> 8; matrix products, arithmetic and copies ran while one was open for 7% -> 2% of each run, Pallas kernels for 17% -> 6%
where the time goes in v2:
time: 87.6 us; the launch traced here: 86.7 us
  starting transfers between devices  34.3 us (39%)
  Pallas kernels  19.1 us (22%)
  waiting for transfers between devices  17.8 us (20%)
  local copies, waits for them, and re-layouts  13.8 us (16%)
  other arithmetic  0.9 us (1%)
    pallas_call x6, Pallas kernels, call(): pl.pallas_call(kernel, out_shape=tuple((jax.ShapeDtypeStruct(s, d) for s,...  19.1 us
    ppermute x4, starting transfers between devices, both_ways(): from_low = lax.ppermute(high, axis, [(i, i + 1) for i in range(ends)])  17.2 us
    unnamed x39, local copies, waits for them, and re-layouts  13.7 us
    ppermute x14, starting transfers between devices, shifted(): return lax.ppermute(x, axis, [(i, (i + k) % count) for i in range(count)])  11.4 us
    ppermute x14, waiting for transfers between devices, shifted(): return lax.ppermute(x, axis, [(i, (i + k) % count) for i in range(count)])  9.83 us
    ppermute x4, waiting for transfers between devices, both_ways(): from_high = lax.ppermute(low, axis, [(i + 1, i) for i in range(ends)])  6.31 us
    ppermute x4, starting transfers between devices, both_ways(): from_high = lax.ppermute(low, axis, [(i + 1, i) for i in range(ends)])  5.17 us
  transfers between devices with their start and end apart: 24, of which 8 were waited for; matrix products, arithmetic and copies ran while one was open for 2% of the time, Pallas kernels for 6%

profile of v2, /device:TPU:0, one launch (start us, length us, event | category | flops | bytes accessed | tf_op | source)
XLA Modules:
  0.0 86.7 jit_solution(13097990067641969645)
XLA Ops:
  0.6 0.6 collective-permute-start.2
  1.2 1.1 %copy-done = f32[16,12,8,128]{3,2,1,0:T(8,128)S(1)} copy-done((f32[16,12,8,128]{3,2,1,0:T(8,128)S(1)}, f32[16,12,8,128]{3,2,1,0:T(8,128)}, u32[]{:S(2)}) %copy-start) | copy-done | bytes 786456
  2.3 2.1 %shard_map.122 = (f32[16,4,8,128]{3,2,1,0:T(8,128)S(1)}, f32[16,4,8,128]{3,2,1,0:T(8,128)}, f32[12,8,128]{2,1,0:T(8,128)S(1)}) custom-call(f32[16,12,8,128]{3,2,1,0:T(8,128)S(1)} %copy-done), custom_call_target="tpu_custom_call" | custom-call | tf_op jit(solution)/shard_map/pallas_call | solution.py:24
  4.5 4.4 %collective-permute-start = (f32[16,4,8,128]{3,2,1,0:T(8,128)}, f32[16,4,8,128]{3,2,1,0:T(8,128)S(1)}, u32[]{:S(2)}, u32[]{:S(2)}) collective-permute-start(f32[16,4,8,128]{3,2,1,0:T(8,128)} %get-tuple-element.13), channel_id=1, source_target_pairs={{0,8},{8,16},{16,24},{1,9},{9,17},{17,25},{2,10},{10,18},{18,26},{... | collective-permute-start | bytes 786440 | tf_op jit(solution)/shard_map/ppermute | solution.py:231
  8.9 1.3 %collective-permute-start.1 = (f32[16,4,8,128]{3,2,1,0:T(8,128)S(1)}, f32[16,4,8,128]{3,2,1,0:T(8,128)S(1)}, u32[]{:S(2)}, u32[]{:S(2)}) collective-permute-start(f32[16,4,8,128]{3,2,1,0:T(8,128)S(1)} %get-tuple-element.14), channel_id=1, source_target_pairs={{8,0},{16,8},{24,16},{9,1},{17,9},{25,17},{10,2},{18,10},{26,18},{... | collective-permute-start | bytes 786440 | tf_op jit(solution)/shard_map/ppermute | solution.py:232
  10.2 1.3 %collective-permute-start.4 = (f32[12,8,128]{2,1,0:T(8,128)S(1)}, f32[12,8,128]{2,1,0:T(8,128)S(1)}, u32[]{:S(2)}, u32[]{:S(2)}) collective-permute-start(f32[12,8,128]{2,1,0:T(8,128)S(1)} %get-tuple-element.15), channel_id=1, source_target_pairs={{1,0},{2,1},{3,2},{5,4},{6,5},{7,6},{9,8},{10,9},{11,10},{13,12},{... | collective-permute-start | bytes 147464 | tf_op jit(solution)/shard_map/ppermute | solution.py:232
  11.5 4.5 %collective-permute-start.3 = (f32[12,8,128]{2,1,0:T(8,128)S(1)}, f32[12,8,128]{2,1,0:T(8,128)S(1)}, u32[]{:S(2)}, u32[]{:S(2)}) collective-permute-start(f32[12,8,128]{2,1,0:T(8,128)S(1)} %get-tuple-element.15), channel_id=1, source_target_pairs={{0,1},{1,2},{2,3},{4,5},{5,6},{6,7},{8,9},{9,10},{10,11},{12,13},{... | collective-permute-start | bytes 147464 | tf_op jit(solution)/shard_map/ppermute | solution.py:231
  16.1 0.8 copy.13.zf_ref
  17.0 1.0 %copy-done.3 = f32[3,128,256]{2,1,0:T(8,128)S(1)} copy-done((f32[3,128,256]{2,1,0:T(8,128)S(1)}, f32[3,128,256]{2,1,0:T(8,128)}, u32[]{:S(2)}) %copy-start.3) | copy-done | bytes 393240
  18.0 0.9 %copy-done.10 = f32[128,256]{1,0:T(8,128)S(1)} copy-done((f32[128,256]{1,0:T(8,128)S(1)}, f32[128,256]{1,0:T(8,128)}, u32[]{:S(2)}) %copy-start.10) | copy-done | bytes 131096
  18.9 0.7 copy-done.14
  19.5 0.7 copy-done.17
  20.2 1.1 %shard_map.123 = (bf16[256,256]{1,0:T(8,128)(2,1)S(1)}, bf16[256,256]{1,0:T(8,128)(2,1)S(1)}) custom-call(f32[16,16]{1,0:T(8,128)S(1)} %copy-done.17, f32[3,16]{1,0:T(4,128)S(1)} %copy-done.14, f32[2]{0:T(128)S(1)} %add_convert_fusion.edge_ref, f32[128,256]{1,0:T(8,128)S(1)} %copy-done.10, f32[3,128,256]{2,1,0:T(8,128)S(1)} %copy-done.3, ...), custom_call_target="tpu_custom_call" | custom-call | tf_op jit(solution)/shard_map/pallas_call | solution.py:24
  21.3 0.6 copy-done.8
  22.0 0.8 collective-permute-done.1.xh_ref
  22.8 1.1 %copy-done.1 = f32[16,12,8,128]{3,2,1,0:T(8,128)S(1)} copy-done((f32[16,12,8,128]{3,2,1,0:T(8,128)S(1)}, f32[16,12,8,128]{3,2,1,0:T(8,128)}, u32[]{:S(2)}) %copy-start.1) | copy-done | bytes 786456
  24.0 0.8 copy-done.4
  24.8 0.8 copy-done.6
  25.6 0.7 copy-done.15
  26.3 6.4 %shard_map.124 = (f32[16,12,8,128]{3,2,1,0:T(8,128)S(1)}, f32[16,4,8,128]{3,2,1,0:T(8,128)S(1)}, f32[16,4,8,128]{3,2,1,0:T(8,128)}, f32[12,8,128]{2,1,0:T(8,128)S(1)}) custom-call(f32[16,12,8,128]{3,2,1,0:T(8,128)S(1)} %copy-done.1, f32[16,4,8,128]{3,2,1,0:T(8,128)S(1)} %collective-permute-done.xl_ref, f32[16,4,8,128]{3,2,1,0:T(8,128)S(1)} %collective-permute-done.1.xh_ref, ...), custom_call_target="tpu_custom_call" | custom-call | tf_op jit(solution)/shard_map/pallas_call | solution.py:24
  32.6 3.7 %collective-permute-start.5 = (f32[16,4,8,128]{3,2,1,0:T(8,128)}, f32[16,4,8,128]{3,2,1,0:T(8,128)S(1)}, u32[]{:S(2)}, u32[]{:S(2)}) collective-permute-start(f32[16,4,8,128]{3,2,1,0:T(8,128)} %get-tuple-element.18), channel_id=1, source_target_pairs={{0,8},{8,16},{16,24},{1,9},{9,17},{17,25},{2,10},{10,18},{18,26},{... | collective-permute-start | bytes 786440 | tf_op jit(solution)/shard_map/ppermute | solution.py:231
  36.4 1.3 %collective-permute-start.6 = (f32[16,4,8,128]{3,2,1,0:T(8,128)S(1)}, f32[16,4,8,128]{3,2,1,0:T(8,128)S(1)}, u32[]{:S(2)}, u32[]{:S(2)}) collective-permute-start(f32[16,4,8,128]{3,2,1,0:T(8,128)S(1)} %get-tuple-element.19), channel_id=1, source_target_pairs={{8,0},{16,8},{24,16},{9,1},{17,9},{25,17},{10,2},{18,10},{26,18},{... | collective-permute-start | bytes 786440 | tf_op jit(solution)/shard_map/ppermute | solution.py:232
  37.7 1.3 %collective-permute-start.9 = (f32[12,8,128]{2,1,0:T(8,128)S(1)}, f32[12,8,128]{2,1,0:T(8,128)S(1)}, u32[]{:S(2)}, u32[]{:S(2)}) collective-permute-start(f32[12,8,128]{2,1,0:T(8,128)S(1)} %get-tuple-element.20), channel_id=1, source_target_pairs={{1,0},{2,1},{3,2},{5,4},{6,5},{7,6},{9,8},{10,9},{11,10},{13,12},{... | collective-permute-start | bytes 147464 | tf_op jit(solution)/shard_map/ppermute | solution.py:232
  39.0 4.5 %collective-permute-start.8 = (f32[12,8,128]{2,1,0:T(8,128)S(1)}, f32[12,8,128]{2,1,0:T(8,128)S(1)}, u32[]{:S(2)}, u32[]{:S(2)}) collective-permute-start(f32[12,8,128]{2,1,0:T(8,128)S(1)} %get-tuple-element.20), channel_id=1, source_target_pairs={{0,1},{1,2},{2,3},{4,5},{5,6},{6,7},{8,9},{9,10},{10,11},{12,13},{... | collective-permute-start | bytes 147464 | tf_op jit(solution)/shard_map/ppermute | solution.py:231
  43.7 1.6 %collective-permute-done.8.zl_ref = f32[12,8,128]{2,1,0:T(8,128)S(1)} collective-permute-done((f32[12,8,128]{2,1,0:T(8,128)S(1)}, f32[12,8,128]{2,1,0:T(8,128)S(1)}, u32[]{:S(2)}, u32[]{:S(2)}) %collective-permute-start.8) | collective-permute-done | bytes 49184 | tf_op jit(solution)/shard_map/ppermute | solution.py:231
  45.3 0.6 copy-done.11
  45.9 5.4 %collective-permute-done.6.xh_ref = f32[16,4,8,128]{3,2,1,0:T(8,128)S(1)} collective-permute-done((f32[16,4,8,128]{3,2,1,0:T(8,128)S(1)}, f32[16,4,8,128]{3,2,1,0:T(8,128)S(1)}, u32[]{:S(2)}, u32[]{:S(2)}) %collective-permute-start.6) | collective-permute-done | bytes 262176 | tf_op jit(solution)/shard_map/ppermute | solution.py:232
  51.3 0.9 %copy-done.9 = bf16[256,256]{1,0:T(8,128)(2,1)S(1)} copy-done((bf16[256,256]{1,0:T(8,128)(2,1)S(1)}, bf16[256,256]{1,0:T(8,128)(2,1)}, u32[]{:S(2)}) %copy-start.9) | copy-done | bytes 131096
  52.2 0.8 copy-done.12
  53.0 0.7 copy-done.16
  53.7 5.3 %shard_map.125 = (f32[16,12,8,128]{3,2,1,0:T(8,128)}, f32[8,96,128]{2,1,0:T(8,128)S(1)}) custom-call(f32[16,12,8,128]{3,2,1,0:T(8,128)S(1)} %copy-done.2, f32[16,12,8,128]{3,2,1,0:T(8,128)S(1)} %get-tuple-element.17.s_ref, f32[16,4,8,128]{3,2,1,0:T(8,128)S(1)} %collective-permute-done.5.xl_ref, f32[16,4,8,128]{3,2,1,0:T(8,128)S(1)} %collective-permute-done.6.xh_ref, ...), custom_call_target="tpu_custom_call" | custom-call | tf_op jit(solution)/shard_map/pallas_call | solution.py:24
  59.0 1.6 %collective-permute-start.14 = (f32[2,96,128]{2,1,0:T(8,128)S(1)}, f32[2,96,128]{2,1,0:T(8,128)S(1)}, u32[]{:S(2)}, u32[]{:S(2)}) collective-permute-start(f32[2,96,128]{2,1,0:T(8,128)S(1)} %get-tuple-element.24), channel_id=1, source_target_pairs={{0,1},{1,2},{2,3},{3,0},{4,5},{5,6},{6,7},{7,4},{8,9},{9,10},{10,1... | collective-permute-start | bytes 294920 | tf_op jit(solution)/shard_map/ppermute | solution.py:218
  60.6 2.2 %collective-permute-start.16 = (f32[2,96,128]{2,1,0:T(8,128)S(1)}, f32[2,96,128]{2,1,0:T(8,128)S(1)}, u32[]{:S(2)}, u32[]{:S(2)}) collective-permute-start(f32[2,96,128]{2,1,0:T(8,128)S(1)} %get-tuple-element.25), channel_id=1, source_target_pairs={{0,3},{1,0},{2,1},{3,2},{4,7},{5,4},{6,5},{7,6},{8,11},{9,8},{10,9... | collective-permute-start | bytes 294920 | tf_op jit(solution)/shard_map/ppermute | solution.py:218
  62.9 0.8 collective-permute-start.15
  63.6 2.1 %collective-permute-start.11 = (s32[1,12]{1,0:T(1,128)}, s32[1,12]{1,0:T(1,128)S(1)}, u32[]{:S(2)}, u32[]{:S(2)}) collective-permute-start(s32[1,12]{1,0:T(1,128)} %bitcast.23), channel_id=1, source_target_pairs={{0,16},{8,24},{16,0},{24,8},{1,17},{9,25},{17,1},{25,9},{2,18},{10... | collective-permute-start | bytes 152 | tf_op jit(solution)/shard_map/ppermute | solution.py:218
  65.7 0.8 collective-permute-done.14
  66.5 0.3 collective-permute-done.16
  66.8 4.7 %collective-permute-done.15 = f32[2,96,128]{2,1,0:T(8,128)S(1)} collective-permute-done((f32[2,96,128]{2,1,0:T(8,128)S(1)}, f32[2,96,128]{2,1,0:T(8,128)S(1)}, u32[]{:S(2)}, u32[]{:S(2)}) %collective-permute-start.15) | collective-permute-done | bytes 98336 | tf_op jit(solution)/shard_map/ppermute | solution.py:218
  71.6 2.1 %collective-permute-start.18 = (f32[2,96,128]{2,1,0:T(8,128)S(1)}, f32[2,96,128]{2,1,0:T(8,128)S(1)}, u32[]{:S(2)}, u32[]{:S(2)}) collective-permute-start(f32[2,96,128]{2,1,0:T(8,128)S(1)} %fusion.1.refs_0_), channel_id=1, source_target_pairs={{0,16},{8,24},{16,0},{24,8},{1,17},{9,25},{17,1},{25,9},{2,18},{10... | collective-permute-start | bytes 294920 | tf_op jit(solution)/shard_map/ppermute | solution.py:218
  73.7 1.5 %collective-permute-start.10 = (s32[1,12]{1,0:T(1,128)}, s32[1,12]{1,0:T(1,128)S(1)}, u32[]{:S(2)}, u32[]{:S(2)}) collective-permute-start(s32[1,12]{1,0:T(1,128)} %bitcast.24), channel_id=1, source_target_pairs={{0,8},{8,16},{16,24},{24,0},{1,9},{9,17},{17,25},{25,1},{2,10},{10... | collective-permute-start | bytes 152 | tf_op jit(solution)/shard_map/ppermute | solution.py:218
  75.2 4.0 %collective-permute-done.10 = s32[1,12]{1,0:T(1,128)S(1)} collective-permute-done((s32[1,12]{1,0:T(1,128)}, s32[1,12]{1,0:T(1,128)S(1)}, u32[]{:S(2)}, u32[]{:S(2)}) %collective-permute-start.10) | collective-permute-done | bytes 80 | tf_op jit(solution)/shard_map/ppermute | solution.py:218
  79.2 0.5 collective-permute-start.23
  79.8 0.4 collective-permute-start.21
  80.3 0.7 pad_add_fusion.rank_ref
  81.0 0.7 copy-done.13
  81.7 0.7 copy-done.18
  82.4 1.9 %shard_map.126.q_ref = bf16[2,768,768]{2,1,0:T(8,128)(2,1)S(1)} custom-call(s32[1,48]{1,0:T(1,128)S(1)} %pad_add_fusion.rank_ref, s32[2]{0:T(128)S(1)} %pad_add_fusion.1.place_ref, f32[48,96]{1,0:T(8,128)S(1)} %copy-done.13, f32[8,64]{1,0:T(8,128)S(1)} %copy-done.18, f32[8,64]{1,0:T(8,128)S(1)} %collective-permute-done.13.refs_1_), custom_call_target="tpu_custom_call" | custom-call | tf_op jit(solution)/shard_map/pallas_call | solution.py:24
  84.4 2.3 %shard_map.127 = f32[4,768,54]{2,1,0:T(8,128)} custom-call(bf16[2,768,768]{2,1,0:T(8,128)(2,1)S(1)} %shard_map.126.q_ref, f32[2,96,128]{2,1,0:T(8,128)S(1)} %fusion.1.refs_0_, f32[2,96,128]{2,1,0:T(8,128)S(1)} %collective-permute-done.17.refs_1_, f32[2,96,128]{2,1,0:T(8,128)S(1)} %collective-permute-done.18.refs_2_, ...), custom_call_target="tpu_custom_call" | custom-call | tf_op jit(solution)/shard_map/pallas_call | solution.py:24
  (50 shorter events, 0.5 us)
Async XLA Ops:
  0.6 22.2 %collective-permute-start.2 = (f32[16,12,8,128]{3,2,1,0:T(8,128)}, f32[16,12,8,128]{3,2,1,0:T(8,128)S(1)}, u32[]{:S(2)}, u32[]{:S(2)}) collective-permute-start(f32[16,12,8,128]{3,2,1,0:T(8,128)} %f_ref.5), channel_id=1, source_target_pairs={{0,4},{4,0},{1,5},{5,1},{2,6},{6,2},{3,7},{7,3},{8,12},{12,8},{9,1... | collective-permute-start | bytes 2359304 | tf_op jit(solution)/shard_map/ppermute | solution.py:238
  1.2 1.1 %copy-start = (f32[16,12,8,128]{3,2,1,0:T(8,128)S(1)}, f32[16,12,8,128]{3,2,1,0:T(8,128)}, u32[]{:S(2)}) copy-start(f32[16,12,8,128]{3,2,1,0:T(8,128)} %f_ref.5) | copy-start | bytes 2359300
  2.3 48.9 %copy-start.2 = (f32[16,12,8,128]{3,2,1,0:T(8,128)S(1)}, f32[16,12,8,128]{3,2,1,0:T(8,128)}, u32[]{:S(2)}) copy-start(f32[16,12,8,128]{3,2,1,0:T(8,128)} %f_ref.5) | copy-start | bytes 2359300
  2.3 48.9 %copy-start.5 = (bf16[256,128]{1,0:T(8,128)(2,1)S(1)}, bf16[256,128]{1,0:T(8,128)(2,1)}, u32[]{:S(2)}) copy-start(bf16[256,128]{1,0:T(8,128)(2,1)} %constant.46.clone.dz_ref) | copy-start | bytes 196612
  2.3 48.9 %copy-start.7 = (bf16[128,128]{1,0:T(8,128)(2,1)S(1)}, bf16[128,128]{1,0:T(8,128)(2,1)}, u32[]{:S(2)}) copy-start(bf16[128,128]{1,0:T(8,128)(2,1)} %constant.47.clone.shift_ref) | copy-start | bytes 98308
  4.5 17.5 %collective-permute-start = (f32[16,4,8,128]{3,2,1,0:T(8,128)}, f32[16,4,8,128]{3,2,1,0:T(8,128)S(1)}, u32[]{:S(2)}, u32[]{:S(2)}) collective-permute-start(f32[16,4,8,128]{3,2,1,0:T(8,128)} %get-tuple-element.13), channel_id=1, source_target_pairs={{0,8},{8,16},{16,24},{1,9},{9,17},{17,25},{2,10},{10,18},{18,26},{... | collective-permute-start | bytes 786440 | tf_op jit(solution)/shard_map/ppermute | solution.py:231
  8.9 14.0 %collective-permute-start.1 = (f32[16,4,8,128]{3,2,1,0:T(8,128)S(1)}, f32[16,4,8,128]{3,2,1,0:T(8,128)S(1)}, u32[]{:S(2)}, u32[]{:S(2)}) collective-permute-start(f32[16,4,8,128]{3,2,1,0:T(8,128)S(1)} %get-tuple-element.14), channel_id=1, source_target_pairs={{8,0},{16,8},{24,16},{9,1},{17,9},{25,17},{10,2},{18,10},{26,18},{... | collective-permute-start | bytes 786440 | tf_op jit(solution)/shard_map/ppermute | solution.py:232
  10.2 11.8 %collective-permute-start.4 = (f32[12,8,128]{2,1,0:T(8,128)S(1)}, f32[12,8,128]{2,1,0:T(8,128)S(1)}, u32[]{:S(2)}, u32[]{:S(2)}) collective-permute-start(f32[12,8,128]{2,1,0:T(8,128)S(1)} %get-tuple-element.15), channel_id=1, source_target_pairs={{1,0},{2,1},{3,2},{5,4},{6,5},{7,6},{9,8},{10,9},{11,10},{13,12},{... | collective-permute-start | bytes 147464 | tf_op jit(solution)/shard_map/ppermute | solution.py:232
  11.5 10.5 %collective-permute-start.3 = (f32[12,8,128]{2,1,0:T(8,128)S(1)}, f32[12,8,128]{2,1,0:T(8,128)S(1)}, u32[]{:S(2)}, u32[]{:S(2)}) collective-permute-start(f32[12,8,128]{2,1,0:T(8,128)S(1)} %get-tuple-element.15), channel_id=1, source_target_pairs={{0,1},{1,2},{2,3},{4,5},{5,6},{6,7},{8,9},{9,10},{10,11},{12,13},{... | collective-permute-start | bytes 147464 | tf_op jit(solution)/shard_map/ppermute | solution.py:231
  17.0 1.0 %copy-start.3 = (f32[3,128,256]{2,1,0:T(8,128)S(1)}, f32[3,128,256]{2,1,0:T(8,128)}, u32[]{:S(2)}) copy-start(f32[3,128,256]{2,1,0:T(8,128)} %constant.49.clone.shift_ref) | copy-start | bytes 1179652
  18.0 0.9 %copy-start.10 = (f32[128,256]{1,0:T(8,128)S(1)}, f32[128,256]{1,0:T(8,128)}, u32[]{:S(2)}) copy-start(f32[128,256]{1,0:T(8,128)} %constant.48.clone.unit_ref) | copy-start | bytes 393220
  18.9 0.7 copy-start.14
  19.5 0.7 copy-start.17
  21.3 0.7 copy-start.8
  22.8 1.1 %copy-start.1 = (f32[16,12,8,128]{3,2,1,0:T(8,128)S(1)}, f32[16,12,8,128]{3,2,1,0:T(8,128)}, u32[]{:S(2)}) copy-start(f32[16,12,8,128]{3,2,1,0:T(8,128)} %f_ref.5) | copy-start | bytes 2359300
  24.0 0.8 copy-start.4
  24.8 0.8 copy-start.6
  25.6 0.7 copy-start.15
  32.6 18.6 %collective-permute-start.7 = (f32[16,12,8,128]{3,2,1,0:T(8,128)S(1)}, f32[16,12,8,128]{3,2,1,0:T(8,128)S(1)}, u32[]{:S(2)}, u32[]{:S(2)}) collective-permute-start(f32[16,12,8,128]{3,2,1,0:T(8,128)S(1)} %get-tuple-element.17.s_ref), channel_id=1, source_target_pairs={{0,4},{4,0},{1,5},{5,1},{2,6},{6,2},{3,7},{7,3},{8,12},{12,8},{9,1... | collective-permute-start | bytes 2359304 | tf_op jit(solution)/shard_map/ppermute | solution.py:238
  32.6 13.2 %collective-permute-start.5 = (f32[16,4,8,128]{3,2,1,0:T(8,128)}, f32[16,4,8,128]{3,2,1,0:T(8,128)S(1)}, u32[]{:S(2)}, u32[]{:S(2)}) collective-permute-start(f32[16,4,8,128]{3,2,1,0:T(8,128)} %get-tuple-element.18), channel_id=1, source_target_pairs={{0,8},{8,16},{16,24},{1,9},{9,17},{17,25},{2,10},{10,18},{18,26},{... | collective-permute-start | bytes 786440 | tf_op jit(solution)/shard_map/ppermute | solution.py:231
  36.4 14.9 %collective-permute-start.6 = (f32[16,4,8,128]{3,2,1,0:T(8,128)S(1)}, f32[16,4,8,128]{3,2,1,0:T(8,128)S(1)}, u32[]{:S(2)}, u32[]{:S(2)}) collective-permute-start(f32[16,4,8,128]{3,2,1,0:T(8,128)S(1)} %get-tuple-element.19), channel_id=1, source_target_pairs={{8,0},{16,8},{24,16},{9,1},{17,9},{25,17},{10,2},{18,10},{26,18},{... | collective-permute-start | bytes 786440 | tf_op jit(solution)/shard_map/ppermute | solution.py:232
  37.7 6.0 %collective-permute-start.9 = (f32[12,8,128]{2,1,0:T(8,128)S(1)}, f32[12,8,128]{2,1,0:T(8,128)S(1)}, u32[]{:S(2)}, u32[]{:S(2)}) collective-permute-start(f32[12,8,128]{2,1,0:T(8,128)S(1)} %get-tuple-element.20), channel_id=1, source_target_pairs={{1,0},{2,1},{3,2},{5,4},{6,5},{7,6},{9,8},{10,9},{11,10},{13,12},{... | collective-permute-start | bytes 147464 | tf_op jit(solution)/shard_map/ppermute | solution.py:232
  39.0 6.3 %collective-permute-start.8 = (f32[12,8,128]{2,1,0:T(8,128)S(1)}, f32[12,8,128]{2,1,0:T(8,128)S(1)}, u32[]{:S(2)}, u32[]{:S(2)}) collective-permute-start(f32[12,8,128]{2,1,0:T(8,128)S(1)} %get-tuple-element.20), channel_id=1, source_target_pairs={{0,1},{1,2},{2,3},{4,5},{5,6},{6,7},{8,9},{9,10},{10,11},{12,13},{... | collective-permute-start | bytes 147464 | tf_op jit(solution)/shard_map/ppermute | solution.py:231
  45.3 0.6 copy-start.11
  51.3 0.9 %copy-start.9 = (bf16[256,256]{1,0:T(8,128)(2,1)S(1)}, bf16[256,256]{1,0:T(8,128)(2,1)}, u32[]{:S(2)}) copy-start(bf16[256,256]{1,0:T(8,128)(2,1)} %copy-done.8) | copy-start | bytes 393220
  52.2 0.8 copy-start.12
  53.0 0.7 copy-start.16
  59.0 7.5 %collective-permute-start.14 = (f32[2,96,128]{2,1,0:T(8,128)S(1)}, f32[2,96,128]{2,1,0:T(8,128)S(1)}, u32[]{:S(2)}, u32[]{:S(2)}) collective-permute-start(f32[2,96,128]{2,1,0:T(8,128)S(1)} %get-tuple-element.24), channel_id=1, source_target_pairs={{0,1},{1,2},{2,3},{3,0},{4,5},{5,6},{6,7},{7,4},{8,9},{9,10},{10,1... | collective-permute-start | bytes 294920 | tf_op jit(solution)/shard_map/ppermute | solution.py:218
  60.6 6.2 %collective-permute-start.16 = (f32[2,96,128]{2,1,0:T(8,128)S(1)}, f32[2,96,128]{2,1,0:T(8,128)S(1)}, u32[]{:S(2)}, u32[]{:S(2)}) collective-permute-start(f32[2,96,128]{2,1,0:T(8,128)S(1)} %get-tuple-element.25), channel_id=1, source_target_pairs={{0,3},{1,0},{2,1},{3,2},{4,7},{5,4},{6,5},{7,6},{8,11},{9,8},{10,9... | collective-permute-start | bytes 294920 | tf_op jit(solution)/shard_map/ppermute | solution.py:218
  62.9 8.6 %collective-permute-start.15 = (f32[2,96,128]{2,1,0:T(8,128)S(1)}, f32[2,96,128]{2,1,0:T(8,128)S(1)}, u32[]{:S(2)}, u32[]{:S(2)}) collective-permute-start(f32[2,96,128]{2,1,0:T(8,128)S(1)} %get-tuple-element.26), channel_id=1, source_target_pairs={{0,2},{1,3},{2,0},{3,1},{4,6},{5,7},{6,4},{7,5},{8,10},{9,11},{10,... | collective-permute-start | bytes 294920 | tf_op jit(solution)/shard_map/ppermute | solution.py:218
  63.6 10.1 %collective-permute-start.12 = (s32[1,12]{1,0:T(1,128)}, s32[1,12]{1,0:T(1,128)S(1)}, u32[]{:S(2)}, u32[]{:S(2)}) collective-permute-start(s32[1,12]{1,0:T(1,128)} %bitcast.22), channel_id=1, source_target_pairs={{0,24},{8,0},{16,8},{24,16},{1,25},{9,1},{17,9},{25,17},{2,26},{10... | collective-permute-start | bytes 152 | tf_op jit(solution)/shard_map/ppermute | solution.py:218
  63.6 11.6 %collective-permute-start.11 = (s32[1,12]{1,0:T(1,128)}, s32[1,12]{1,0:T(1,128)S(1)}, u32[]{:S(2)}, u32[]{:S(2)}) collective-permute-start(s32[1,12]{1,0:T(1,128)} %bitcast.23), channel_id=1, source_target_pairs={{0,16},{8,24},{16,0},{24,8},{1,17},{9,25},{17,1},{25,9},{2,18},{10... | collective-permute-start | bytes 152 | tf_op jit(solution)/shard_map/ppermute | solution.py:218
  71.5 7.7 %collective-permute-start.19 = (f32[2,96,128]{2,1,0:T(8,128)S(1)}, f32[2,96,128]{2,1,0:T(8,128)S(1)}, u32[]{:S(2)}, u32[]{:S(2)}) collective-permute-start(f32[2,96,128]{2,1,0:T(8,128)S(1)} %fusion.1.refs_0_), channel_id=1, source_target_pairs={{0,24},{8,0},{16,8},{24,16},{1,25},{9,1},{17,9},{25,17},{2,26},{10... | collective-permute-start | bytes 294920 | tf_op jit(solution)/shard_map/ppermute | solution.py:218
  71.6 8.2 %collective-permute-start.18 = (f32[2,96,128]{2,1,0:T(8,128)S(1)}, f32[2,96,128]{2,1,0:T(8,128)S(1)}, u32[]{:S(2)}, u32[]{:S(2)}) collective-permute-start(f32[2,96,128]{2,1,0:T(8,128)S(1)} %fusion.1.refs_0_), channel_id=1, source_target_pairs={{0,16},{8,24},{16,0},{24,8},{1,17},{9,25},{17,1},{25,9},{2,18},{10... | collective-permute-start | bytes 294920 | tf_op jit(solution)/shard_map/ppermute | solution.py:218
  73.6 6.2 %collective-permute-start.17 = (f32[2,96,128]{2,1,0:T(8,128)S(1)}, f32[2,96,128]{2,1,0:T(8,128)S(1)}, u32[]{:S(2)}, u32[]{:S(2)}) collective-permute-start(f32[2,96,128]{2,1,0:T(8,128)S(1)} %fusion.1.refs_0_), channel_id=1, source_target_pairs={{0,8},{8,16},{16,24},{24,0},{1,9},{9,17},{17,25},{25,1},{2,10},{10... | collective-permute-start | bytes 294920 | tf_op jit(solution)/shard_map/ppermute | solution.py:218
  73.7 5.5 %collective-permute-start.10 = (s32[1,12]{1,0:T(1,128)}, s32[1,12]{1,0:T(1,128)S(1)}, u32[]{:S(2)}, u32[]{:S(2)}) collective-permute-start(s32[1,12]{1,0:T(1,128)} %bitcast.24), channel_id=1, source_target_pairs={{0,8},{8,16},{16,24},{24,0},{1,9},{9,17},{17,25},{25,1},{2,10},{10... | collective-permute-start | bytes 152 | tf_op jit(solution)/shard_map/ppermute | solution.py:218
  75.2 5.8 %collective-permute-start.13 = (f32[8,64]{1,0:T(8,128)}, f32[8,64]{1,0:T(8,128)S(1)}, u32[]{:S(2)}, u32[]{:S(2)}) collective-permute-start(f32[8,64]{1,0:T(8,128)} %refs_0_.1), channel_id=1, source_target_pairs={{0,4},{4,0},{1,5},{5,1},{2,6},{6,2},{3,7},{7,3},{8,12},{12,8},{9,1... | collective-permute-start | bytes 6152 | tf_op jit(solution)/shard_map/ppermute | solution.py:218
  79.2 5.1 %collective-permute-start.20 = (f32[2,96,128]{2,1,0:T(8,128)S(1)}, f32[2,96,128]{2,1,0:T(8,128)S(1)}, u32[]{:S(2)}, u32[]{:S(2)}) collective-permute-start(f32[2,96,128]{2,1,0:T(8,128)S(1)} %fusion.1.refs_0_), channel_id=1, source_target_pairs={{0,4},{4,0},{1,5},{5,1},{2,6},{6,2},{3,7},{7,3},{8,12},{12,8},{9,1... | collective-permute-start | bytes 294920 | tf_op jit(solution)/shard_map/ppermute | solution.py:218
  79.2 5.1 %collective-permute-start.23 = (f32[2,96,128]{2,1,0:T(8,128)S(1)}, f32[2,96,128]{2,1,0:T(8,128)S(1)}, u32[]{:S(2)}, u32[]{:S(2)}) collective-permute-start(f32[2,96,128]{2,1,0:T(8,128)S(1)} %collective-permute-done.19.refs_3_), channel_id=1, source_target_pairs={{0,4},{4,0},{1,5},{5,1},{2,6},{6,2},{3,7},{7,3},{8,12},{12,8},{9,1... | collective-permute-start | bytes 294920 | tf_op jit(solution)/shard_map/ppermute | solution.py:218
  79.8 4.6 %collective-permute-start.22 = (f32[2,96,128]{2,1,0:T(8,128)S(1)}, f32[2,96,128]{2,1,0:T(8,128)S(1)}, u32[]{:S(2)}, u32[]{:S(2)}) collective-permute-start(f32[2,96,128]{2,1,0:T(8,128)S(1)} %collective-permute-done.18.refs_2_), channel_id=1, source_target_pairs={{0,4},{4,0},{1,5},{5,1},{2,6},{6,2},{3,7},{7,3},{8,12},{12,8},{9,1... | collective-permute-start | bytes 294920 | tf_op jit(solution)/shard_map/ppermute | solution.py:218
  79.8 4.5 %collective-permute-start.21 = (f32[2,96,128]{2,1,0:T(8,128)S(1)}, f32[2,96,128]{2,1,0:T(8,128)S(1)}, u32[]{:S(2)}, u32[]{:S(2)}) collective-permute-start(f32[2,96,128]{2,1,0:T(8,128)S(1)} %collective-permute-done.17.refs_1_), channel_id=1, source_target_pairs={{0,4},{4,0},{1,5},{5,1},{2,6},{6,2},{3,7},{7,3},{8,12},{12,8},{9,1... | collective-permute-start | bytes 294920 | tf_op jit(solution)/shard_map/ppermute | solution.py:218
  81.0 0.7 copy-start.13
  81.7 0.7 copy-start.18

commit v3 on v2

v3 whole, which is shorter than its diff:
```python
import functools

import jax
import jax.numpy as jnp
from jax import lax
from jax.experimental import pallas as pl
from jax.experimental.pallas import tpu as pltpu
from jax.sharding import PartitionSpec as P

COEFFS = (0.8, -0.2, 4.0 / 105.0, -1.0 / 280.0)
SCALE = 840.0
WHOLE = (672.0, -168.0, 32.0, -3.0)
TIME_STEP = 0.45
REACH = len(COEFFS)
HALF = 64
F32, BF16 = jnp.float32, jnp.bfloat16
HIGHEST = lax.Precision.HIGHEST
VMEM = pl.BlockSpec(memory_space=pltpu.VMEM)
SMEM = pl.BlockSpec(memory_space=pltpu.SMEM)


def call(kernel, out_shapes, in_specs, args, scratch=(), room=16):
    return pl.pallas_call(
        kernel,
        out_shape=tuple(jax.ShapeDtypeStruct(s, d) for s, d in out_shapes),
        in_specs=in_specs,
        out_specs=tuple(VMEM for _ in out_shapes),
        scratch_shapes=list(scratch),
        compiler_params=pltpu.CompilerParams(vmem_limit_bytes=room * 2**20),
    )(*args)


def dot(a, b):
    return jnp.dot(a, b, preferred_element_type=F32)


def exact(a, b, dims=((1,), (0,))):
    return lax.dot_general(a, b, (dims, ((), ())), precision=HIGHEST, preferred_element_type=F32)


def split(x):
    high = x.astype(BF16)
    return high, (x - high.astype(F32)).astype(BF16)


def rim_kernel(f_ref, low_ref, high_ref, sems):
    top = f_ref.shape[1] - REACH
    copies = [
        pltpu.make_async_copy(f_ref.at[:, pl.ds(start, REACH)], target, sems.at[i])
        for i, (start, target) in enumerate(((0, low_ref), (top, high_ref)))
    ]
    for copy in copies:
        copy.start()
    for copy in copies:
        copy.wait()


def pack_rim(v, values, rim_ref):
    width = values.shape[2]
    group = lax.shift_right_logical(lax.broadcasted_iota(jnp.int32, values.shape, 2), 2)
    last = pltpu.roll(values, REACH * v + REACH, 2)
    first = pltpu.roll(values, width // 2 + REACH * v, 2)
    rim = jnp.where(group == v, last, rim_ref[...])
    rim_ref[...] = jnp.where(group == v + width // 2 // REACH, first, rim)


def pack_kernel(f_ref, rim_ref):
    rim_ref[...] = jnp.zeros_like(rim_ref)

    def step(v, carry):
        pack_rim(v, f_ref[v], rim_ref)
        return carry

    lax.fori_loop(0, f_ref.shape[0], step, 0, unroll=4)


def iota(shape, dim):
    return lax.broadcasted_iota(jnp.int32, shape, dim)


def low_bits(x, size):
    return lax.rem(x, jnp.int32(size))


def weight_kernel(kin_ref, speed_ref, zf_ref, w_ref, zf_out_ref, dz_ref, shift_ref, scale_ref, wide_ref):
    nvars = kin_ref.shape[0]
    rows, columns = w_ref.shape[0] // 2, w_ref.shape[1]
    ny = rows // nvars
    spread = (iota((rows, nvars), 0) // ny == iota((rows, nvars), 1)).astype(F32)
    gather = (iota((nvars, columns), 1) // (2 * ny) == iota((nvars, columns), 0)).astype(F32)
    rates = exact(exact(spread, kin_ref[...]), gather)
    speed = exact(spread, speed_ref[...], ((1,), (1,)))[:, 1:2]
    row, column = iota((rows, columns), 0), iota((rows, columns), 1)
    y, other = low_bits(row, ny), low_bits(column, 2 * ny)
    iy = lax.axis_index("gy")
    below, above = iy > 0, iy < lax.axis_size("gy") - 1
    far = 8 * ny
    up = jnp.where(above, other - y, far)
    down = jnp.where(below, other - 2 * ny - y, far)
    offset = jnp.where(other < ny, other - y, jnp.where(other < ny + REACH, up, down))
    shifts = jnp.zeros((rows, columns), F32)
    for k in range(1, REACH + 1):
        shifts = jnp.where(offset == k, COEFFS[k - 1], jnp.where(offset == -k, -COEFFS[k - 1], shifts))
    shifts = jnp.where(row // ny == column // (2 * ny), speed * shifts, 0.0)
    high, low = split(TIME_STEP * (jnp.where(other == y, rates, 0.0) - shifts))
    w_ref[0:rows] = high
    w_ref[rows:] = low

    depth, rank = zf_ref.shape[1], zf_ref.shape[0]
    identity = (iota((depth, depth), 0) == iota((depth, depth), 1)).astype(F32)
    wide_ref[...] = jnp.zeros_like(wide_ref)
    wide_ref[:, 0:rank] = exact(identity, zf_ref[...], ((1,), (1,)))
    high, low = split(wide_ref[...])
    zf_out_ref[0:depth, 0 : 2 * HALF] = high
    zf_out_ref[0:depth, 2 * HALF :] = low
    high, low = split(pltpu.roll(wide_ref[...], HALF, 1))
    zf_out_ref[depth:, 0 : 2 * HALF] = high
    zf_out_ref[depth:, 2 * HALF :] = low

    source, target = iota((depth, depth), 0), iota((depth, depth), 1)
    offset = source - target
    inner = jnp.zeros((depth, depth), F32)
    for k in range(1, REACH + 1):
        inner = jnp.where(offset == k, WHOLE[k - 1], jnp.where(offset == -k, -WHOLE[k - 1], inner))
    dz_ref[0:depth] = inner.astype(BF16)
    dz_ref[depth:] = inner.astype(BF16)
    turn = low_bits(target, REACH) - low_bits(source, REACH)
    first = source < depth // 2
    offset = REACH + jnp.where(first, turn, -turn)
    outer = jnp.zeros((depth, depth), F32)
    for k in range(1, REACH + 1):
        outer = jnp.where(offset == k, WHOLE[k - 1], outer)
    outer = jnp.where(source // REACH == target // REACH, jnp.where(first, -outer, outer), 0.0)
    shift_ref[...] = outer.astype(BF16)

    tile = scale_ref.shape[2:]
    for v in range(nvars):
        scale_ref[v, 0] = jnp.broadcast_to(TIME_STEP * speed_ref[0:1, v : v + 1], tile)
        scale_ref[v, 1] = jnp.broadcast_to(TIME_STEP / SCALE * speed_ref[2:3, v : v + 1], tile)


def mix_planes(q_ref, beside_ref, w_ref, rate_ref):
    nvars, nx, ny, nz = q_ref.shape
    rows = nvars * ny

    def step(i, carry):
        high, low = [], []
        for p in (2 * i, 2 * i + 1):
            cells = jnp.concatenate([q_ref[:, p], beside_ref[:, p]], axis=1)
            h, l = split(cells.reshape(2 * rows, nz))
            high.append(h)
            low.append(l)
        both = dot(w_ref[...], jnp.concatenate(high, axis=1))
        total = both[:rows] + both[rows:] + dot(w_ref[0:rows], jnp.concatenate(low, axis=1))
        for j in range(2):
            rate_ref[:, 2 * i + j] = total[:, j * nz : (j + 1) * nz].reshape(nvars, ny, nz)
        return carry

    lax.fori_loop(0, nx // 2, step, 0, unroll=True)


def join_rims(zl_ref, zh_ref, shift_ref, rim_ref):
    nx, ny, nz = rim_ref.shape
    lane = lax.broadcasted_iota(jnp.int32, rim_ref.shape, 2)
    rim = jnp.where(lane < nz // 2, zl_ref[...], zh_ref[...]).reshape(nx * ny, nz)
    high, low = split(rim)
    rim_ref[...] = (dot(high, shift_ref[...]) + dot(low, shift_ref[...])).reshape(rim_ref.shape)


def step_of(v, q_ref, xl_ref, xh_ref, dz_ref, rate_ref, rim_ref, scale_ref):
    nvars, nx, ny, nz = q_ref.shape
    q = q_ref[v]
    tall = jnp.concatenate([xl_ref[v], q, xh_ref[v]], axis=0)
    gx = None
    for k in range(1, REACH + 1):
        part = COEFFS[k - 1] * (tall[REACH + k : REACH + k + nx] - tall[REACH - k : REACH - k + nx])
        gx = part if gx is None else gx + part
    high, low = split(q.reshape(nx * ny, nz))
    gz = dot(jnp.concatenate([high, low], axis=1), dz_ref[...]).reshape(nx, ny, nz)
    lane = lax.broadcasted_iota(jnp.int32, q.shape, 2)
    rim = rim_ref[...]
    first = pltpu.roll(rim, lax.rem(nz - REACH * v, nz), 2)
    last = pltpu.roll(rim, nz // 2 - REACH - REACH * v, 2)
    gz = gz + jnp.where(lane < REACH, first, jnp.where(lane >= nz - REACH, last, 0.0))
    return rate_ref[v] - scale_ref[v, 0] * gx - scale_ref[v, 1] * gz


def section_kernel(
    f_ref, xl_ref, xh_ref, beside_ref, zl_ref, zh_ref, w_ref, dz_ref, shift_ref, scale_ref,
    s_ref, low_ref, high_ref, out_rim_ref, rate_ref, rim_ref,
):
    mix_planes(f_ref, beside_ref, w_ref, rate_ref)
    join_rims(zl_ref, zh_ref, shift_ref, rim_ref)
    out_rim_ref[...] = jnp.zeros_like(out_rim_ref)

    def step(v, carry):
        s = f_ref[v] + step_of(v, f_ref, xl_ref, xh_ref, dz_ref, rate_ref, rim_ref, scale_ref)
        s_ref[v] = s
        low_ref[v] = s[:REACH]
        high_ref[v] = s[s.shape[0] - REACH :]
        pack_rim(v, s, out_rim_ref)
        return carry

    lax.fori_loop(0, f_ref.shape[0], step, 0, unroll=4)


def next_kernel(
    f_ref, s_ref, xl_ref, xh_ref, beside_ref, zl_ref, zh_ref, w_ref, dz_ref, shift_ref, zf_ref, scale_ref,
    next_ref, proj_ref, rate_ref, rim_ref,
):
    nvars, nx, ny, nz = f_ref.shape
    mix_planes(s_ref, beside_ref, w_ref, rate_ref)
    join_rims(zl_ref, zh_ref, shift_ref, rim_ref)

    def step(p, carry):
        both = []
        for v in (2 * p, 2 * p + 1):
            rate = step_of(v, s_ref, xl_ref, xh_ref, dz_ref, rate_ref, rim_ref, scale_ref)
            new = 0.5 * (f_ref[v] + s_ref[v] + rate)
            next_ref[v] = new
            both.append(new.reshape(nx * ny, nz))
        high, low = split(jnp.concatenate(both, axis=1))
        wide = dot(high, zf_ref[...])
        proj_ref[p] = wide[:, : 2 * HALF] + wide[:, 2 * HALF :] + dot(low, zf_ref[:, : 2 * HALF])
        return carry

    lax.fori_loop(0, nvars // 2, step, 0, unroll=2)


def factor_kernel(rank_ref, xf_ref, *refs):
    y_refs, (out_ref, xt_ref) = refs[:-2], refs[-2:]
    planes, a_count = rank_ref.shape[1], xt_ref.shape[0]
    ny = y_refs[0].shape[0]
    width = planes * ny
    b_count = out_ref.shape[1] // a_count

    def own(count, total, place):
        column = lax.broadcasted_iota(jnp.int32, (count, total), 1)
        return (column == lax.broadcasted_iota(jnp.int32, (count, total), 0) + place * count).astype(F32)

    mine = exact(own(a_count, xf_ref.shape[1], lax.axis_index("gx")), xf_ref[...], ((1,), (1,)))
    pick = lax.broadcasted_iota(jnp.int32, (xf_ref.shape[0], planes), 0) == rank_ref[...]
    mine = exact(mine, pick.astype(F32))
    column = lax.broadcasted_iota(jnp.int32, (planes, width), 1)
    spread = lax.broadcasted_iota(jnp.int32, (planes, width), 0) == column // ny
    xt_ref[...] = exact(mine, spread.astype(F32))
    column = lax.broadcasted_iota(jnp.int32, (ny, width), 1)
    spread = lax.broadcasted_iota(jnp.int32, (ny, width), 0) == lax.rem(column, ny)
    for i, y_ref in enumerate(y_refs):
        rows = exact(own(b_count, y_ref.shape[1], lax.axis_index("gy")), y_ref[...], ((1,), (1,)))
        yt = exact(rows, spread.astype(F32))
        for a in range(a_count):
            high, low = split(xt_ref[a : a + 1, :] * yt)
            out_ref[0, a * b_count : (a + 1) * b_count, i * width : (i + 1) * width] = high
            out_ref[1, a * b_count : (a + 1) * b_count, i * width : (i + 1) * width] = low


def core_kernel(q_ref, *refs):
    out_ref = refs[-1]
    pairs = refs[0].shape[0]
    rank = out_ref.shape[2]
    columns = [jnp.concatenate([r[p] for r in refs[:-1]], axis=0) for p in range(pairs)]
    high, low = split(jnp.concatenate(columns, axis=1))
    result = dot(q_ref[0], high) + (dot(q_ref[0], low) + dot(q_ref[1], high))
    for v in range(2 * pairs):
        out_ref[v] = result[:, v * HALF : v * HALF + rank]


def shifted(x, axis, count, k):
    return lax.ppermute(x, axis, [(i, (i + k) % count) for i in range(count)])


def gathered(x, axis):
    count = lax.axis_size(axis)
    if count <= 4:
        return [x] + [shifted(x, axis, count, k) for k in range(1, count)]
    blocks = lax.all_gather(x, axis)
    return [blocks[k] for k in range(count)]


def both_ways(low, high, axis):
    ends = lax.axis_size(axis) - 1
    from_low = lax.ppermute(high, axis, [(i, i + 1) for i in range(ends)])
    from_high = lax.ppermute(low, axis, [(i + 1, i) for i in range(ends)])
    return from_low, from_high


def beside(block, axis):
    if lax.axis_size(axis) == 2:
        return lax.ppermute(block, axis, [(0, 1), (1, 0)])
    from_low, from_high = both_ways(block, block, axis)
    row = lax.broadcasted_iota(jnp.int32, block.shape, 2)
    return jnp.where(row < REACH, from_high, from_low)


def local(fields, speeds, kinetics, block_rank, x_factor, y_factor, z_factor):
    nvars, nx, ny, nz = fields.shape
    rank = z_factor.shape[1]
    gx, gy, gz = (lax.axis_size(axis) for axis in ("gx", "gy", "gz"))
    iz = lax.axis_index("gz")
    rim = (nvars, REACH, ny, nz)
    plane = (nx, ny, nz)
    scratch = [pltpu.VMEM(fields.shape, F32), pltpu.VMEM(plane, F32)]

    low, high = call(
        rim_kernel,
        [(rim, F32), (rim, F32)],
        [pl.BlockSpec(memory_space=pl.ANY)],
        (fields,),
        [pltpu.SemaphoreType.DMA((2,))],
    )
    xl, xh = both_ways(low, high, "gx")
    (packed,) = call(pack_kernel, [(plane, F32)], [VMEM], (fields,))
    zl, zh = both_ways(packed, packed, "gz")
    other = beside(fields, "gy")
    ranks = gathered(block_rank.reshape(1, nx), "gx")
    y_rows = gathered(y_factor, "gy")
    weights, zf, dz, rim_shift, scales = call(
        weight_kernel,
        [
            ((2 * nvars * ny, 2 * nvars * ny), BF16),
            ((2 * nz, 4 * HALF), BF16),
            ((2 * nz, nz), BF16),
            ((nz, nz), BF16),
            ((nvars, 2, ny, nz), F32),
        ],
        [VMEM] * 3,
        (kinetics, speeds, z_factor.T),
        [pltpu.VMEM((nz, 2 * HALF), F32)],
    )
    section, low, high, packed = call(
        section_kernel,
        [(fields.shape, F32), (rim, F32), (rim, F32), (plane, F32)],
        [VMEM] * 10,
        (fields, xl, xh, other, zl, zh, weights, dz, rim_shift, scales),
        scratch,
    )
    low, high, packed, section, ranks, y_rows = lax.optimization_barrier((low, high, packed, section, ranks, y_rows))
    xl, xh = both_ways(low, high, "gx")
    zl, zh = both_ways(packed, packed, "gz")
    other = beside(section, "gy")
    a_count, b_count = x_factor.shape[1] // gx, y_factor.shape[1] // gy
    cells = gx * nx * gy * ny
    (factor,) = call(
        factor_kernel,
        [((2, a_count * b_count, cells), BF16)],
        [VMEM] * (2 + gy),
        (jnp.concatenate(ranks, axis=1), x_factor, *y_rows),
        [pltpu.VMEM((a_count, gx * nx * ny), F32)],
    )
    xl, xh, zl, zh, other, factor = lax.optimization_barrier((xl, xh, zl, zh, other, factor))
    fields_next, proj = call(
        next_kernel,
        [(fields.shape, F32), ((nvars // 2, nx * ny, 2 * HALF), F32)],
        [VMEM] * 12,
        (fields, section, xl, xh, other, zl, zh, weights, dz, rim_shift, zf, scales),
        scratch,
    )

    pairs = nvars // 2 // gz
    chunks = proj.reshape(gz, pairs, nx * ny, 2 * HALF)
    own = lax.dynamic_index_in_dim(chunks, iz, 0, keepdims=False)
    for k in range(1, gz):
        piece = lax.dynamic_index_in_dim(chunks, lax.rem(iz + k, gz), 0, keepdims=False)
        own = own + shifted(piece, "gz", gz, k)
    blocks = [gathered(block, "gy") for block in gathered(own, "gx")]
    parts = [blocks[i][j] for j in range(gy) for i in range(gx)]
    (core,) = call(
        core_kernel,
        [((2 * pairs, a_count * b_count, rank), F32)],
        [VMEM] * (1 + len(parts)),
        (factor, *parts),
        room=16 if cells <= 1024 else 50,
    )
    return fields_next, core.reshape(2 * pairs, a_count, b_count, rank)


def solution(mesh):
    placed = (P(None, "gx", "gy", "gz"), P(), P(), P("gx"), P(), P("gy", None), P("gz", None))
    return jax.shard_map(
        local,
        mesh=mesh,
        in_specs=placed,
        out_specs=(P(None, "gx", "gy", "gz"), P("gz", "gx", "gy", None)),
        check_vma=False,
    )
```

time: 87.6 us -> 75.4 us (0.86)
  local copies, waits for them, and re-layouts: 13.8 us -> 6.71 us
  Pallas kernels: 19.1 us -> 12.5 us
  starting transfers between devices: 34.3 us -> 39.8 us
  waiting for transfers between devices: 17.8 us -> 13.4 us
    unnamed x39 -> x24, local copies, waits for them, and re-layouts: 13.7 us -> 6.69 us
    pallas_call x6 -> x7, Pallas kernels: 19.1 us -> 12.5 us  [call(): pl.pallas_call(kernel, out_shape=tuple((jax.ShapeDtypeStruct(s, d) for s,...]
    ppermute x14, starting transfers between devices: 11.4 us -> 17.4 us  [shifted(): return lax.ppermute(x, axis, [(i, (i + k) % count) for i in range(count)])]
    ppermute x4, waiting for transfers between devices: 6.31 us -> 4.3 us  [both_ways(): from_high = lax.ppermute(low, axis, [(i + 1, i) for i in range(ends)])]
    ppermute x4, waiting for transfers between devices: 1.61 us -> 0.44 us  [both_ways(): from_low = lax.ppermute(high, axis, [(i, i + 1) for i in range(ends)])]
    ppermute x14, waiting for transfers between devices: 9.83 us -> 8.67 us  [shifted(): return lax.ppermute(x, axis, [(i, (i + k) % count) for i in range(count)])]
    add x1, other arithmetic: 0.02 us -> 0.92 us  [local(): own = own + shifted(piece, 'gz', gz, k)]
  transfers between devices with their start and end apart: 24 -> 24, of which waited for: 8 -> 9; matrix products, arithmetic and copies ran while one was open for 2% -> 0% of each run, Pallas kernels for 6% -> 7%
where the time goes in v3:
time: 75.4 us; the launch traced here: 74.3 us
  starting transfers between devices  39.8 us (53%)
  waiting for transfers between devices  13.4 us (18%)
  Pallas kernels  12.5 us (17%)
  local copies, waits for them, and re-layouts  6.71 us (9%)
  other arithmetic  0.99 us (1%)
  between operations  0.83 us (1%)
    ppermute x14, starting transfers between devices, shifted(): return lax.ppermute(x, axis, [(i, (i + k) % count) for i in range(count)])  17.4 us
    ppermute x4, starting transfers between devices, both_ways(): from_low = lax.ppermute(high, axis, [(i, i + 1) for i in range(ends)])  16.6 us
    pallas_call x7, Pallas kernels, call(): pl.pallas_call(kernel, out_shape=tuple((jax.ShapeDtypeStruct(s, d) for s,...  12.5 us
    ppermute x14, waiting for transfers between devices, shifted(): return lax.ppermute(x, axis, [(i, (i + k) % count) for i in range(count)])  8.67 us
    unnamed x24, local copies, waits for them, and re-layouts  6.69 us
    ppermute x4, starting transfers between devices, both_ways(): from_high = lax.ppermute(low, axis, [(i + 1, i) for i in range(ends)])  5.17 us
    ppermute x4, waiting for transfers between devices, both_ways(): from_high = lax.ppermute(low, axis, [(i + 1, i) for i in range(ends)])  4.3 us
  transfers between devices with their start and end apart: 24, of which 9 were waited for; matrix products, arithmetic and copies ran while one was open for 0% of the time, Pallas kernels for 7%

profile of v3, /device:TPU:0, one launch (start us, length us, event | category | flops | bytes accessed | tf_op | source)
XLA Modules:
  0.0 74.3 jit_solution(2629004768995851486)
XLA Ops:
  0.6 0.6 collective-permute-start.2
  1.2 1.1 %copy-done = f32[16,12,8,128]{3,2,1,0:T(8,128)S(1)} copy-done((f32[16,12,8,128]{3,2,1,0:T(8,128)S(1)}, f32[16,12,8,128]{3,2,1,0:T(8,128)}, u32[]{:S(2)}) %copy-start) | copy-done | bytes 786456
  2.3 0.1 shard_map.86
  2.4 4.4 %collective-permute-start = (f32[16,4,8,128]{3,2,1,0:T(8,128)S(1)}, f32[16,4,8,128]{3,2,1,0:T(8,128)S(1)}, u32[]{:S(2)}, u32[]{:S(2)}) collective-permute-start(f32[16,4,8,128]{3,2,1,0:T(8,128)S(1)} %get-tuple-element.31), channel_id=1, source_target_pairs={{0,8},{8,16},{16,24},{1,9},{9,17},{17,25},{2,10},{10,18},{18,26},{... | collective-permute-start | bytes 786440 | tf_op jit(solution)/shard_map/ppermute | solution.py:283
  6.8 1.3 %collective-permute-start.1 = (f32[16,4,8,128]{3,2,1,0:T(8,128)S(1)}, f32[16,4,8,128]{3,2,1,0:T(8,128)S(1)}, u32[]{:S(2)}, u32[]{:S(2)}) collective-permute-start(f32[16,4,8,128]{3,2,1,0:T(8,128)S(1)} %get-tuple-element.32), channel_id=1, source_target_pairs={{8,0},{16,8},{24,16},{9,1},{17,9},{25,17},{10,2},{18,10},{26,18},{... | collective-permute-start | bytes 786440 | tf_op jit(solution)/shard_map/ppermute | solution.py:284
  8.1 0.7 shard_map.87
  8.8 3.5 %collective-permute-start.3 = (f32[12,8,128]{2,1,0:T(8,128)S(1)}, f32[12,8,128]{2,1,0:T(8,128)S(1)}, u32[]{:S(2)}, u32[]{:S(2)}) collective-permute-start(f32[12,8,128]{2,1,0:T(8,128)S(1)} %shard_map.87), channel_id=1, source_target_pairs={{0,1},{1,2},{2,3},{4,5},{5,6},{6,7},{8,9},{9,10},{10,11},{12,13},{... | collective-permute-start | bytes 147464 | tf_op jit(solution)/shard_map/ppermute | solution.py:283
  12.3 1.3 %collective-permute-start.4 = (f32[12,8,128]{2,1,0:T(8,128)S(1)}, f32[12,8,128]{2,1,0:T(8,128)S(1)}, u32[]{:S(2)}, u32[]{:S(2)}) collective-permute-start(f32[12,8,128]{2,1,0:T(8,128)S(1)} %shard_map.87), channel_id=1, source_target_pairs={{1,0},{2,1},{3,2},{5,4},{6,5},{7,6},{9,8},{10,9},{11,10},{13,12},{... | collective-permute-start | bytes 147464 | tf_op jit(solution)/shard_map/ppermute | solution.py:284
  13.6 0.4 collective-permute-done.3.zl_ref
  14.0 0.7 %copy-done.6 = f32[128,54]{0,1:T(8,128)S(1)} copy-done((f32[128,54]{0,1:T(8,128)S(1)}, f32[128,54]{0,1:T(8,128)}, u32[]{:S(2)}) %copy-start.6) | copy-done | bytes 27672
  14.8 0.7 copy-done.8
  15.5 0.7 copy-done.10
  16.2 0.6 shard_map.88
  16.8 0.6 copy-done.4
  17.4 0.9 %collective-permute-done.4.zh_ref = f32[12,8,128]{2,1,0:T(8,128)S(1)} collective-permute-done((f32[12,8,128]{2,1,0:T(8,128)S(1)}, f32[12,8,128]{2,1,0:T(8,128)S(1)}, u32[]{:S(2)}, u32[]{:S(2)}) %collective-permute-start.4) | collective-permute-done | bytes 49184 | tf_op jit(solution)/shard_map/ppermute | solution.py:284
  18.3 2.6 %collective-permute-start.5 = (s32[1,12]{1,0:T(1,128)}, s32[1,12]{1,0:T(1,128)S(1)}, u32[]{:S(2)}, u32[]{:S(2)}) collective-permute-start(s32[1,12]{1,0:T(1,128)} %bitcast.20), channel_id=1, source_target_pairs={{0,8},{8,16},{16,24},{24,0},{1,9},{9,17},{17,25},{25,1},{2,10},{10... | collective-permute-start | bytes 152 | tf_op jit(solution)/shard_map/ppermute | solution.py:270
  20.9 1.5 %collective-permute-start.6 = (s32[1,12]{1,0:T(1,128)}, s32[1,12]{1,0:T(1,128)S(1)}, u32[]{:S(2)}, u32[]{:S(2)}) collective-permute-start(s32[1,12]{1,0:T(1,128)} %bitcast.21), channel_id=1, source_target_pairs={{0,16},{8,24},{16,0},{24,8},{1,17},{9,25},{17,1},{25,9},{2,18},{10... | collective-permute-start | bytes 152 | tf_op jit(solution)/shard_map/ppermute | solution.py:270
  22.4 2.3 %collective-permute-start.7 = (s32[1,12]{1,0:T(1,128)}, s32[1,12]{1,0:T(1,128)S(1)}, u32[]{:S(2)}, u32[]{:S(2)}) collective-permute-start(s32[1,12]{1,0:T(1,128)} %bitcast.22), channel_id=1, source_target_pairs={{0,24},{8,0},{16,8},{24,16},{1,25},{9,1},{17,9},{25,17},{2,26},{10... | collective-permute-start | bytes 152 | tf_op jit(solution)/shard_map/ppermute | solution.py:270
  24.8 0.0 collective-permute-done.2.beside_ref
  24.8 1.1 %copy-done.1 = f32[16,12,8,128]{3,2,1,0:T(8,128)S(1)} copy-done((f32[16,12,8,128]{3,2,1,0:T(8,128)S(1)}, f32[16,12,8,128]{3,2,1,0:T(8,128)}, u32[]{:S(2)}) %copy-start.1) | copy-done | bytes 786456
  25.9 2.8 %shard_map.89 = (f32[16,12,8,128]{3,2,1,0:T(8,128)}, f32[16,4,8,128]{3,2,1,0:T(8,128)}, f32[16,4,8,128]{3,2,1,0:T(8,128)}, f32[12,8,128]{2,1,0:T(8,128)}) custom-call(f32[16,12,8,128]{3,2,1,0:T(8,128)S(1)} %copy-done.1, f32[16,4,8,128]{3,2,1,0:T(8,128)S(1)} %collective-permute-done.xl_ref, f32[16,4,8,128]{3,2,1,0:T(8,128)S(1)} %collective-permute-done.1.xh_ref, ...), custom_call_target="tpu_custom_call" | custom-call | tf_op jit(solution)/shard_map/pallas_call | solution.py:23
  28.7 0.0 collective-permute-done.7
  28.7 0.1 collective-permute-start.13
  28.8 1.3 %collective-permute-start.10 = (f32[16,4,8,128]{3,2,1,0:T(8,128)}, f32[16,4,8,128]{3,2,1,0:T(8,128)}, u32[]{:S(2)}, u32[]{:S(2)}) collective-permute-start(f32[16,4,8,128]{3,2,1,0:T(8,128)} %get-tuple-element.43), channel_id=1, source_target_pairs={{8,0},{16,8},{24,16},{9,1},{17,9},{25,17},{10,2},{18,10},{26,18},{... | collective-permute-start | bytes 786440 | tf_op jit(solution)/shard_map/ppermute | solution.py:284
  30.1 5.3 %collective-permute-start.9 = (f32[16,4,8,128]{3,2,1,0:T(8,128)}, f32[16,4,8,128]{3,2,1,0:T(8,128)}, u32[]{:S(2)}, u32[]{:S(2)}) collective-permute-start(f32[16,4,8,128]{3,2,1,0:T(8,128)} %get-tuple-element.42), channel_id=1, source_target_pairs={{0,8},{8,16},{16,24},{1,9},{9,17},{17,25},{2,10},{10,18},{18,26},{... | collective-permute-start | bytes 786440 | tf_op jit(solution)/shard_map/ppermute | solution.py:283
  35.4 3.5 %collective-permute-start.11 = (f32[12,8,128]{2,1,0:T(8,128)}, f32[12,8,128]{2,1,0:T(8,128)S(1)}, u32[]{:S(2)}, u32[]{:S(2)}) collective-permute-start(f32[12,8,128]{2,1,0:T(8,128)} %get-tuple-element.44), channel_id=1, source_target_pairs={{0,1},{1,2},{2,3},{4,5},{5,6},{6,7},{8,9},{9,10},{10,11},{12,13},{... | collective-permute-start | bytes 147464 | tf_op jit(solution)/shard_map/ppermute | solution.py:283
  38.8 1.3 %collective-permute-start.12 = (f32[12,8,128]{2,1,0:T(8,128)}, f32[12,8,128]{2,1,0:T(8,128)S(1)}, u32[]{:S(2)}, u32[]{:S(2)}) collective-permute-start(f32[12,8,128]{2,1,0:T(8,128)} %get-tuple-element.44), channel_id=1, source_target_pairs={{1,0},{2,1},{3,2},{5,4},{6,5},{7,6},{9,8},{10,9},{11,10},{13,12},{... | collective-permute-start | bytes 147464 | tf_op jit(solution)/shard_map/ppermute | solution.py:284
  40.2 0.1 pad_add_fusion.rank_ref
  40.2 1.4 %shard_map.90.q_ref = bf16[2,768,768]{2,1,0:T(8,128)(2,1)S(1)} custom-call(s32[1,48]{1,0:T(1,128)S(1)} %pad_add_fusion.rank_ref, f32[48,96]{1,0:T(8,128)S(1)} %copy-done.7, f32[8,64]{1,0:T(8,128)S(1)} %copy-done.9, f32[8,64]{1,0:T(8,128)S(1)} %collective-permute-done.8.refs_1_), custom_call_target="tpu_custom_call" | custom-call | tf_op jit(solution)/shard_map/pallas_call | solution.py:23
  41.6 3.4 %collective-permute-done.12.zh_ref = f32[12,8,128]{2,1,0:T(8,128)S(1)} collective-permute-done((f32[12,8,128]{2,1,0:T(8,128)}, f32[12,8,128]{2,1,0:T(8,128)S(1)}, u32[]{:S(2)}, u32[]{:S(2)}) %collective-permute-start.12) | collective-permute-done | bytes 49184 | tf_op jit(solution)/shard_map/ppermute | solution.py:284
  45.1 0.9 %copy-done.5 = bf16[256,256]{1,0:T(8,128)(2,1)S(1)} copy-done((bf16[256,256]{1,0:T(8,128)(2,1)S(1)}, bf16[256,256]{1,0:T(8,128)(2,1)}, u32[]{:S(2)}) %copy-start.5) | copy-done | bytes 131096
  46.0 4.7 %shard_map.91 = (f32[16,12,8,128]{3,2,1,0:T(8,128)}, f32[8,96,128]{2,1,0:T(8,128)S(1)}) custom-call(f32[16,12,8,128]{3,2,1,0:T(8,128)S(1)} %copy-done.2, f32[16,12,8,128]{3,2,1,0:T(8,128)} %get-tuple-element.41.s_ref, f32[16,4,8,128]{3,2,1,0:T(8,128)} %collective-permute-done.9.xl_ref, f32[16,4,8,128]{3,2,1,0:T(8,128)} %collective-permute-done.10.xh_ref, ...), custom_call_target="tpu_custom_call" | custom-call | tf_op jit(solution)/shard_map/pallas_call | solution.py:23
  50.7 0.7 %copy-done.3 = f32[8,96,128]{2,1,0:T(8,128)} copy-done((f32[8,96,128]{2,1,0:T(8,128)}, f32[8,96,128]{2,1,0:T(8,128)S(1)}, u32[]{:S(2)}) %copy-start.3) | copy-done | bytes 393240
  51.4 1.6 %collective-permute-start.14 = (f32[2,96,128]{2,1,0:T(8,128)S(1)}, f32[2,96,128]{2,1,0:T(8,128)S(1)}, u32[]{:S(2)}, u32[]{:S(2)}) collective-permute-start(f32[2,96,128]{2,1,0:T(8,128)S(1)} %get-tuple-element.60), channel_id=1, source_target_pairs={{0,1},{1,2},{2,3},{3,0},{4,5},{5,6},{6,7},{7,4},{8,9},{9,10},{10,1... | collective-permute-start | bytes 294920 | tf_op jit(solution)/shard_map/ppermute | solution.py:270
  53.1 1.0 %collective-permute-start.15 = (f32[2,96,128]{2,1,0:T(8,128)S(1)}, f32[2,96,128]{2,1,0:T(8,128)S(1)}, u32[]{:S(2)}, u32[]{:S(2)}) collective-permute-start(f32[2,96,128]{2,1,0:T(8,128)S(1)} %get-tuple-element.62), channel_id=1, source_target_pairs={{0,2},{1,3},{2,0},{3,1},{4,6},{5,7},{6,4},{7,5},{8,10},{9,11},{10,... | collective-permute-start | bytes 294920 | tf_op jit(solution)/shard_map/ppermute | solution.py:270
  54.0 2.8 %collective-permute-start.16 = (f32[2,96,128]{2,1,0:T(8,128)S(1)}, f32[2,96,128]{2,1,0:T(8,128)S(1)}, u32[]{:S(2)}, u32[]{:S(2)}) collective-permute-start(f32[2,96,128]{2,1,0:T(8,128)S(1)} %get-tuple-element.61), channel_id=1, source_target_pairs={{0,3},{1,0},{2,1},{3,2},{4,7},{5,4},{6,5},{7,6},{8,11},{9,8},{10,9... | collective-permute-start | bytes 294920 | tf_op jit(solution)/shard_map/ppermute | solution.py:270
  56.9 2.0 %collective-permute-done.14 = f32[2,96,128]{2,1,0:T(8,128)S(1)} collective-permute-done((f32[2,96,128]{2,1,0:T(8,128)S(1)}, f32[2,96,128]{2,1,0:T(8,128)S(1)}, u32[]{:S(2)}, u32[]{:S(2)}) %collective-permute-start.14) | collective-permute-done | bytes 98336 | tf_op jit(solution)/shard_map/ppermute | solution.py:270
  58.9 2.5 %collective-permute-done.15 = f32[2,96,128]{2,1,0:T(8,128)S(1)} collective-permute-done((f32[2,96,128]{2,1,0:T(8,128)S(1)}, f32[2,96,128]{2,1,0:T(8,128)S(1)}, u32[]{:S(2)}, u32[]{:S(2)}) %collective-permute-start.15) | collective-permute-done | bytes 98336 | tf_op jit(solution)/shard_map/ppermute | solution.py:270
  61.4 0.9 %fusion.1.refs_0_ = f32[2,96,128]{2,1,0:T(8,128)S(1)} fusion(f32[2,96,128]{2,1,0:T(8,128)S(1)} %collective-permute-done.16, f32[2,96,128]{2,1,0:T(8,128)S(1)} %collective-permute-done.15, f32[2,96,128]{2,1,0:T(8,128)S(1)} %collective-permute-done.14, f32[4,2,96,128]{3,2,1,0:T(8,128)} %bitcast.17, s32[]{:T(128)S(6)} %select_n.13), kind=kLoop, calls=%fused_computation.2 | loop fusion | flops 73728 | bytes 491524 | tf_op jit(solution)/shard_map/add | solution.py:365
  62.3 0.6 collective-permute-start.17
  63.0 1.9 %collective-permute-start.18 = (f32[2,96,128]{2,1,0:T(8,128)S(1)}, f32[2,96,128]{2,1,0:T(8,128)S(1)}, u32[]{:S(2)}, u32[]{:S(2)}) collective-permute-start(f32[2,96,128]{2,1,0:T(8,128)S(1)} %fusion.1.refs_0_), channel_id=1, source_target_pairs={{0,16},{8,24},{16,0},{24,8},{1,17},{9,25},{17,1},{25,9},{2,18},{10... | collective-permute-start | bytes 294920 | tf_op jit(solution)/shard_map/ppermute | solution.py:270
  64.9 2.8 %collective-permute-start.19 = (f32[2,96,128]{2,1,0:T(8,128)S(1)}, f32[2,96,128]{2,1,0:T(8,128)S(1)}, u32[]{:S(2)}, u32[]{:S(2)}) collective-permute-start(f32[2,96,128]{2,1,0:T(8,128)S(1)} %fusion.1.refs_0_), channel_id=1, source_target_pairs={{0,24},{8,0},{16,8},{24,16},{1,25},{9,1},{17,9},{25,17},{2,26},{10... | collective-permute-start | bytes 294920 | tf_op jit(solution)/shard_map/ppermute | solution.py:270
  67.7 0.5 collective-permute-done.17.refs_1_
  68.2 0.1 collective-permute-start.21
  68.3 0.5 collective-permute-done.18.refs_2_
  68.8 1.8 %collective-permute-done.19.refs_3_ = f32[2,96,128]{2,1,0:T(8,128)S(1)} collective-permute-done((f32[2,96,128]{2,1,0:T(8,128)S(1)}, f32[2,96,128]{2,1,0:T(8,128)S(1)}, u32[]{:S(2)}, u32[]{:S(2)}) %collective-permute-start.19) | collective-permute-done | bytes 98336 | tf_op jit(solution)/shard_map/ppermute | solution.py:270
  70.7 1.3 %collective-permute-done.23.refs_7_ = f32[2,96,128]{2,1,0:T(8,128)S(1)} collective-permute-done((f32[2,96,128]{2,1,0:T(8,128)S(1)}, f32[2,96,128]{2,1,0:T(8,128)S(1)}, u32[]{:S(2)}, u32[]{:S(2)}) %collective-permute-start.23) | collective-permute-done | bytes 98336 | tf_op jit(solution)/shard_map/ppermute | solution.py:270
  72.0 2.3 %shard_map.92 = f32[4,768,54]{2,1,0:T(8,128)} custom-call(bf16[2,768,768]{2,1,0:T(8,128)(2,1)S(1)} %shard_map.90.q_ref, f32[2,96,128]{2,1,0:T(8,128)S(1)} %fusion.1.refs_0_, f32[2,96,128]{2,1,0:T(8,128)S(1)} %collective-permute-done.17.refs_1_, f32[2,96,128]{2,1,0:T(8,128)S(1)} %collective-permute-done.18.refs_2_, ...), custom_call_target="tpu_custom_call" | custom-call | tf_op jit(solution)/shard_map/pallas_call | solution.py:23
  (34 shorter events, 0.1 us)
Async XLA Ops:
  0.6 24.1 %collective-permute-start.2 = (f32[16,12,8,128]{3,2,1,0:T(8,128)}, f32[16,12,8,128]{3,2,1,0:T(8,128)S(1)}, u32[]{:S(2)}, u32[]{:S(2)}) collective-permute-start(f32[16,12,8,128]{3,2,1,0:T(8,128)} %f_ref.7), channel_id=1, source_target_pairs={{0,4},{4,0},{1,5},{5,1},{2,6},{6,2},{3,7},{7,3},{8,12},{12,8},{9,1... | collective-permute-start | bytes 2359304 | tf_op jit(solution)/shard_map/ppermute | solution.py:290
  1.2 1.1 %copy-start = (f32[16,12,8,128]{3,2,1,0:T(8,128)S(1)}, f32[16,12,8,128]{3,2,1,0:T(8,128)}, u32[]{:S(2)}) copy-start(f32[16,12,8,128]{3,2,1,0:T(8,128)} %f_ref.7) | copy-start | bytes 2359300
  2.3 37.8 %copy-start.11 = (s32[12]{0:T(128)S(1)}, s32[12]{0:T(128)}, u32[]{:S(2)}) copy-start(s32[12]{0:T(128)} %param.10) | copy-start | bytes 148
  2.3 37.9 %copy-start.7 = (f32[48,96]{1,0:T(8,128)S(1)}, f32[48,96]{1,0:T(8,128)}, u32[]{:S(2)}) copy-start(f32[48,96]{1,0:T(8,128)} %xf_ref.1) | copy-start | bytes 55300
  2.3 37.9 %copy-start.9 = (f32[8,64]{1,0:T(8,128)S(1)}, f32[8,64]{1,0:T(8,128)}, u32[]{:S(2)}) copy-start(f32[8,64]{1,0:T(8,128)} %refs_0_) | copy-start | bytes 6148
  2.4 18.5 %collective-permute-start = (f32[16,4,8,128]{3,2,1,0:T(8,128)S(1)}, f32[16,4,8,128]{3,2,1,0:T(8,128)S(1)}, u32[]{:S(2)}, u32[]{:S(2)}) collective-permute-start(f32[16,4,8,128]{3,2,1,0:T(8,128)S(1)} %get-tuple-element.31), channel_id=1, source_target_pairs={{0,8},{8,16},{16,24},{1,9},{9,17},{17,25},{2,10},{10,18},{18,26},{... | collective-permute-start | bytes 786440 | tf_op jit(solution)/shard_map/ppermute | solution.py:283
  6.8 15.6 %collective-permute-start.1 = (f32[16,4,8,128]{3,2,1,0:T(8,128)S(1)}, f32[16,4,8,128]{3,2,1,0:T(8,128)S(1)}, u32[]{:S(2)}, u32[]{:S(2)}) collective-permute-start(f32[16,4,8,128]{3,2,1,0:T(8,128)S(1)} %get-tuple-element.32), channel_id=1, source_target_pairs={{8,0},{16,8},{24,16},{9,1},{17,9},{25,17},{10,2},{18,10},{26,18},{... | collective-permute-start | bytes 786440 | tf_op jit(solution)/shard_map/ppermute | solution.py:284
  8.8 5.2 %collective-permute-start.3 = (f32[12,8,128]{2,1,0:T(8,128)S(1)}, f32[12,8,128]{2,1,0:T(8,128)S(1)}, u32[]{:S(2)}, u32[]{:S(2)}) collective-permute-start(f32[12,8,128]{2,1,0:T(8,128)S(1)} %shard_map.87), channel_id=1, source_target_pairs={{0,1},{1,2},{2,3},{4,5},{5,6},{6,7},{8,9},{9,10},{10,11},{12,13},{... | collective-permute-start | bytes 147464 | tf_op jit(solution)/shard_map/ppermute | solution.py:283
  12.3 6.0 %collective-permute-start.4 = (f32[12,8,128]{2,1,0:T(8,128)S(1)}, f32[12,8,128]{2,1,0:T(8,128)S(1)}, u32[]{:S(2)}, u32[]{:S(2)}) collective-permute-start(f32[12,8,128]{2,1,0:T(8,128)S(1)} %shard_map.87), channel_id=1, source_target_pairs={{1,0},{2,1},{3,2},{5,4},{6,5},{7,6},{9,8},{10,9},{11,10},{13,12},{... | collective-permute-start | bytes 147464 | tf_op jit(solution)/shard_map/ppermute | solution.py:284
  14.0 14.7 %collective-permute-start.8 = (f32[8,64]{1,0:T(8,128)}, f32[8,64]{1,0:T(8,128)S(1)}, u32[]{:S(2)}, u32[]{:S(2)}) collective-permute-start(f32[8,64]{1,0:T(8,128)} %refs_0_), channel_id=1, source_target_pairs={{0,4},{4,0},{1,5},{5,1},{2,6},{6,2},{3,7},{7,3},{8,12},{12,8},{9,1... | collective-permute-start | bytes 6152 | tf_op jit(solution)/shard_map/ppermute | solution.py:270
  14.0 0.7 %copy-start.6 = (f32[128,54]{0,1:T(8,128)S(1)}, f32[128,54]{0,1:T(8,128)}, u32[]{:S(2)}) copy-start(f32[128,54]{0,1:T(8,128)} %param.13) | copy-start | bytes 82948
  14.8 0.7 copy-start.8
  15.5 0.7 copy-start.10
  16.7 0.7 copy-start.4
  18.3 10.4 %collective-permute-start.5 = (s32[1,12]{1,0:T(1,128)}, s32[1,12]{1,0:T(1,128)S(1)}, u32[]{:S(2)}, u32[]{:S(2)}) collective-permute-start(s32[1,12]{1,0:T(1,128)} %bitcast.20), channel_id=1, source_target_pairs={{0,8},{8,16},{16,24},{24,0},{1,9},{9,17},{17,25},{25,1},{2,10},{10... | collective-permute-start | bytes 152 | tf_op jit(solution)/shard_map/ppermute | solution.py:270
  20.9 7.8 %collective-permute-start.6 = (s32[1,12]{1,0:T(1,128)}, s32[1,12]{1,0:T(1,128)S(1)}, u32[]{:S(2)}, u32[]{:S(2)}) collective-permute-start(s32[1,12]{1,0:T(1,128)} %bitcast.21), channel_id=1, source_target_pairs={{0,16},{8,24},{16,0},{24,8},{1,17},{9,25},{17,1},{25,9},{2,18},{10... | collective-permute-start | bytes 152 | tf_op jit(solution)/shard_map/ppermute | solution.py:270
  22.4 6.3 %collective-permute-start.7 = (s32[1,12]{1,0:T(1,128)}, s32[1,12]{1,0:T(1,128)S(1)}, u32[]{:S(2)}, u32[]{:S(2)}) collective-permute-start(s32[1,12]{1,0:T(1,128)} %bitcast.22), channel_id=1, source_target_pairs={{0,24},{8,0},{16,8},{24,16},{1,25},{9,1},{17,9},{25,17},{2,26},{10... | collective-permute-start | bytes 152 | tf_op jit(solution)/shard_map/ppermute | solution.py:270
  24.8 1.1 %copy-start.1 = (f32[16,12,8,128]{3,2,1,0:T(8,128)S(1)}, f32[16,12,8,128]{3,2,1,0:T(8,128)}, u32[]{:S(2)}) copy-start(f32[16,12,8,128]{3,2,1,0:T(8,128)} %f_ref.7) | copy-start | bytes 2359300
  25.9 19.2 %copy-start.2 = (f32[16,12,8,128]{3,2,1,0:T(8,128)S(1)}, f32[16,12,8,128]{3,2,1,0:T(8,128)}, u32[]{:S(2)}) copy-start(f32[16,12,8,128]{3,2,1,0:T(8,128)} %f_ref.7) | copy-start | bytes 2359300
  28.7 16.3 %collective-permute-start.13 = (f32[16,12,8,128]{3,2,1,0:T(8,128)}, f32[16,12,8,128]{3,2,1,0:T(8,128)}, u32[]{:S(2)}, u32[]{:S(2)}) collective-permute-start(f32[16,12,8,128]{3,2,1,0:T(8,128)} %get-tuple-element.41.s_ref), channel_id=1, source_target_pairs={{0,4},{4,0},{1,5},{5,1},{2,6},{6,2},{3,7},{7,3},{8,12},{12,8},{9,1... | collective-permute-start | bytes 2359304 | tf_op jit(solution)/shard_map/ppermute | solution.py:290
  28.8 16.2 %collective-permute-start.10 = (f32[16,4,8,128]{3,2,1,0:T(8,128)}, f32[16,4,8,128]{3,2,1,0:T(8,128)}, u32[]{:S(2)}, u32[]{:S(2)}) collective-permute-start(f32[16,4,8,128]{3,2,1,0:T(8,128)} %get-tuple-element.43), channel_id=1, source_target_pairs={{8,0},{16,8},{24,16},{9,1},{17,9},{25,17},{10,2},{18,10},{26,18},{... | collective-permute-start | bytes 786440 | tf_op jit(solution)/shard_map/ppermute | solution.py:284
  30.1 14.9 %collective-permute-start.9 = (f32[16,4,8,128]{3,2,1,0:T(8,128)}, f32[16,4,8,128]{3,2,1,0:T(8,128)}, u32[]{:S(2)}, u32[]{:S(2)}) collective-permute-start(f32[16,4,8,128]{3,2,1,0:T(8,128)} %get-tuple-element.42), channel_id=1, source_target_pairs={{0,8},{8,16},{16,24},{1,9},{9,17},{17,25},{2,10},{10,18},{18,26},{... | collective-permute-start | bytes 786440 | tf_op jit(solution)/shard_map/ppermute | solution.py:283
  35.4 6.2 %collective-permute-start.11 = (f32[12,8,128]{2,1,0:T(8,128)}, f32[12,8,128]{2,1,0:T(8,128)S(1)}, u32[]{:S(2)}, u32[]{:S(2)}) collective-permute-start(f32[12,8,128]{2,1,0:T(8,128)} %get-tuple-element.44), channel_id=1, source_target_pairs={{0,1},{1,2},{2,3},{4,5},{5,6},{6,7},{8,9},{9,10},{10,11},{12,13},{... | collective-permute-start | bytes 147464 | tf_op jit(solution)/shard_map/ppermute | solution.py:283
  38.8 6.2 %collective-permute-start.12 = (f32[12,8,128]{2,1,0:T(8,128)}, f32[12,8,128]{2,1,0:T(8,128)S(1)}, u32[]{:S(2)}, u32[]{:S(2)}) collective-permute-start(f32[12,8,128]{2,1,0:T(8,128)} %get-tuple-element.44), channel_id=1, source_target_pairs={{1,0},{2,1},{3,2},{5,4},{6,5},{7,6},{9,8},{10,9},{11,10},{13,12},{... | collective-permute-start | bytes 147464 | tf_op jit(solution)/shard_map/ppermute | solution.py:284
  45.1 0.9 %copy-start.5 = (bf16[256,256]{1,0:T(8,128)(2,1)S(1)}, bf16[256,256]{1,0:T(8,128)(2,1)}, u32[]{:S(2)}) copy-start(bf16[256,256]{1,0:T(8,128)(2,1)} %copy-done.4) | copy-start | bytes 393220
  50.7 0.7 %copy-start.3 = (f32[8,96,128]{2,1,0:T(8,128)}, f32[8,96,128]{2,1,0:T(8,128)S(1)}, u32[]{:S(2)}) copy-start(f32[8,96,128]{2,1,0:T(8,128)S(1)} %get-tuple-element.59) | copy-start | bytes 1179652
  51.4 7.5 %collective-permute-start.14 = (f32[2,96,128]{2,1,0:T(8,128)S(1)}, f32[2,96,128]{2,1,0:T(8,128)S(1)}, u32[]{:S(2)}, u32[]{:S(2)}) collective-permute-start(f32[2,96,128]{2,1,0:T(8,128)S(1)} %get-tuple-element.60), channel_id=1, source_target_pairs={{0,1},{1,2},{2,3},{3,0},{4,5},{5,6},{6,7},{7,4},{8,9},{9,10},{10,1... | collective-permute-start | bytes 294920 | tf_op jit(solution)/shard_map/ppermute | solution.py:270
  53.1 8.3 %collective-permute-start.15 = (f32[2,96,128]{2,1,0:T(8,128)S(1)}, f32[2,96,128]{2,1,0:T(8,128)S(1)}, u32[]{:S(2)}, u32[]{:S(2)}) collective-permute-start(f32[2,96,128]{2,1,0:T(8,128)S(1)} %get-tuple-element.62), channel_id=1, source_target_pairs={{0,2},{1,3},{2,0},{3,1},{4,6},{5,7},{6,4},{7,5},{8,10},{9,11},{10,... | collective-permute-start | bytes 294920 | tf_op jit(solution)/shard_map/ppermute | solution.py:270
  54.0 7.4 %collective-permute-start.16 = (f32[2,96,128]{2,1,0:T(8,128)S(1)}, f32[2,96,128]{2,1,0:T(8,128)S(1)}, u32[]{:S(2)}, u32[]{:S(2)}) collective-permute-start(f32[2,96,128]{2,1,0:T(8,128)S(1)} %get-tuple-element.61), channel_id=1, source_target_pairs={{0,3},{1,0},{2,1},{3,2},{4,7},{5,4},{6,5},{7,6},{8,11},{9,8},{10,9... | collective-permute-start | bytes 294920 | tf_op jit(solution)/shard_map/ppermute | solution.py:270
  62.3 5.9 %collective-permute-start.17 = (f32[2,96,128]{2,1,0:T(8,128)S(1)}, f32[2,96,128]{2,1,0:T(8,128)S(1)}, u32[]{:S(2)}, u32[]{:S(2)}) collective-permute-start(f32[2,96,128]{2,1,0:T(8,128)S(1)} %fusion.1.refs_0_), channel_id=1, source_target_pairs={{0,8},{8,16},{16,24},{24,0},{1,9},{9,17},{17,25},{25,1},{2,10},{10... | collective-permute-start | bytes 294920 | tf_op jit(solution)/shard_map/ppermute | solution.py:270
  63.0 5.8 %collective-permute-start.18 = (f32[2,96,128]{2,1,0:T(8,128)S(1)}, f32[2,96,128]{2,1,0:T(8,128)S(1)}, u32[]{:S(2)}, u32[]{:S(2)}) collective-permute-start(f32[2,96,128]{2,1,0:T(8,128)S(1)} %fusion.1.refs_0_), channel_id=1, source_target_pairs={{0,16},{8,24},{16,0},{24,8},{1,17},{9,25},{17,1},{25,9},{2,18},{10... | collective-permute-start | bytes 294920 | tf_op jit(solution)/shard_map/ppermute | solution.py:270
  64.9 5.8 %collective-permute-start.19 = (f32[2,96,128]{2,1,0:T(8,128)S(1)}, f32[2,96,128]{2,1,0:T(8,128)S(1)}, u32[]{:S(2)}, u32[]{:S(2)}) collective-permute-start(f32[2,96,128]{2,1,0:T(8,128)S(1)} %fusion.1.refs_0_), channel_id=1, source_target_pairs={{0,24},{8,0},{16,8},{24,16},{1,25},{9,1},{17,9},{25,17},{2,26},{10... | collective-permute-start | bytes 294920 | tf_op jit(solution)/shard_map/ppermute | solution.py:270
  67.7 2.9 %collective-permute-start.20 = (f32[2,96,128]{2,1,0:T(8,128)S(1)}, f32[2,96,128]{2,1,0:T(8,128)S(1)}, u32[]{:S(2)}, u32[]{:S(2)}) collective-permute-start(f32[2,96,128]{2,1,0:T(8,128)S(1)} %fusion.1.refs_0_), channel_id=1, source_target_pairs={{0,4},{4,0},{1,5},{5,1},{2,6},{6,2},{3,7},{7,3},{8,12},{12,8},{9,1... | collective-permute-start | bytes 294920 | tf_op jit(solution)/shard_map/ppermute | solution.py:270
  68.2 2.5 %collective-permute-start.21 = (f32[2,96,128]{2,1,0:T(8,128)S(1)}, f32[2,96,128]{2,1,0:T(8,128)S(1)}, u32[]{:S(2)}, u32[]{:S(2)}) collective-permute-start(f32[2,96,128]{2,1,0:T(8,128)S(1)} %collective-permute-done.17.refs_1_), channel_id=1, source_target_pairs={{0,4},{4,0},{1,5},{5,1},{2,6},{6,2},{3,7},{7,3},{8,12},{12,8},{9,1... | collective-permute-start | bytes 294920 | tf_op jit(solution)/shard_map/ppermute | solution.py:270
  68.8 1.9 %collective-permute-start.22 = (f32[2,96,128]{2,1,0:T(8,128)S(1)}, f32[2,96,128]{2,1,0:T(8,128)S(1)}, u32[]{:S(2)}, u32[]{:S(2)}) collective-permute-start(f32[2,96,128]{2,1,0:T(8,128)S(1)} %collective-permute-done.18.refs_2_), channel_id=1, source_target_pairs={{0,4},{4,0},{1,5},{5,1},{2,6},{6,2},{3,7},{7,3},{8,12},{12,8},{9,1... | collective-permute-start | bytes 294920 | tf_op jit(solution)/shard_map/ppermute | solution.py:270
  70.6 1.3 %collective-permute-start.23 = (f32[2,96,128]{2,1,0:T(8,128)S(1)}, f32[2,96,128]{2,1,0:T(8,128)S(1)}, u32[]{:S(2)}, u32[]{:S(2)}) collective-permute-start(f32[2,96,128]{2,1,0:T(8,128)S(1)} %collective-permute-done.19.refs_3_), channel_id=1, source_target_pairs={{0,4},{4,0},{1,5},{5,1},{2,6},{6,2},{3,7},{7,3},{8,12},{12,8},{9,1... | collective-permute-start | bytes 294920 | tf_op jit(solution)/shard_map/ppermute | solution.py:270

commit v4 on v3

--- a/solution.py
+++ b/solution.py
@@ -1,5 +1,3 @@
-import functools
-
 import jax
 import jax.numpy as jnp
 from jax import lax
@@ -43,11 +41,15 @@
     return high, (x - high.astype(F32)).astype(BF16)
 
 
-def rim_kernel(f_ref, low_ref, high_ref, sems):
-    top = f_ref.shape[1] - REACH
+def odd(axis):
+    return lax.rem(lax.axis_index(axis), jnp.int32(2))
+
+
+def rim_kernel(f_ref, first_ref, second_ref, sems):
+    top, parity = f_ref.shape[1] - REACH, odd("gx")
     copies = [
         pltpu.make_async_copy(f_ref.at[:, pl.ds(start, REACH)], target, sems.at[i])
-        for i, (start, target) in enumerate(((0, low_ref), (top, high_ref)))
+        for i, (start, target) in enumerate(((top * (1 - parity), first_ref), (top * parity, second_ref)))
     ]
     for copy in copies:
         copy.start()
@@ -64,11 +66,13 @@
     rim_ref[...] = jnp.where(group == v + width // 2 // REACH, first, rim)
 
 
-def pack_kernel(f_ref, rim_ref):
+def pack_kernel(f_ref, rim_ref, same_ref):
     rim_ref[...] = jnp.zeros_like(rim_ref)
 
     def step(v, carry):
-        pack_rim(v, f_ref[v], rim_ref)
+        values = f_ref[v]
+        same_ref[v] = values
+        pack_rim(v, values, rim_ref)
         return carry
 
     lax.fori_loop(0, f_ref.shape[0], step, 0, unroll=4)
@@ -82,7 +86,7 @@
     return lax.rem(x, jnp.int32(size))
 
 
-def weight_kernel(kin_ref, speed_ref, zf_ref, w_ref, zf_out_ref, dz_ref, shift_ref, scale_ref, wide_ref):
+def weight_kernel(kin_ref, speed_ref, w_ref, dz_ref, shift_ref, scale_ref):
     nvars = kin_ref.shape[0]
     rows, columns = w_ref.shape[0] // 2, w_ref.shape[1]
     ny = rows // nvars
@@ -106,17 +110,7 @@
     w_ref[0:rows] = high
     w_ref[rows:] = low
 
-    depth, rank = zf_ref.shape[1], zf_ref.shape[0]
-    identity = (iota((depth, depth), 0) == iota((depth, depth), 1)).astype(F32)
-    wide_ref[...] = jnp.zeros_like(wide_ref)
-    wide_ref[:, 0:rank] = exact(identity, zf_ref[...], ((1,), (1,)))
-    high, low = split(wide_ref[...])
-    zf_out_ref[0:depth, 0 : 2 * HALF] = high
-    zf_out_ref[0:depth, 2 * HALF :] = low
-    high, low = split(pltpu.roll(wide_ref[...], HALF, 1))
-    zf_out_ref[depth:, 0 : 2 * HALF] = high
-    zf_out_ref[depth:, 2 * HALF :] = low
-
+    depth = dz_ref.shape[1]
     source, target = iota((depth, depth), 0), iota((depth, depth), 1)
     offset = source - target
     inner = jnp.zeros((depth, depth), F32)
@@ -139,6 +133,19 @@
         scale_ref[v, 1] = jnp.broadcast_to(TIME_STEP / SCALE * speed_ref[2:3, v : v + 1], tile)
 
 
+def project_kernel(zf_ref, zf_out_ref, wide_ref):
+    depth, rank = zf_ref.shape[1], zf_ref.shape[0]
+    identity = (iota((depth, depth), 0) == iota((depth, depth), 1)).astype(F32)
+    wide_ref[...] = jnp.zeros_like(wide_ref)
+    wide_ref[:, 0:rank] = exact(identity, zf_ref[...], ((1,), (1,)))
+    high, low = split(wide_ref[...])
+    zf_out_ref[0:depth, 0 : 2 * HALF] = high
+    zf_out_ref[0:depth, 2 * HALF :] = low
+    high, low = split(pltpu.roll(wide_ref[...], HALF, 1))
+    zf_out_ref[depth:, 0 : 2 * HALF] = high
+    zf_out_ref[depth:, 2 * HALF :] = low
+
+
 def mix_planes(q_ref, beside_ref, w_ref, rate_ref):
     nvars, nx, ny, nz = q_ref.shape
     rows = nvars * ny
@@ -159,18 +166,21 @@
     lax.fori_loop(0, nx // 2, step, 0, unroll=True)
 
 
-def join_rims(zl_ref, zh_ref, shift_ref, rim_ref):
+def join_rims(first_ref, second_ref, shift_ref, rim_ref):
     nx, ny, nz = rim_ref.shape
-    lane = lax.broadcasted_iota(jnp.int32, rim_ref.shape, 2)
-    rim = jnp.where(lane < nz // 2, zl_ref[...], zh_ref[...]).reshape(nx * ny, nz)
+    upper = lax.shift_right_logical(iota(rim_ref.shape, 2) * 2 // nz, 0)
+    rim = jnp.where(upper == odd("gz"), second_ref[...], first_ref[...]).reshape(nx * ny, nz)
     high, low = split(rim)
     rim_ref[...] = (dot(high, shift_ref[...]) + dot(low, shift_ref[...])).reshape(rim_ref.shape)
 
 
-def step_of(v, q_ref, xl_ref, xh_ref, dz_ref, rate_ref, rim_ref, scale_ref):
-    nvars, nx, ny, nz = q_ref.shape
+def step_of(v, q_ref, first_ref, second_ref, dz_ref, rate_ref, rim_ref, scale_ref):
+    _, nx, ny, nz = q_ref.shape
     q = q_ref[v]
-    tall = jnp.concatenate([xl_ref[v], q, xh_ref[v]], axis=0)
+    even = jnp.full((REACH, ny, nz), odd("gx")) == 0
+    low_rim = jnp.where(even, second_ref[v], first_ref[v])
+    high_rim = jnp.where(even, first_ref[v], second_ref[v])
+    tall = jnp.concatenate([low_rim, q, high_rim], axis=0)
     gx = None
     for k in range(1, REACH + 1):
         part = COEFFS[k - 1] * (tall[REACH + k : REACH + k + nx] - tall[REACH - k : REACH - k + nx])
@@ -186,18 +196,20 @@
 
 
 def section_kernel(
-    f_ref, xl_ref, xh_ref, beside_ref, zl_ref, zh_ref, w_ref, dz_ref, shift_ref, scale_ref,
-    s_ref, low_ref, high_ref, out_rim_ref, rate_ref, rim_ref,
+    f_ref, x1_ref, x2_ref, beside_ref, z1_ref, z2_ref, w_ref, dz_ref, shift_ref, scale_ref,
+    s_ref, first_ref, second_ref, out_rim_ref, rate_ref, rim_ref,
 ):
     mix_planes(f_ref, beside_ref, w_ref, rate_ref)
-    join_rims(zl_ref, zh_ref, shift_ref, rim_ref)
+    join_rims(z1_ref, z2_ref, shift_ref, rim_ref)
     out_rim_ref[...] = jnp.zeros_like(out_rim_ref)
 
     def step(v, carry):
-        s = f_ref[v] + step_of(v, f_ref, xl_ref, xh_ref, dz_ref, rate_ref, rim_ref, scale_ref)
+        s = f_ref[v] + step_of(v, f_ref, x1_ref, x2_ref, dz_ref, rate_ref, rim_ref, scale_ref)
         s_ref[v] = s
-        low_ref[v] = s[:REACH]
-        high_ref[v] = s[s.shape[0] - REACH :]
+        low, high = s[:REACH], s[s.shape[0] - REACH :]
+        even = jnp.full(low.shape, odd("gx")) == 0
+        first_ref[v] = jnp.where(even, high, low)
+        second_ref[v] = jnp.where(even, low, high)
         pack_rim(v, s, out_rim_ref)
         return carry
 
@@ -205,26 +217,33 @@
 
 
 def next_kernel(
-    f_ref, s_ref, xl_ref, xh_ref, beside_ref, zl_ref, zh_ref, w_ref, dz_ref, shift_ref, zf_ref, scale_ref,
-    next_ref, proj_ref, rate_ref, rim_ref,
+    f_ref, s_ref, x1_ref, x2_ref, beside_ref, z1_ref, z2_ref, w_ref, dz_ref, shift_ref, scale_ref, zf_ref,
+    next_ref, *refs,
 ):
-    nvars, nx, ny, nz = f_ref.shape
+    _, nx, ny, nz = f_ref.shape
+    chunk_refs, (rate_ref, rim_ref) = refs[:-2], refs[-2:]
     mix_planes(s_ref, beside_ref, w_ref, rate_ref)
-    join_rims(zl_ref, zh_ref, shift_ref, rim_ref)
-
-    def step(p, carry):
-        both = []
-        for v in (2 * p, 2 * p + 1):
-            rate = step_of(v, s_ref, xl_ref, xh_ref, dz_ref, rate_ref, rim_ref, scale_ref)
-            new = 0.5 * (f_ref[v] + s_ref[v] + rate)
-            next_ref[v] = new
-            both.append(new.reshape(nx * ny, nz))
-        high, low = split(jnp.concatenate(both, axis=1))
-        wide = dot(high, zf_ref[...])
-        proj_ref[p] = wide[:, : 2 * HALF] + wide[:, 2 * HALF :] + dot(low, zf_ref[:, : 2 * HALF])
-        return carry
-
-    lax.fori_loop(0, nvars // 2, step, 0, unroll=2)
+    join_rims(z1_ref, z2_ref, shift_ref, rim_ref)
+    count, pairs = len(chunk_refs), chunk_refs[0].shape[0]
+    for k, chunk_ref in enumerate(chunk_refs):
+        start = lax.rem(lax.axis_index("gz") + k, jnp.int32(count)) * (2 * pairs)
+        for j in range(pairs):
+            both = []
+            for v in (start + 2 * j, start + 2 * j + 1):
+                rate = step_of(v, s_ref, x1_ref, x2_ref, dz_ref, rate_ref, rim_ref, scale_ref)
+                new = 0.5 * (f_ref[v] + s_ref[v] + rate)
+                next_ref[v] = new
+                both.append(new.reshape(nx * ny, nz))
+            high, low = split(jnp.concatenate(both, axis=1))
+            wide = dot(high, zf_ref[...])
+            chunk_ref[j] = wide[:, : 2 * HALF] + wide[:, 2 * HALF :] + dot(low, zf_ref[:, : 2 * HALF])
+
+
+def sum_kernel(*refs):
+    total = refs[0][...]
+    for ref in refs[1:-1]:
+        total = total + ref[...]
+    refs[-1][...] = total
 
 
 def factor_kernel(rank_ref, xf_ref, *refs):
@@ -266,29 +285,33 @@
         out_ref[v] = result[:, v * HALF : v * HALF + rank]
 
 
-def shifted(x, axis, count, k):
+def shifted(x, axis, k):
+    count = lax.axis_size(axis)
     return lax.ppermute(x, axis, [(i, (i + k) % count) for i in range(count)])
 
 
 def gathered(x, axis):
     count = lax.axis_size(axis)
     if count <= 4:
-        return [x] + [shifted(x, axis, count, k) for k in range(1, count)]
+        return [x] + [shifted(x, axis, k) for k in range(1, count)]
     blocks = lax.all_gather(x, axis)
     return [blocks[k] for k in range(count)]
 
 
-def both_ways(low, high, axis):
-    ends = lax.axis_size(axis) - 1
-    from_low = lax.ppermute(high, axis, [(i, i + 1) for i in range(ends)])
-    from_high = lax.ppermute(low, axis, [(i + 1, i) for i in range(ends)])
-    return from_low, from_high
+def paired(first, second, axis):
+    out = []
+    for x, start in ((first, 0), (second, 1)):
+        links = [(i, i + 1) for i in range(start, lax.axis_size(axis) - 1, 2)]
+        out.append(lax.ppermute(x, axis, links + [(j, i) for i, j in links]))
+    return out
 
 
 def beside(block, axis):
-    if lax.axis_size(axis) == 2:
+    count = lax.axis_size(axis)
+    if count == 2:
         return lax.ppermute(block, axis, [(0, 1), (1, 0)])
-    from_low, from_high = both_ways(block, block, axis)
+    from_low = lax.ppermute(block, axis, [(i, i + 1) for i in range(count - 1)])
+    from_high = lax.ppermute(block, axis, [(i + 1, i) for i in range(count - 1)])
     row = lax.broadcasted_iota(jnp.int32, block.shape, 2)
     return jnp.where(row < REACH, from_high, from_low)
 
@@ -297,48 +320,54 @@
     nvars, nx, ny, nz = fields.shape
     rank = z_factor.shape[1]
     gx, gy, gz = (lax.axis_size(axis) for axis in ("gx", "gy", "gz"))
-    iz = lax.axis_index("gz")
     rim = (nvars, REACH, ny, nz)
     plane = (nx, ny, nz)
     scratch = [pltpu.VMEM(fields.shape, F32), pltpu.VMEM(plane, F32)]
-
-    low, high = call(
+    pairs = nvars // 2 // gz
+    chunk = (pairs, nx * ny, 2 * HALF)
+    barrier = lax.optimization_barrier
+
+    first, second = call(
         rim_kernel,
         [(rim, F32), (rim, F32)],
-        [pl.BlockSpec(memory_space=pl.ANY)],
+        [pl.BlockSpec(memory_space=pltpu.HBM)],
         (fields,),
         [pltpu.SemaphoreType.DMA((2,))],
     )
-    xl, xh = both_ways(low, high, "gx")
-    (packed,) = call(pack_kernel, [(plane, F32)], [VMEM], (fields,))
-    zl, zh = both_ways(packed, packed, "gz")
+    x1, x2 = paired(first, second, "gx")
+    packed, same = call(pack_kernel, [(plane, F32), (fields.shape, F32)], [VMEM], (fields,))
+    z1, z2 = paired(packed, packed, "gz")
     other = beside(fields, "gy")
-    ranks = gathered(block_rank.reshape(1, nx), "gx")
-    y_rows = gathered(y_factor, "gy")
-    weights, zf, dz, rim_shift, scales = call(
+    weights, dz, rim_shift, scales = call(
         weight_kernel,
-        [
-            ((2 * nvars * ny, 2 * nvars * ny), BF16),
-            ((2 * nz, 4 * HALF), BF16),
-            ((2 * nz, nz), BF16),
-            ((nz, nz), BF16),
-            ((nvars, 2, ny, nz), F32),
-        ],
-        [VMEM] * 3,
-        (kinetics, speeds, z_factor.T),
-        [pltpu.VMEM((nz, 2 * HALF), F32)],
-    )
-    section, low, high, packed = call(
+        [((2 * nvars * ny, 2 * nvars * ny), BF16), ((2 * nz, nz), BF16), ((nz, nz), BF16), ((nvars, 2, ny, nz), F32)],
+        [VMEM] * 2,
+        (kinetics, speeds),
+    )
+    section, first, second, packed = call(
         section_kernel,
         [(fields.shape, F32), (rim, F32), (rim, F32), (plane, F32)],
         [VMEM] * 10,
-        (fields, xl, xh, other, zl, zh, weights, dz, rim_shift, scales),
+        (same, x1, x2, other, z1, z2, weights, dz, rim_shift, scales),
         scratch,
     )
-    low, high, packed, section, ranks, y_rows = lax.optimization_barrier((low, high, packed, section, ranks, y_rows))
-    xl, xh = both_ways(low, high, "gx")
-    zl, zh = both_ways(packed, packed, "gz")
+    section, first, second, packed, z_factor = barrier((section, first, second, packed, z_factor))
+    x1, x2 = paired(first, second, "gx")
+    z1, z2 = paired(packed, packed, "gz")
     other = beside(section, "gy")
+    (zf,) = call(project_kernel, [((2 * nz, 4 * HALF), BF16)], [VMEM], (z_factor.T,), [pltpu.VMEM((nz, 2 * HALF), F32)])
+    fields_next, *chunks = call(
+        next_kernel,
+        [(fields.shape, F32)] + [(chunk, F32)] * gz,
+        [VMEM] * 12,
+        (fields, section, x1, x2, other, z1, z2, weights, dz, rim_shift, scales, zf),
+        scratch,
+    )
+    chunks, block_rank, y_factor = barrier((chunks, block_rank, y_factor))
+    parts = [chunks[0]] + [shifted(chunks[k], "gz", k) for k in range(1, gz)]
+    ranks = gathered(block_rank.reshape(1, nx), "gx")
+    y_rows = gathered(y_factor, "gy")
+    (own,) = call(sum_kernel, [(chunk, F32)], [VMEM] * gz, parts)
     a_count, b_count = x_factor.shape[1] // gx, y_factor.shape[1] // gy
     cells = gx * nx * gy * ny
     (factor,) = call(
@@ -348,21 +377,6 @@
         (jnp.concatenate(ranks, axis=1), x_factor, *y_rows),
         [pltpu.VMEM((a_count, gx * nx * ny), F32)],
     )
-    xl, xh, zl, zh, other, factor = lax.optimization_barrier((xl, xh, zl, zh, other, factor))
-    fields_next, proj = call(
-        next_kernel,
-        [(fields.shape, F32), ((nvars // 2, nx * ny, 2 * HALF), F32)],
-        [VMEM] * 12,
-        (fields, section, xl, xh, other, zl, zh, weights, dz, rim_shift, zf, scales),
-        scratch,
-    )
-
-    pairs = nvars // 2 // gz
-    chunks = proj.reshape(gz, pairs, nx * ny, 2 * HALF)
-    own = lax.dynamic_index_in_dim(chunks, iz, 0, keepdims=False)
-    for k in range(1, gz):
-        piece = lax.dynamic_index_in_dim(chunks, lax.rem(iz + k, gz), 0, keepdims=False)
-        own = own + shifted(piece, "gz", gz, k)
     blocks = [gathered(block, "gy") for block in gathered(own, "gx")]
     parts = [blocks[i][j] for j in range(gy) for i in range(gx)]
     (core,) = call(

time: 75.4 us -> 65.1 us (0.86); the launches traced: 74.3 us -> 64.8 us
  local copies, waits for them, and re-layouts: 6.71 us -> 2.54 us
  Pallas kernels: 12.5 us -> 9.99 us
  starting transfers between devices: 39.8 us -> 38.6 us
  other arithmetic: 0.99 us -> 0.08 us
    unnamed x24 -> x16, local copies, waits for them, and re-layouts: 6.69 us -> 2.54 us
    ppermute x8, waiting for transfers between devices: 4.74 us -> 1.85 us  [paired(): out.append(lax.ppermute(x, axis, links + [(j, i) for i, j in links]))]
    pallas_call x7 -> x9, Pallas kernels: 12.5 us -> 9.99 us  [call(): pl.pallas_call(kernel, out_shape=tuple((jax.ShapeDtypeStruct(s, d) for s,...]
    ppermute x14, waiting for transfers between devices: 8.67 us -> 10.9 us  [shifted(): return lax.ppermute(x, axis, [(i, (i + k) % count) for i in range(count)])]
    add x1 -> x0, other arithmetic: 0.92 us -> none  [local(): own = own + shifted(piece, 'gz', gz, k)]
    ppermute x8, starting transfers between devices: 21.8 us -> 20.9 us  [paired(): out.append(lax.ppermute(x, axis, links + [(j, i) for i, j in links]))]
  transfers between devices with their start and end apart: 24 -> 24, of which waited for: 9 -> 7; matrix products, arithmetic and copies ran while one was open for 0% -> 0% of each run, Pallas kernels for 7% -> 5%
where the time goes in v4:
time: 65.1 us; the launch traced here: 64.8 us
  starting transfers between devices  38.6 us (59%)
  waiting for transfers between devices  12.8 us (20%)
  Pallas kernels  9.99 us (15%)
  local copies, waits for them, and re-layouts  2.54 us (4%)
  between operations  0.83 us (1%)
    ppermute x8, starting transfers between devices, paired(): out.append(lax.ppermute(x, axis, links + [(j, i) for i, j in links]))  20.9 us
    ppermute x14, starting transfers between devices, shifted(): return lax.ppermute(x, axis, [(i, (i + k) % count) for i in range(count)])  17.1 us
    ppermute x14, waiting for transfers between devices, shifted(): return lax.ppermute(x, axis, [(i, (i + k) % count) for i in range(count)])  10.9 us
    pallas_call x9, Pallas kernels, call(): pl.pallas_call(kernel, out_shape=tuple((jax.ShapeDtypeStruct(s, d) for s,...  9.99 us
    unnamed x16, local copies, waits for them, and re-layouts  2.54 us
    ppermute x8, waiting for transfers between devices, paired(): out.append(lax.ppermute(x, axis, links + [(j, i) for i, j in links]))  1.85 us
  transfers between devices with their start and end apart: 24, of which 7 were waited for; matrix products, arithmetic and copies ran while one was open for 0% of the time, Pallas kernels for 5%

profile of v4, /device:TPU:0, one launch (start us, length us, event | category | flops | bytes accessed | tf_op | source)
XLA Modules:
  0.0 64.8 jit_solution(2941946330100847046)
XLA Ops:
  0.6 0.6 collective-permute-start.2
  1.2 1.1 %copy-done = f32[16,12,8,128]{3,2,1,0:T(8,128)S(1)} copy-done((f32[16,12,8,128]{3,2,1,0:T(8,128)S(1)}, f32[16,12,8,128]{3,2,1,0:T(8,128)}, u32[]{:S(2)}) %copy-start) | copy-done | bytes 786456
  2.3 0.1 shard_map.87
  2.4 2.6 %collective-permute-start = (f32[16,4,8,128]{3,2,1,0:T(8,128)S(1)}, f32[16,4,8,128]{3,2,1,0:T(8,128)S(1)}, u32[]{:S(2)}, u32[]{:S(2)}) collective-permute-start(f32[16,4,8,128]{3,2,1,0:T(8,128)S(1)} %get-tuple-element.31), channel_id=1, source_target_pairs={{0,8},{16,24},{8,0},{24,16},{1,9},{17,25},{9,1},{25,17},{2,10},{18... | collective-permute-start | bytes 786440 | tf_op jit(solution)/shard_map/ppermute | solution.py:305
  4.9 0.7 %collective-permute-start.1 = (f32[16,4,8,128]{3,2,1,0:T(8,128)S(1)}, f32[16,4,8,128]{3,2,1,0:T(8,128)S(1)}, u32[]{:S(2)}, u32[]{:S(2)}) collective-permute-start(f32[16,4,8,128]{3,2,1,0:T(8,128)S(1)} %get-tuple-element.32), channel_id=1, source_target_pairs={{8,16},{16,8},{9,17},{17,9},{10,18},{18,10},{11,19},{19,11},{12,20... | collective-permute-start | bytes 786440 | tf_op jit(solution)/shard_map/ppermute | solution.py:305
  5.6 0.7 %shard_map.86 = (f32[12,8,128]{2,1,0:T(8,128)S(1)}, f32[16,12,8,128]{3,2,1,0:T(8,128)S(1)}) custom-call(f32[16,12,8,128]{3,2,1,0:T(8,128)S(1)} %copy-done), custom_call_target="tpu_custom_call" | custom-call | tf_op jit(solution)/shard_map/pallas_call | solution.py:21
  6.3 0.7 %collective-permute-start.4 = (f32[12,8,128]{2,1,0:T(8,128)S(1)}, f32[12,8,128]{2,1,0:T(8,128)S(1)}, u32[]{:S(2)}, u32[]{:S(2)}) collective-permute-start(f32[12,8,128]{2,1,0:T(8,128)S(1)} %get-tuple-element.33), channel_id=1, source_target_pairs={{1,2},{2,1},{5,6},{6,5},{9,10},{10,9},{13,14},{14,13},{17,18},{18,... | collective-permute-start | bytes 147464 | tf_op jit(solution)/shard_map/ppermute | solution.py:305
  7.0 4.5 %collective-permute-start.3 = (f32[12,8,128]{2,1,0:T(8,128)S(1)}, f32[12,8,128]{2,1,0:T(8,128)S(1)}, u32[]{:S(2)}, u32[]{:S(2)}) collective-permute-start(f32[12,8,128]{2,1,0:T(8,128)S(1)} %get-tuple-element.33), channel_id=1, source_target_pairs={{0,1},{2,3},{1,0},{3,2},{4,5},{6,7},{5,4},{7,6},{8,9},{10,11},{9,8... | collective-permute-start | bytes 147464 | tf_op jit(solution)/shard_map/ppermute | solution.py:305
  11.5 0.7 %copy-done.4 = f32[16,16]{1,0:T(8,128)S(1)} copy-done((f32[16,16]{1,0:T(8,128)S(1)}, f32[16,16]{1,0:T(8,128)}, u32[]{:S(2)}) %copy-start.4) | copy-done | bytes 1048
  12.1 0.7 %copy-done.6 = f32[3,16]{1,0:T(4,128)S(1)} copy-done((f32[3,16]{1,0:T(4,128)S(1)}, f32[3,16]{1,0:T(4,128)}, u32[]{:S(2)}) %copy-start.6) | copy-done | bytes 216
  12.8 0.6 shard_map.88
  13.4 0.0 collective-permute-done.4.z2_ref
  13.5 0.1 collective-permute-done.3.z1_ref
  13.5 0.0 collective-permute-done.1.x2_ref
  13.5 0.0 collective-permute-done.2.beside_ref
  13.5 1.9 %shard_map.89 = (f32[16,12,8,128]{3,2,1,0:T(8,128)S(1)}, f32[16,4,8,128]{3,2,1,0:T(8,128)S(1)}, f32[16,4,8,128]{3,2,1,0:T(8,128)S(1)}, f32[12,8,128]{2,1,0:T(8,128)S(1)}) custom-call(f32[16,12,8,128]{3,2,1,0:T(8,128)S(1)} %get-tuple-element.30.f_ref, f32[16,4,8,128]{3,2,1,0:T(8,128)S(1)} %collective-permute-done.x1_ref, ...), custom_call_target="tpu_custom_call" | custom-call | tf_op jit(solution)/shard_map/pallas_call | solution.py:21
  15.4 0.0 copy-start.7
  15.4 0.0 copy-start.5
  15.4 0.0 copy-start.3
  15.5 0.1 collective-permute-start.7
  15.5 6.8 %collective-permute-start.5 = (f32[16,4,8,128]{3,2,1,0:T(8,128)S(1)}, f32[16,4,8,128]{3,2,1,0:T(8,128)S(1)}, u32[]{:S(2)}, u32[]{:S(2)}) collective-permute-start(f32[16,4,8,128]{3,2,1,0:T(8,128)S(1)} %get-tuple-element.43), channel_id=1, source_target_pairs={{0,8},{16,24},{8,0},{24,16},{1,9},{17,25},{9,1},{25,17},{2,10},{18... | collective-permute-start | bytes 786440 | tf_op jit(solution)/shard_map/ppermute | solution.py:305
  22.3 0.7 %collective-permute-start.6 = (f32[16,4,8,128]{3,2,1,0:T(8,128)S(1)}, f32[16,4,8,128]{3,2,1,0:T(8,128)S(1)}, u32[]{:S(2)}, u32[]{:S(2)}) collective-permute-start(f32[16,4,8,128]{3,2,1,0:T(8,128)S(1)} %get-tuple-element.44), channel_id=1, source_target_pairs={{8,16},{16,8},{9,17},{17,9},{10,18},{18,10},{11,19},{19,11},{12,20... | collective-permute-start | bytes 786440 | tf_op jit(solution)/shard_map/ppermute | solution.py:305
  23.0 0.7 %collective-permute-start.9 = (f32[12,8,128]{2,1,0:T(8,128)S(1)}, f32[12,8,128]{2,1,0:T(8,128)S(1)}, u32[]{:S(2)}, u32[]{:S(2)}) collective-permute-start(f32[12,8,128]{2,1,0:T(8,128)S(1)} %get-tuple-element.45), channel_id=1, source_target_pairs={{1,2},{2,1},{5,6},{6,5},{9,10},{10,9},{13,14},{14,13},{17,18},{18,... | collective-permute-start | bytes 147464 | tf_op jit(solution)/shard_map/ppermute | solution.py:305
  23.6 4.5 %collective-permute-start.8 = (f32[12,8,128]{2,1,0:T(8,128)S(1)}, f32[12,8,128]{2,1,0:T(8,128)S(1)}, u32[]{:S(2)}, u32[]{:S(2)}) collective-permute-start(f32[12,8,128]{2,1,0:T(8,128)S(1)} %get-tuple-element.45), channel_id=1, source_target_pairs={{0,1},{2,3},{1,0},{3,2},{4,5},{6,7},{5,4},{7,6},{8,9},{10,11},{9,8... | collective-permute-start | bytes 147464 | tf_op jit(solution)/shard_map/ppermute | solution.py:305
  28.1 0.3 shard_map.90.zf_ref
  28.4 1.8 %collective-permute-done.8.z1_ref = f32[12,8,128]{2,1,0:T(8,128)S(1)} collective-permute-done((f32[12,8,128]{2,1,0:T(8,128)S(1)}, f32[12,8,128]{2,1,0:T(8,128)S(1)}, u32[]{:S(2)}, u32[]{:S(2)}) %collective-permute-start.8) | collective-permute-done | bytes 49184 | tf_op jit(solution)/shard_map/ppermute | solution.py:305
  30.2 2.8 %shard_map.91 = (f32[16,12,8,128]{3,2,1,0:T(8,128)}, f32[2,96,128]{2,1,0:T(8,128)S(1)}, f32[2,96,128]{2,1,0:T(8,128)S(1)}, f32[2,96,128]{2,1,0:T(8,128)S(1)}, f32[2,96,128]{2,1,0:T(8,128)S(1)}) custom-call(f32[16,12,8,128]{3,2,1,0:T(8,128)S(1)} %copy-done.1, f32[16,12,8,128]{3,2,1,0:T(8,128)S(1)} %get-tuple-element.42.s_ref, ...), custom_call_target="tpu_custom_call" | custom-call | tf_op jit(solution)/shard_map/pallas_call | solution.py:21
  33.0 2.0 %collective-permute-start.14 = (f32[2,96,128]{2,1,0:T(8,128)S(1)}, f32[2,96,128]{2,1,0:T(8,128)S(1)}, u32[]{:S(2)}, u32[]{:S(2)}) collective-permute-start(f32[2,96,128]{2,1,0:T(8,128)S(1)} %get-tuple-element.55), channel_id=1, source_target_pairs={{0,1},{1,2},{2,3},{3,0},{4,5},{5,6},{6,7},{7,4},{8,9},{9,10},{10,1... | collective-permute-start | bytes 294920 | tf_op jit(solution)/shard_map/ppermute | solution.py:290
  35.0 1.4 %collective-permute-start.15 = (f32[2,96,128]{2,1,0:T(8,128)S(1)}, f32[2,96,128]{2,1,0:T(8,128)S(1)}, u32[]{:S(2)}, u32[]{:S(2)}) collective-permute-start(f32[2,96,128]{2,1,0:T(8,128)S(1)} %get-tuple-element.56), channel_id=1, source_target_pairs={{0,2},{1,3},{2,0},{3,1},{4,6},{5,7},{6,4},{7,5},{8,10},{9,11},{10,... | collective-permute-start | bytes 294920 | tf_op jit(solution)/shard_map/ppermute | solution.py:290
  36.4 1.4 %collective-permute-start.16 = (f32[2,96,128]{2,1,0:T(8,128)S(1)}, f32[2,96,128]{2,1,0:T(8,128)S(1)}, u32[]{:S(2)}, u32[]{:S(2)}) collective-permute-start(f32[2,96,128]{2,1,0:T(8,128)S(1)} %get-tuple-element.57), channel_id=1, source_target_pairs={{0,3},{1,0},{2,1},{3,2},{4,7},{5,4},{6,5},{7,6},{8,11},{9,8},{10,9... | collective-permute-start | bytes 294920 | tf_op jit(solution)/shard_map/ppermute | solution.py:290
  37.8 2.7 %collective-permute-done.14.refs_1_ = f32[2,96,128]{2,1,0:T(8,128)S(1)} collective-permute-done((f32[2,96,128]{2,1,0:T(8,128)S(1)}, f32[2,96,128]{2,1,0:T(8,128)S(1)}, u32[]{:S(2)}, u32[]{:S(2)}) %collective-permute-start.14) | collective-permute-done | bytes 98336 | tf_op jit(solution)/shard_map/ppermute | solution.py:290
  40.5 2.6 %collective-permute-done.15.refs_2_ = f32[2,96,128]{2,1,0:T(8,128)S(1)} collective-permute-done((f32[2,96,128]{2,1,0:T(8,128)S(1)}, f32[2,96,128]{2,1,0:T(8,128)S(1)}, u32[]{:S(2)}, u32[]{:S(2)}) %collective-permute-start.15) | collective-permute-done | bytes 98336 | tf_op jit(solution)/shard_map/ppermute | solution.py:290
  43.2 0.0 collective-permute-done.16.refs_3_
  43.2 0.5 collective-permute-start.19
  43.8 6.6 %collective-permute-start.18 = (f32[2,96,128]{2,1,0:T(8,128)S(1)}, f32[2,96,128]{2,1,0:T(8,128)S(1)}, u32[]{:S(2)}, u32[]{:S(2)}) collective-permute-start(f32[2,96,128]{2,1,0:T(8,128)S(1)} %shard_map.93.refs_0_), channel_id=1, source_target_pairs={{0,16},{8,24},{16,0},{24,8},{1,17},{9,25},{17,1},{25,9},{2,18},{10... | collective-permute-start | bytes 294920 | tf_op jit(solution)/shard_map/ppermute | solution.py:290
  50.4 1.5 %collective-permute-start.17 = (f32[2,96,128]{2,1,0:T(8,128)S(1)}, f32[2,96,128]{2,1,0:T(8,128)S(1)}, u32[]{:S(2)}, u32[]{:S(2)}) collective-permute-start(f32[2,96,128]{2,1,0:T(8,128)S(1)} %shard_map.93.refs_0_), channel_id=1, source_target_pairs={{0,8},{8,16},{16,24},{24,0},{1,9},{9,17},{17,25},{25,1},{2,10},{10... | collective-permute-start | bytes 294920 | tf_op jit(solution)/shard_map/ppermute | solution.py:290
  51.9 1.4 %collective-permute-start.12 = (s32[1,12]{1,0:T(1,128)S(1)}, s32[1,12]{1,0:T(1,128)S(1)}, u32[]{:S(2)}, u32[]{:S(2)}) collective-permute-start(s32[1,12]{1,0:T(1,128)S(1)} %bitcast.5), channel_id=1, source_target_pairs={{0,24},{8,0},{16,8},{24,16},{1,25},{9,1},{17,9},{25,17},{2,26},{10... | collective-permute-start | bytes 152 | tf_op jit(solution)/shard_map/ppermute | solution.py:290
  53.3 0.1 collective-permute-start.11
  53.4 2.1 %collective-permute-done.12 = s32[1,12]{1,0:T(1,128)S(1)} collective-permute-done((s32[1,12]{1,0:T(1,128)S(1)}, s32[1,12]{1,0:T(1,128)S(1)}, u32[]{:S(2)}, u32[]{:S(2)}) %collective-permute-start.12) | collective-permute-done | bytes 80 | tf_op jit(solution)/shard_map/ppermute | solution.py:290
  55.5 1.1 %collective-permute-start.10 = (s32[1,12]{1,0:T(1,128)S(1)}, s32[1,12]{1,0:T(1,128)S(1)}, u32[]{:S(2)}, u32[]{:S(2)}) collective-permute-start(s32[1,12]{1,0:T(1,128)S(1)} %bitcast.7), channel_id=1, source_target_pairs={{0,8},{8,16},{16,24},{24,0},{1,9},{9,17},{17,25},{25,1},{2,10},{10... | collective-permute-start | bytes 152 | tf_op jit(solution)/shard_map/ppermute | solution.py:290
  56.6 0.3 collective-permute-done.11
  56.9 3.1 %collective-permute-done.10 = s32[1,12]{1,0:T(1,128)S(1)} collective-permute-done((s32[1,12]{1,0:T(1,128)S(1)}, s32[1,12]{1,0:T(1,128)S(1)}, u32[]{:S(2)}, u32[]{:S(2)}) %collective-permute-start.10) | collective-permute-done | bytes 80 | tf_op jit(solution)/shard_map/ppermute | solution.py:290
  60.0 0.5 collective-permute-start.23
  60.5 0.1 collective-permute-start.22
  60.6 0.4 collective-permute-start.21
  61.0 0.1 pad_add_fusion.rank_ref
  61.1 1.4 %shard_map.92.q_ref = bf16[2,768,768]{2,1,0:T(8,128)(2,1)S(1)} custom-call(s32[1,48]{1,0:T(1,128)S(1)} %pad_add_fusion.rank_ref, f32[48,96]{1,0:T(8,128)S(1)} %copy-done.3, f32[8,64]{1,0:T(8,128)S(1)} %copy-done.5, f32[8,64]{1,0:T(8,128)S(1)} %collective-permute-done.13.refs_1_), custom_call_target="tpu_custom_call" | custom-call | tf_op jit(solution)/shard_map/pallas_call | solution.py:21
  62.5 2.3 %shard_map.94 = f32[4,768,54]{2,1,0:T(8,128)} custom-call(bf16[2,768,768]{2,1,0:T(8,128)(2,1)S(1)} %shard_map.92.q_ref, f32[2,96,128]{2,1,0:T(8,128)S(1)} %shard_map.93.refs_0_, f32[2,96,128]{2,1,0:T(8,128)S(1)} %collective-permute-done.17.refs_1_, f32[2,96,128]{2,1,0:T(8,128)S(1)} %collective-permute-done.18.refs_2_, ...), custom_call_target="tpu_custom_call" | custom-call | tf_op jit(solution)/shard_map/pallas_call | solution.py:21
  (26 shorter events, 0.1 us)
Async XLA Ops:
  0.6 12.9 %collective-permute-start.2 = (f32[16,12,8,128]{3,2,1,0:T(8,128)}, f32[16,12,8,128]{3,2,1,0:T(8,128)S(1)}, u32[]{:S(2)}, u32[]{:S(2)}) collective-permute-start(f32[16,12,8,128]{3,2,1,0:T(8,128)} %f_ref.5), channel_id=1, source_target_pairs={{0,4},{4,0},{1,5},{5,1},{2,6},{6,2},{3,7},{7,3},{8,12},{12,8},{9,1... | collective-permute-start | bytes 2359304 | tf_op jit(solution)/shard_map/ppermute | solution.py:312
  1.2 1.1 %copy-start = (f32[16,12,8,128]{3,2,1,0:T(8,128)S(1)}, f32[16,12,8,128]{3,2,1,0:T(8,128)}, u32[]{:S(2)}) copy-start(f32[16,12,8,128]{3,2,1,0:T(8,128)} %f_ref.5) | copy-start | bytes 2359300
  2.3 25.8 %copy-start.2 = (f32[128,54]{0,1:T(8,128)S(1)}, f32[128,54]{0,1:T(8,128)}, u32[]{:S(2)}) copy-start(f32[128,54]{0,1:T(8,128)} %param.13) | copy-start | bytes 82948
  2.3 27.9 %copy-start.1 = (f32[16,12,8,128]{3,2,1,0:T(8,128)S(1)}, f32[16,12,8,128]{3,2,1,0:T(8,128)}, u32[]{:S(2)}) copy-start(f32[16,12,8,128]{3,2,1,0:T(8,128)} %f_ref.5) | copy-start | bytes 2359300
  2.4 11.1 %collective-permute-start = (f32[16,4,8,128]{3,2,1,0:T(8,128)S(1)}, f32[16,4,8,128]{3,2,1,0:T(8,128)S(1)}, u32[]{:S(2)}, u32[]{:S(2)}) collective-permute-start(f32[16,4,8,128]{3,2,1,0:T(8,128)S(1)} %get-tuple-element.31), channel_id=1, source_target_pairs={{0,8},{16,24},{8,0},{24,16},{1,9},{17,25},{9,1},{25,17},{2,10},{18... | collective-permute-start | bytes 786440 | tf_op jit(solution)/shard_map/ppermute | solution.py:305
  4.9 8.6 %collective-permute-start.1 = (f32[16,4,8,128]{3,2,1,0:T(8,128)S(1)}, f32[16,4,8,128]{3,2,1,0:T(8,128)S(1)}, u32[]{:S(2)}, u32[]{:S(2)}) collective-permute-start(f32[16,4,8,128]{3,2,1,0:T(8,128)S(1)} %get-tuple-element.32), channel_id=1, source_target_pairs={{8,16},{16,8},{9,17},{17,9},{10,18},{18,10},{11,19},{19,11},{12,20... | collective-permute-start | bytes 786440 | tf_op jit(solution)/shard_map/ppermute | solution.py:305
  6.3 7.1 %collective-permute-start.4 = (f32[12,8,128]{2,1,0:T(8,128)S(1)}, f32[12,8,128]{2,1,0:T(8,128)S(1)}, u32[]{:S(2)}, u32[]{:S(2)}) collective-permute-start(f32[12,8,128]{2,1,0:T(8,128)S(1)} %get-tuple-element.33), channel_id=1, source_target_pairs={{1,2},{2,1},{5,6},{6,5},{9,10},{10,9},{13,14},{14,13},{17,18},{18,... | collective-permute-start | bytes 147464 | tf_op jit(solution)/shard_map/ppermute | solution.py:305
  7.0 6.5 %collective-permute-start.3 = (f32[12,8,128]{2,1,0:T(8,128)S(1)}, f32[12,8,128]{2,1,0:T(8,128)S(1)}, u32[]{:S(2)}, u32[]{:S(2)}) collective-permute-start(f32[12,8,128]{2,1,0:T(8,128)S(1)} %get-tuple-element.33), channel_id=1, source_target_pairs={{0,1},{2,3},{1,0},{3,2},{4,5},{6,7},{5,4},{7,6},{8,9},{10,11},{9,8... | collective-permute-start | bytes 147464 | tf_op jit(solution)/shard_map/ppermute | solution.py:305
  11.4 0.7 %copy-start.4 = (f32[16,16]{1,0:T(8,128)S(1)}, f32[16,16]{1,0:T(8,128)}, u32[]{:S(2)}) copy-start(f32[16,16]{1,0:T(8,128)} %kin_ref.1) | copy-start | bytes 3076
  12.1 0.7 %copy-start.6 = (f32[3,16]{1,0:T(4,128)S(1)}, f32[3,16]{1,0:T(4,128)}, u32[]{:S(2)}) copy-start(f32[3,16]{1,0:T(4,128)} %speed_ref.1) | copy-start | bytes 580
  15.4 36.5 %copy-start.7 = (s32[12]{0:T(128)S(1)}, s32[12]{0:T(128)}, u32[]{:S(2)}) copy-start(s32[12]{0:T(128)} %param.10) | copy-start | bytes 148
  15.4 41.5 %copy-start.5 = (f32[8,64]{1,0:T(8,128)S(1)}, f32[8,64]{1,0:T(8,128)}, u32[]{:S(2)}) copy-start(f32[8,64]{1,0:T(8,128)} %refs_0_) | copy-start | bytes 6148
  15.4 45.7 %copy-start.3 = (f32[48,96]{1,0:T(8,128)S(1)}, f32[48,96]{1,0:T(8,128)}, u32[]{:S(2)}) copy-start(f32[48,96]{1,0:T(8,128)} %xf_ref.1) | copy-start | bytes 55300
  15.5 14.7 %collective-permute-start.7 = (f32[16,12,8,128]{3,2,1,0:T(8,128)S(1)}, f32[16,12,8,128]{3,2,1,0:T(8,128)S(1)}, u32[]{:S(2)}, u32[]{:S(2)}) collective-permute-start(f32[16,12,8,128]{3,2,1,0:T(8,128)S(1)} %get-tuple-element.42.s_ref), channel_id=1, source_target_pairs={{0,4},{4,0},{1,5},{5,1},{2,6},{6,2},{3,7},{7,3},{8,12},{12,8},{9,1... | collective-permute-start | bytes 2359304 | tf_op jit(solution)/shard_map/ppermute | solution.py:312
  15.5 14.6 %collective-permute-start.5 = (f32[16,4,8,128]{3,2,1,0:T(8,128)S(1)}, f32[16,4,8,128]{3,2,1,0:T(8,128)S(1)}, u32[]{:S(2)}, u32[]{:S(2)}) collective-permute-start(f32[16,4,8,128]{3,2,1,0:T(8,128)S(1)} %get-tuple-element.43), channel_id=1, source_target_pairs={{0,8},{16,24},{8,0},{24,16},{1,9},{17,25},{9,1},{25,17},{2,10},{18... | collective-permute-start | bytes 786440 | tf_op jit(solution)/shard_map/ppermute | solution.py:305
  22.3 7.9 %collective-permute-start.6 = (f32[16,4,8,128]{3,2,1,0:T(8,128)S(1)}, f32[16,4,8,128]{3,2,1,0:T(8,128)S(1)}, u32[]{:S(2)}, u32[]{:S(2)}) collective-permute-start(f32[16,4,8,128]{3,2,1,0:T(8,128)S(1)} %get-tuple-element.44), channel_id=1, source_target_pairs={{8,16},{16,8},{9,17},{17,9},{10,18},{18,10},{11,19},{19,11},{12,20... | collective-permute-start | bytes 786440 | tf_op jit(solution)/shard_map/ppermute | solution.py:305
  23.0 5.4 %collective-permute-start.9 = (f32[12,8,128]{2,1,0:T(8,128)S(1)}, f32[12,8,128]{2,1,0:T(8,128)S(1)}, u32[]{:S(2)}, u32[]{:S(2)}) collective-permute-start(f32[12,8,128]{2,1,0:T(8,128)S(1)} %get-tuple-element.45), channel_id=1, source_target_pairs={{1,2},{2,1},{5,6},{6,5},{9,10},{10,9},{13,14},{14,13},{17,18},{18,... | collective-permute-start | bytes 147464 | tf_op jit(solution)/shard_map/ppermute | solution.py:305
  23.6 6.5 %collective-permute-start.8 = (f32[12,8,128]{2,1,0:T(8,128)S(1)}, f32[12,8,128]{2,1,0:T(8,128)S(1)}, u32[]{:S(2)}, u32[]{:S(2)}) collective-permute-start(f32[12,8,128]{2,1,0:T(8,128)S(1)} %get-tuple-element.45), channel_id=1, source_target_pairs={{0,1},{2,3},{1,0},{3,2},{4,5},{6,7},{5,4},{7,6},{8,9},{10,11},{9,8... | collective-permute-start | bytes 147464 | tf_op jit(solution)/shard_map/ppermute | solution.py:305
  33.0 7.6 %collective-permute-start.14 = (f32[2,96,128]{2,1,0:T(8,128)S(1)}, f32[2,96,128]{2,1,0:T(8,128)S(1)}, u32[]{:S(2)}, u32[]{:S(2)}) collective-permute-start(f32[2,96,128]{2,1,0:T(8,128)S(1)} %get-tuple-element.55), channel_id=1, source_target_pairs={{0,1},{1,2},{2,3},{3,0},{4,5},{5,6},{6,7},{7,4},{8,9},{9,10},{10,1... | collective-permute-start | bytes 294920 | tf_op jit(solution)/shard_map/ppermute | solution.py:290
  35.0 8.2 %collective-permute-start.15 = (f32[2,96,128]{2,1,0:T(8,128)S(1)}, f32[2,96,128]{2,1,0:T(8,128)S(1)}, u32[]{:S(2)}, u32[]{:S(2)}) collective-permute-start(f32[2,96,128]{2,1,0:T(8,128)S(1)} %get-tuple-element.56), channel_id=1, source_target_pairs={{0,2},{1,3},{2,0},{3,1},{4,6},{5,7},{6,4},{7,5},{8,10},{9,11},{10,... | collective-permute-start | bytes 294920 | tf_op jit(solution)/shard_map/ppermute | solution.py:290
  36.4 6.8 %collective-permute-start.16 = (f32[2,96,128]{2,1,0:T(8,128)S(1)}, f32[2,96,128]{2,1,0:T(8,128)S(1)}, u32[]{:S(2)}, u32[]{:S(2)}) collective-permute-start(f32[2,96,128]{2,1,0:T(8,128)S(1)} %get-tuple-element.57), channel_id=1, source_target_pairs={{0,3},{1,0},{2,1},{3,2},{4,7},{5,4},{6,5},{7,6},{8,11},{9,8},{10,9... | collective-permute-start | bytes 294920 | tf_op jit(solution)/shard_map/ppermute | solution.py:290
  43.2 16.7 %collective-permute-start.19 = (f32[2,96,128]{2,1,0:T(8,128)S(1)}, f32[2,96,128]{2,1,0:T(8,128)S(1)}, u32[]{:S(2)}, u32[]{:S(2)}) collective-permute-start(f32[2,96,128]{2,1,0:T(8,128)S(1)} %shard_map.93.refs_0_), channel_id=1, source_target_pairs={{0,24},{8,0},{16,8},{24,16},{1,25},{9,1},{17,9},{25,17},{2,26},{10... | collective-permute-start | bytes 294920 | tf_op jit(solution)/shard_map/ppermute | solution.py:290
  43.8 16.7 %collective-permute-start.18 = (f32[2,96,128]{2,1,0:T(8,128)S(1)}, f32[2,96,128]{2,1,0:T(8,128)S(1)}, u32[]{:S(2)}, u32[]{:S(2)}) collective-permute-start(f32[2,96,128]{2,1,0:T(8,128)S(1)} %shard_map.93.refs_0_), channel_id=1, source_target_pairs={{0,16},{8,24},{16,0},{24,8},{1,17},{9,25},{17,1},{25,9},{2,18},{10... | collective-permute-start | bytes 294920 | tf_op jit(solution)/shard_map/ppermute | solution.py:290
  50.4 10.2 %collective-permute-start.17 = (f32[2,96,128]{2,1,0:T(8,128)S(1)}, f32[2,96,128]{2,1,0:T(8,128)S(1)}, u32[]{:S(2)}, u32[]{:S(2)}) collective-permute-start(f32[2,96,128]{2,1,0:T(8,128)S(1)} %shard_map.93.refs_0_), channel_id=1, source_target_pairs={{0,8},{8,16},{16,24},{24,0},{1,9},{9,17},{17,25},{25,1},{2,10},{10... | collective-permute-start | bytes 294920 | tf_op jit(solution)/shard_map/ppermute | solution.py:290
  51.9 3.6 %collective-permute-start.12 = (s32[1,12]{1,0:T(1,128)S(1)}, s32[1,12]{1,0:T(1,128)S(1)}, u32[]{:S(2)}, u32[]{:S(2)}) collective-permute-start(s32[1,12]{1,0:T(1,128)S(1)} %bitcast.5), channel_id=1, source_target_pairs={{0,24},{8,0},{16,8},{24,16},{1,25},{9,1},{17,9},{25,17},{2,26},{10... | collective-permute-start | bytes 152 | tf_op jit(solution)/shard_map/ppermute | solution.py:290
  53.3 3.6 %collective-permute-start.11 = (s32[1,12]{1,0:T(1,128)S(1)}, s32[1,12]{1,0:T(1,128)S(1)}, u32[]{:S(2)}, u32[]{:S(2)}) collective-permute-start(s32[1,12]{1,0:T(1,128)S(1)} %bitcast.6), channel_id=1, source_target_pairs={{0,16},{8,24},{16,0},{24,8},{1,17},{9,25},{17,1},{25,9},{2,18},{10... | collective-permute-start | bytes 152 | tf_op jit(solution)/shard_map/ppermute | solution.py:290
  55.5 4.5 %collective-permute-start.10 = (s32[1,12]{1,0:T(1,128)S(1)}, s32[1,12]{1,0:T(1,128)S(1)}, u32[]{:S(2)}, u32[]{:S(2)}) collective-permute-start(s32[1,12]{1,0:T(1,128)S(1)} %bitcast.7), channel_id=1, source_target_pairs={{0,8},{8,16},{16,24},{24,0},{1,9},{9,17},{17,25},{25,1},{2,10},{10... | collective-permute-start | bytes 152 | tf_op jit(solution)/shard_map/ppermute | solution.py:290
  56.9 4.2 %collective-permute-start.13 = (f32[8,64]{1,0:T(8,128)S(1)}, f32[8,64]{1,0:T(8,128)S(1)}, u32[]{:S(2)}, u32[]{:S(2)}) collective-permute-start(f32[8,64]{1,0:T(8,128)S(1)} %copy-done.5), channel_id=1, source_target_pairs={{0,4},{4,0},{1,5},{5,1},{2,6},{6,2},{3,7},{7,3},{8,12},{12,8},{9,1... | collective-permute-start | bytes 6152 | tf_op jit(solution)/shard_map/ppermute | solution.py:290
  60.0 2.5 %collective-permute-start.20 = (f32[2,96,128]{2,1,0:T(8,128)S(1)}, f32[2,96,128]{2,1,0:T(8,128)S(1)}, u32[]{:S(2)}, u32[]{:S(2)}) collective-permute-start(f32[2,96,128]{2,1,0:T(8,128)S(1)} %shard_map.93.refs_0_), channel_id=1, source_target_pairs={{0,4},{4,0},{1,5},{5,1},{2,6},{6,2},{3,7},{7,3},{8,12},{12,8},{9,1... | collective-permute-start | bytes 294920 | tf_op jit(solution)/shard_map/ppermute | solution.py:290
  60.0 2.5 %collective-permute-start.23 = (f32[2,96,128]{2,1,0:T(8,128)S(1)}, f32[2,96,128]{2,1,0:T(8,128)S(1)}, u32[]{:S(2)}, u32[]{:S(2)}) collective-permute-start(f32[2,96,128]{2,1,0:T(8,128)S(1)} %collective-permute-done.19.refs_3_), channel_id=1, source_target_pairs={{0,4},{4,0},{1,5},{5,1},{2,6},{6,2},{3,7},{7,3},{8,12},{12,8},{9,1... | collective-permute-start | bytes 294920 | tf_op jit(solution)/shard_map/ppermute | solution.py:290
  60.5 2.0 %collective-permute-start.22 = (f32[2,96,128]{2,1,0:T(8,128)S(1)}, f32[2,96,128]{2,1,0:T(8,128)S(1)}, u32[]{:S(2)}, u32[]{:S(2)}) collective-permute-start(f32[2,96,128]{2,1,0:T(8,128)S(1)} %collective-permute-done.18.refs_2_), channel_id=1, source_target_pairs={{0,4},{4,0},{1,5},{5,1},{2,6},{6,2},{3,7},{7,3},{8,12},{12,8},{9,1... | collective-permute-start | bytes 294920 | tf_op jit(solution)/shard_map/ppermute | solution.py:290
  60.6 1.9 %collective-permute-start.21 = (f32[2,96,128]{2,1,0:T(8,128)S(1)}, f32[2,96,128]{2,1,0:T(8,128)S(1)}, u32[]{:S(2)}, u32[]{:S(2)}) collective-permute-start(f32[2,96,128]{2,1,0:T(8,128)S(1)} %collective-permute-done.17.refs_1_), channel_id=1, source_target_pairs={{0,4},{4,0},{1,5},{5,1},{2,6},{6,2},{3,7},{7,3},{8,12},{12,8},{9,1... | collective-permute-start | bytes 294920 | tf_op jit(solution)/shard_map/ppermute | solution.py:290

commit v5 on v4

--- a/solution.py
+++ b/solution.py
@@ -15,14 +15,16 @@
 HIGHEST = lax.Precision.HIGHEST
 VMEM = pl.BlockSpec(memory_space=pltpu.VMEM)
 SMEM = pl.BlockSpec(memory_space=pltpu.SMEM)
-
-
-def call(kernel, out_shapes, in_specs, args, scratch=(), room=16):
+ANY = pl.BlockSpec(memory_space=pl.ANY)
+HBM = pl.BlockSpec(memory_space=pltpu.HBM)
+
+
+def call(kernel, out_shapes, in_specs, args, scratch=(), room=16, out_spec=VMEM):
     return pl.pallas_call(
         kernel,
         out_shape=tuple(jax.ShapeDtypeStruct(s, d) for s, d in out_shapes),
         in_specs=in_specs,
-        out_specs=tuple(VMEM for _ in out_shapes),
+        out_specs=tuple(out_spec for _ in out_shapes),
         scratch_shapes=list(scratch),
         compiler_params=pltpu.CompilerParams(vmem_limit_bytes=room * 2**20),
     )(*args)
@@ -246,25 +248,26 @@
     refs[-1][...] = total
 
 
-def factor_kernel(rank_ref, xf_ref, *refs):
+def store_kernel(in_ref, out_ref, sem):
+    copy = pltpu.make_async_copy(in_ref, out_ref, sem)
+    copy.start()
+    copy.wait()
+
+
+def factor_kernel(xf_ref, *refs):
     y_refs, (out_ref, xt_ref) = refs[:-2], refs[-2:]
-    planes, a_count = rank_ref.shape[1], xt_ref.shape[0]
+    planes, a_count = xf_ref.shape[0], xt_ref.shape[0]
     ny = y_refs[0].shape[0]
     width = planes * ny
     b_count = out_ref.shape[1] // a_count
 
     def own(count, total, place):
-        column = lax.broadcasted_iota(jnp.int32, (count, total), 1)
-        return (column == lax.broadcasted_iota(jnp.int32, (count, total), 0) + place * count).astype(F32)
+        return (iota((count, total), 1) == iota((count, total), 0) + place * count).astype(F32)
 
     mine = exact(own(a_count, xf_ref.shape[1], lax.axis_index("gx")), xf_ref[...], ((1,), (1,)))
-    pick = lax.broadcasted_iota(jnp.int32, (xf_ref.shape[0], planes), 0) == rank_ref[...]
-    mine = exact(mine, pick.astype(F32))
-    column = lax.broadcasted_iota(jnp.int32, (planes, width), 1)
-    spread = lax.broadcasted_iota(jnp.int32, (planes, width), 0) == column // ny
+    spread = iota((planes, width), 0) == iota((planes, width), 1) // ny
     xt_ref[...] = exact(mine, spread.astype(F32))
-    column = lax.broadcasted_iota(jnp.int32, (ny, width), 1)
-    spread = lax.broadcasted_iota(jnp.int32, (ny, width), 0) == lax.rem(column, ny)
+    spread = iota((ny, width), 0) == low_bits(iota((ny, width), 1), ny)
     for i, y_ref in enumerate(y_refs):
         rows = exact(own(b_count, y_ref.shape[1], lax.axis_index("gy")), y_ref[...], ((1,), (1,)))
         yt = exact(rows, spread.astype(F32))
@@ -274,15 +277,32 @@
             out_ref[1, a * b_count : (a + 1) * b_count, i * width : (i + 1) * width] = low
 
 
-def core_kernel(q_ref, *refs):
-    out_ref = refs[-1]
-    pairs = refs[0].shape[0]
+def core_kernel(rank_ref, q_ref, *refs):
+    block_refs, (out_ref, placed_ref, result_ref, sems) = refs[:-4], refs[-4:]
+    pairs, blocks_y, planes, ny, nz = placed_ref.shape
+    nx = block_refs[0].shape[1] // ny
     rank = out_ref.shape[2]
-    columns = [jnp.concatenate([r[p] for r in refs[:-1]], axis=0) for p in range(pairs)]
+    rows = out_ref.shape[1] // sems.shape[0]
+    for i in range(planes // nx):
+        for x in range(nx):
+            row = rank_ref[i * nx + x]
+            for j in range(blocks_y):
+                for p in range(pairs):
+                    block_ref = block_refs[i * blocks_y + j]
+                    placed_ref[p, j, row] = block_ref[p, x * ny : (x + 1) * ny, :]
+    columns = [placed_ref[p].reshape(blocks_y * planes * ny, nz) for p in range(pairs)]
     high, low = split(jnp.concatenate(columns, axis=1))
-    result = dot(q_ref[0], high) + (dot(q_ref[0], low) + dot(q_ref[1], high))
-    for v in range(2 * pairs):
-        out_ref[v] = result[:, v * HALF : v * HALF + rank]
+    copies = []
+    for m in range(sems.shape[0]):
+        here = slice(m * rows, (m + 1) * rows)
+        q_high = q_ref[0, here]
+        result = dot(q_high, high) + (dot(q_high, low) + dot(q_ref[1, here], high))
+        for v in range(2 * pairs):
+            result_ref[v, here] = result[:, v * HALF : v * HALF + rank]
+        copies.append(pltpu.make_async_copy(result_ref.at[:, here], out_ref.at[:, here], sems.at[m]))
+        copies[-1].start()
+    for copy in copies:
+        copy.wait()
 
 
 def shifted(x, axis, k):
@@ -296,6 +316,18 @@
         return [x] + [shifted(x, axis, k) for k in range(1, count)]
     blocks = lax.all_gather(x, axis)
     return [blocks[k] for k in range(count)]
+
+
+def gathered_on_chip(x):
+    count = lax.axis_size("gx")
+    if count != 4 or lax.axis_size("gy") != 2:
+        return gathered(x, "gx")
+    ring = [((i, j), ((i + (1, 3)[j]) % 4, j)) for i in range(4) for j in range(2)]
+    mine = lax.ppermute(x, ("gx", "gy"), [(2 * i + j, 2 * k + l) for (i, j), (k, l) in ring])
+    across = shifted(x, "gx", 2)
+    theirs = lax.ppermute(mine, "gy", [(0, 1), (1, 0)])
+    upper = lax.axis_index("gy") == 1
+    return [x, jnp.where(upper, theirs, mine), across, jnp.where(upper, mine, theirs)]
 
 
 def paired(first, second, axis):
@@ -330,7 +362,7 @@
     first, second = call(
         rim_kernel,
         [(rim, F32), (rim, F32)],
-        [pl.BlockSpec(memory_space=pltpu.HBM)],
+        [HBM],
         (fields,),
         [pltpu.SemaphoreType.DMA((2,))],
     )
@@ -351,40 +383,51 @@
         (same, x1, x2, other, z1, z2, weights, dz, rim_shift, scales),
         scratch,
     )
-    section, first, second, packed, z_factor = barrier((section, first, second, packed, z_factor))
+    a_count, b_count = x_factor.shape[1] // gx, y_factor.shape[1] // gy
+    rows, planes = a_count * b_count, gx * nx
+    cells = planes * gy * ny
+    section, first, second, packed, z_factor, x_factor, y_factor = barrier(
+        (section, first, second, packed, z_factor, x_factor, y_factor)
+    )
     x1, x2 = paired(first, second, "gx")
     z1, z2 = paired(packed, packed, "gz")
     other = beside(section, "gy")
+    y_rows = gathered(y_factor, "gy")
     (zf,) = call(project_kernel, [((2 * nz, 4 * HALF), BF16)], [VMEM], (z_factor.T,), [pltpu.VMEM((nz, 2 * HALF), F32)])
-    fields_next, *chunks = call(
+    (factor,) = call(
+        factor_kernel,
+        [((2, rows, cells), BF16)],
+        [VMEM] * (1 + gy),
+        (x_factor, *y_rows),
+        [pltpu.VMEM((a_count, planes * ny), F32)],
+    )
+    x1, x2, z1, z2, other, zf, factor = barrier((x1, x2, z1, z2, other, zf, factor))
+    new, *chunks = call(
         next_kernel,
         [(fields.shape, F32)] + [(chunk, F32)] * gz,
         [VMEM] * 12,
         (fields, section, x1, x2, other, z1, z2, weights, dz, rim_shift, scales, zf),
         scratch,
     )
-    chunks, block_rank, y_factor = barrier((chunks, block_rank, y_factor))
+    new, chunks, block_rank = barrier((new, chunks, block_rank))
     parts = [chunks[0]] + [shifted(chunks[k], "gz", k) for k in range(1, gz)]
-    ranks = gathered(block_rank.reshape(1, nx), "gx")
-    y_rows = gathered(y_factor, "gy")
+    ranks = jnp.concatenate(gathered_on_chip(block_rank), axis=0)
+    (fields_next,) = call(store_kernel, [(fields.shape, F32)], [ANY], (new,), [pltpu.SemaphoreType.DMA], out_spec=HBM)
     (own,) = call(sum_kernel, [(chunk, F32)], [VMEM] * gz, parts)
-    a_count, b_count = x_factor.shape[1] // gx, y_factor.shape[1] // gy
-    cells = gx * nx * gy * ny
-    (factor,) = call(
-        factor_kernel,
-        [((2, a_count * b_count, cells), BF16)],
-        [VMEM] * (2 + gy),
-        (jnp.concatenate(ranks, axis=1), x_factor, *y_rows),
-        [pltpu.VMEM((a_count, gx * nx * ny), F32)],
-    )
     blocks = [gathered(block, "gy") for block in gathered(own, "gx")]
-    parts = [blocks[i][j] for j in range(gy) for i in range(gx)]
+    pieces = 4 if rows % 128 == 0 else 1
     (core,) = call(
         core_kernel,
-        [((2 * pairs, a_count * b_count, rank), F32)],
-        [VMEM] * (1 + len(parts)),
-        (factor, *parts),
-        room=16 if cells <= 1024 else 50,
+        [((2 * pairs, rows, rank), F32)],
+        [SMEM] + [VMEM] * (1 + gx * gy),
+        (ranks, factor, *(block for line in blocks for block in line)),
+        [
+            pltpu.VMEM((pairs, gy, planes, ny, nz), F32),
+            pltpu.VMEM((2 * pairs, rows, rank), F32),
+            pltpu.SemaphoreType.DMA((pieces,)),
+        ],
+        room=16 if cells <= 1024 else 56,
+        out_spec=HBM,
     )
     return fields_next, core.reshape(2 * pairs, a_count, b_count, rank)
 

time: 65.1 us -> 60.9 us (0.935)
  waiting for transfers between devices: 12.8 us -> 8.24 us
  starting transfers between devices: 38.6 us -> 37.8 us
    ppermute x14 -> x12, waiting for transfers between devices: 10.9 us -> 3.96 us  [shifted(): return lax.ppermute(x, axis, [(i, (i + k) % count) for i in range(count)])]
    ppermute x0 -> x2, starting transfers between devices: none -> 4.58 us  [the longest x1 4.51 us: gathered_on_chip(): lax.ppermute(x, ('gx', 'gy'), [(2 * i + j, 2 * k + l) for (i, j), (k, l)...]
    ppermute x8, starting transfers between devices: 20.9 us -> 16.6 us  [paired(): out.append(lax.ppermute(x, axis, links + [(j, i) for i, j in links]))]
    ppermute x8, waiting for transfers between devices: 1.85 us -> 4.27 us  [paired(): out.append(lax.ppermute(x, axis, links + [(j, i) for i, j in links]))]
    ppermute x14 -> x12, starting transfers between devices: 17.1 us -> 16 us  [shifted(): return lax.ppermute(x, axis, [(i, (i + k) % count) for i in range(count)])]
    pallas_call x9 -> x10, Pallas kernels: 9.99 us -> 10.6 us  [call(): pl.pallas_call(kernel, out_shape=tuple((jax.ShapeDtypeStruct(s, d) for s,...]
  transfers between devices with their start and end apart: 24 -> 24, of which waited for: 7 -> 6; matrix products, arithmetic and copies ran while one was open for 0% -> 0% of each run, Pallas kernels for 5% -> 6%
where the time goes in v5:
time: 60.9 us; the launch traced here: 60.1 us
  starting transfers between devices  37.8 us (62%)
  Pallas kernels  10.6 us (17%)
  waiting for transfers between devices  8.24 us (14%)
  local copies, waits for them, and re-layouts  2.53 us (4%)
  between operations  0.88 us (1%)
    ppermute x8, starting transfers between devices, paired(): out.append(lax.ppermute(x, axis, links + [(j, i) for i, j in links]))  16.6 us
    ppermute x12, starting transfers between devices, shifted(): return lax.ppermute(x, axis, [(i, (i + k) % count) for i in range(count)])  16 us
    pallas_call x10, Pallas kernels, call(): pl.pallas_call(kernel, out_shape=tuple((jax.ShapeDtypeStruct(s, d) for s,...  10.6 us
    ppermute x1, starting transfers between devices, gathered_on_chip(): lax.ppermute(x, ('gx', 'gy'), [(2 * i + j, 2 * k + l) for (i, j), (k, l)...  4.51 us
    ppermute x8, waiting for transfers between devices, paired(): out.append(lax.ppermute(x, axis, links + [(j, i) for i, j in links]))  4.27 us
    ppermute x12, waiting for transfers between devices, shifted(): return lax.ppermute(x, axis, [(i, (i + k) % count) for i in range(count)])  3.96 us
    unnamed x16, local copies, waits for them, and re-layouts  2.53 us
  transfers between devices with their start and end apart: 24, of which 6 were waited for; matrix products, arithmetic and copies ran while one was open for 0% of the time, Pallas kernels for 6%

profile of v5, /device:TPU:0, one launch (start us, length us, event | category | flops | bytes accessed | tf_op | source)
XLA Modules:
  0.0 60.1 jit_solution(2503336081623418477)
XLA Ops:
  0.6 0.6 collective-permute-start.2
  1.2 1.1 %copy-done = f32[16,12,8,128]{3,2,1,0:T(8,128)S(1)} copy-done((f32[16,12,8,128]{3,2,1,0:T(8,128)S(1)}, f32[16,12,8,128]{3,2,1,0:T(8,128)}, u32[]{:S(2)}) %copy-start) | copy-done | bytes 786456
  2.3 0.1 shard_map.87
  2.4 2.6 %collective-permute-start = (f32[16,4,8,128]{3,2,1,0:T(8,128)S(1)}, f32[16,4,8,128]{3,2,1,0:T(8,128)S(1)}, u32[]{:S(2)}, u32[]{:S(2)}) collective-permute-start(f32[16,4,8,128]{3,2,1,0:T(8,128)S(1)} %get-tuple-element.40), channel_id=1, source_target_pairs={{0,8},{16,24},{8,0},{24,16},{1,9},{17,25},{9,1},{25,17},{2,10},{18... | collective-permute-start | bytes 786440 | tf_op jit(solution)/shard_map/ppermute | solution.py:337
  4.9 0.7 %collective-permute-start.1 = (f32[16,4,8,128]{3,2,1,0:T(8,128)S(1)}, f32[16,4,8,128]{3,2,1,0:T(8,128)S(1)}, u32[]{:S(2)}, u32[]{:S(2)}) collective-permute-start(f32[16,4,8,128]{3,2,1,0:T(8,128)S(1)} %get-tuple-element.41), channel_id=1, source_target_pairs={{8,16},{16,8},{9,17},{17,9},{10,18},{18,10},{11,19},{19,11},{12,20... | collective-permute-start | bytes 786440 | tf_op jit(solution)/shard_map/ppermute | solution.py:337
  5.6 0.7 %shard_map.86 = (f32[12,8,128]{2,1,0:T(8,128)S(1)}, f32[16,12,8,128]{3,2,1,0:T(8,128)S(1)}) custom-call(f32[16,12,8,128]{3,2,1,0:T(8,128)S(1)} %copy-done), custom_call_target="tpu_custom_call" | custom-call | tf_op jit(solution)/shard_map/pallas_call | solution.py:23
  6.3 1.6 %collective-permute-start.3 = (f32[12,8,128]{2,1,0:T(8,128)S(1)}, f32[12,8,128]{2,1,0:T(8,128)S(1)}, u32[]{:S(2)}, u32[]{:S(2)}) collective-permute-start(f32[12,8,128]{2,1,0:T(8,128)S(1)} %get-tuple-element.42), channel_id=1, source_target_pairs={{0,1},{2,3},{1,0},{3,2},{4,5},{6,7},{5,4},{7,6},{8,9},{10,11},{9,8... | collective-permute-start | bytes 147464 | tf_op jit(solution)/shard_map/ppermute | solution.py:337
  8.0 0.7 %collective-permute-start.4 = (f32[12,8,128]{2,1,0:T(8,128)S(1)}, f32[12,8,128]{2,1,0:T(8,128)S(1)}, u32[]{:S(2)}, u32[]{:S(2)}) collective-permute-start(f32[12,8,128]{2,1,0:T(8,128)S(1)} %get-tuple-element.42), channel_id=1, source_target_pairs={{1,2},{2,1},{5,6},{6,5},{9,10},{10,9},{13,14},{14,13},{17,18},{18,... | collective-permute-start | bytes 147464 | tf_op jit(solution)/shard_map/ppermute | solution.py:337
  8.6 0.0 copy-start.4
  8.6 0.7 %copy-done.4 = f32[16,16]{1,0:T(8,128)S(1)} copy-done((f32[16,16]{1,0:T(8,128)S(1)}, f32[16,16]{1,0:T(8,128)}, u32[]{:S(2)}) %copy-start.4) | copy-done | bytes 1048
  9.3 0.7 %copy-done.6 = f32[3,16]{1,0:T(4,128)S(1)} copy-done((f32[3,16]{1,0:T(4,128)S(1)}, f32[3,16]{1,0:T(4,128)}, u32[]{:S(2)}) %copy-start.6) | copy-done | bytes 216
  10.0 0.6 %shard_map.88 = (bf16[256,256]{1,0:T(8,128)(2,1)S(1)}, bf16[256,128]{1,0:T(8,128)(2,1)S(1)}, bf16[128,128]{1,0:T(8,128)(2,1)S(1)}, f32[16,2,8,128]{3,2,1,0:T(8,128)S(1)}) custom-call(f32[16,16]{1,0:T(8,128)S(1)} %copy-done.4, f32[3,16]{1,0:T(4,128)S(1)} %copy-done.6), custom_call_target="tpu_custom_call" | custom-call | tf_op jit(solution)/shard_map/pallas_call | solution.py:23
  10.6 0.0 collective-permute-done.3.z1_ref
  10.6 0.0 collective-permute-done.4.z2_ref
  10.6 1.5 %collective-permute-done.x1_ref = f32[16,4,8,128]{3,2,1,0:T(8,128)S(1)} collective-permute-done((f32[16,4,8,128]{3,2,1,0:T(8,128)S(1)}, f32[16,4,8,128]{3,2,1,0:T(8,128)S(1)}, u32[]{:S(2)}, u32[]{:S(2)}) %collective-permute-start) | collective-permute-done | bytes 262176 | tf_op jit(solution)/shard_map/ppermute | solution.py:337
  12.1 0.0 collective-permute-done.1.x2_ref
  12.1 1.8 %shard_map.89 = (f32[16,12,8,128]{3,2,1,0:T(8,128)S(1)}, f32[16,4,8,128]{3,2,1,0:T(8,128)S(1)}, f32[16,4,8,128]{3,2,1,0:T(8,128)S(1)}, f32[12,8,128]{2,1,0:T(8,128)S(1)}) custom-call(f32[16,12,8,128]{3,2,1,0:T(8,128)S(1)} %get-tuple-element.39.f_ref, f32[16,4,8,128]{3,2,1,0:T(8,128)S(1)} %collective-permute-done.x1_ref, ...), custom_call_target="tpu_custom_call" | custom-call | tf_op jit(solution)/shard_map/pallas_call | solution.py:23
  14.0 0.1 collective-permute-start.9
  14.0 8.2 %collective-permute-start.5 = (f32[16,4,8,128]{3,2,1,0:T(8,128)S(1)}, f32[16,4,8,128]{3,2,1,0:T(8,128)S(1)}, u32[]{:S(2)}, u32[]{:S(2)}) collective-permute-start(f32[16,4,8,128]{3,2,1,0:T(8,128)S(1)} %get-tuple-element.52), channel_id=1, source_target_pairs={{0,8},{16,24},{8,0},{24,16},{1,9},{17,25},{9,1},{25,17},{2,10},{18... | collective-permute-start | bytes 786440 | tf_op jit(solution)/shard_map/ppermute | solution.py:337
  22.2 0.7 %collective-permute-start.6 = (f32[16,4,8,128]{3,2,1,0:T(8,128)S(1)}, f32[16,4,8,128]{3,2,1,0:T(8,128)S(1)}, u32[]{:S(2)}, u32[]{:S(2)}) collective-permute-start(f32[16,4,8,128]{3,2,1,0:T(8,128)S(1)} %get-tuple-element.53), channel_id=1, source_target_pairs={{8,16},{16,8},{9,17},{17,9},{10,18},{18,10},{11,19},{19,11},{12,20... | collective-permute-start | bytes 786440 | tf_op jit(solution)/shard_map/ppermute | solution.py:337
  22.9 0.2 collective-permute-start.10
  23.1 1.6 %collective-permute-start.7 = (f32[12,8,128]{2,1,0:T(8,128)S(1)}, f32[12,8,128]{2,1,0:T(8,128)S(1)}, u32[]{:S(2)}, u32[]{:S(2)}) collective-permute-start(f32[12,8,128]{2,1,0:T(8,128)S(1)} %get-tuple-element.54), channel_id=1, source_target_pairs={{0,1},{2,3},{1,0},{3,2},{4,5},{6,7},{5,4},{7,6},{8,9},{10,11},{9,8... | collective-permute-start | bytes 147464 | tf_op jit(solution)/shard_map/ppermute | solution.py:337
  24.7 0.7 %collective-permute-start.8 = (f32[12,8,128]{2,1,0:T(8,128)S(1)}, f32[12,8,128]{2,1,0:T(8,128)S(1)}, u32[]{:S(2)}, u32[]{:S(2)}) collective-permute-start(f32[12,8,128]{2,1,0:T(8,128)S(1)} %get-tuple-element.54), channel_id=1, source_target_pairs={{1,2},{2,1},{5,6},{6,5},{9,10},{10,9},{13,14},{14,13},{17,18},{18,... | collective-permute-start | bytes 147464 | tf_op jit(solution)/shard_map/ppermute | solution.py:337
  25.4 0.3 shard_map.90.zf_ref
  25.7 0.0 copy-start.7
  25.7 0.9 %shard_map.91.q_ref = bf16[2,768,768]{2,1,0:T(8,128)(2,1)S(1)} custom-call(f32[48,96]{1,0:T(8,128)S(1)} %copy-done.3, f32[8,64]{1,0:T(8,128)S(1)} %copy-done.5, f32[8,64]{1,0:T(8,128)S(1)} %collective-permute-done.10.refs_1_), custom_call_target="tpu_custom_call" | custom-call | tf_op jit(solution)/shard_map/pallas_call | solution.py:23
  26.6 0.6 %collective-permute-done.7.z1_ref = f32[12,8,128]{2,1,0:T(8,128)S(1)} collective-permute-done((f32[12,8,128]{2,1,0:T(8,128)S(1)}, f32[12,8,128]{2,1,0:T(8,128)S(1)}, u32[]{:S(2)}, u32[]{:S(2)}) %collective-permute-start.7) | collective-permute-done | bytes 49184 | tf_op jit(solution)/shard_map/ppermute | solution.py:337
  27.2 2.2 %collective-permute-done.5.x1_ref = f32[16,4,8,128]{3,2,1,0:T(8,128)S(1)} collective-permute-done((f32[16,4,8,128]{3,2,1,0:T(8,128)S(1)}, f32[16,4,8,128]{3,2,1,0:T(8,128)S(1)}, u32[]{:S(2)}, u32[]{:S(2)}) %collective-permute-start.5) | collective-permute-done | bytes 262176 | tf_op jit(solution)/shard_map/ppermute | solution.py:337
  29.4 0.0 collective-permute-done.9.beside_ref
  29.4 2.6 %shard_map.92 = (f32[16,12,8,128]{3,2,1,0:T(8,128)S(1)}, f32[2,96,128]{2,1,0:T(8,128)S(1)}, f32[2,96,128]{2,1,0:T(8,128)}, f32[2,96,128]{2,1,0:T(8,128)}, f32[2,96,128]{2,1,0:T(8,128)}) custom-call(f32[16,12,8,128]{3,2,1,0:T(8,128)S(1)} %copy-done.1, f32[16,12,8,128]{3,2,1,0:T(8,128)S(1)} %get-tuple-element.51.s_ref, ...), custom_call_target="tpu_custom_call" | custom-call | tf_op jit(solution)/shard_map/pallas_call | solution.py:23
  32.0 2.4 %collective-permute-start.14 = (f32[2,96,128]{2,1,0:T(8,128)}, f32[2,96,128]{2,1,0:T(8,128)S(1)}, u32[]{:S(2)}, u32[]{:S(2)}) collective-permute-start(f32[2,96,128]{2,1,0:T(8,128)} %get-tuple-element.73), channel_id=1, source_target_pairs={{0,1},{1,2},{2,3},{3,0},{4,5},{5,6},{6,7},{7,4},{8,9},{9,10},{10,1... | collective-permute-start | bytes 294920 | tf_op jit(solution)/shard_map/ppermute | solution.py:310
  34.5 1.7 %collective-permute-start.15 = (f32[2,96,128]{2,1,0:T(8,128)}, f32[2,96,128]{2,1,0:T(8,128)S(1)}, u32[]{:S(2)}, u32[]{:S(2)}) collective-permute-start(f32[2,96,128]{2,1,0:T(8,128)} %get-tuple-element.74), channel_id=1, source_target_pairs={{0,2},{1,3},{2,0},{3,1},{4,6},{5,7},{6,4},{7,5},{8,10},{9,11},{10,... | collective-permute-start | bytes 294920 | tf_op jit(solution)/shard_map/ppermute | solution.py:310
  36.2 2.7 %collective-permute-start.16 = (f32[2,96,128]{2,1,0:T(8,128)}, f32[2,96,128]{2,1,0:T(8,128)S(1)}, u32[]{:S(2)}, u32[]{:S(2)}) collective-permute-start(f32[2,96,128]{2,1,0:T(8,128)} %get-tuple-element.75), channel_id=1, source_target_pairs={{0,3},{1,0},{2,1},{3,2},{4,7},{5,4},{6,5},{7,6},{8,11},{9,8},{10,9... | collective-permute-start | bytes 294920 | tf_op jit(solution)/shard_map/ppermute | solution.py:310
  38.8 4.5 %collective-permute-start.11 = (s32[12]{0:T(128)S(1)}, s32[12]{0:T(128)S(1)}, u32[]{:S(2)}, u32[]{:S(2)}) collective-permute-start(s32[12]{0:T(128)S(1)} %copy-done.7), channel_id=1, source_target_pairs={{0,8},{4,28},{8,16},{12,4},{16,24},{20,12},{24,0},{28,20},{1,9},{5... | collective-permute-start | bytes 152 | tf_op jit(solution)/shard_map/ppermute | solution.py:326
  43.4 1.0 %collective-permute-start.13 = (s32[12]{0:T(128)S(1)}, s32[12]{0:T(128)S(1)}, u32[]{:S(2)}, u32[]{:S(2)}) collective-permute-start(s32[12]{0:T(128)S(1)} %copy-done.7), channel_id=1, source_target_pairs={{0,16},{8,24},{16,0},{24,8},{1,17},{9,25},{17,1},{25,9},{2,18},{10... | collective-permute-start | bytes 152 | tf_op jit(solution)/shard_map/ppermute | solution.py:310
  44.4 0.9 %shard_map.93 = f32[16,12,8,128]{3,2,1,0:T(8,128)} custom-call(f32[16,12,8,128]{3,2,1,0:T(8,128)S(1)} %get-tuple-element.69.in_ref), custom_call_target="tpu_custom_call" | custom-call | tf_op jit(solution)/shard_map/pallas_call | solution.py:23
  45.3 0.1 collective-permute-start.12
  45.3 0.0 collective-permute-done.14.refs_1_
  45.4 0.0 collective-permute-done.16.refs_3_
  45.4 3.5 %collective-permute-start.18 = (f32[2,96,128]{2,1,0:T(8,128)S(1)}, f32[2,96,128]{2,1,0:T(8,128)S(1)}, u32[]{:S(2)}, u32[]{:S(2)}) collective-permute-start(f32[2,96,128]{2,1,0:T(8,128)S(1)} %shard_map.94.refs_0_), channel_id=1, source_target_pairs={{0,8},{8,16},{16,24},{24,0},{1,9},{9,17},{17,25},{25,1},{2,10},{10... | collective-permute-start | bytes 294920 | tf_op jit(solution)/shard_map/ppermute | solution.py:310
  48.9 1.1 %collective-permute-start.20 = (f32[2,96,128]{2,1,0:T(8,128)S(1)}, f32[2,96,128]{2,1,0:T(8,128)S(1)}, u32[]{:S(2)}, u32[]{:S(2)}) collective-permute-start(f32[2,96,128]{2,1,0:T(8,128)S(1)} %shard_map.94.refs_0_), channel_id=1, source_target_pairs={{0,16},{8,24},{16,0},{24,8},{1,17},{9,25},{17,1},{25,9},{2,18},{10... | collective-permute-start | bytes 294920 | tf_op jit(solution)/shard_map/ppermute | solution.py:310
  50.0 2.8 %collective-permute-start.22 = (f32[2,96,128]{2,1,0:T(8,128)S(1)}, f32[2,96,128]{2,1,0:T(8,128)S(1)}, u32[]{:S(2)}, u32[]{:S(2)}) collective-permute-start(f32[2,96,128]{2,1,0:T(8,128)S(1)} %shard_map.94.refs_0_), channel_id=1, source_target_pairs={{0,24},{8,0},{16,8},{24,16},{1,25},{9,1},{17,9},{25,17},{2,26},{10... | collective-permute-start | bytes 294920 | tf_op jit(solution)/shard_map/ppermute | solution.py:310
  52.9 0.5 collective-permute-start.19
  53.4 0.9 %collective-permute-done.20.refs_4_ = f32[2,96,128]{2,1,0:T(8,128)S(1)} collective-permute-done((f32[2,96,128]{2,1,0:T(8,128)S(1)}, f32[2,96,128]{2,1,0:T(8,128)S(1)}, u32[]{:S(2)}, u32[]{:S(2)}) %collective-permute-start.20) | collective-permute-done | bytes 98336 | tf_op jit(solution)/shard_map/ppermute | solution.py:310
  54.2 1.8 %collective-permute-done.22.refs_6_ = f32[2,96,128]{2,1,0:T(8,128)S(1)} collective-permute-done((f32[2,96,128]{2,1,0:T(8,128)S(1)}, f32[2,96,128]{2,1,0:T(8,128)S(1)}, u32[]{:S(2)}, u32[]{:S(2)}) %collective-permute-start.22) | collective-permute-done | bytes 98336 | tf_op jit(solution)/shard_map/ppermute | solution.py:310
  56.1 0.1 pad_add_fusion.rank_ref
  56.2 1.2 %collective-permute-done.23.refs_7_ = f32[2,96,128]{2,1,0:T(8,128)S(1)} collective-permute-done((f32[2,96,128]{2,1,0:T(8,128)S(1)}, f32[2,96,128]{2,1,0:T(8,128)S(1)}, u32[]{:S(2)}, u32[]{:S(2)}) %collective-permute-start.23) | collective-permute-done | bytes 98336 | tf_op jit(solution)/shard_map/ppermute | solution.py:310
  57.4 2.7 %shard_map.95 = f32[4,768,54]{2,1,0:T(8,128)} custom-call(s32[48]{0:T(128)S(1)} %pad_add_fusion.rank_ref, bf16[2,768,768]{2,1,0:T(8,128)(2,1)S(1)} %shard_map.91.q_ref, f32[2,96,128]{2,1,0:T(8,128)S(1)} %shard_map.94.refs_0_, f32[2,96,128]{2,1,0:T(8,128)S(1)} %collective-permute-done.17.refs_1_, f32[2,96,128]{2,1,0:T(8,128)S(1)} %collective-permute-done.18.refs_2_, ...), custom_call_target="tpu_custom_call" | custom-call | tf_op jit(solution)/shard_map/pallas_call | solution.py:23
  (28 shorter events, 0.1 us)
Async XLA Ops:
  0.6 11.5 %collective-permute-start.2 = (f32[16,12,8,128]{3,2,1,0:T(8,128)}, f32[16,12,8,128]{3,2,1,0:T(8,128)S(1)}, u32[]{:S(2)}, u32[]{:S(2)}) collective-permute-start(f32[16,12,8,128]{3,2,1,0:T(8,128)} %f_ref.5), channel_id=1, source_target_pairs={{0,4},{4,0},{1,5},{5,1},{2,6},{6,2},{3,7},{7,3},{8,12},{12,8},{9,1... | collective-permute-start | bytes 2359304 | tf_op jit(solution)/shard_map/ppermute | solution.py:344
  1.2 1.1 %copy-start = (f32[16,12,8,128]{3,2,1,0:T(8,128)S(1)}, f32[16,12,8,128]{3,2,1,0:T(8,128)}, u32[]{:S(2)}) copy-start(f32[16,12,8,128]{3,2,1,0:T(8,128)} %f_ref.5) | copy-start | bytes 2359300
  2.3 20.6 %copy-start.5 = (f32[8,64]{1,0:T(8,128)S(1)}, f32[8,64]{1,0:T(8,128)}, u32[]{:S(2)}) copy-start(f32[8,64]{1,0:T(8,128)} %refs_0_) | copy-start | bytes 6148
  2.3 23.0 %copy-start.2 = (f32[128,54]{0,1:T(8,128)S(1)}, f32[128,54]{0,1:T(8,128)}, u32[]{:S(2)}) copy-start(f32[128,54]{0,1:T(8,128)} %param.13) | copy-start | bytes 82948
  2.3 23.3 %copy-start.3 = (f32[48,96]{1,0:T(8,128)S(1)}, f32[48,96]{1,0:T(8,128)}, u32[]{:S(2)}) copy-start(f32[48,96]{1,0:T(8,128)} %xf_ref) | copy-start | bytes 55300
  2.4 9.7 %collective-permute-start = (f32[16,4,8,128]{3,2,1,0:T(8,128)S(1)}, f32[16,4,8,128]{3,2,1,0:T(8,128)S(1)}, u32[]{:S(2)}, u32[]{:S(2)}) collective-permute-start(f32[16,4,8,128]{3,2,1,0:T(8,128)S(1)} %get-tuple-element.40), channel_id=1, source_target_pairs={{0,8},{16,24},{8,0},{24,16},{1,9},{17,25},{9,1},{25,17},{2,10},{18... | collective-permute-start | bytes 786440 | tf_op jit(solution)/shard_map/ppermute | solution.py:337
  4.9 7.2 %collective-permute-start.1 = (f32[16,4,8,128]{3,2,1,0:T(8,128)S(1)}, f32[16,4,8,128]{3,2,1,0:T(8,128)S(1)}, u32[]{:S(2)}, u32[]{:S(2)}) collective-permute-start(f32[16,4,8,128]{3,2,1,0:T(8,128)S(1)} %get-tuple-element.41), channel_id=1, source_target_pairs={{8,16},{16,8},{9,17},{17,9},{10,18},{18,10},{11,19},{19,11},{12,20... | collective-permute-start | bytes 786440 | tf_op jit(solution)/shard_map/ppermute | solution.py:337
  6.3 4.3 %collective-permute-start.3 = (f32[12,8,128]{2,1,0:T(8,128)S(1)}, f32[12,8,128]{2,1,0:T(8,128)S(1)}, u32[]{:S(2)}, u32[]{:S(2)}) collective-permute-start(f32[12,8,128]{2,1,0:T(8,128)S(1)} %get-tuple-element.42), channel_id=1, source_target_pairs={{0,1},{2,3},{1,0},{3,2},{4,5},{6,7},{5,4},{7,6},{8,9},{10,11},{9,8... | collective-permute-start | bytes 147464 | tf_op jit(solution)/shard_map/ppermute | solution.py:337
  8.0 2.7 %collective-permute-start.4 = (f32[12,8,128]{2,1,0:T(8,128)S(1)}, f32[12,8,128]{2,1,0:T(8,128)S(1)}, u32[]{:S(2)}, u32[]{:S(2)}) collective-permute-start(f32[12,8,128]{2,1,0:T(8,128)S(1)} %get-tuple-element.42), channel_id=1, source_target_pairs={{1,2},{2,1},{5,6},{6,5},{9,10},{10,9},{13,14},{14,13},{17,18},{18,... | collective-permute-start | bytes 147464 | tf_op jit(solution)/shard_map/ppermute | solution.py:337
  8.6 0.7 %copy-start.4 = (f32[16,16]{1,0:T(8,128)S(1)}, f32[16,16]{1,0:T(8,128)}, u32[]{:S(2)}) copy-start(f32[16,16]{1,0:T(8,128)} %kin_ref.1) | copy-start | bytes 3076
  9.3 0.7 %copy-start.6 = (f32[3,16]{1,0:T(4,128)S(1)}, f32[3,16]{1,0:T(4,128)}, u32[]{:S(2)}) copy-start(f32[3,16]{1,0:T(4,128)} %speed_ref.1) | copy-start | bytes 580
  12.1 17.3 %copy-start.1 = (f32[16,12,8,128]{3,2,1,0:T(8,128)S(1)}, f32[16,12,8,128]{3,2,1,0:T(8,128)}, u32[]{:S(2)}) copy-start(f32[16,12,8,128]{3,2,1,0:T(8,128)} %f_ref.5) | copy-start | bytes 2359300
  14.0 15.4 %collective-permute-start.9 = (f32[16,12,8,128]{3,2,1,0:T(8,128)S(1)}, f32[16,12,8,128]{3,2,1,0:T(8,128)S(1)}, u32[]{:S(2)}, u32[]{:S(2)}) collective-permute-start(f32[16,12,8,128]{3,2,1,0:T(8,128)S(1)} %get-tuple-element.51.s_ref), channel_id=1, source_target_pairs={{0,4},{4,0},{1,5},{5,1},{2,6},{6,2},{3,7},{7,3},{8,12},{12,8},{9,1... | collective-permute-start | bytes 2359304 | tf_op jit(solution)/shard_map/ppermute | solution.py:344
  14.0 15.3 %collective-permute-start.5 = (f32[16,4,8,128]{3,2,1,0:T(8,128)S(1)}, f32[16,4,8,128]{3,2,1,0:T(8,128)S(1)}, u32[]{:S(2)}, u32[]{:S(2)}) collective-permute-start(f32[16,4,8,128]{3,2,1,0:T(8,128)S(1)} %get-tuple-element.52), channel_id=1, source_target_pairs={{0,8},{16,24},{8,0},{24,16},{1,9},{17,25},{9,1},{25,17},{2,10},{18... | collective-permute-start | bytes 786440 | tf_op jit(solution)/shard_map/ppermute | solution.py:337
  22.2 7.2 %collective-permute-start.6 = (f32[16,4,8,128]{3,2,1,0:T(8,128)S(1)}, f32[16,4,8,128]{3,2,1,0:T(8,128)S(1)}, u32[]{:S(2)}, u32[]{:S(2)}) collective-permute-start(f32[16,4,8,128]{3,2,1,0:T(8,128)S(1)} %get-tuple-element.53), channel_id=1, source_target_pairs={{8,16},{16,8},{9,17},{17,9},{10,18},{18,10},{11,19},{19,11},{12,20... | collective-permute-start | bytes 786440 | tf_op jit(solution)/shard_map/ppermute | solution.py:337
  22.9 1.8 %collective-permute-start.10 = (f32[8,64]{1,0:T(8,128)S(1)}, f32[8,64]{1,0:T(8,128)S(1)}, u32[]{:S(2)}, u32[]{:S(2)}) collective-permute-start(f32[8,64]{1,0:T(8,128)S(1)} %copy-done.5), channel_id=1, source_target_pairs={{0,4},{4,0},{1,5},{5,1},{2,6},{6,2},{3,7},{7,3},{8,12},{12,8},{9,1... | collective-permute-start | bytes 6152 | tf_op jit(solution)/shard_map/ppermute | solution.py:310
  23.1 4.1 %collective-permute-start.7 = (f32[12,8,128]{2,1,0:T(8,128)S(1)}, f32[12,8,128]{2,1,0:T(8,128)S(1)}, u32[]{:S(2)}, u32[]{:S(2)}) collective-permute-start(f32[12,8,128]{2,1,0:T(8,128)S(1)} %get-tuple-element.54), channel_id=1, source_target_pairs={{0,1},{2,3},{1,0},{3,2},{4,5},{6,7},{5,4},{7,6},{8,9},{10,11},{9,8... | collective-permute-start | bytes 147464 | tf_op jit(solution)/shard_map/ppermute | solution.py:337
  24.7 2.5 %collective-permute-start.8 = (f32[12,8,128]{2,1,0:T(8,128)S(1)}, f32[12,8,128]{2,1,0:T(8,128)S(1)}, u32[]{:S(2)}, u32[]{:S(2)}) collective-permute-start(f32[12,8,128]{2,1,0:T(8,128)S(1)} %get-tuple-element.54), channel_id=1, source_target_pairs={{1,2},{2,1},{5,6},{6,5},{9,10},{10,9},{13,14},{14,13},{17,18},{18,... | collective-permute-start | bytes 147464 | tf_op jit(solution)/shard_map/ppermute | solution.py:337
  25.7 13.2 %copy-start.7 = (s32[12]{0:T(128)S(1)}, s32[12]{0:T(128)}, u32[]{:S(2)}) copy-start(s32[12]{0:T(128)} %param.10) | copy-start | bytes 148
  32.0 13.3 %collective-permute-start.14 = (f32[2,96,128]{2,1,0:T(8,128)}, f32[2,96,128]{2,1,0:T(8,128)S(1)}, u32[]{:S(2)}, u32[]{:S(2)}) collective-permute-start(f32[2,96,128]{2,1,0:T(8,128)} %get-tuple-element.73), channel_id=1, source_target_pairs={{0,1},{1,2},{2,3},{3,0},{4,5},{5,6},{6,7},{7,4},{8,9},{9,10},{10,1... | collective-permute-start | bytes 294920 | tf_op jit(solution)/shard_map/ppermute | solution.py:310
  34.5 10.9 %collective-permute-start.15 = (f32[2,96,128]{2,1,0:T(8,128)}, f32[2,96,128]{2,1,0:T(8,128)S(1)}, u32[]{:S(2)}, u32[]{:S(2)}) collective-permute-start(f32[2,96,128]{2,1,0:T(8,128)} %get-tuple-element.74), channel_id=1, source_target_pairs={{0,2},{1,3},{2,0},{3,1},{4,6},{5,7},{6,4},{7,5},{8,10},{9,11},{10,... | collective-permute-start | bytes 294920 | tf_op jit(solution)/shard_map/ppermute | solution.py:310
  36.2 9.2 %collective-permute-start.16 = (f32[2,96,128]{2,1,0:T(8,128)}, f32[2,96,128]{2,1,0:T(8,128)S(1)}, u32[]{:S(2)}, u32[]{:S(2)}) collective-permute-start(f32[2,96,128]{2,1,0:T(8,128)} %get-tuple-element.75), channel_id=1, source_target_pairs={{0,3},{1,0},{2,1},{3,2},{4,7},{5,4},{6,5},{7,6},{8,11},{9,8},{10,9... | collective-permute-start | bytes 294920 | tf_op jit(solution)/shard_map/ppermute | solution.py:310
  38.8 6.4 %collective-permute-start.11 = (s32[12]{0:T(128)S(1)}, s32[12]{0:T(128)S(1)}, u32[]{:S(2)}, u32[]{:S(2)}) collective-permute-start(s32[12]{0:T(128)S(1)} %copy-done.7), channel_id=1, source_target_pairs={{0,8},{4,28},{8,16},{12,4},{16,24},{20,12},{24,0},{28,20},{1,9},{5... | collective-permute-start | bytes 152 | tf_op jit(solution)/shard_map/ppermute | solution.py:326
  43.4 12.7 %collective-permute-start.13 = (s32[12]{0:T(128)S(1)}, s32[12]{0:T(128)S(1)}, u32[]{:S(2)}, u32[]{:S(2)}) collective-permute-start(s32[12]{0:T(128)S(1)} %copy-done.7), channel_id=1, source_target_pairs={{0,16},{8,24},{16,0},{24,8},{1,17},{9,25},{17,1},{25,9},{2,18},{10... | collective-permute-start | bytes 152 | tf_op jit(solution)/shard_map/ppermute | solution.py:310
  45.3 7.6 %collective-permute-start.12 = (s32[12]{0:T(128)S(1)}, s32[12]{0:T(128)S(1)}, u32[]{:S(2)}, u32[]{:S(2)}) collective-permute-start(s32[12]{0:T(128)S(1)} %collective-permute-done.11), channel_id=1, source_target_pairs={{0,4},{4,0},{1,5},{5,1},{2,6},{6,2},{3,7},{7,3},{8,12},{12,8},{9,1... | collective-permute-start | bytes 152 | tf_op jit(solution)/shard_map/ppermute | solution.py:328
  45.4 7.5 %collective-permute-start.18 = (f32[2,96,128]{2,1,0:T(8,128)S(1)}, f32[2,96,128]{2,1,0:T(8,128)S(1)}, u32[]{:S(2)}, u32[]{:S(2)}) collective-permute-start(f32[2,96,128]{2,1,0:T(8,128)S(1)} %shard_map.94.refs_0_), channel_id=1, source_target_pairs={{0,8},{8,16},{16,24},{24,0},{1,9},{9,17},{17,25},{25,1},{2,10},{10... | collective-permute-start | bytes 294920 | tf_op jit(solution)/shard_map/ppermute | solution.py:310
  48.9 5.3 %collective-permute-start.20 = (f32[2,96,128]{2,1,0:T(8,128)S(1)}, f32[2,96,128]{2,1,0:T(8,128)S(1)}, u32[]{:S(2)}, u32[]{:S(2)}) collective-permute-start(f32[2,96,128]{2,1,0:T(8,128)S(1)} %shard_map.94.refs_0_), channel_id=1, source_target_pairs={{0,16},{8,24},{16,0},{24,8},{1,17},{9,25},{17,1},{25,9},{2,18},{10... | collective-permute-start | bytes 294920 | tf_op jit(solution)/shard_map/ppermute | solution.py:310
  50.0 6.1 %collective-permute-start.22 = (f32[2,96,128]{2,1,0:T(8,128)S(1)}, f32[2,96,128]{2,1,0:T(8,128)S(1)}, u32[]{:S(2)}, u32[]{:S(2)}) collective-permute-start(f32[2,96,128]{2,1,0:T(8,128)S(1)} %shard_map.94.refs_0_), channel_id=1, source_target_pairs={{0,24},{8,0},{16,8},{24,16},{1,25},{9,1},{17,9},{25,17},{2,26},{10... | collective-permute-start | bytes 294920 | tf_op jit(solution)/shard_map/ppermute | solution.py:310
  52.8 3.3 %collective-permute-start.17 = (f32[2,96,128]{2,1,0:T(8,128)S(1)}, f32[2,96,128]{2,1,0:T(8,128)S(1)}, u32[]{:S(2)}, u32[]{:S(2)}) collective-permute-start(f32[2,96,128]{2,1,0:T(8,128)S(1)} %shard_map.94.refs_0_), channel_id=1, source_target_pairs={{0,4},{4,0},{1,5},{5,1},{2,6},{6,2},{3,7},{7,3},{8,12},{12,8},{9,1... | collective-permute-start | bytes 294920 | tf_op jit(solution)/shard_map/ppermute | solution.py:310
  52.9 3.3 %collective-permute-start.19 = (f32[2,96,128]{2,1,0:T(8,128)S(1)}, f32[2,96,128]{2,1,0:T(8,128)S(1)}, u32[]{:S(2)}, u32[]{:S(2)}) collective-permute-start(f32[2,96,128]{2,1,0:T(8,128)S(1)} %collective-permute-done.18.refs_2_), channel_id=1, source_target_pairs={{0,4},{4,0},{1,5},{5,1},{2,6},{6,2},{3,7},{7,3},{8,12},{12,8},{9,1... | collective-permute-start | bytes 294920 | tf_op jit(solution)/shard_map/ppermute | solution.py:310
  54.2 1.9 %collective-permute-start.21 = (f32[2,96,128]{2,1,0:T(8,128)S(1)}, f32[2,96,128]{2,1,0:T(8,128)S(1)}, u32[]{:S(2)}, u32[]{:S(2)}) collective-permute-start(f32[2,96,128]{2,1,0:T(8,128)S(1)} %collective-permute-done.20.refs_4_), channel_id=1, source_target_pairs={{0,4},{4,0},{1,5},{5,1},{2,6},{6,2},{3,7},{7,3},{8,12},{12,8},{9,1... | collective-permute-start | bytes 294920 | tf_op jit(solution)/shard_map/ppermute | solution.py:310
  56.1 1.3 %collective-permute-start.23 = (f32[2,96,128]{2,1,0:T(8,128)S(1)}, f32[2,96,128]{2,1,0:T(8,128)S(1)}, u32[]{:S(2)}, u32[]{:S(2)}) collective-permute-start(f32[2,96,128]{2,1,0:T(8,128)S(1)} %collective-permute-done.22.refs_6_), channel_id=1, source_target_pairs={{0,4},{4,0},{1,5},{5,1},{2,6},{6,2},{3,7},{7,3},{8,12},{12,8},{9,1... | collective-permute-start | bytes 294920 | tf_op jit(solution)/shard_map/ppermute | solution.py:310

commit v6 on v5

--- a/solution.py
+++ b/solution.py
@@ -68,16 +68,18 @@
     rim_ref[...] = jnp.where(group == v + width // 2 // REACH, first, rim)
 
 
-def pack_kernel(f_ref, rim_ref, same_ref):
+def pack_kernel(f_ref, rim_ref, same_ref, sems):
+    count = f_ref.shape[0] // sems.shape[0]
+    copies = []
+    for i in range(sems.shape[0]):
+        part = pl.ds(i * count, count)
+        copies.append(pltpu.make_async_copy(f_ref.at[part], same_ref.at[part], sems.at[i]))
+        copies[-1].start()
     rim_ref[...] = jnp.zeros_like(rim_ref)
-
-    def step(v, carry):
-        values = f_ref[v]
-        same_ref[v] = values
-        pack_rim(v, values, rim_ref)
-        return carry
-
-    lax.fori_loop(0, f_ref.shape[0], step, 0, unroll=4)
+    for i, copy in enumerate(copies):
+        copy.wait()
+        for v in range(i * count, (i + 1) * count):
+            pack_rim(v, same_ref[v], rim_ref)
 
 
 def iota(shape, dim):
@@ -367,7 +369,9 @@
         [pltpu.SemaphoreType.DMA((2,))],
     )
     x1, x2 = paired(first, second, "gx")
-    packed, same = call(pack_kernel, [(plane, F32), (fields.shape, F32)], [VMEM], (fields,))
+    packed, same = call(
+        pack_kernel, [(plane, F32), (fields.shape, F32)], [HBM], (fields,), [pltpu.SemaphoreType.DMA((4,))]
+    )
     z1, z2 = paired(packed, packed, "gz")
     other = beside(fields, "gy")
     weights, dz, rim_shift, scales = call(
@@ -406,7 +410,7 @@
         next_kernel,
         [(fields.shape, F32)] + [(chunk, F32)] * gz,
         [VMEM] * 12,
-        (fields, section, x1, x2, other, z1, z2, weights, dz, rim_shift, scales, zf),
+        (same, section, x1, x2, other, z1, z2, weights, dz, rim_shift, scales, zf),
         scratch,
     )
     new, chunks, block_rank = barrier((new, chunks, block_rank))

time: 60.9 us -> 61 us (level)
  Pallas kernels: 10.6 us -> 11.7 us
  waiting for transfers between devices: 8.24 us -> 7.2 us
    pallas_call x10, Pallas kernels: 10.6 us -> 11.7 us  [call(): pl.pallas_call(kernel, out_shape=tuple((jax.ShapeDtypeStruct(s, d) for s,...]
    ppermute x8, waiting for transfers between devices: 4.27 us -> 3.23 us  [paired(): out.append(lax.ppermute(x, axis, links + [(j, i) for i, j in links]))]
    unnamed x16 -> x14, local copies, waits for them, and re-layouts: 2.53 us -> 2.52 us
  transfers between devices with their start and end apart: 24 -> 24, of which waited for: 6 -> 6; matrix products, arithmetic and copies ran while one was open for 0% -> 0% of each run, Pallas kernels for 6% -> 7%
where the time goes in v6:
time: 61 us; the launch traced here: 60.1 us
  starting transfers between devices  37.8 us (62%)
  Pallas kernels  11.7 us (19%)
  waiting for transfers between devices  7.2 us (12%)
  local copies, waits for them, and re-layouts  2.52 us (4%)
  between operations  0.87 us (1%)
    ppermute x8, starting transfers between devices, paired(): out.append(lax.ppermute(x, axis, links + [(j, i) for i, j in links]))  16.6 us
    ppermute x12, starting transfers between devices, shifted(): return lax.ppermute(x, axis, [(i, (i + k) % count) for i in range(count)])  16 us
    pallas_call x10, Pallas kernels, call(): pl.pallas_call(kernel, out_shape=tuple((jax.ShapeDtypeStruct(s, d) for s,...  11.7 us
    ppermute x1, starting transfers between devices, gathered_on_chip(): lax.ppermute(x, ('gx', 'gy'), [(2 * i + j, 2 * k + l) for (i, j), (k, l)...  4.52 us
    ppermute x12, waiting for transfers between devices, shifted(): return lax.ppermute(x, axis, [(i, (i + k) % count) for i in range(count)])  3.96 us
    ppermute x8, waiting for transfers between devices, paired(): out.append(lax.ppermute(x, axis, links + [(j, i) for i, j in links]))  3.23 us
    unnamed x14, local copies, waits for them, and re-layouts  2.52 us
  transfers between devices with their start and end apart: 24, of which 6 were waited for; matrix products, arithmetic and copies ran while one was open for 0% of the time, Pallas kernels for 7%

profile of v6, /device:TPU:0, one launch (start us, length us, event | category | flops | bytes accessed | tf_op | source)
XLA Modules:
  0.0 60.1 jit_solution(16259198895339384075)
XLA Ops:
  0.6 0.6 collective-permute-start.2
  1.2 1.1 %copy-done = f32[16,12,8,128]{3,2,1,0:T(8,128)S(1)} copy-done((f32[16,12,8,128]{3,2,1,0:T(8,128)S(1)}, f32[16,12,8,128]{3,2,1,0:T(8,128)}, u32[]{:S(2)}) %copy-start) | copy-done | bytes 786456
  2.3 0.1 shard_map.87
  2.4 2.6 %collective-permute-start = (f32[16,4,8,128]{3,2,1,0:T(8,128)S(1)}, f32[16,4,8,128]{3,2,1,0:T(8,128)S(1)}, u32[]{:S(2)}, u32[]{:S(2)}) collective-permute-start(f32[16,4,8,128]{3,2,1,0:T(8,128)S(1)} %get-tuple-element.40), channel_id=1, source_target_pairs={{0,8},{16,24},{8,0},{24,16},{1,9},{17,25},{9,1},{25,17},{2,10},{18... | collective-permute-start | bytes 786440 | tf_op jit(solution)/shard_map/ppermute | solution.py:339
  4.9 0.7 %collective-permute-start.1 = (f32[16,4,8,128]{3,2,1,0:T(8,128)S(1)}, f32[16,4,8,128]{3,2,1,0:T(8,128)S(1)}, u32[]{:S(2)}, u32[]{:S(2)}) collective-permute-start(f32[16,4,8,128]{3,2,1,0:T(8,128)S(1)} %get-tuple-element.41), channel_id=1, source_target_pairs={{8,16},{16,8},{9,17},{17,9},{10,18},{18,10},{11,19},{19,11},{12,20... | collective-permute-start | bytes 786440 | tf_op jit(solution)/shard_map/ppermute | solution.py:339
  5.6 1.7 %shard_map.86 = (f32[12,8,128]{2,1,0:T(8,128)S(1)}, f32[16,12,8,128]{3,2,1,0:T(8,128)S(1)}) custom-call(f32[16,12,8,128]{3,2,1,0:T(8,128)S(1)} %copy-done), custom_call_target="tpu_custom_call" | custom-call | tf_op jit(solution)/shard_map/pallas_call | solution.py:23
  7.4 1.6 %collective-permute-start.3 = (f32[12,8,128]{2,1,0:T(8,128)S(1)}, f32[12,8,128]{2,1,0:T(8,128)S(1)}, u32[]{:S(2)}, u32[]{:S(2)}) collective-permute-start(f32[12,8,128]{2,1,0:T(8,128)S(1)} %get-tuple-element.42), channel_id=1, source_target_pairs={{0,1},{2,3},{1,0},{3,2},{4,5},{6,7},{5,4},{7,6},{8,9},{10,11},{9,8... | collective-permute-start | bytes 147464 | tf_op jit(solution)/shard_map/ppermute | solution.py:339
  9.0 0.7 %collective-permute-start.4 = (f32[12,8,128]{2,1,0:T(8,128)S(1)}, f32[12,8,128]{2,1,0:T(8,128)S(1)}, u32[]{:S(2)}, u32[]{:S(2)}) collective-permute-start(f32[12,8,128]{2,1,0:T(8,128)S(1)} %get-tuple-element.42), channel_id=1, source_target_pairs={{1,2},{2,1},{5,6},{6,5},{9,10},{10,9},{13,14},{14,13},{17,18},{18,... | collective-permute-start | bytes 147464 | tf_op jit(solution)/shard_map/ppermute | solution.py:339
  9.7 0.0 copy-start.3
  9.7 0.7 %copy-done.3 = f32[16,16]{1,0:T(8,128)S(1)} copy-done((f32[16,16]{1,0:T(8,128)S(1)}, f32[16,16]{1,0:T(8,128)}, u32[]{:S(2)}) %copy-start.3) | copy-done | bytes 1048
  10.4 0.7 %copy-done.5 = f32[3,16]{1,0:T(4,128)S(1)} copy-done((f32[3,16]{1,0:T(4,128)S(1)}, f32[3,16]{1,0:T(4,128)}, u32[]{:S(2)}) %copy-start.5) | copy-done | bytes 216
  11.0 0.6 %shard_map.88 = (bf16[256,256]{1,0:T(8,128)(2,1)S(1)}, bf16[256,128]{1,0:T(8,128)(2,1)S(1)}, bf16[128,128]{1,0:T(8,128)(2,1)S(1)}, f32[16,2,8,128]{3,2,1,0:T(8,128)S(1)}) custom-call(f32[16,16]{1,0:T(8,128)S(1)} %copy-done.3, f32[3,16]{1,0:T(4,128)S(1)} %copy-done.5), custom_call_target="tpu_custom_call" | custom-call | tf_op jit(solution)/shard_map/pallas_call | solution.py:23
  11.7 0.0 collective-permute-done.3.z1_ref
  11.7 0.4 collective-permute-done.x1_ref
  12.1 0.0 collective-permute-done.1.x2_ref
  12.1 1.8 %shard_map.89 = (f32[16,12,8,128]{3,2,1,0:T(8,128)S(1)}, f32[16,4,8,128]{3,2,1,0:T(8,128)S(1)}, f32[16,4,8,128]{3,2,1,0:T(8,128)S(1)}, f32[12,8,128]{2,1,0:T(8,128)S(1)}) custom-call(f32[16,12,8,128]{3,2,1,0:T(8,128)S(1)} %get-tuple-element.39.f_ref, f32[16,4,8,128]{3,2,1,0:T(8,128)S(1)} %collective-permute-done.x1_ref, ...), custom_call_target="tpu_custom_call" | custom-call | tf_op jit(solution)/shard_map/pallas_call | solution.py:23
  14.0 0.1 collective-permute-start.9
  14.0 8.2 %collective-permute-start.5 = (f32[16,4,8,128]{3,2,1,0:T(8,128)S(1)}, f32[16,4,8,128]{3,2,1,0:T(8,128)S(1)}, u32[]{:S(2)}, u32[]{:S(2)}) collective-permute-start(f32[16,4,8,128]{3,2,1,0:T(8,128)S(1)} %get-tuple-element.52), channel_id=1, source_target_pairs={{0,8},{16,24},{8,0},{24,16},{1,9},{17,25},{9,1},{25,17},{2,10},{18... | collective-permute-start | bytes 786440 | tf_op jit(solution)/shard_map/ppermute | solution.py:339
  22.2 0.7 %collective-permute-start.6 = (f32[16,4,8,128]{3,2,1,0:T(8,128)S(1)}, f32[16,4,8,128]{3,2,1,0:T(8,128)S(1)}, u32[]{:S(2)}, u32[]{:S(2)}) collective-permute-start(f32[16,4,8,128]{3,2,1,0:T(8,128)S(1)} %get-tuple-element.53), channel_id=1, source_target_pairs={{8,16},{16,8},{9,17},{17,9},{10,18},{18,10},{11,19},{19,11},{12,20... | collective-permute-start | bytes 786440 | tf_op jit(solution)/shard_map/ppermute | solution.py:339
  22.9 0.2 collective-permute-start.10
  23.1 1.6 %collective-permute-start.7 = (f32[12,8,128]{2,1,0:T(8,128)S(1)}, f32[12,8,128]{2,1,0:T(8,128)S(1)}, u32[]{:S(2)}, u32[]{:S(2)}) collective-permute-start(f32[12,8,128]{2,1,0:T(8,128)S(1)} %get-tuple-element.54), channel_id=1, source_target_pairs={{0,1},{2,3},{1,0},{3,2},{4,5},{6,7},{5,4},{7,6},{8,9},{10,11},{9,8... | collective-permute-start | bytes 147464 | tf_op jit(solution)/shard_map/ppermute | solution.py:339
  24.7 0.0 collective-permute-done.10.refs_1_
  24.7 0.7 %collective-permute-start.8 = (f32[12,8,128]{2,1,0:T(8,128)S(1)}, f32[12,8,128]{2,1,0:T(8,128)S(1)}, u32[]{:S(2)}, u32[]{:S(2)}) collective-permute-start(f32[12,8,128]{2,1,0:T(8,128)S(1)} %get-tuple-element.54), channel_id=1, source_target_pairs={{1,2},{2,1},{5,6},{6,5},{9,10},{10,9},{13,14},{14,13},{17,18},{18,... | collective-permute-start | bytes 147464 | tf_op jit(solution)/shard_map/ppermute | solution.py:339
  25.4 0.3 shard_map.90.zf_ref
  25.7 0.0 copy-start.6
  25.7 0.9 %shard_map.91.q_ref = bf16[2,768,768]{2,1,0:T(8,128)(2,1)S(1)} custom-call(f32[48,96]{1,0:T(8,128)S(1)} %copy-done.2, f32[8,64]{1,0:T(8,128)S(1)} %copy-done.4, f32[8,64]{1,0:T(8,128)S(1)} %collective-permute-done.10.refs_1_), custom_call_target="tpu_custom_call" | custom-call | tf_op jit(solution)/shard_map/pallas_call | solution.py:23
  26.6 0.6 %collective-permute-done.7.z1_ref = f32[12,8,128]{2,1,0:T(8,128)S(1)} collective-permute-done((f32[12,8,128]{2,1,0:T(8,128)S(1)}, f32[12,8,128]{2,1,0:T(8,128)S(1)}, u32[]{:S(2)}, u32[]{:S(2)}) %collective-permute-start.7) | collective-permute-done | bytes 49184 | tf_op jit(solution)/shard_map/ppermute | solution.py:339
  27.2 0.0 collective-permute-done.8.z2_ref
  27.2 2.2 %collective-permute-done.5.x1_ref = f32[16,4,8,128]{3,2,1,0:T(8,128)S(1)} collective-permute-done((f32[16,4,8,128]{3,2,1,0:T(8,128)S(1)}, f32[16,4,8,128]{3,2,1,0:T(8,128)S(1)}, u32[]{:S(2)}, u32[]{:S(2)}) %collective-permute-start.5) | collective-permute-done | bytes 262176 | tf_op jit(solution)/shard_map/ppermute | solution.py:339
  29.4 0.0 collective-permute-done.6.x2_ref
  29.4 2.6 %shard_map.92 = (f32[16,12,8,128]{3,2,1,0:T(8,128)S(1)}, f32[2,96,128]{2,1,0:T(8,128)S(1)}, f32[2,96,128]{2,1,0:T(8,128)}, f32[2,96,128]{2,1,0:T(8,128)}, f32[2,96,128]{2,1,0:T(8,128)}) custom-call(f32[16,12,8,128]{3,2,1,0:T(8,128)S(1)} %get-tuple-element.39.f_ref, f32[16,12,8,128]{3,2,1,0:T(8,128)S(1)} %get-tuple-element.51.s_ref, ...), custom_call_target="tpu_custom_call" | custom-call | tf_op jit(solution)/shard_map/pallas_call | solution.py:23
  32.0 2.4 %collective-permute-start.14 = (f32[2,96,128]{2,1,0:T(8,128)}, f32[2,96,128]{2,1,0:T(8,128)S(1)}, u32[]{:S(2)}, u32[]{:S(2)}) collective-permute-start(f32[2,96,128]{2,1,0:T(8,128)} %get-tuple-element.73), channel_id=1, source_target_pairs={{0,1},{1,2},{2,3},{3,0},{4,5},{5,6},{6,7},{7,4},{8,9},{9,10},{10,1... | collective-permute-start | bytes 294920 | tf_op jit(solution)/shard_map/ppermute | solution.py:312
  34.5 1.7 %collective-permute-start.15 = (f32[2,96,128]{2,1,0:T(8,128)}, f32[2,96,128]{2,1,0:T(8,128)S(1)}, u32[]{:S(2)}, u32[]{:S(2)}) collective-permute-start(f32[2,96,128]{2,1,0:T(8,128)} %get-tuple-element.74), channel_id=1, source_target_pairs={{0,2},{1,3},{2,0},{3,1},{4,6},{5,7},{6,4},{7,5},{8,10},{9,11},{10,... | collective-permute-start | bytes 294920 | tf_op jit(solution)/shard_map/ppermute | solution.py:312
  36.2 2.7 %collective-permute-start.16 = (f32[2,96,128]{2,1,0:T(8,128)}, f32[2,96,128]{2,1,0:T(8,128)S(1)}, u32[]{:S(2)}, u32[]{:S(2)}) collective-permute-start(f32[2,96,128]{2,1,0:T(8,128)} %get-tuple-element.75), channel_id=1, source_target_pairs={{0,3},{1,0},{2,1},{3,2},{4,7},{5,4},{6,5},{7,6},{8,11},{9,8},{10,9... | collective-permute-start | bytes 294920 | tf_op jit(solution)/shard_map/ppermute | solution.py:312
  38.8 4.5 %collective-permute-start.11 = (s32[12]{0:T(128)S(1)}, s32[12]{0:T(128)S(1)}, u32[]{:S(2)}, u32[]{:S(2)}) collective-permute-start(s32[12]{0:T(128)S(1)} %copy-done.6), channel_id=1, source_target_pairs={{0,8},{4,28},{8,16},{12,4},{16,24},{20,12},{24,0},{28,20},{1,9},{5... | collective-permute-start | bytes 152 | tf_op jit(solution)/shard_map/ppermute | solution.py:328
  43.4 1.0 %collective-permute-start.13 = (s32[12]{0:T(128)S(1)}, s32[12]{0:T(128)S(1)}, u32[]{:S(2)}, u32[]{:S(2)}) collective-permute-start(s32[12]{0:T(128)S(1)} %copy-done.6), channel_id=1, source_target_pairs={{0,16},{8,24},{16,0},{24,8},{1,17},{9,25},{17,1},{25,9},{2,18},{10... | collective-permute-start | bytes 152 | tf_op jit(solution)/shard_map/ppermute | solution.py:312
  44.4 0.9 %shard_map.93 = f32[16,12,8,128]{3,2,1,0:T(8,128)} custom-call(f32[16,12,8,128]{3,2,1,0:T(8,128)S(1)} %get-tuple-element.69.in_ref), custom_call_target="tpu_custom_call" | custom-call | tf_op jit(solution)/shard_map/pallas_call | solution.py:23
  45.3 0.0 collective-permute-done.11
  45.3 0.1 collective-permute-start.12
  45.4 3.5 %collective-permute-start.18 = (f32[2,96,128]{2,1,0:T(8,128)S(1)}, f32[2,96,128]{2,1,0:T(8,128)S(1)}, u32[]{:S(2)}, u32[]{:S(2)}) collective-permute-start(f32[2,96,128]{2,1,0:T(8,128)S(1)} %shard_map.94.refs_0_), channel_id=1, source_target_pairs={{0,8},{8,16},{16,24},{24,0},{1,9},{9,17},{17,25},{25,1},{2,10},{10... | collective-permute-start | bytes 294920 | tf_op jit(solution)/shard_map/ppermute | solution.py:312
  48.9 1.1 %collective-permute-start.20 = (f32[2,96,128]{2,1,0:T(8,128)S(1)}, f32[2,96,128]{2,1,0:T(8,128)S(1)}, u32[]{:S(2)}, u32[]{:S(2)}) collective-permute-start(f32[2,96,128]{2,1,0:T(8,128)S(1)} %shard_map.94.refs_0_), channel_id=1, source_target_pairs={{0,16},{8,24},{16,0},{24,8},{1,17},{9,25},{17,1},{25,9},{2,18},{10... | collective-permute-start | bytes 294920 | tf_op jit(solution)/shard_map/ppermute | solution.py:312
  50.0 2.8 %collective-permute-start.22 = (f32[2,96,128]{2,1,0:T(8,128)S(1)}, f32[2,96,128]{2,1,0:T(8,128)S(1)}, u32[]{:S(2)}, u32[]{:S(2)}) collective-permute-start(f32[2,96,128]{2,1,0:T(8,128)S(1)} %shard_map.94.refs_0_), channel_id=1, source_target_pairs={{0,24},{8,0},{16,8},{24,16},{1,25},{9,1},{17,9},{25,17},{2,26},{10... | collective-permute-start | bytes 294920 | tf_op jit(solution)/shard_map/ppermute | solution.py:312
  52.9 0.5 collective-permute-start.19
  53.4 0.9 %collective-permute-done.20.refs_4_ = f32[2,96,128]{2,1,0:T(8,128)S(1)} collective-permute-done((f32[2,96,128]{2,1,0:T(8,128)S(1)}, f32[2,96,128]{2,1,0:T(8,128)S(1)}, u32[]{:S(2)}, u32[]{:S(2)}) %collective-permute-start.20) | collective-permute-done | bytes 98336 | tf_op jit(solution)/shard_map/ppermute | solution.py:312
  54.3 1.8 %collective-permute-done.22.refs_6_ = f32[2,96,128]{2,1,0:T(8,128)S(1)} collective-permute-done((f32[2,96,128]{2,1,0:T(8,128)S(1)}, f32[2,96,128]{2,1,0:T(8,128)S(1)}, u32[]{:S(2)}, u32[]{:S(2)}) %collective-permute-start.22) | collective-permute-done | bytes 98336 | tf_op jit(solution)/shard_map/ppermute | solution.py:312
  56.1 0.1 pad_add_fusion.rank_ref
  56.2 1.2 %collective-permute-done.23.refs_7_ = f32[2,96,128]{2,1,0:T(8,128)S(1)} collective-permute-done((f32[2,96,128]{2,1,0:T(8,128)S(1)}, f32[2,96,128]{2,1,0:T(8,128)S(1)}, u32[]{:S(2)}, u32[]{:S(2)}) %collective-permute-start.23) | collective-permute-done | bytes 98336 | tf_op jit(solution)/shard_map/ppermute | solution.py:312
  57.4 2.7 %shard_map.95 = f32[4,768,54]{2,1,0:T(8,128)} custom-call(s32[48]{0:T(128)S(1)} %pad_add_fusion.rank_ref, bf16[2,768,768]{2,1,0:T(8,128)(2,1)S(1)} %shard_map.91.q_ref, f32[2,96,128]{2,1,0:T(8,128)S(1)} %shard_map.94.refs_0_, f32[2,96,128]{2,1,0:T(8,128)S(1)} %collective-permute-done.17.refs_1_, f32[2,96,128]{2,1,0:T(8,128)S(1)} %collective-permute-done.18.refs_2_, ...), custom_call_target="tpu_custom_call" | custom-call | tf_op jit(solution)/shard_map/pallas_call | solution.py:23
  (26 shorter events, 0.1 us)
Async XLA Ops:
  0.6 11.5 %collective-permute-start.2 = (f32[16,12,8,128]{3,2,1,0:T(8,128)}, f32[16,12,8,128]{3,2,1,0:T(8,128)S(1)}, u32[]{:S(2)}, u32[]{:S(2)}) collective-permute-start(f32[16,12,8,128]{3,2,1,0:T(8,128)} %f_ref.3), channel_id=1, source_target_pairs={{0,4},{4,0},{1,5},{5,1},{2,6},{6,2},{3,7},{7,3},{8,12},{12,8},{9,1... | collective-permute-start | bytes 2359304 | tf_op jit(solution)/shard_map/ppermute | solution.py:346
  1.2 1.1 %copy-start = (f32[16,12,8,128]{3,2,1,0:T(8,128)S(1)}, f32[16,12,8,128]{3,2,1,0:T(8,128)}, u32[]{:S(2)}) copy-start(f32[16,12,8,128]{3,2,1,0:T(8,128)} %f_ref.3) | copy-start | bytes 2359300
  2.3 20.6 %copy-start.4 = (f32[8,64]{1,0:T(8,128)S(1)}, f32[8,64]{1,0:T(8,128)}, u32[]{:S(2)}) copy-start(f32[8,64]{1,0:T(8,128)} %refs_0_) | copy-start | bytes 6148
  2.3 23.0 %copy-start.1 = (f32[128,54]{0,1:T(8,128)S(1)}, f32[128,54]{0,1:T(8,128)}, u32[]{:S(2)}) copy-start(f32[128,54]{0,1:T(8,128)} %param.13) | copy-start | bytes 82948
  2.3 23.3 %copy-start.2 = (f32[48,96]{1,0:T(8,128)S(1)}, f32[48,96]{1,0:T(8,128)}, u32[]{:S(2)}) copy-start(f32[48,96]{1,0:T(8,128)} %xf_ref) | copy-start | bytes 55300
  2.4 9.7 %collective-permute-start = (f32[16,4,8,128]{3,2,1,0:T(8,128)S(1)}, f32[16,4,8,128]{3,2,1,0:T(8,128)S(1)}, u32[]{:S(2)}, u32[]{:S(2)}) collective-permute-start(f32[16,4,8,128]{3,2,1,0:T(8,128)S(1)} %get-tuple-element.40), channel_id=1, source_target_pairs={{0,8},{16,24},{8,0},{24,16},{1,9},{17,25},{9,1},{25,17},{2,10},{18... | collective-permute-start | bytes 786440 | tf_op jit(solution)/shard_map/ppermute | solution.py:339
  4.9 7.2 %collective-permute-start.1 = (f32[16,4,8,128]{3,2,1,0:T(8,128)S(1)}, f32[16,4,8,128]{3,2,1,0:T(8,128)S(1)}, u32[]{:S(2)}, u32[]{:S(2)}) collective-permute-start(f32[16,4,8,128]{3,2,1,0:T(8,128)S(1)} %get-tuple-element.41), channel_id=1, source_target_pairs={{8,16},{16,8},{9,17},{17,9},{10,18},{18,10},{11,19},{19,11},{12,20... | collective-permute-start | bytes 786440 | tf_op jit(solution)/shard_map/ppermute | solution.py:339
  7.4 4.3 %collective-permute-start.3 = (f32[12,8,128]{2,1,0:T(8,128)S(1)}, f32[12,8,128]{2,1,0:T(8,128)S(1)}, u32[]{:S(2)}, u32[]{:S(2)}) collective-permute-start(f32[12,8,128]{2,1,0:T(8,128)S(1)} %get-tuple-element.42), channel_id=1, source_target_pairs={{0,1},{2,3},{1,0},{3,2},{4,5},{6,7},{5,4},{7,6},{8,9},{10,11},{9,8... | collective-permute-start | bytes 147464 | tf_op jit(solution)/shard_map/ppermute | solution.py:339
  9.0 2.7 %collective-permute-start.4 = (f32[12,8,128]{2,1,0:T(8,128)S(1)}, f32[12,8,128]{2,1,0:T(8,128)S(1)}, u32[]{:S(2)}, u32[]{:S(2)}) collective-permute-start(f32[12,8,128]{2,1,0:T(8,128)S(1)} %get-tuple-element.42), channel_id=1, source_target_pairs={{1,2},{2,1},{5,6},{6,5},{9,10},{10,9},{13,14},{14,13},{17,18},{18,... | collective-permute-start | bytes 147464 | tf_op jit(solution)/shard_map/ppermute | solution.py:339
  9.7 0.7 %copy-start.3 = (f32[16,16]{1,0:T(8,128)S(1)}, f32[16,16]{1,0:T(8,128)}, u32[]{:S(2)}) copy-start(f32[16,16]{1,0:T(8,128)} %kin_ref.1) | copy-start | bytes 3076
  10.4 0.7 %copy-start.5 = (f32[3,16]{1,0:T(4,128)S(1)}, f32[3,16]{1,0:T(4,128)}, u32[]{:S(2)}) copy-start(f32[3,16]{1,0:T(4,128)} %speed_ref.1) | copy-start | bytes 580
  14.0 15.4 %collective-permute-start.9 = (f32[16,12,8,128]{3,2,1,0:T(8,128)S(1)}, f32[16,12,8,128]{3,2,1,0:T(8,128)S(1)}, u32[]{:S(2)}, u32[]{:S(2)}) collective-permute-start(f32[16,12,8,128]{3,2,1,0:T(8,128)S(1)} %get-tuple-element.51.s_ref), channel_id=1, source_target_pairs={{0,4},{4,0},{1,5},{5,1},{2,6},{6,2},{3,7},{7,3},{8,12},{12,8},{9,1... | collective-permute-start | bytes 2359304 | tf_op jit(solution)/shard_map/ppermute | solution.py:346
  14.0 15.3 %collective-permute-start.5 = (f32[16,4,8,128]{3,2,1,0:T(8,128)S(1)}, f32[16,4,8,128]{3,2,1,0:T(8,128)S(1)}, u32[]{:S(2)}, u32[]{:S(2)}) collective-permute-start(f32[16,4,8,128]{3,2,1,0:T(8,128)S(1)} %get-tuple-element.52), channel_id=1, source_target_pairs={{0,8},{16,24},{8,0},{24,16},{1,9},{17,25},{9,1},{25,17},{2,10},{18... | collective-permute-start | bytes 786440 | tf_op jit(solution)/shard_map/ppermute | solution.py:339
  22.2 7.2 %collective-permute-start.6 = (f32[16,4,8,128]{3,2,1,0:T(8,128)S(1)}, f32[16,4,8,128]{3,2,1,0:T(8,128)S(1)}, u32[]{:S(2)}, u32[]{:S(2)}) collective-permute-start(f32[16,4,8,128]{3,2,1,0:T(8,128)S(1)} %get-tuple-element.53), channel_id=1, source_target_pairs={{8,16},{16,8},{9,17},{17,9},{10,18},{18,10},{11,19},{19,11},{12,20... | collective-permute-start | bytes 786440 | tf_op jit(solution)/shard_map/ppermute | solution.py:339
  22.9 1.8 %collective-permute-start.10 = (f32[8,64]{1,0:T(8,128)S(1)}, f32[8,64]{1,0:T(8,128)S(1)}, u32[]{:S(2)}, u32[]{:S(2)}) collective-permute-start(f32[8,64]{1,0:T(8,128)S(1)} %copy-done.4), channel_id=1, source_target_pairs={{0,4},{4,0},{1,5},{5,1},{2,6},{6,2},{3,7},{7,3},{8,12},{12,8},{9,1... | collective-permute-start | bytes 6152 | tf_op jit(solution)/shard_map/ppermute | solution.py:312
  23.1 4.1 %collective-permute-start.7 = (f32[12,8,128]{2,1,0:T(8,128)S(1)}, f32[12,8,128]{2,1,0:T(8,128)S(1)}, u32[]{:S(2)}, u32[]{:S(2)}) collective-permute-start(f32[12,8,128]{2,1,0:T(8,128)S(1)} %get-tuple-element.54), channel_id=1, source_target_pairs={{0,1},{2,3},{1,0},{3,2},{4,5},{6,7},{5,4},{7,6},{8,9},{10,11},{9,8... | collective-permute-start | bytes 147464 | tf_op jit(solution)/shard_map/ppermute | solution.py:339
  24.7 2.5 %collective-permute-start.8 = (f32[12,8,128]{2,1,0:T(8,128)S(1)}, f32[12,8,128]{2,1,0:T(8,128)S(1)}, u32[]{:S(2)}, u32[]{:S(2)}) collective-permute-start(f32[12,8,128]{2,1,0:T(8,128)S(1)} %get-tuple-element.54), channel_id=1, source_target_pairs={{1,2},{2,1},{5,6},{6,5},{9,10},{10,9},{13,14},{14,13},{17,18},{18,... | collective-permute-start | bytes 147464 | tf_op jit(solution)/shard_map/ppermute | solution.py:339
  25.7 13.2 %copy-start.6 = (s32[12]{0:T(128)S(1)}, s32[12]{0:T(128)}, u32[]{:S(2)}) copy-start(s32[12]{0:T(128)} %param.10) | copy-start | bytes 148
  32.0 13.3 %collective-permute-start.14 = (f32[2,96,128]{2,1,0:T(8,128)}, f32[2,96,128]{2,1,0:T(8,128)S(1)}, u32[]{:S(2)}, u32[]{:S(2)}) collective-permute-start(f32[2,96,128]{2,1,0:T(8,128)} %get-tuple-element.73), channel_id=1, source_target_pairs={{0,1},{1,2},{2,3},{3,0},{4,5},{5,6},{6,7},{7,4},{8,9},{9,10},{10,1... | collective-permute-start | bytes 294920 | tf_op jit(solution)/shard_map/ppermute | solution.py:312
  34.5 10.9 %collective-permute-start.15 = (f32[2,96,128]{2,1,0:T(8,128)}, f32[2,96,128]{2,1,0:T(8,128)S(1)}, u32[]{:S(2)}, u32[]{:S(2)}) collective-permute-start(f32[2,96,128]{2,1,0:T(8,128)} %get-tuple-element.74), channel_id=1, source_target_pairs={{0,2},{1,3},{2,0},{3,1},{4,6},{5,7},{6,4},{7,5},{8,10},{9,11},{10,... | collective-permute-start | bytes 294920 | tf_op jit(solution)/shard_map/ppermute | solution.py:312
  36.2 9.2 %collective-permute-start.16 = (f32[2,96,128]{2,1,0:T(8,128)}, f32[2,96,128]{2,1,0:T(8,128)S(1)}, u32[]{:S(2)}, u32[]{:S(2)}) collective-permute-start(f32[2,96,128]{2,1,0:T(8,128)} %get-tuple-element.75), channel_id=1, source_target_pairs={{0,3},{1,0},{2,1},{3,2},{4,7},{5,4},{6,5},{7,6},{8,11},{9,8},{10,9... | collective-permute-start | bytes 294920 | tf_op jit(solution)/shard_map/ppermute | solution.py:312
  38.8 6.4 %collective-permute-start.11 = (s32[12]{0:T(128)S(1)}, s32[12]{0:T(128)S(1)}, u32[]{:S(2)}, u32[]{:S(2)}) collective-permute-start(s32[12]{0:T(128)S(1)} %copy-done.6), channel_id=1, source_target_pairs={{0,8},{4,28},{8,16},{12,4},{16,24},{20,12},{24,0},{28,20},{1,9},{5... | collective-permute-start | bytes 152 | tf_op jit(solution)/shard_map/ppermute | solution.py:328
  43.4 12.7 %collective-permute-start.13 = (s32[12]{0:T(128)S(1)}, s32[12]{0:T(128)S(1)}, u32[]{:S(2)}, u32[]{:S(2)}) collective-permute-start(s32[12]{0:T(128)S(1)} %copy-done.6), channel_id=1, source_target_pairs={{0,16},{8,24},{16,0},{24,8},{1,17},{9,25},{17,1},{25,9},{2,18},{10... | collective-permute-start | bytes 152 | tf_op jit(solution)/shard_map/ppermute | solution.py:312
  45.3 7.6 %collective-permute-start.12 = (s32[12]{0:T(128)S(1)}, s32[12]{0:T(128)S(1)}, u32[]{:S(2)}, u32[]{:S(2)}) collective-permute-start(s32[12]{0:T(128)S(1)} %collective-permute-done.11), channel_id=1, source_target_pairs={{0,4},{4,0},{1,5},{5,1},{2,6},{6,2},{3,7},{7,3},{8,12},{12,8},{9,1... | collective-permute-start | bytes 152 | tf_op jit(solution)/shard_map/ppermute | solution.py:330
  45.4 7.5 %collective-permute-start.18 = (f32[2,96,128]{2,1,0:T(8,128)S(1)}, f32[2,96,128]{2,1,0:T(8,128)S(1)}, u32[]{:S(2)}, u32[]{:S(2)}) collective-permute-start(f32[2,96,128]{2,1,0:T(8,128)S(1)} %shard_map.94.refs_0_), channel_id=1, source_target_pairs={{0,8},{8,16},{16,24},{24,0},{1,9},{9,17},{17,25},{25,1},{2,10},{10... | collective-permute-start | bytes 294920 | tf_op jit(solution)/shard_map/ppermute | solution.py:312
  48.9 5.3 %collective-permute-start.20 = (f32[2,96,128]{2,1,0:T(8,128)S(1)}, f32[2,96,128]{2,1,0:T(8,128)S(1)}, u32[]{:S(2)}, u32[]{:S(2)}) collective-permute-start(f32[2,96,128]{2,1,0:T(8,128)S(1)} %shard_map.94.refs_0_), channel_id=1, source_target_pairs={{0,16},{8,24},{16,0},{24,8},{1,17},{9,25},{17,1},{25,9},{2,18},{10... | collective-permute-start | bytes 294920 | tf_op jit(solution)/shard_map/ppermute | solution.py:312
  50.0 6.1 %collective-permute-start.22 = (f32[2,96,128]{2,1,0:T(8,128)S(1)}, f32[2,96,128]{2,1,0:T(8,128)S(1)}, u32[]{:S(2)}, u32[]{:S(2)}) collective-permute-start(f32[2,96,128]{2,1,0:T(8,128)S(1)} %shard_map.94.refs_0_), channel_id=1, source_target_pairs={{0,24},{8,0},{16,8},{24,16},{1,25},{9,1},{17,9},{25,17},{2,26},{10... | collective-permute-start | bytes 294920 | tf_op jit(solution)/shard_map/ppermute | solution.py:312
  52.9 3.3 %collective-permute-start.17 = (f32[2,96,128]{2,1,0:T(8,128)S(1)}, f32[2,96,128]{2,1,0:T(8,128)S(1)}, u32[]{:S(2)}, u32[]{:S(2)}) collective-permute-start(f32[2,96,128]{2,1,0:T(8,128)S(1)} %shard_map.94.refs_0_), channel_id=1, source_target_pairs={{0,4},{4,0},{1,5},{5,1},{2,6},{6,2},{3,7},{7,3},{8,12},{12,8},{9,1... | collective-permute-start | bytes 294920 | tf_op jit(solution)/shard_map/ppermute | solution.py:312
  52.9 3.3 %collective-permute-start.19 = (f32[2,96,128]{2,1,0:T(8,128)S(1)}, f32[2,96,128]{2,1,0:T(8,128)S(1)}, u32[]{:S(2)}, u32[]{:S(2)}) collective-permute-start(f32[2,96,128]{2,1,0:T(8,128)S(1)} %collective-permute-done.18.refs_2_), channel_id=1, source_target_pairs={{0,4},{4,0},{1,5},{5,1},{2,6},{6,2},{3,7},{7,3},{8,12},{12,8},{9,1... | collective-permute-start | bytes 294920 | tf_op jit(solution)/shard_map/ppermute | solution.py:312
  54.2 1.9 %collective-permute-start.21 = (f32[2,96,128]{2,1,0:T(8,128)S(1)}, f32[2,96,128]{2,1,0:T(8,128)S(1)}, u32[]{:S(2)}, u32[]{:S(2)}) collective-permute-start(f32[2,96,128]{2,1,0:T(8,128)S(1)} %collective-permute-done.20.refs_4_), channel_id=1, source_target_pairs={{0,4},{4,0},{1,5},{5,1},{2,6},{6,2},{3,7},{7,3},{8,12},{12,8},{9,1... | collective-permute-start | bytes 294920 | tf_op jit(solution)/shard_map/ppermute | solution.py:312
  56.1 1.3 %collective-permute-start.23 = (f32[2,96,128]{2,1,0:T(8,128)S(1)}, f32[2,96,128]{2,1,0:T(8,128)S(1)}, u32[]{:S(2)}, u32[]{:S(2)}) collective-permute-start(f32[2,96,128]{2,1,0:T(8,128)S(1)} %collective-permute-done.22.refs_6_), channel_id=1, source_target_pairs={{0,4},{4,0},{1,5},{5,1},{2,6},{6,2},{3,7},{7,3},{8,12},{12,8},{9,1... | collective-permute-start | bytes 294920 | tf_op jit(solution)/shard_map/ppermute | solution.py:312

commit v7 on v6

--- a/solution.py
+++ b/solution.py
@@ -68,7 +68,7 @@
     rim_ref[...] = jnp.where(group == v + width // 2 // REACH, first, rim)
 
 
-def pack_kernel(f_ref, rim_ref, same_ref, sems):
+def pack_kernel(f_ref, zf_ref, rim_ref, same_ref, pad_ref, sems):
     count = f_ref.shape[0] // sems.shape[0]
     copies = []
     for i in range(sems.shape[0]):
@@ -76,10 +76,19 @@
         copies.append(pltpu.make_async_copy(f_ref.at[part], same_ref.at[part], sems.at[i]))
         copies[-1].start()
     rim_ref[...] = jnp.zeros_like(rim_ref)
+    nx = rim_ref.shape[0] - 1
+    depth = zf_ref.shape[1]
+    row = iota((2 * REACH, depth), 0)
+    wanted = jnp.where(row < REACH, row + depth - REACH, row - REACH)
+    pick = (iota((2 * REACH, depth), 1) == wanted).astype(F32)
+    pad_ref[...] = jnp.zeros_like(pad_ref)
+    pad_ref[:, 0 : zf_ref.shape[0]] = exact(pick, zf_ref[...], ((1,), (1,)))
+    rim_ref[nx] = pad_ref[...]
+    planes_ref = rim_ref.at[pl.ds(0, nx)]
     for i, copy in enumerate(copies):
         copy.wait()
         for v in range(i * count, (i + 1) * count):
-            pack_rim(v, same_ref[v], rim_ref)
+            pack_rim(v, same_ref[v], planes_ref)
 
 
 def iota(shape, dim):
@@ -90,7 +99,7 @@
     return lax.rem(x, jnp.int32(size))
 
 
-def weight_kernel(kin_ref, speed_ref, w_ref, dz_ref, shift_ref, scale_ref):
+def weight_kernel(kin_ref, speed_ref, w_ref, dz_ref, shift_ref, scale_ref, pair_ref):
     nvars = kin_ref.shape[0]
     rows, columns = w_ref.shape[0] // 2, w_ref.shape[1]
     ny = rows // nvars
@@ -135,19 +144,49 @@
     for v in range(nvars):
         scale_ref[v, 0] = jnp.broadcast_to(TIME_STEP * speed_ref[0:1, v : v + 1], tile)
         scale_ref[v, 1] = jnp.broadcast_to(TIME_STEP / SCALE * speed_ref[2:3, v : v + 1], tile)
-
-
-def project_kernel(zf_ref, zf_out_ref, wide_ref):
+    even = iota(tile, 1) < HALF
+    for p in range(nvars // 2):
+        for i in range(2):
+            pair_ref[p, i] = 0.5 * jnp.where(even, scale_ref[2 * p, i], scale_ref[2 * p + 1, i])
+
+
+def lay_out(wide_ref, out_ref):
+    depth = wide_ref.shape[0]
+    for start, table in ((0, wide_ref[...]), (depth, pltpu.roll(wide_ref[...], HALF, 1))):
+        high, low = split(table)
+        out_ref[start : start + depth, 0 : 2 * HALF] = high
+        out_ref[start : start + depth, 2 * HALF :] = low
+
+
+def project_kernel(zf_ref, out_ref, wide_ref):
     depth, rank = zf_ref.shape[1], zf_ref.shape[0]
     identity = (iota((depth, depth), 0) == iota((depth, depth), 1)).astype(F32)
     wide_ref[...] = jnp.zeros_like(wide_ref)
     wide_ref[:, 0:rank] = exact(identity, zf_ref[...], ((1,), (1,)))
-    high, low = split(wide_ref[...])
-    zf_out_ref[0:depth, 0 : 2 * HALF] = high
-    zf_out_ref[0:depth, 2 * HALF :] = low
-    high, low = split(pltpu.roll(wide_ref[...], HALF, 1))
-    zf_out_ref[depth:, 0 : 2 * HALF] = high
-    zf_out_ref[depth:, 2 * HALF :] = low
+    lay_out(wide_ref, out_ref)
+
+
+def adjoint_kernel(zf_ref, z1_ref, z2_ref, dz_ref, out_ref, wide_ref):
+    depth, rank = zf_ref.shape[1], zf_ref.shape[0]
+    last = z1_ref.shape[0] - 1
+    wide_ref[...] = jnp.zeros_like(wide_ref)
+    wide_ref[:, 0:rank] = exact(dz_ref[0:depth].astype(F32), zf_ref[...], ((1,), (1,)))
+    upper = iota(z1_ref.shape[1:], 0) // REACH
+    rows = jnp.where(upper == odd("gz"), z2_ref[last], z1_ref[last])
+    source, place = iota((depth, 2 * REACH), 0), iota((depth, 2 * REACH), 1)
+    below = place < REACH
+    offset = jnp.where(below, source + REACH - place, depth + place - REACH - source)
+    reach = jnp.zeros((depth, 2 * REACH), F32)
+    for k in range(1, REACH + 1):
+        reach = jnp.where(offset == k, WHOLE[k - 1], reach)
+    wide_ref[...] = wide_ref[...] + exact(jnp.where(below, reach, -reach), rows)
+    lay_out(wide_ref, out_ref)
+
+
+def projected(pair, zf_ref):
+    high, low = split(pair)
+    wide = dot(high, zf_ref[...])
+    return wide[:, : 2 * HALF] + wide[:, 2 * HALF :] + dot(low, zf_ref[:, : 2 * HALF])
 
 
 def mix_planes(q_ref, beside_ref, w_ref, rate_ref):
@@ -173,74 +212,145 @@
 def join_rims(first_ref, second_ref, shift_ref, rim_ref):
     nx, ny, nz = rim_ref.shape
     upper = lax.shift_right_logical(iota(rim_ref.shape, 2) * 2 // nz, 0)
-    rim = jnp.where(upper == odd("gz"), second_ref[...], first_ref[...]).reshape(nx * ny, nz)
+    rim = jnp.where(upper == odd("gz"), second_ref[0:nx], first_ref[0:nx]).reshape(nx * ny, nz)
     high, low = split(rim)
     rim_ref[...] = (dot(high, shift_ref[...]) + dot(low, shift_ref[...])).reshape(rim_ref.shape)
 
 
-def step_of(v, q_ref, first_ref, second_ref, dz_ref, rate_ref, rim_ref, scale_ref):
-    _, nx, ny, nz = q_ref.shape
-    q = q_ref[v]
-    even = jnp.full((REACH, ny, nz), odd("gx")) == 0
-    low_rim = jnp.where(even, second_ref[v], first_ref[v])
-    high_rim = jnp.where(even, first_ref[v], second_ref[v])
-    tall = jnp.concatenate([low_rim, q, high_rim], axis=0)
-    gx = None
-    for k in range(1, REACH + 1):
-        part = COEFFS[k - 1] * (tall[REACH + k : REACH + k + nx] - tall[REACH - k : REACH - k + nx])
-        gx = part if gx is None else gx + part
+def z_slope(v, q, dz_ref, rim_ref):
+    nx, ny, nz = q.shape
     high, low = split(q.reshape(nx * ny, nz))
-    gz = dot(jnp.concatenate([high, low], axis=1), dz_ref[...]).reshape(nx, ny, nz)
+    slope = dot(jnp.concatenate([high, low], axis=1), dz_ref[...]).reshape(nx, ny, nz)
     lane = lax.broadcasted_iota(jnp.int32, q.shape, 2)
     rim = rim_ref[...]
     first = pltpu.roll(rim, lax.rem(nz - REACH * v, nz), 2)
     last = pltpu.roll(rim, nz // 2 - REACH - REACH * v, 2)
-    gz = gz + jnp.where(lane < REACH, first, jnp.where(lane >= nz - REACH, last, 0.0))
-    return rate_ref[v] - scale_ref[v, 0] * gx - scale_ref[v, 1] * gz
+    return slope + jnp.where(lane < REACH, first, jnp.where(lane >= nz - REACH, last, 0.0))
+
+
+def x_slope(low_rim, q, high_rim):
+    nx = q.shape[0]
+    tall = jnp.concatenate([low_rim, q, high_rim], axis=0)
+    slope = None
+    for k in range(1, REACH + 1):
+        part = COEFFS[k - 1] * (tall[REACH + k : REACH + k + nx] - tall[REACH - k : REACH - k + nx])
+        slope = part if slope is None else slope + part
+    return slope
+
+
+def rim_slopes(low_rim, high_rim):
+    first, last = [], []
+    for p in range(REACH):
+        under = over = None
+        for k in range(p + 1, REACH + 1):
+            term = COEFFS[k - 1] * low_rim[REACH + p - k]
+            under = term if under is None else under + term
+        for k in range(REACH - p, REACH + 1):
+            term = COEFFS[k - 1] * high_rim[p + k - REACH]
+            over = term if over is None else over + term
+        first.append(-under[None])
+        last.append(over[None])
+    return jnp.concatenate(first, axis=0), jnp.concatenate(last, axis=0)
+
+
+def by_side(first, second):
+    even = jnp.full(first.shape, odd("gx")) == 0
+    return jnp.where(even, second, first), jnp.where(even, first, second)
 
 
 def section_kernel(
-    f_ref, x1_ref, x2_ref, beside_ref, z1_ref, z2_ref, w_ref, dz_ref, shift_ref, scale_ref,
-    s_ref, first_ref, second_ref, out_rim_ref, rate_ref, rim_ref,
+    f_ref, x1_ref, x2_ref, beside_ref, z1_ref, z2_ref, w_ref, dz_ref, shift_ref, scale_ref, zf_ref,
+    s_ref, first_ref, second_ref, out_rim_ref, u1_ref, u2_ref, rate_ref, rim_ref,
 ):
+    nvars, nx, ny, nz = f_ref.shape
     mix_planes(f_ref, beside_ref, w_ref, rate_ref)
     join_rims(z1_ref, z2_ref, shift_ref, rim_ref)
     out_rim_ref[...] = jnp.zeros_like(out_rim_ref)
 
-    def step(v, carry):
-        s = f_ref[v] + step_of(v, f_ref, x1_ref, x2_ref, dz_ref, rate_ref, rim_ref, scale_ref)
-        s_ref[v] = s
-        low, high = s[:REACH], s[s.shape[0] - REACH :]
-        even = jnp.full(low.shape, odd("gx")) == 0
-        first_ref[v] = jnp.where(even, high, low)
-        second_ref[v] = jnp.where(even, low, high)
-        pack_rim(v, s, out_rim_ref)
+    def step(p, carry):
+        both = []
+        for v in (2 * p, 2 * p + 1):
+            f = f_ref[v]
+            low_rim, high_rim = by_side(x1_ref[v], x2_ref[v])
+            slope = scale_ref[v, 0] * x_slope(low_rim, f, high_rim)
+            s = f + rate_ref[v] - slope - scale_ref[v, 1] * z_slope(v, f, dz_ref, rim_ref)
+            s_ref[v] = s
+            second, first = by_side(s[nx - REACH :], s[:REACH])
+            first_ref[v] = first
+            second_ref[v] = second
+            pack_rim(v, s, out_rim_ref)
+            both.append(jnp.concatenate([first, second], axis=0).reshape(2 * REACH * ny, nz))
+        u = projected(jnp.concatenate(both, axis=1), zf_ref)
+        u1_ref[p] = u[: REACH * ny].reshape(REACH, ny, 2 * HALF)
+        u2_ref[p] = u[REACH * ny :].reshape(REACH, ny, 2 * HALF)
         return carry
 
-    lax.fori_loop(0, f_ref.shape[0], step, 0, unroll=4)
-
-
-def next_kernel(
-    f_ref, s_ref, x1_ref, x2_ref, beside_ref, z1_ref, z2_ref, w_ref, dz_ref, shift_ref, scale_ref, zf_ref,
-    next_ref, *refs,
+    lax.fori_loop(0, nvars // 2, step, 0, unroll=2)
+
+
+def chunk_pairs(chunk_refs):
+    count, pairs = len(chunk_refs), chunk_refs[0].shape[0]
+    for k in range(count):
+        start = lax.rem(lax.axis_index("gz") + k, jnp.int32(count)) * pairs
+        for j in range(pairs):
+            yield k, j, start + j
+
+
+def near_kernel(
+    f_ref, s_ref, beside_ref, w_ref, scale_ref, pair_ref, zf_ref, adjoint_ref,
+    hold_ref, *refs,
 ):
     _, nx, ny, nz = f_ref.shape
-    chunk_refs, (rate_ref, rim_ref) = refs[:-2], refs[-2:]
+    chunk_refs, rate_ref = refs[:-1], refs[-1]
     mix_planes(s_ref, beside_ref, w_ref, rate_ref)
+    nothing = jnp.zeros((REACH, ny, nz), F32)
+    for k, j, p in chunk_pairs(chunk_refs):
+        holds, sections = [], []
+        for v in (2 * p, 2 * p + 1):
+            s = s_ref[v]
+            rate = rate_ref[v] - scale_ref[v, 0] * x_slope(nothing, s, nothing)
+            hold = 0.5 * (f_ref[v] + s + rate)
+            hold_ref[v] = hold
+            holds.append(hold.reshape(nx * ny, nz))
+            sections.append(s.reshape(nx * ny, nz))
+        slope = projected(jnp.concatenate(sections, axis=1), adjoint_ref).reshape(nx, ny, 2 * HALF)
+        total = projected(jnp.concatenate(holds, axis=1), zf_ref).reshape(nx, ny, 2 * HALF)
+        chunk_refs[k][j] = (total - pair_ref[p, 1] * slope).reshape(nx * ny, 2 * HALF)
+
+
+def far_kernel(u1_ref, u2_ref, pair_ref, *refs):
+    count = len(refs) // 2
+    edge = REACH * u1_ref.shape[2]
+    rows = refs[0].shape[1]
+    for k, j, p in chunk_pairs(refs[count:]):
+        old_ref, new_ref = refs[k], refs[count + k]
+        low_rim, high_rim = by_side(u1_ref[p], u2_ref[p])
+        first, last = rim_slopes(low_rim, high_rim)
+        scale = pair_ref[p, 0]
+        new_ref[j, :edge] = old_ref[j, :edge] - (scale * first).reshape(edge, 2 * HALF)
+        new_ref[j, edge : rows - edge] = old_ref[j, edge : rows - edge]
+        new_ref[j, rows - edge :] = old_ref[j, rows - edge :] - (scale * last).reshape(edge, 2 * HALF)
+
+
+def finish_kernel(
+    hold_ref, s_ref, x1_ref, x2_ref, z1_ref, z2_ref, dz_ref, shift_ref, scale_ref, out_ref, next_ref, rim_ref, sems
+):
+    nvars, nx, _, _ = hold_ref.shape
     join_rims(z1_ref, z2_ref, shift_ref, rim_ref)
-    count, pairs = len(chunk_refs), chunk_refs[0].shape[0]
-    for k, chunk_ref in enumerate(chunk_refs):
-        start = lax.rem(lax.axis_index("gz") + k, jnp.int32(count)) * (2 * pairs)
-        for j in range(pairs):
-            both = []
-            for v in (start + 2 * j, start + 2 * j + 1):
-                rate = step_of(v, s_ref, x1_ref, x2_ref, dz_ref, rate_ref, rim_ref, scale_ref)
-                new = 0.5 * (f_ref[v] + s_ref[v] + rate)
-                next_ref[v] = new
-                both.append(new.reshape(nx * ny, nz))
-            high, low = split(jnp.concatenate(both, axis=1))
-            wide = dot(high, zf_ref[...])
-            chunk_ref[j] = wide[:, : 2 * HALF] + wide[:, 2 * HALF :] + dot(low, zf_ref[:, : 2 * HALF])
+    count = nvars // sems.shape[0]
+    copies = []
+    for i in range(sems.shape[0]):
+        for v in range(i * count, (i + 1) * count):
+            slope = scale_ref[v, 1] * z_slope(v, s_ref[v], dz_ref, rim_ref)
+            first, last = rim_slopes(*by_side(x1_ref[v], x2_ref[v]))
+            next_ref[v] = hold_ref[v] - 0.5 * slope
+            next_ref[v, :REACH] -= 0.5 * scale_ref[v, 0] * first
+            next_ref[v, nx - REACH :] -= 0.5 * scale_ref[v, 0] * last
+        part = pl.ds(i * count, count)
+        copies.append(pltpu.make_async_copy(next_ref.at[part], out_ref.at[part], sems.at[i]))
+        copies[-1].start()
+    for copy in copies:
+        copy.wait()
 
 
 def sum_kernel(*refs):
@@ -248,12 +358,6 @@
     for ref in refs[1:-1]:
         total = total + ref[...]
     refs[-1][...] = total
-
-
-def store_kernel(in_ref, out_ref, sem):
-    copy = pltpu.make_async_copy(in_ref, out_ref, sem)
-    copy.start()
-    copy.wait()
 
 
 def factor_kernel(xf_ref, *refs):
@@ -332,11 +436,15 @@
     return [x, jnp.where(upper, theirs, mine), across, jnp.where(upper, mine, theirs)]
 
 
+def paired_once(x, axis, start):
+    links = [(i, i + 1) for i in range(start, lax.axis_size(axis) - 1, 2)]
+    return (lax.ppermute(x, axis, links + [(j, i) for i, j in links]),)
+
+
 def paired(first, second, axis):
-    out = []
+    out = ()
     for x, start in ((first, 0), (second, 1)):
-        links = [(i, i + 1) for i in range(start, lax.axis_size(axis) - 1, 2)]
-        out.append(lax.ppermute(x, axis, links + [(j, i) for i, j in links]))
+        out += paired_once(x, axis, start)
     return out
 
 
@@ -356,48 +464,72 @@
     gx, gy, gz = (lax.axis_size(axis) for axis in ("gx", "gy", "gz"))
     rim = (nvars, REACH, ny, nz)
     plane = (nx, ny, nz)
-    scratch = [pltpu.VMEM(fields.shape, F32), pltpu.VMEM(plane, F32)]
+    u_rim = (nvars // 2, REACH, ny, 2 * HALF)
+    table = ((2 * nz, 4 * HALF), BF16)
+    wide = pltpu.VMEM((nz, 2 * HALF), F32)
     pairs = nvars // 2 // gz
     chunk = (pairs, nx * ny, 2 * HALF)
-    barrier = lax.optimization_barrier
-
-    first, second = call(
-        rim_kernel,
-        [(rim, F32), (rim, F32)],
-        [HBM],
-        (fields,),
-        [pltpu.SemaphoreType.DMA((2,))],
-    )
-    x1, x2 = paired(first, second, "gx")
-    packed, same = call(
-        pack_kernel, [(plane, F32), (fields.shape, F32)], [HBM], (fields,), [pltpu.SemaphoreType.DMA((4,))]
-    )
-    z1, z2 = paired(packed, packed, "gz")
-    other = beside(fields, "gy")
-    weights, dz, rim_shift, scales = call(
-        weight_kernel,
-        [((2 * nvars * ny, 2 * nvars * ny), BF16), ((2 * nz, nz), BF16), ((nz, nz), BF16), ((nvars, 2, ny, nz), F32)],
-        [VMEM] * 2,
-        (kinetics, speeds),
-    )
-    section, first, second, packed = call(
-        section_kernel,
-        [(fields.shape, F32), (rim, F32), (rim, F32), (plane, F32)],
-        [VMEM] * 10,
-        (same, x1, x2, other, z1, z2, weights, dz, rim_shift, scales),
-        scratch,
-    )
     a_count, b_count = x_factor.shape[1] // gx, y_factor.shape[1] // gy
     rows, planes = a_count * b_count, gx * nx
     cells = planes * gy * ny
-    section, first, second, packed, z_factor, x_factor, y_factor = barrier(
-        (section, first, second, packed, z_factor, x_factor, y_factor)
+    barrier = lax.optimization_barrier
+    transposed = z_factor.T
+
+    first, second = call(
+        rim_kernel, [(rim, F32), (rim, F32)], [HBM], (fields,), [pltpu.SemaphoreType.DMA((2,))]
     )
     x1, x2 = paired(first, second, "gx")
+    packed, same = call(
+        pack_kernel,
+        [((nx + 1, ny, nz), F32), (fields.shape, F32)],
+        [HBM, VMEM],
+        (fields, transposed),
+        [pltpu.VMEM((2 * REACH, nz), F32), pltpu.SemaphoreType.DMA((4,))],
+    )
     z1, z2 = paired(packed, packed, "gz")
+    other = beside(fields, "gy")
+    weights, dz, rim_shift, scales, pair_scales = call(
+        weight_kernel,
+        [
+            ((2 * nvars * ny, 2 * nvars * ny), BF16),
+            ((2 * nz, nz), BF16),
+            ((nz, nz), BF16),
+            ((nvars, 2, ny, nz), F32),
+            ((nvars // 2, 2, ny, nz), F32),
+        ],
+        [VMEM] * 2,
+        (kinetics, speeds),
+    )
+    (zf,) = call(project_kernel, [table], [VMEM], (transposed,), [wide])
+    section, first, second, packed, u1, u2 = call(
+        section_kernel,
+        [(fields.shape, F32), (rim, F32), (rim, F32), (plane, F32), (u_rim, F32), (u_rim, F32)],
+        [VMEM] * 11,
+        (same, x1, x2, other, z1, z2, weights, dz, rim_shift, scales, zf),
+        [pltpu.VMEM(fields.shape, F32), pltpu.VMEM(plane, F32)],
+    )
+    section, first, second, packed, u1, u2, transposed, x_factor, y_factor = barrier(
+        (section, first, second, packed, u1, u2, transposed, x_factor, y_factor)
+    )
     other = beside(section, "gy")
+    u1, u2 = paired(u1, u2, "gx")
+    (x1,) = paired_once(first, "gx", 0)
+    (adjoint,) = call(adjoint_kernel, [table], [VMEM] * 4, (transposed, z1, z2, dz), [wide])
+    hold, *chunks = call(
+        near_kernel,
+        [(fields.shape, F32)] + [(chunk, F32)] * gz,
+        [VMEM] * 8,
+        (same, section, other, weights, scales, pair_scales, zf, adjoint),
+        [pltpu.VMEM(fields.shape, F32)],
+    )
+    chunks = call(
+        far_kernel, [(chunk, F32)] * gz, [VMEM] * (3 + gz), (u1, u2, pair_scales, *chunks)
+    )
+    chunks, block_rank, second, packed, hold = barrier((chunks, block_rank, second, packed, hold))
+    parts = [chunks[0]] + [shifted(chunks[k], "gz", k) for k in range(1, gz)]
+    ranks = jnp.concatenate(gathered_on_chip(block_rank), axis=0)
+    (x2,) = paired_once(second, "gx", 1)
     y_rows = gathered(y_factor, "gy")
-    (zf,) = call(project_kernel, [((2 * nz, 4 * HALF), BF16)], [VMEM], (z_factor.T,), [pltpu.VMEM((nz, 2 * HALF), F32)])
     (factor,) = call(
         factor_kernel,
         [((2, rows, cells), BF16)],
@@ -405,20 +537,17 @@
         (x_factor, *y_rows),
         [pltpu.VMEM((a_count, planes * ny), F32)],
     )
-    x1, x2, z1, z2, other, zf, factor = barrier((x1, x2, z1, z2, other, zf, factor))
-    new, *chunks = call(
-        next_kernel,
-        [(fields.shape, F32)] + [(chunk, F32)] * gz,
-        [VMEM] * 12,
-        (same, section, x1, x2, other, z1, z2, weights, dz, rim_shift, scales, zf),
-        scratch,
-    )
-    new, chunks, block_rank = barrier((new, chunks, block_rank))
-    parts = [chunks[0]] + [shifted(chunks[k], "gz", k) for k in range(1, gz)]
-    ranks = jnp.concatenate(gathered_on_chip(block_rank), axis=0)
-    (fields_next,) = call(store_kernel, [(fields.shape, F32)], [ANY], (new,), [pltpu.SemaphoreType.DMA], out_spec=HBM)
     (own,) = call(sum_kernel, [(chunk, F32)], [VMEM] * gz, parts)
     blocks = [gathered(block, "gy") for block in gathered(own, "gx")]
+    z1, z2 = paired(packed, packed, "gz")
+    (fields_next,) = call(
+        finish_kernel,
+        [(fields.shape, F32)],
+        [VMEM] * 9,
+        (hold, section, x1, x2, z1, z2, dz, rim_shift, scales),
+        [pltpu.VMEM(fields.shape, F32), pltpu.VMEM(plane, F32), pltpu.SemaphoreType.DMA((4,))],
+        out_spec=HBM,
+    )
     pieces = 4 if rows % 128 == 0 else 1
     (core,) = call(
         core_kernel,

time: 61 us -> 68.1 us (1.12)
  waiting for transfers between devices: 7.2 us -> 16.4 us
  starting transfers between devices: 37.8 us -> 35 us
  local copies, waits for them, and re-layouts: 2.52 us -> 3.27 us
    ppermute x8 -> x10, waiting for transfers between devices: 3.23 us -> 7.56 us  [paired_once(): return (lax.ppermute(x, axis, links + [(j, i) for i, j in links]),)]
    ppermute x12, waiting for transfers between devices: 3.96 us -> 7.83 us  [shifted(): return lax.ppermute(x, axis, [(i, (i + k) % count) for i in range(count)])]
    ppermute x1, starting transfers between devices: 4.52 us -> 1.43 us  [gathered_on_chip(): lax.ppermute(x, ('gx', 'gy'), [(2 * i + j, 2 * k + l) for (i, j), (k, l)...]
    ppermute x1, waiting for transfers between devices: 0.01 us -> 0.98 us  [gathered_on_chip(): lax.ppermute(x, ('gx', 'gy'), [(2 * i + j, 2 * k + l) for (i, j), (k, l)...]
    unnamed x14, local copies, waits for them, and re-layouts: 2.52 us -> 3.27 us
    pallas_call x10 -> x12, Pallas kernels: 11.7 us -> 12.1 us  [call(): pl.pallas_call(kernel, out_shape=tuple((jax.ShapeDtypeStruct(s, d) for s,...]
    ppermute x8 -> x10, starting transfers between devices: 16.6 us -> 16.3 us  [paired_once(): return (lax.ppermute(x, axis, links + [(j, i) for i, j in links]),)]
  transfers between devices with their start and end apart: 24 -> 26, of which waited for: 6 -> 4; matrix products, arithmetic and copies ran while one was open for 0% -> 0% of each run, Pallas kernels for 7% -> 10%
where the time goes in v7:
time: 68.1 us; the launch traced here: 67.7 us
  starting transfers between devices  35 us (51%)
  waiting for transfers between devices  16.4 us (24%)
  Pallas kernels  12.1 us (18%)
  local copies, waits for them, and re-layouts  3.27 us (5%)
  between operations  0.92 us (1%)
    ppermute x12, starting transfers between devices, shifted(): return lax.ppermute(x, axis, [(i, (i + k) % count) for i in range(count)])  16.6 us
    ppermute x10, starting transfers between devices, paired_once(): return (lax.ppermute(x, axis, links + [(j, i) for i, j in links]),)  16.3 us
    pallas_call x12, Pallas kernels, call(): pl.pallas_call(kernel, out_shape=tuple((jax.ShapeDtypeStruct(s, d) for s,...  12.1 us
    ppermute x12, waiting for transfers between devices, shifted(): return lax.ppermute(x, axis, [(i, (i + k) % count) for i in range(count)])  7.83 us
    ppermute x10, waiting for transfers between devices, paired_once(): return (lax.ppermute(x, axis, links + [(j, i) for i, j in links]),)  7.56 us
    unnamed x14, local copies, waits for them, and re-layouts  3.27 us
    ppermute x1, starting transfers between devices, gathered_on_chip(): lax.ppermute(x, ('gx', 'gy'), [(2 * i + j, 2 * k + l) for (i, j), (k, l)...  1.43 us
  transfers between devices with their start and end apart: 26, of which 4 were waited for; matrix products, arithmetic and copies ran while one was open for 0% of the time, Pallas kernels for 10%

profile of v7, /device:TPU:0, one launch (start us, length us, event | category | flops | bytes accessed | tf_op | source)
XLA Modules:
  0.0 67.7 jit_solution(7354475050724889215)
XLA Ops:
  0.6 0.6 collective-permute-start.2
  1.2 1.1 %copy-done = f32[16,12,8,128]{3,2,1,0:T(8,128)S(1)} copy-done((f32[16,12,8,128]{3,2,1,0:T(8,128)S(1)}, f32[16,12,8,128]{3,2,1,0:T(8,128)}, u32[]{:S(2)}) %copy-start) | copy-done | bytes 786456
  2.3 0.1 shard_map.87
  2.4 2.6 %collective-permute-start = (f32[16,4,8,128]{3,2,1,0:T(8,128)S(1)}, f32[16,4,8,128]{3,2,1,0:T(8,128)S(1)}, u32[]{:S(2)}, u32[]{:S(2)}) collective-permute-start(f32[16,4,8,128]{3,2,1,0:T(8,128)S(1)} %get-tuple-element.44), channel_id=1, source_target_pairs={{0,8},{16,24},{8,0},{24,16},{1,9},{17,25},{9,1},{25,17},{2,10},{18... | collective-permute-start | bytes 786440 | tf_op jit(solution)/shard_map/ppermute | solution.py:441
  4.9 0.7 collective-permute-start.1
  5.6 0.0 copy-start.1
  5.6 0.7 %copy-done.1 = f32[128,54]{0,1:T(8,128)S(1)} copy-done((f32[128,54]{0,1:T(8,128)S(1)}, f32[128,54]{0,1:T(8,128)}, u32[]{:S(2)}) %copy-start.1) | copy-done | bytes 27672
  6.4 1.9 %shard_map.86 = (f32[13,8,128]{2,1,0:T(8,128)S(1)}, f32[16,12,8,128]{3,2,1,0:T(8,128)S(1)}) custom-call(f32[16,12,8,128]{3,2,1,0:T(8,128)S(1)} %copy-done, f32[54,128]{1,0:T(8,128)S(1)} %bitcast.2), custom_call_target="tpu_custom_call" | custom-call | tf_op jit(solution)/shard_map/pallas_call | solution.py:23
  8.2 0.7 collective-permute-start.4
  8.9 4.5 %collective-permute-start.3 = (f32[13,8,128]{2,1,0:T(8,128)S(1)}, f32[13,8,128]{2,1,0:T(8,128)S(1)}, u32[]{:S(2)}, u32[]{:S(2)}) collective-permute-start(f32[13,8,128]{2,1,0:T(8,128)S(1)} %get-tuple-element.46), channel_id=1, source_target_pairs={{0,1},{2,3},{1,0},{3,2},{4,5},{6,7},{5,4},{7,6},{8,9},{10,11},{9,8... | collective-permute-start | bytes 159752 | tf_op jit(solution)/shard_map/ppermute | solution.py:441
  13.4 0.3 shard_map.89.zf_ref
  13.6 0.0 copy-start.3
  13.7 0.7 %copy-done.3 = f32[16,16]{1,0:T(8,128)S(1)} copy-done((f32[16,16]{1,0:T(8,128)S(1)}, f32[16,16]{1,0:T(8,128)}, u32[]{:S(2)}) %copy-start.3) | copy-done | bytes 1048
  14.4 0.7 %copy-done.5 = f32[3,16]{1,0:T(4,128)S(1)} copy-done((f32[3,16]{1,0:T(4,128)S(1)}, f32[3,16]{1,0:T(4,128)}, u32[]{:S(2)}) %copy-start.5) | copy-done | bytes 216
  15.0 0.6 shard_map.88
  15.6 0.0 collective-permute-done.4.z2_ref
  15.7 2.5 %shard_map.90 = (f32[16,12,8,128]{3,2,1,0:T(8,128)S(1)}, f32[16,4,8,128]{3,2,1,0:T(8,128)S(1)}, f32[16,4,8,128]{3,2,1,0:T(8,128)S(1)}, f32[12,8,128]{2,1,0:T(8,1...) custom-call(f32[16,12,8,128]{3,2,1,0:T(8,128)S(1)} %get-tuple-element.43.f_ref, ...), custom_call_target="tpu_custom_call" | custom-call | tf_op jit(solution)/shard_map/pallas_call | solution.py:23
  18.2 0.0 copy-start.4
  18.2 0.0 copy-start.2
  18.3 0.1 collective-permute-start.7
  18.3 4.6 %collective-permute-start.8 = (f32[16,4,8,128]{3,2,1,0:T(8,128)S(1)}, f32[16,4,8,128]{3,2,1,0:T(8,128)S(1)}, u32[]{:S(2)}, u32[]{:S(2)}) collective-permute-start(f32[16,4,8,128]{3,2,1,0:T(8,128)S(1)} %get-tuple-element.74), channel_id=1, source_target_pairs={{0,8},{16,24},{8,0},{24,16},{1,9},{17,25},{9,1},{25,17},{2,10},{18... | collective-permute-start | bytes 786440 | tf_op jit(solution)/shard_map/ppermute | solution.py:441
  22.9 0.1 collective-permute-start.5
  23.0 0.7 collective-permute-start.6
  23.7 0.4 shard_map.91.adjoint_ref
  24.0 0.0 copy-start.6
  24.1 1.3 %shard_map.92 = (f32[16,12,8,128]{3,2,1,0:T(8,128)S(1)}, f32[2,96,128]{2,1,0:T(8,128)S(1)}, f32[2,96,128]{2,1,0:T(8,128)S(1)}, f32[2,96,128]{2,1,0:T(8,128)S(1)}, f32[2,96,128]{2,1,0:T(8,128)S(1)}) custom-call(f32[16,12,8,128]{3,2,1,0:T(8,128)S(1)} %get-tuple-element.43.f_ref, f32[16,12,8,128]{3,2,1,0:T(8,128)S(1)} %get-tuple-element.60.s_ref, ...), custom_call_target="tpu_custom_call" | custom-call | tf_op jit(solution)/shard_map/pallas_call | solution.py:23
  25.3 7.5 %collective-permute-done.5.u1_ref = f32[8,4,8,128]{3,2,1,0:T(8,128)S(1)} collective-permute-done((f32[8,4,8,128]{3,2,1,0:T(8,128)S(1)}, f32[8,4,8,128]{3,2,1,0:T(8,128)S(1)}, u32[]{:S(2)}, u32[]{:S(2)}) %collective-permute-start.5) | collective-permute-done | bytes 131104 | tf_op jit(solution)/shard_map/ppermute | solution.py:441
  32.9 0.1 shard_map.93
  33.0 1.6 %collective-permute-start.16 = (f32[2,96,128]{2,1,0:T(8,128)S(1)}, f32[2,96,128]{2,1,0:T(8,128)S(1)}, u32[]{:S(2)}, u32[]{:S(2)}) collective-permute-start(f32[2,96,128]{2,1,0:T(8,128)S(1)} %get-tuple-element.81), channel_id=1, source_target_pairs={{0,1},{1,2},{2,3},{3,0},{4,5},{5,6},{6,7},{7,4},{8,9},{9,10},{10,1... | collective-permute-start | bytes 294920 | tf_op jit(solution)/shard_map/ppermute | solution.py:416
  34.6 2.6 %collective-permute-start.17 = (f32[2,96,128]{2,1,0:T(8,128)S(1)}, f32[2,96,128]{2,1,0:T(8,128)S(1)}, u32[]{:S(2)}, u32[]{:S(2)}) collective-permute-start(f32[2,96,128]{2,1,0:T(8,128)S(1)} %get-tuple-element.82), channel_id=1, source_target_pairs={{0,2},{1,3},{2,0},{3,1},{4,6},{5,7},{6,4},{7,5},{8,10},{9,11},{10,... | collective-permute-start | bytes 294920 | tf_op jit(solution)/shard_map/ppermute | solution.py:416
  37.2 1.3 %collective-permute-start.18 = (f32[2,96,128]{2,1,0:T(8,128)S(1)}, f32[2,96,128]{2,1,0:T(8,128)S(1)}, u32[]{:S(2)}, u32[]{:S(2)}) collective-permute-start(f32[2,96,128]{2,1,0:T(8,128)S(1)} %get-tuple-element.83), channel_id=1, source_target_pairs={{0,3},{1,0},{2,1},{3,2},{4,7},{5,4},{6,5},{7,6},{8,11},{9,8},{10,9... | collective-permute-start | bytes 294920 | tf_op jit(solution)/shard_map/ppermute | solution.py:416
  38.6 1.2 %collective-permute-done.15.refs_1_ = f32[8,64]{1,0:T(8,128)S(1)} collective-permute-done((f32[8,64]{1,0:T(8,128)S(1)}, f32[8,64]{1,0:T(8,128)S(1)}, u32[]{:S(2)}, u32[]{:S(2)}) %collective-permute-start.15) | collective-permute-done | bytes 2080 | tf_op jit(solution)/shard_map/ppermute | solution.py:416
  39.7 0.7 collective-permute-start.11
  40.4 0.9 %shard_map.95.q_ref = bf16[2,768,768]{2,1,0:T(8,128)(2,1)S(1)} custom-call(f32[48,96]{1,0:T(8,128)S(1)} %copy-done.2, f32[8,64]{1,0:T(8,128)S(1)} %copy-done.4, f32[8,64]{1,0:T(8,128)S(1)} %collective-permute-done.15.refs_1_), custom_call_target="tpu_custom_call" | custom-call | tf_op jit(solution)/shard_map/pallas_call | solution.py:23
  41.3 4.1 %collective-permute-start.14 = (s32[12]{0:T(128)S(1)}, s32[12]{0:T(128)S(1)}, u32[]{:S(2)}, u32[]{:S(2)}) collective-permute-start(s32[12]{0:T(128)S(1)} %copy-done.6), channel_id=1, source_target_pairs={{0,16},{8,24},{16,0},{24,8},{1,17},{9,25},{17,1},{25,9},{2,18},{10... | collective-permute-start | bytes 152 | tf_op jit(solution)/shard_map/ppermute | solution.py:416
  45.4 1.4 %collective-permute-start.12 = (s32[12]{0:T(128)S(1)}, s32[12]{0:T(128)S(1)}, u32[]{:S(2)}, u32[]{:S(2)}) collective-permute-start(s32[12]{0:T(128)S(1)} %copy-done.6), channel_id=1, source_target_pairs={{0,8},{4,28},{8,16},{12,4},{16,24},{20,12},{24,0},{28,20},{1,9},{5... | collective-permute-start | bytes 152 | tf_op jit(solution)/shard_map/ppermute | solution.py:432
  46.8 1.3 %collective-permute-start.10 = (f32[12,8,128]{2,1,0:T(8,128)S(1)}, f32[12,8,128]{2,1,0:T(8,128)S(1)}, u32[]{:S(2)}, u32[]{:S(2)}) collective-permute-start(f32[12,8,128]{2,1,0:T(8,128)S(1)} %get-tuple-element.76), channel_id=1, source_target_pairs={{0,1},{2,3},{1,0},{3,2},{4,5},{6,7},{5,4},{7,6},{8,9},{10,11},{9,8... | collective-permute-start | bytes 147464 | tf_op jit(solution)/shard_map/ppermute | solution.py:441
  48.2 0.7 collective-permute-start.9
  48.9 1.0 %collective-permute-done.12 = s32[12]{0:T(128)S(1)} collective-permute-done((s32[12]{0:T(128)S(1)}, s32[12]{0:T(128)S(1)}, u32[]{:S(2)}, u32[]{:S(2)}) %collective-permute-start.12) | collective-permute-done | bytes 80 | tf_op jit(solution)/shard_map/ppermute | solution.py:432
  49.9 1.5 %collective-permute-start.24 = (f32[2,96,128]{2,1,0:T(8,128)S(1)}, f32[2,96,128]{2,1,0:T(8,128)S(1)}, u32[]{:S(2)}, u32[]{:S(2)}) collective-permute-start(f32[2,96,128]{2,1,0:T(8,128)S(1)} %shard_map.96.refs_0_), channel_id=1, source_target_pairs={{0,24},{8,0},{16,8},{24,16},{1,25},{9,1},{17,9},{25,17},{2,26},{10... | collective-permute-start | bytes 294920 | tf_op jit(solution)/shard_map/ppermute | solution.py:416
  51.4 4.1 %collective-permute-start.22 = (f32[2,96,128]{2,1,0:T(8,128)S(1)}, f32[2,96,128]{2,1,0:T(8,128)S(1)}, u32[]{:S(2)}, u32[]{:S(2)}) collective-permute-start(f32[2,96,128]{2,1,0:T(8,128)S(1)} %shard_map.96.refs_0_), channel_id=1, source_target_pairs={{0,16},{8,24},{16,0},{24,8},{1,17},{9,25},{17,1},{25,9},{2,18},{10... | collective-permute-start | bytes 294920 | tf_op jit(solution)/shard_map/ppermute | solution.py:416
  55.5 0.7 %collective-permute-start.20 = (f32[2,96,128]{2,1,0:T(8,128)S(1)}, f32[2,96,128]{2,1,0:T(8,128)S(1)}, u32[]{:S(2)}, u32[]{:S(2)}) collective-permute-start(f32[2,96,128]{2,1,0:T(8,128)S(1)} %shard_map.96.refs_0_), channel_id=1, source_target_pairs={{0,8},{8,16},{16,24},{24,0},{1,9},{9,17},{17,25},{25,1},{2,10},{10... | collective-permute-start | bytes 294920 | tf_op jit(solution)/shard_map/ppermute | solution.py:416
  56.2 6.6 %collective-permute-done.24.refs_6_ = f32[2,96,128]{2,1,0:T(8,128)S(1)} collective-permute-done((f32[2,96,128]{2,1,0:T(8,128)S(1)}, f32[2,96,128]{2,1,0:T(8,128)S(1)}, u32[]{:S(2)}, u32[]{:S(2)}) %collective-permute-start.24) | collective-permute-done | bytes 98336 | tf_op jit(solution)/shard_map/ppermute | solution.py:416
  62.9 0.5 collective-permute-start.23
  63.4 0.1 collective-permute-start.21
  63.5 0.1 pad_add_fusion.rank_ref
  63.5 1.4 %shard_map.94 = f32[16,12,8,128]{3,2,1,0:T(8,128)} custom-call(f32[16,12,8,128]{3,2,1,0:T(8,128)S(1)} %get-tuple-element.73.hold_ref, f32[16,12,8,128]{3,2,1,0:T(8,128)S(1)} %get-tuple-element.60.s_ref, f32[16,4,8,128]{3,2,1,0:T(8,128)S(1)} %collective-permute-done.8.x1_ref, f32[16,4,8,128]{3,2,1,0:T(8,128)S(1)} %collective-permute-done.9.x2_ref, ...), custom_call_target="tpu_custom_call" | custom-call | tf_op jit(solution)/shard_map/pallas_call | solution.py:23
  65.0 2.8 %shard_map.97 = f32[4,768,54]{2,1,0:T(8,128)} custom-call(s32[48]{0:T(128)S(1)} %pad_add_fusion.rank_ref, bf16[2,768,768]{2,1,0:T(8,128)(2,1)S(1)} %shard_map.95.q_ref, f32[2,96,128]{2,1,0:T(8,128)S(1)} %shard_map.96.refs_0_, f32[2,96,128]{2,1,0:T(8,128)S(1)} %collective-permute-done.19.refs_1_, f32[2,96,128]{2,1,0:T(8,128)S(1)} %collective-permute-done.20.refs_2_, ...), custom_call_target="tpu_custom_call" | custom-call | tf_op jit(solution)/shard_map/pallas_call | solution.py:23
  (32 shorter events, 0.1 us)
Async XLA Ops:
  0.6 15.1 %collective-permute-start.2 = (f32[16,12,8,128]{3,2,1,0:T(8,128)}, f32[16,12,8,128]{3,2,1,0:T(8,128)S(1)}, u32[]{:S(2)}, u32[]{:S(2)}) collective-permute-start(f32[16,12,8,128]{3,2,1,0:T(8,128)} %f_ref.3), channel_id=1, source_target_pairs={{0,4},{4,0},{1,5},{5,1},{2,6},{6,2},{3,7},{7,3},{8,12},{12,8},{9,1... | collective-permute-start | bytes 2359304 | tf_op jit(solution)/shard_map/ppermute | solution.py:454
  1.2 1.1 %copy-start = (f32[16,12,8,128]{3,2,1,0:T(8,128)S(1)}, f32[16,12,8,128]{3,2,1,0:T(8,128)}, u32[]{:S(2)}) copy-start(f32[16,12,8,128]{3,2,1,0:T(8,128)} %f_ref.3) | copy-start | bytes 2359300
  2.4 13.3 %collective-permute-start = (f32[16,4,8,128]{3,2,1,0:T(8,128)S(1)}, f32[16,4,8,128]{3,2,1,0:T(8,128)S(1)}, u32[]{:S(2)}, u32[]{:S(2)}) collective-permute-start(f32[16,4,8,128]{3,2,1,0:T(8,128)S(1)} %get-tuple-element.44), channel_id=1, source_target_pairs={{0,8},{16,24},{8,0},{24,16},{1,9},{17,25},{9,1},{25,17},{2,10},{18... | collective-permute-start | bytes 786440 | tf_op jit(solution)/shard_map/ppermute | solution.py:441
  4.9 10.7 %collective-permute-start.1 = (f32[16,4,8,128]{3,2,1,0:T(8,128)S(1)}, f32[16,4,8,128]{3,2,1,0:T(8,128)S(1)}, u32[]{:S(2)}, u32[]{:S(2)}) collective-permute-start(f32[16,4,8,128]{3,2,1,0:T(8,128)S(1)} %get-tuple-element.45), channel_id=1, source_target_pairs={{8,16},{16,8},{9,17},{17,9},{10,18},{18,10},{11,19},{19,11},{12,20... | collective-permute-start | bytes 786440 | tf_op jit(solution)/shard_map/ppermute | solution.py:441
  5.6 0.8 %copy-start.1 = (f32[128,54]{0,1:T(8,128)S(1)}, f32[128,54]{0,1:T(8,128)}, u32[]{:S(2)}) copy-start(f32[128,54]{0,1:T(8,128)} %param.13) | copy-start | bytes 82948
  8.2 7.4 %collective-permute-start.4 = (f32[13,8,128]{2,1,0:T(8,128)S(1)}, f32[13,8,128]{2,1,0:T(8,128)S(1)}, u32[]{:S(2)}, u32[]{:S(2)}) collective-permute-start(f32[13,8,128]{2,1,0:T(8,128)S(1)} %get-tuple-element.46), channel_id=1, source_target_pairs={{1,2},{2,1},{5,6},{6,5},{9,10},{10,9},{13,14},{14,13},{17,18},{18,... | collective-permute-start | bytes 159752 | tf_op jit(solution)/shard_map/ppermute | solution.py:441
  8.9 6.8 %collective-permute-start.3 = (f32[13,8,128]{2,1,0:T(8,128)S(1)}, f32[13,8,128]{2,1,0:T(8,128)S(1)}, u32[]{:S(2)}, u32[]{:S(2)}) collective-permute-start(f32[13,8,128]{2,1,0:T(8,128)S(1)} %get-tuple-element.46), channel_id=1, source_target_pairs={{0,1},{2,3},{1,0},{3,2},{4,5},{6,7},{5,4},{7,6},{8,9},{10,11},{9,8... | collective-permute-start | bytes 159752 | tf_op jit(solution)/shard_map/ppermute | solution.py:441
  13.6 0.7 %copy-start.3 = (f32[16,16]{1,0:T(8,128)S(1)}, f32[16,16]{1,0:T(8,128)}, u32[]{:S(2)}) copy-start(f32[16,16]{1,0:T(8,128)} %kin_ref.1) | copy-start | bytes 3076
  14.3 0.7 %copy-start.5 = (f32[3,16]{1,0:T(4,128)S(1)}, f32[3,16]{1,0:T(4,128)}, u32[]{:S(2)}) copy-start(f32[3,16]{1,0:T(4,128)} %speed_ref.1) | copy-start | bytes 580
  18.2 20.3 %copy-start.4 = (f32[8,64]{1,0:T(8,128)S(1)}, f32[8,64]{1,0:T(8,128)}, u32[]{:S(2)}) copy-start(f32[8,64]{1,0:T(8,128)} %refs_0_) | copy-start | bytes 6148
  18.2 22.1 %copy-start.2 = (f32[48,96]{1,0:T(8,128)S(1)}, f32[48,96]{1,0:T(8,128)}, u32[]{:S(2)}) copy-start(f32[48,96]{1,0:T(8,128)} %xf_ref) | copy-start | bytes 55300
  18.3 5.8 %collective-permute-start.7 = (f32[16,12,8,128]{3,2,1,0:T(8,128)S(1)}, f32[16,12,8,128]{3,2,1,0:T(8,128)S(1)}, u32[]{:S(2)}, u32[]{:S(2)}) collective-permute-start(f32[16,12,8,128]{3,2,1,0:T(8,128)S(1)} %get-tuple-element.60.s_ref), channel_id=1, source_target_pairs={{0,4},{4,0},{1,5},{5,1},{2,6},{6,2},{3,7},{7,3},{8,12},{12,8},{9,1... | collective-permute-start | bytes 2359304 | tf_op jit(solution)/shard_map/ppermute | solution.py:454
  18.3 29.9 %collective-permute-start.8 = (f32[16,4,8,128]{3,2,1,0:T(8,128)S(1)}, f32[16,4,8,128]{3,2,1,0:T(8,128)S(1)}, u32[]{:S(2)}, u32[]{:S(2)}) collective-permute-start(f32[16,4,8,128]{3,2,1,0:T(8,128)S(1)} %get-tuple-element.74), channel_id=1, source_target_pairs={{0,8},{16,24},{8,0},{24,16},{1,9},{17,25},{9,1},{25,17},{2,10},{18... | collective-permute-start | bytes 786440 | tf_op jit(solution)/shard_map/ppermute | solution.py:441
  22.9 10.0 %collective-permute-start.5 = (f32[8,4,8,128]{3,2,1,0:T(8,128)S(1)}, f32[8,4,8,128]{3,2,1,0:T(8,128)S(1)}, u32[]{:S(2)}, u32[]{:S(2)}) collective-permute-start(f32[8,4,8,128]{3,2,1,0:T(8,128)S(1)} %get-tuple-element.57), channel_id=1, source_target_pairs={{0,8},{16,24},{8,0},{24,16},{1,9},{17,25},{9,1},{25,17},{2,10},{18... | collective-permute-start | bytes 393224 | tf_op jit(solution)/shard_map/ppermute | solution.py:441
  23.0 9.9 %collective-permute-start.6 = (f32[8,4,8,128]{3,2,1,0:T(8,128)S(1)}, f32[8,4,8,128]{3,2,1,0:T(8,128)S(1)}, u32[]{:S(2)}, u32[]{:S(2)}) collective-permute-start(f32[8,4,8,128]{3,2,1,0:T(8,128)S(1)} %get-tuple-element.58), channel_id=1, source_target_pairs={{8,16},{16,8},{9,17},{17,9},{10,18},{18,10},{11,19},{19,11},{12,20... | collective-permute-start | bytes 393224 | tf_op jit(solution)/shard_map/ppermute | solution.py:441
  24.0 17.3 %copy-start.6 = (s32[12]{0:T(128)S(1)}, s32[12]{0:T(128)}, u32[]{:S(2)}) copy-start(s32[12]{0:T(128)} %param.10) | copy-start | bytes 148
  33.0 8.3 %collective-permute-start.16 = (f32[2,96,128]{2,1,0:T(8,128)S(1)}, f32[2,96,128]{2,1,0:T(8,128)S(1)}, u32[]{:S(2)}, u32[]{:S(2)}) collective-permute-start(f32[2,96,128]{2,1,0:T(8,128)S(1)} %get-tuple-element.81), channel_id=1, source_target_pairs={{0,1},{1,2},{2,3},{3,0},{4,5},{5,6},{6,7},{7,4},{8,9},{9,10},{10,1... | collective-permute-start | bytes 294920 | tf_op jit(solution)/shard_map/ppermute | solution.py:416
  34.6 10.8 %collective-permute-start.17 = (f32[2,96,128]{2,1,0:T(8,128)S(1)}, f32[2,96,128]{2,1,0:T(8,128)S(1)}, u32[]{:S(2)}, u32[]{:S(2)}) collective-permute-start(f32[2,96,128]{2,1,0:T(8,128)S(1)} %get-tuple-element.82), channel_id=1, source_target_pairs={{0,2},{1,3},{2,0},{3,1},{4,6},{5,7},{6,4},{7,5},{8,10},{9,11},{10,... | collective-permute-start | bytes 294920 | tf_op jit(solution)/shard_map/ppermute | solution.py:416
  37.2 9.6 %collective-permute-start.18 = (f32[2,96,128]{2,1,0:T(8,128)S(1)}, f32[2,96,128]{2,1,0:T(8,128)S(1)}, u32[]{:S(2)}, u32[]{:S(2)}) collective-permute-start(f32[2,96,128]{2,1,0:T(8,128)S(1)} %get-tuple-element.83), channel_id=1, source_target_pairs={{0,3},{1,0},{2,1},{3,2},{4,7},{5,4},{6,5},{7,6},{8,11},{9,8},{10,9... | collective-permute-start | bytes 294920 | tf_op jit(solution)/shard_map/ppermute | solution.py:416
  38.6 1.2 %collective-permute-start.15 = (f32[8,64]{1,0:T(8,128)S(1)}, f32[8,64]{1,0:T(8,128)S(1)}, u32[]{:S(2)}, u32[]{:S(2)}) collective-permute-start(f32[8,64]{1,0:T(8,128)S(1)} %copy-done.4), channel_id=1, source_target_pairs={{0,4},{4,0},{1,5},{5,1},{2,6},{6,2},{3,7},{7,3},{8,12},{12,8},{9,1... | collective-permute-start | bytes 6152 | tf_op jit(solution)/shard_map/ppermute | solution.py:416
  39.7 15.8 %collective-permute-start.11 = (f32[12,8,128]{2,1,0:T(8,128)S(1)}, f32[12,8,128]{2,1,0:T(8,128)S(1)}, u32[]{:S(2)}, u32[]{:S(2)}) collective-permute-start(f32[12,8,128]{2,1,0:T(8,128)S(1)} %get-tuple-element.76), channel_id=1, source_target_pairs={{1,2},{2,1},{5,6},{6,5},{9,10},{10,9},{13,14},{14,13},{17,18},{18,... | collective-permute-start | bytes 147464 | tf_op jit(solution)/shard_map/ppermute | solution.py:441
  41.3 8.6 %collective-permute-start.14 = (s32[12]{0:T(128)S(1)}, s32[12]{0:T(128)S(1)}, u32[]{:S(2)}, u32[]{:S(2)}) collective-permute-start(s32[12]{0:T(128)S(1)} %copy-done.6), channel_id=1, source_target_pairs={{0,16},{8,24},{16,0},{24,8},{1,17},{9,25},{17,1},{25,9},{2,18},{10... | collective-permute-start | bytes 152 | tf_op jit(solution)/shard_map/ppermute | solution.py:416
  45.4 4.5 %collective-permute-start.12 = (s32[12]{0:T(128)S(1)}, s32[12]{0:T(128)S(1)}, u32[]{:S(2)}, u32[]{:S(2)}) collective-permute-start(s32[12]{0:T(128)S(1)} %copy-done.6), channel_id=1, source_target_pairs={{0,8},{4,28},{8,16},{12,4},{16,24},{20,12},{24,0},{28,20},{1,9},{5... | collective-permute-start | bytes 152 | tf_op jit(solution)/shard_map/ppermute | solution.py:432
  46.8 9.4 %collective-permute-start.10 = (f32[12,8,128]{2,1,0:T(8,128)S(1)}, f32[12,8,128]{2,1,0:T(8,128)S(1)}, u32[]{:S(2)}, u32[]{:S(2)}) collective-permute-start(f32[12,8,128]{2,1,0:T(8,128)S(1)} %get-tuple-element.76), channel_id=1, source_target_pairs={{0,1},{2,3},{1,0},{3,2},{4,5},{6,7},{5,4},{7,6},{8,9},{10,11},{9,8... | collective-permute-start | bytes 147464 | tf_op jit(solution)/shard_map/ppermute | solution.py:441
  48.2 15.3 %collective-permute-start.9 = (f32[16,4,8,128]{3,2,1,0:T(8,128)S(1)}, f32[16,4,8,128]{3,2,1,0:T(8,128)S(1)}, u32[]{:S(2)}, u32[]{:S(2)}) collective-permute-start(f32[16,4,8,128]{3,2,1,0:T(8,128)S(1)} %get-tuple-element.75), channel_id=1, source_target_pairs={{8,16},{16,8},{9,17},{17,9},{10,18},{18,10},{11,19},{19,11},{12,20... | collective-permute-start | bytes 786440 | tf_op jit(solution)/shard_map/ppermute | solution.py:441
  49.9 1.5 %collective-permute-start.13 = (s32[12]{0:T(128)S(1)}, s32[12]{0:T(128)S(1)}, u32[]{:S(2)}, u32[]{:S(2)}) collective-permute-start(s32[12]{0:T(128)S(1)} %collective-permute-done.12), channel_id=1, source_target_pairs={{0,4},{4,0},{1,5},{5,1},{2,6},{6,2},{3,7},{7,3},{8,12},{12,8},{9,1... | collective-permute-start | bytes 152 | tf_op jit(solution)/shard_map/ppermute | solution.py:434
  49.9 13.0 %collective-permute-start.24 = (f32[2,96,128]{2,1,0:T(8,128)S(1)}, f32[2,96,128]{2,1,0:T(8,128)S(1)}, u32[]{:S(2)}, u32[]{:S(2)}) collective-permute-start(f32[2,96,128]{2,1,0:T(8,128)S(1)} %shard_map.96.refs_0_), channel_id=1, source_target_pairs={{0,24},{8,0},{16,8},{24,16},{1,25},{9,1},{17,9},{25,17},{2,26},{10... | collective-permute-start | bytes 294920 | tf_op jit(solution)/shard_map/ppermute | solution.py:416
  51.4 11.5 %collective-permute-start.22 = (f32[2,96,128]{2,1,0:T(8,128)S(1)}, f32[2,96,128]{2,1,0:T(8,128)S(1)}, u32[]{:S(2)}, u32[]{:S(2)}) collective-permute-start(f32[2,96,128]{2,1,0:T(8,128)S(1)} %shard_map.96.refs_0_), channel_id=1, source_target_pairs={{0,16},{8,24},{16,0},{24,8},{1,17},{9,25},{17,1},{25,9},{2,18},{10... | collective-permute-start | bytes 294920 | tf_op jit(solution)/shard_map/ppermute | solution.py:416
  55.5 7.9 %collective-permute-start.20 = (f32[2,96,128]{2,1,0:T(8,128)S(1)}, f32[2,96,128]{2,1,0:T(8,128)S(1)}, u32[]{:S(2)}, u32[]{:S(2)}) collective-permute-start(f32[2,96,128]{2,1,0:T(8,128)S(1)} %shard_map.96.refs_0_), channel_id=1, source_target_pairs={{0,8},{8,16},{16,24},{24,0},{1,9},{9,17},{17,25},{25,1},{2,10},{10... | collective-permute-start | bytes 294920 | tf_op jit(solution)/shard_map/ppermute | solution.py:416
  56.2 8.7 %collective-permute-start.19 = (f32[2,96,128]{2,1,0:T(8,128)S(1)}, f32[2,96,128]{2,1,0:T(8,128)S(1)}, u32[]{:S(2)}, u32[]{:S(2)}) collective-permute-start(f32[2,96,128]{2,1,0:T(8,128)S(1)} %shard_map.96.refs_0_), channel_id=1, source_target_pairs={{0,4},{4,0},{1,5},{5,1},{2,6},{6,2},{3,7},{7,3},{8,12},{12,8},{9,1... | collective-permute-start | bytes 294920 | tf_op jit(solution)/shard_map/ppermute | solution.py:416
  62.9 2.1 %collective-permute-start.25 = (f32[2,96,128]{2,1,0:T(8,128)S(1)}, f32[2,96,128]{2,1,0:T(8,128)S(1)}, u32[]{:S(2)}, u32[]{:S(2)}) collective-permute-start(f32[2,96,128]{2,1,0:T(8,128)S(1)} %collective-permute-done.24.refs_6_), channel_id=1, source_target_pairs={{0,4},{4,0},{1,5},{5,1},{2,6},{6,2},{3,7},{7,3},{8,12},{12,8},{9,1... | collective-permute-start | bytes 294920 | tf_op jit(solution)/shard_map/ppermute | solution.py:416
  62.9 2.1 %collective-permute-start.23 = (f32[2,96,128]{2,1,0:T(8,128)S(1)}, f32[2,96,128]{2,1,0:T(8,128)S(1)}, u32[]{:S(2)}, u32[]{:S(2)}) collective-permute-start(f32[2,96,128]{2,1,0:T(8,128)S(1)} %collective-permute-done.22.refs_4_), channel_id=1, source_target_pairs={{0,4},{4,0},{1,5},{5,1},{2,6},{6,2},{3,7},{7,3},{8,12},{12,8},{9,1... | collective-permute-start | bytes 294920 | tf_op jit(solution)/shard_map/ppermute | solution.py:416
  63.4 1.6 %collective-permute-start.21 = (f32[2,96,128]{2,1,0:T(8,128)S(1)}, f32[2,96,128]{2,1,0:T(8,128)S(1)}, u32[]{:S(2)}, u32[]{:S(2)}) collective-permute-start(f32[2,96,128]{2,1,0:T(8,128)S(1)} %collective-permute-done.20.refs_2_), channel_id=1, source_target_pairs={{0,4},{4,0},{1,5},{5,1},{2,6},{6,2},{3,7},{7,3},{8,12},{12,8},{9,1... | collective-permute-start | bytes 294920 | tf_op jit(solution)/shard_map/ppermute | solution.py:416

commit v8 on v6

--- a/solution.py
+++ b/solution.py
@@ -1,3 +1,5 @@
+import functools
+
 import jax
 import jax.numpy as jnp
 from jax import lax
@@ -47,16 +49,12 @@
     return lax.rem(lax.axis_index(axis), jnp.int32(2))
 
 
-def rim_kernel(f_ref, first_ref, second_ref, sems):
+def rim_kernel(turn, f_ref, out_ref, sem):
     top, parity = f_ref.shape[1] - REACH, odd("gx")
-    copies = [
-        pltpu.make_async_copy(f_ref.at[:, pl.ds(start, REACH)], target, sems.at[i])
-        for i, (start, target) in enumerate(((top * (1 - parity), first_ref), (top * parity, second_ref)))
-    ]
-    for copy in copies:
-        copy.start()
-    for copy in copies:
-        copy.wait()
+    start = top * (parity if turn else 1 - parity)
+    copy = pltpu.make_async_copy(f_ref.at[:, pl.ds(start, REACH)], out_ref, sem)
+    copy.start()
+    copy.wait()
 
 
 def pack_rim(v, values, rim_ref):
@@ -256,55 +254,59 @@
     copy.wait()
 
 
-def factor_kernel(xf_ref, *refs):
-    y_refs, (out_ref, xt_ref) = refs[:-2], refs[-2:]
-    planes, a_count = xf_ref.shape[0], xt_ref.shape[0]
+def factor_kernel(rank_ref, xf_ref, *refs):
+    y_refs, out_ref = refs[:-1], refs[-1]
+    blocks, _, rows, width = out_ref.shape
     ny = y_refs[0].shape[0]
-    width = planes * ny
-    b_count = out_ref.shape[1] // a_count
+    nx = rank_ref.shape[1] // blocks
+    a_count = xf_ref.shape[1] // lax.axis_size("gx")
+    b_count = rows // a_count
 
     def own(count, total, place):
         return (iota((count, total), 1) == iota((count, total), 0) + place * count).astype(F32)
 
     mine = exact(own(a_count, xf_ref.shape[1], lax.axis_index("gx")), xf_ref[...], ((1,), (1,)))
-    spread = iota((planes, width), 0) == iota((planes, width), 1) // ny
-    xt_ref[...] = exact(mine, spread.astype(F32))
-    spread = iota((ny, width), 0) == low_bits(iota((ny, width), 1), ny)
-    for i, y_ref in enumerate(y_refs):
-        rows = exact(own(b_count, y_ref.shape[1], lax.axis_index("gy")), y_ref[...], ((1,), (1,)))
-        yt = exact(rows, spread.astype(F32))
+    pick = iota((xf_ref.shape[0], rank_ref.shape[1]), 0) == rank_ref[...]
+    mine = exact(mine, pick.astype(F32))
+    column = iota((nx, width), 1)
+    spread_x = (iota((nx, width), 0) == low_bits(column // ny, nx)).astype(F32)
+    column = iota((ny, width), 1)
+    yt = None
+    for j, y_ref in enumerate(y_refs):
+        mine_y = exact(own(b_count, y_ref.shape[1], lax.axis_index("gy")), y_ref[...], ((1,), (1,)))
+        here = (iota((ny, width), 0) == low_bits(column, ny)) & (column // (nx * ny) == j)
+        part = exact(mine_y, here.astype(F32))
+        yt = part if yt is None else yt + part
+    for i in range(blocks):
+        xt = exact(mine[:, i * nx : (i + 1) * nx], spread_x)
         for a in range(a_count):
-            high, low = split(xt_ref[a : a + 1, :] * yt)
-            out_ref[0, a * b_count : (a + 1) * b_count, i * width : (i + 1) * width] = high
-            out_ref[1, a * b_count : (a + 1) * b_count, i * width : (i + 1) * width] = low
-
-
-def core_kernel(rank_ref, q_ref, *refs):
-    block_refs, (out_ref, placed_ref, result_ref, sems) = refs[:-4], refs[-4:]
-    pairs, blocks_y, planes, ny, nz = placed_ref.shape
-    nx = block_refs[0].shape[1] // ny
+            high, low = split(xt[a : a + 1, :] * yt)
+            out_ref[i, 0, a * b_count : (a + 1) * b_count] = high
+            out_ref[i, 1, a * b_count : (a + 1) * b_count] = low
+
+
+def contracted(factor_ref, i, block_refs):
+    pairs = block_refs[0].shape[0]
+    columns = [jnp.concatenate([r[p] for r in block_refs], axis=0) for p in range(pairs)]
+    high, low = split(jnp.concatenate(columns, axis=1))
+    q_high, q_low = factor_ref[i, 0], factor_ref[i, 1]
+    return dot(q_high, high) + (dot(q_high, low) + dot(q_low, high))
+
+
+def early_kernel(blocks_y, factor_ref, *refs):
+    total = None
+    for i in range((len(refs) - 1) // blocks_y):
+        part = contracted(factor_ref, i, refs[i * blocks_y : (i + 1) * blocks_y])
+        total = part if total is None else total + part
+    refs[-1][...] = total
+
+
+def core_kernel(factor_ref, total_ref, *refs):
+    out_ref = refs[-1]
     rank = out_ref.shape[2]
-    rows = out_ref.shape[1] // sems.shape[0]
-    for i in range(planes // nx):
-        for x in range(nx):
-            row = rank_ref[i * nx + x]
-            for j in range(blocks_y):
-                for p in range(pairs):
-                    block_ref = block_refs[i * blocks_y + j]
-                    placed_ref[p, j, row] = block_ref[p, x * ny : (x + 1) * ny, :]
-    columns = [placed_ref[p].reshape(blocks_y * planes * ny, nz) for p in range(pairs)]
-    high, low = split(jnp.concatenate(columns, axis=1))
-    copies = []
-    for m in range(sems.shape[0]):
-        here = slice(m * rows, (m + 1) * rows)
-        q_high = q_ref[0, here]
-        result = dot(q_high, high) + (dot(q_high, low) + dot(q_ref[1, here], high))
-        for v in range(2 * pairs):
-            result_ref[v, here] = result[:, v * HALF : v * HALF + rank]
-        copies.append(pltpu.make_async_copy(result_ref.at[:, here], out_ref.at[:, here], sems.at[m]))
-        copies[-1].start()
-    for copy in copies:
-        copy.wait()
+    result = total_ref[...] + contracted(factor_ref, factor_ref.shape[0] - 1, refs[:-1])
+    for v in range(out_ref.shape[0]):
+        out_ref[v] = result[:, v * HALF : v * HALF + rank]
 
 
 def shifted(x, axis, k):
@@ -361,12 +363,9 @@
     chunk = (pairs, nx * ny, 2 * HALF)
     barrier = lax.optimization_barrier
 
-    first, second = call(
-        rim_kernel,
-        [(rim, F32), (rim, F32)],
-        [HBM],
-        (fields,),
-        [pltpu.SemaphoreType.DMA((2,))],
+    first, second = (
+        call(functools.partial(rim_kernel, turn), [(rim, F32)], [HBM], (fields,), [pltpu.SemaphoreType.DMA])[0]
+        for turn in (0, 1)
     )
     x1, x2 = paired(first, second, "gx")
     packed, same = call(
@@ -398,14 +397,7 @@
     other = beside(section, "gy")
     y_rows = gathered(y_factor, "gy")
     (zf,) = call(project_kernel, [((2 * nz, 4 * HALF), BF16)], [VMEM], (z_factor.T,), [pltpu.VMEM((nz, 2 * HALF), F32)])
-    (factor,) = call(
-        factor_kernel,
-        [((2, rows, cells), BF16)],
-        [VMEM] * (1 + gy),
-        (x_factor, *y_rows),
-        [pltpu.VMEM((a_count, planes * ny), F32)],
-    )
-    x1, x2, z1, z2, other, zf, factor = barrier((x1, x2, z1, z2, other, zf, factor))
+    x1, x2, z1, z2, other, zf = barrier((x1, x2, z1, z2, other, zf))
     new, *chunks = call(
         next_kernel,
         [(fields.shape, F32)] + [(chunk, F32)] * gz,
@@ -415,23 +407,34 @@
     )
     new, chunks, block_rank = barrier((new, chunks, block_rank))
     parts = [chunks[0]] + [shifted(chunks[k], "gz", k) for k in range(1, gz)]
-    ranks = jnp.concatenate(gathered_on_chip(block_rank), axis=0)
+    ranks = jnp.concatenate(gathered_on_chip(block_rank.reshape(1, nx)), axis=1)
     (fields_next,) = call(store_kernel, [(fields.shape, F32)], [ANY], (new,), [pltpu.SemaphoreType.DMA], out_spec=HBM)
+    (factor,) = call(
+        factor_kernel,
+        [((gx, 2, rows, gy * nx * ny), BF16)],
+        [VMEM] * (2 + gy),
+        (ranks, x_factor, *y_rows),
+        room=16 if cells <= 1024 else 56,
+    )
     (own,) = call(sum_kernel, [(chunk, F32)], [VMEM] * gz, parts)
-    blocks = [gathered(block, "gy") for block in gathered(own, "gx")]
-    pieces = 4 if rows % 128 == 0 else 1
+    *blocks, last = gathered(own, "gx")
+    blocks = [gathered(block, "gy") for block in blocks]
+    blocks.append(gathered(last, "gy"))
+    room = 16 if cells <= 1024 else 56
+    early = [block for line in blocks[:-1] for block in line]
+    (total,) = call(
+        functools.partial(early_kernel, gy),
+        [((rows, 2 * pairs * HALF), F32)],
+        [VMEM] * (1 + len(early)),
+        (factor, *early),
+        room=room,
+    )
     (core,) = call(
         core_kernel,
         [((2 * pairs, rows, rank), F32)],
-        [SMEM] + [VMEM] * (1 + gx * gy),
-        (ranks, factor, *(block for line in blocks for block in line)),
-        [
-            pltpu.VMEM((pairs, gy, planes, ny, nz), F32),
-            pltpu.VMEM((2 * pairs, rows, rank), F32),
-            pltpu.SemaphoreType.DMA((pieces,)),
-        ],
-        room=16 if cells <= 1024 else 56,
-        out_spec=HBM,
+        [VMEM] * (2 + gy),
+        (factor, total, *blocks[-1]),
+        room=room,
     )
     return fields_next, core.reshape(2 * pairs, a_count, b_count, rank)
 

time: 61 us -> 63.9 us (1.048)
  waiting for transfers between devices: 7.2 us -> 13.2 us
  starting transfers between devices: 37.8 us -> 35.5 us
    ppermute x12, starting transfers between devices: 16 us -> 11.4 us  [shifted(): return lax.ppermute(x, axis, [(i, (i + k) % count) for i in range(count)])]
    ppermute x8, waiting for transfers between devices: 3.23 us -> 6.36 us  [paired(): out.append(lax.ppermute(x, axis, links + [(j, i) for i, j in links]))]
    ppermute x1, starting transfers between devices: 4.52 us -> 6.56 us  [gathered_on_chip(): lax.ppermute(x, ('gx', 'gy'), [(2 * i + j, 2 * k + l) for (i, j), (k, l)...]
    ppermute x12, waiting for transfers between devices: 3.96 us -> 5.51 us  [shifted(): return lax.ppermute(x, axis, [(i, (i + k) % count) for i in range(count)])]
    ppermute x1, waiting for transfers between devices: 0.01 us -> 1.3 us  [gathered_on_chip(): lax.ppermute(x, ('gx', 'gy'), [(2 * i + j, 2 * k + l) for (i, j), (k, l)...]
    pallas_call x10 -> x12, Pallas kernels: 11.7 us -> 11.4 us  [call(): pl.pallas_call(kernel, out_shape=tuple((jax.ShapeDtypeStruct(s, d) for s,...]
  transfers between devices with their start and end apart: 24 -> 24, of which waited for: 6 -> 7; matrix products, arithmetic and copies ran while one was open for 0% -> 0% of each run, Pallas kernels for 7% -> 9%
where the time goes in v8:
time: 63.9 us; the launch traced here: 63.6 us
  starting transfers between devices  35.5 us (56%)
  waiting for transfers between devices  13.2 us (21%)
  Pallas kernels  11.4 us (18%)
  local copies, waits for them, and re-layouts  2.53 us (4%)
  between operations  0.87 us (1%)
    ppermute x8, starting transfers between devices, paired(): out.append(lax.ppermute(x, axis, links + [(j, i) for i, j in links]))  17 us
    pallas_call x12, Pallas kernels, call(): pl.pallas_call(kernel, out_shape=tuple((jax.ShapeDtypeStruct(s, d) for s,...  11.4 us
    ppermute x12, starting transfers between devices, shifted(): return lax.ppermute(x, axis, [(i, (i + k) % count) for i in range(count)])  11.4 us
    ppermute x1, starting transfers between devices, gathered_on_chip(): lax.ppermute(x, ('gx', 'gy'), [(2 * i + j, 2 * k + l) for (i, j), (k, l)...  6.56 us
    ppermute x8, waiting for transfers between devices, paired(): out.append(lax.ppermute(x, axis, links + [(j, i) for i, j in links]))  6.36 us
    ppermute x12, waiting for transfers between devices, shifted(): return lax.ppermute(x, axis, [(i, (i + k) % count) for i in range(count)])  5.51 us
    unnamed x14, local copies, waits for them, and re-layouts  2.53 us
    ppermute x1, waiting for transfers between devices, gathered_on_chip(): lax.ppermute(x, ('gx', 'gy'), [(2 * i + j, 2 * k + l) for (i, j), (k, l)...  1.3 us
  transfers between devices with their start and end apart: 24, of which 7 were waited for; matrix products, arithmetic and copies ran while one was open for 0% of the time, Pallas kernels for 9%

profile of v8, /device:TPU:0, one launch (start us, length us, event | category | flops | bytes accessed | tf_op | source)
XLA Modules:
  0.0 63.6 jit_solution(6207541165497988769)
XLA Ops:
  0.6 0.6 collective-permute-start.2
  1.2 1.1 %copy-done = f32[16,12,8,128]{3,2,1,0:T(8,128)S(1)} copy-done((f32[16,12,8,128]{3,2,1,0:T(8,128)S(1)}, f32[16,12,8,128]{3,2,1,0:T(8,128)}, u32[]{:S(2)}) %copy-start) | copy-done | bytes 786456
  2.4 0.7 %collective-permute-start.1 = (f32[16,4,8,128]{3,2,1,0:T(8,128)S(1)}, f32[16,4,8,128]{3,2,1,0:T(8,128)S(1)}, u32[]{:S(2)}, u32[]{:S(2)}) collective-permute-start(f32[16,4,8,128]{3,2,1,0:T(8,128)S(1)} %shard_map.88), channel_id=1, source_target_pairs={{8,16},{16,8},{9,17},{17,9},{10,18},{18,10},{11,19},{19,11},{12,20... | collective-permute-start | bytes 786440 | tf_op jit(solution)/shard_map/ppermute | solution.py:341
  3.1 5.3 %collective-permute-start = (f32[16,4,8,128]{3,2,1,0:T(8,128)S(1)}, f32[16,4,8,128]{3,2,1,0:T(8,128)S(1)}, u32[]{:S(2)}, u32[]{:S(2)}) collective-permute-start(f32[16,4,8,128]{3,2,1,0:T(8,128)S(1)} %shard_map.87), channel_id=1, source_target_pairs={{0,8},{16,24},{8,0},{24,16},{1,9},{17,25},{9,1},{25,17},{2,10},{18... | collective-permute-start | bytes 786440 | tf_op jit(solution)/shard_map/ppermute | solution.py:341
  8.4 1.7 %shard_map.86 = (f32[12,8,128]{2,1,0:T(8,128)S(1)}, f32[16,12,8,128]{3,2,1,0:T(8,128)S(1)}) custom-call(f32[16,12,8,128]{3,2,1,0:T(8,128)S(1)} %copy-done), custom_call_target="tpu_custom_call" | custom-call | tf_op jit(solution)/shard_map/pallas_call | solution.py:25
  10.1 0.7 %collective-permute-start.4 = (f32[12,8,128]{2,1,0:T(8,128)S(1)}, f32[12,8,128]{2,1,0:T(8,128)S(1)}, u32[]{:S(2)}, u32[]{:S(2)}) collective-permute-start(f32[12,8,128]{2,1,0:T(8,128)S(1)} %get-tuple-element.37), channel_id=1, source_target_pairs={{1,2},{2,1},{5,6},{6,5},{9,10},{10,9},{13,14},{14,13},{17,18},{18,... | collective-permute-start | bytes 147464 | tf_op jit(solution)/shard_map/ppermute | solution.py:341
  10.8 4.5 %collective-permute-start.3 = (f32[12,8,128]{2,1,0:T(8,128)S(1)}, f32[12,8,128]{2,1,0:T(8,128)S(1)}, u32[]{:S(2)}, u32[]{:S(2)}) collective-permute-start(f32[12,8,128]{2,1,0:T(8,128)S(1)} %get-tuple-element.37), channel_id=1, source_target_pairs={{0,1},{2,3},{1,0},{3,2},{4,5},{6,7},{5,4},{7,6},{8,9},{10,11},{9,8... | collective-permute-start | bytes 147464 | tf_op jit(solution)/shard_map/ppermute | solution.py:341
  15.2 0.7 %copy-done.3 = f32[16,16]{1,0:T(8,128)S(1)} copy-done((f32[16,16]{1,0:T(8,128)S(1)}, f32[16,16]{1,0:T(8,128)}, u32[]{:S(2)}) %copy-start.3) | copy-done | bytes 1048
  15.9 0.7 %copy-done.5 = f32[3,16]{1,0:T(4,128)S(1)} copy-done((f32[3,16]{1,0:T(4,128)S(1)}, f32[3,16]{1,0:T(4,128)}, u32[]{:S(2)}) %copy-start.5) | copy-done | bytes 216
  16.6 0.6 shard_map.89
  17.2 0.1 collective-permute-done.3.z1_ref
  17.3 3.2 %collective-permute-done.x1_ref = f32[16,4,8,128]{3,2,1,0:T(8,128)S(1)} collective-permute-done((f32[16,4,8,128]{3,2,1,0:T(8,128)S(1)}, f32[16,4,8,128]{3,2,1,0:T(8,128)S(1)}, u32[]{:S(2)}, u32[]{:S(2)}) %collective-permute-start) | collective-permute-done | bytes 262176 | tf_op jit(solution)/shard_map/ppermute | solution.py:341
  20.5 0.0 collective-permute-done.2.beside_ref
  20.5 1.8 %shard_map.90 = (f32[16,12,8,128]{3,2,1,0:T(8,128)S(1)}, f32[16,4,8,128]{3,2,1,0:T(8,128)S(1)}, f32[16,4,8,128]{3,2,1,0:T(8,128)S(1)}, f32[12,8,128]{2,1,0:T(8,128)S(1)}) custom-call(f32[16,12,8,128]{3,2,1,0:T(8,128)S(1)} %get-tuple-element.36.f_ref, f32[16,4,8,128]{3,2,1,0:T(8,128)S(1)} %collective-permute-done.x1_ref, ...), custom_call_target="tpu_custom_call" | custom-call | tf_op jit(solution)/shard_map/pallas_call | solution.py:25
  22.4 0.0 copy-start.6
  22.4 0.0 copy-start.2
  22.4 0.1 collective-permute-start.9
  22.5 0.1 collective-permute-start.5
  22.6 0.7 %collective-permute-start.6 = (f32[16,4,8,128]{3,2,1,0:T(8,128)S(1)}, f32[16,4,8,128]{3,2,1,0:T(8,128)S(1)}, u32[]{:S(2)}, u32[]{:S(2)}) collective-permute-start(f32[16,4,8,128]{3,2,1,0:T(8,128)S(1)} %get-tuple-element.48), channel_id=1, source_target_pairs={{8,16},{16,8},{9,17},{17,9},{10,18},{18,10},{11,19},{19,11},{12,20... | collective-permute-start | bytes 786440 | tf_op jit(solution)/shard_map/ppermute | solution.py:341
  23.2 0.7 %collective-permute-start.8 = (f32[12,8,128]{2,1,0:T(8,128)S(1)}, f32[12,8,128]{2,1,0:T(8,128)S(1)}, u32[]{:S(2)}, u32[]{:S(2)}) collective-permute-start(f32[12,8,128]{2,1,0:T(8,128)S(1)} %get-tuple-element.49), channel_id=1, source_target_pairs={{1,2},{2,1},{5,6},{6,5},{9,10},{10,9},{13,14},{14,13},{17,18},{18,... | collective-permute-start | bytes 147464 | tf_op jit(solution)/shard_map/ppermute | solution.py:341
  23.9 4.5 %collective-permute-start.7 = (f32[12,8,128]{2,1,0:T(8,128)S(1)}, f32[12,8,128]{2,1,0:T(8,128)S(1)}, u32[]{:S(2)}, u32[]{:S(2)}) collective-permute-start(f32[12,8,128]{2,1,0:T(8,128)S(1)} %get-tuple-element.49), channel_id=1, source_target_pairs={{0,1},{2,3},{1,0},{3,2},{4,5},{6,7},{5,4},{7,6},{8,9},{10,11},{9,8... | collective-permute-start | bytes 147464 | tf_op jit(solution)/shard_map/ppermute | solution.py:341
  28.4 0.3 shard_map.91.zf_ref
  28.7 1.8 %collective-permute-done.7.z1_ref = f32[12,8,128]{2,1,0:T(8,128)S(1)} collective-permute-done((f32[12,8,128]{2,1,0:T(8,128)S(1)}, f32[12,8,128]{2,1,0:T(8,128)S(1)}, u32[]{:S(2)}, u32[]{:S(2)}) %collective-permute-start.7) | collective-permute-done | bytes 49184 | tf_op jit(solution)/shard_map/ppermute | solution.py:341
  30.4 1.3 %collective-permute-done.5.x1_ref = f32[16,4,8,128]{3,2,1,0:T(8,128)S(1)} collective-permute-done((f32[16,4,8,128]{3,2,1,0:T(8,128)S(1)}, f32[16,4,8,128]{3,2,1,0:T(8,128)S(1)}, u32[]{:S(2)}, u32[]{:S(2)}) %collective-permute-start.5) | collective-permute-done | bytes 262176 | tf_op jit(solution)/shard_map/ppermute | solution.py:341
  31.7 2.0 %shard_map.92 = (f32[16,12,8,128]{3,2,1,0:T(8,128)S(1)}, f32[2,96,128]{2,1,0:T(8,128)S(1)}, f32[2,96,128]{2,1,0:T(8,128)S(1)}, f32[2,96,128]{2,1,0:T(8,128)S(1)}, f32[2,96,128]{2,1,0:T(8,128)S(1)}) custom-call(f32[16,12,8,128]{3,2,1,0:T(8,128)S(1)} %get-tuple-element.36.f_ref, f32[16,12,8,128]{3,2,1,0:T(8,128)S(1)} %get-tuple-element.46.s_ref, ...), custom_call_target="tpu_custom_call" | custom-call | tf_op jit(solution)/shard_map/pallas_call | solution.py:25
  33.7 1.6 %collective-permute-start.14 = (f32[2,96,128]{2,1,0:T(8,128)S(1)}, f32[2,96,128]{2,1,0:T(8,128)S(1)}, u32[]{:S(2)}, u32[]{:S(2)}) collective-permute-start(f32[2,96,128]{2,1,0:T(8,128)S(1)} %get-tuple-element.67), channel_id=1, source_target_pairs={{0,1},{1,2},{2,3},{3,0},{4,5},{5,6},{6,7},{7,4},{8,9},{9,10},{10,1... | collective-permute-start | bytes 294920 | tf_op jit(solution)/shard_map/ppermute | solution.py:314
  35.4 2.6 %collective-permute-start.15 = (f32[2,96,128]{2,1,0:T(8,128)S(1)}, f32[2,96,128]{2,1,0:T(8,128)S(1)}, u32[]{:S(2)}, u32[]{:S(2)}) collective-permute-start(f32[2,96,128]{2,1,0:T(8,128)S(1)} %get-tuple-element.68), channel_id=1, source_target_pairs={{0,2},{1,3},{2,0},{3,1},{4,6},{5,7},{6,4},{7,5},{8,10},{9,11},{10,... | collective-permute-start | bytes 294920 | tf_op jit(solution)/shard_map/ppermute | solution.py:314
  38.0 1.3 %collective-permute-start.16 = (f32[2,96,128]{2,1,0:T(8,128)S(1)}, f32[2,96,128]{2,1,0:T(8,128)S(1)}, u32[]{:S(2)}, u32[]{:S(2)}) collective-permute-start(f32[2,96,128]{2,1,0:T(8,128)S(1)} %get-tuple-element.69), channel_id=1, source_target_pairs={{0,3},{1,0},{2,1},{3,2},{4,7},{5,4},{6,5},{7,6},{8,11},{9,8},{10,9... | collective-permute-start | bytes 294920 | tf_op jit(solution)/shard_map/ppermute | solution.py:314
  39.3 0.0 collective-permute-start.13
  39.3 0.9 %shard_map.93 = f32[16,12,8,128]{3,2,1,0:T(8,128)} custom-call(f32[16,12,8,128]{3,2,1,0:T(8,128)S(1)} %get-tuple-element.62.in_ref), custom_call_target="tpu_custom_call" | custom-call | tf_op jit(solution)/shard_map/pallas_call | solution.py:25
  40.2 6.6 %collective-permute-start.10 = (s32[1,12]{1,0:T(1,128)S(1)}, s32[1,12]{1,0:T(1,128)S(1)}, u32[]{:S(2)}, u32[]{:S(2)}) collective-permute-start(s32[1,12]{1,0:T(1,128)S(1)} %bitcast.5), channel_id=1, source_target_pairs={{0,8},{4,28},{8,16},{12,4},{16,24},{20,12},{24,0},{28,20},{1,9},{5... | collective-permute-start | bytes 152 | tf_op jit(solution)/shard_map/ppermute | solution.py:330
  46.8 1.3 %collective-permute-done.10 = s32[1,12]{1,0:T(1,128)S(1)} collective-permute-done((s32[1,12]{1,0:T(1,128)S(1)}, s32[1,12]{1,0:T(1,128)S(1)}, u32[]{:S(2)}, u32[]{:S(2)}) %collective-permute-start.10) | collective-permute-done | bytes 80 | tf_op jit(solution)/shard_map/ppermute | solution.py:330
  48.1 3.2 %collective-permute-start.12 = (s32[1,12]{1,0:T(1,128)S(1)}, s32[1,12]{1,0:T(1,128)S(1)}, u32[]{:S(2)}, u32[]{:S(2)}) collective-permute-start(s32[1,12]{1,0:T(1,128)S(1)} %bitcast.6), channel_id=1, source_target_pairs={{0,16},{8,24},{16,0},{24,8},{1,17},{9,25},{17,1},{25,9},{2,18},{10... | collective-permute-start | bytes 152 | tf_op jit(solution)/shard_map/ppermute | solution.py:314
  51.3 0.0 collective-permute-done.14.refs_1_
  51.3 0.0 collective-permute-start.11
  51.3 0.0 collective-permute-done.15.refs_2_
  51.3 0.8 %collective-permute-start.22 = (f32[2,96,128]{2,1,0:T(8,128)S(1)}, f32[2,96,128]{2,1,0:T(8,128)S(1)}, u32[]{:S(2)}, u32[]{:S(2)}) collective-permute-start(f32[2,96,128]{2,1,0:T(8,128)S(1)} %shard_map.95.refs_0_), channel_id=1, source_target_pairs={{0,24},{8,0},{16,8},{24,16},{1,25},{9,1},{17,9},{25,17},{2,26},{10... | collective-permute-start | bytes 294920 | tf_op jit(solution)/shard_map/ppermute | solution.py:314
  52.2 0.3 collective-permute-start.20
  52.5 1.0 %collective-permute-start.18 = (f32[2,96,128]{2,1,0:T(8,128)S(1)}, f32[2,96,128]{2,1,0:T(8,128)S(1)}, u32[]{:S(2)}, u32[]{:S(2)}) collective-permute-start(f32[2,96,128]{2,1,0:T(8,128)S(1)} %shard_map.95.refs_0_), channel_id=1, source_target_pairs={{0,8},{8,16},{16,24},{24,0},{1,9},{9,17},{17,25},{25,1},{2,10},{10... | collective-permute-start | bytes 294920 | tf_op jit(solution)/shard_map/ppermute | solution.py:314
  53.4 0.0 collective-permute-done.12
  53.4 0.0 collective-permute-start.17
  53.4 3.6 %collective-permute-done.22.refs_0_ = f32[2,96,128]{2,1,0:T(8,128)S(1)} collective-permute-done((f32[2,96,128]{2,1,0:T(8,128)S(1)}, f32[2,96,128]{2,1,0:T(8,128)S(1)}, u32[]{:S(2)}, u32[]{:S(2)}) %collective-permute-start.22) | collective-permute-done | bytes 98336 | tf_op jit(solution)/shard_map/ppermute | solution.py:314
  57.1 1.9 %collective-permute-done.20.refs_4_ = f32[2,96,128]{2,1,0:T(8,128)S(1)} collective-permute-done((f32[2,96,128]{2,1,0:T(8,128)S(1)}, f32[2,96,128]{2,1,0:T(8,128)S(1)}, u32[]{:S(2)}, u32[]{:S(2)}) %collective-permute-start.20) | collective-permute-done | bytes 98336 | tf_op jit(solution)/shard_map/ppermute | solution.py:314
  58.9 0.5 collective-permute-start.19
  59.4 0.1 pad_add_fusion.rank_ref
  59.5 1.2 %shard_map.94.factor_ref = bf16[4,2,768,192]{3,2,1,0:T(8,128)(2,1)S(1)} custom-call(s32[1,48]{1,0:T(1,128)S(1)} %pad_add_fusion.rank_ref, f32[48,96]{1,0:T(8,128)S(1)} %copy-done.2, f32[8,64]{1,0:T(8,128)S(1)} %copy-done.4, f32[8,64]{1,0:T(8,128)S(1)} %collective-permute-done.13.refs_1_), custom_call_target="tpu_custom_call" | custom-call | tf_op jit(solution)/shard_map/pallas_call | solution.py:25
  60.8 1.1 %shard_map.96.total_ref = f32[768,256]{1,0:T(8,128)S(1)} custom-call(bf16[4,2,768,192]{3,2,1,0:T(8,128)(2,1)S(1)} %shard_map.94.factor_ref, f32[2,96,128]{2,1,0:T(8,128)S(1)} %shard_map.95.refs_0_, f32[2,96,128]{2,1,0:T(8,128)S(1)} %collective-permute-done.17.refs_1_, f32[2,96,128]{2,1,0:T(8,128)S(1)} %collective-permute-done.18.refs_2_, ...), custom_call_target="tpu_custom_call" | custom-call | tf_op jit(solution)/shard_map/pallas_call | solution.py:25
  61.9 1.7 %shard_map.97 = f32[4,768,54]{2,1,0:T(8,128)} custom-call(bf16[4,2,768,192]{3,2,1,0:T(8,128)(2,1)S(1)} %shard_map.94.factor_ref, f32[768,256]{1,0:T(8,128)S(1)} %shard_map.96.total_ref, f32[2,96,128]{2,1,0:T(8,128)S(1)} %collective-permute-done.22.refs_0_, f32[2,96,128]{2,1,0:T(8,128)S(1)} %collective-permute-done.23.refs_1_), custom_call_target="tpu_custom_call" | custom-call | tf_op jit(solution)/shard_map/pallas_call | solution.py:25
  (28 shorter events, 0.2 us)
Async XLA Ops:
  0.6 19.9 %collective-permute-start.2 = (f32[16,12,8,128]{3,2,1,0:T(8,128)}, f32[16,12,8,128]{3,2,1,0:T(8,128)S(1)}, u32[]{:S(2)}, u32[]{:S(2)}) collective-permute-start(f32[16,12,8,128]{3,2,1,0:T(8,128)} %f_ref.5), channel_id=1, source_target_pairs={{0,4},{4,0},{1,5},{5,1},{2,6},{6,2},{3,7},{7,3},{8,12},{12,8},{9,1... | collective-permute-start | bytes 2359304 | tf_op jit(solution)/shard_map/ppermute | solution.py:348
  1.2 1.1 %copy-start = (f32[16,12,8,128]{3,2,1,0:T(8,128)S(1)}, f32[16,12,8,128]{3,2,1,0:T(8,128)}, u32[]{:S(2)}) copy-start(f32[16,12,8,128]{3,2,1,0:T(8,128)} %f_ref.5) | copy-start | bytes 2359300
  2.3 26.1 %copy-start.1 = (f32[128,54]{0,1:T(8,128)S(1)}, f32[128,54]{0,1:T(8,128)}, u32[]{:S(2)}) copy-start(f32[128,54]{0,1:T(8,128)} %param.13) | copy-start | bytes 82948
  2.4 14.9 %collective-permute-start.1 = (f32[16,4,8,128]{3,2,1,0:T(8,128)S(1)}, f32[16,4,8,128]{3,2,1,0:T(8,128)S(1)}, u32[]{:S(2)}, u32[]{:S(2)}) collective-permute-start(f32[16,4,8,128]{3,2,1,0:T(8,128)S(1)} %shard_map.88), channel_id=1, source_target_pairs={{8,16},{16,8},{9,17},{17,9},{10,18},{18,10},{11,19},{19,11},{12,20... | collective-permute-start | bytes 786440 | tf_op jit(solution)/shard_map/ppermute | solution.py:341
  3.1 17.4 %collective-permute-start = (f32[16,4,8,128]{3,2,1,0:T(8,128)S(1)}, f32[16,4,8,128]{3,2,1,0:T(8,128)S(1)}, u32[]{:S(2)}, u32[]{:S(2)}) collective-permute-start(f32[16,4,8,128]{3,2,1,0:T(8,128)S(1)} %shard_map.87), channel_id=1, source_target_pairs={{0,8},{16,24},{8,0},{24,16},{1,9},{17,25},{9,1},{25,17},{2,10},{18... | collective-permute-start | bytes 786440 | tf_op jit(solution)/shard_map/ppermute | solution.py:341
  8.4 30.9 %copy-start.4 = (f32[8,64]{1,0:T(8,128)S(1)}, f32[8,64]{1,0:T(8,128)}, u32[]{:S(2)}) copy-start(f32[8,64]{1,0:T(8,128)} %refs_0_) | copy-start | bytes 6148
  10.1 7.1 %collective-permute-start.4 = (f32[12,8,128]{2,1,0:T(8,128)S(1)}, f32[12,8,128]{2,1,0:T(8,128)S(1)}, u32[]{:S(2)}, u32[]{:S(2)}) collective-permute-start(f32[12,8,128]{2,1,0:T(8,128)S(1)} %get-tuple-element.37), channel_id=1, source_target_pairs={{1,2},{2,1},{5,6},{6,5},{9,10},{10,9},{13,14},{14,13},{17,18},{18,... | collective-permute-start | bytes 147464 | tf_op jit(solution)/shard_map/ppermute | solution.py:341
  10.8 6.5 %collective-permute-start.3 = (f32[12,8,128]{2,1,0:T(8,128)S(1)}, f32[12,8,128]{2,1,0:T(8,128)S(1)}, u32[]{:S(2)}, u32[]{:S(2)}) collective-permute-start(f32[12,8,128]{2,1,0:T(8,128)S(1)} %get-tuple-element.37), channel_id=1, source_target_pairs={{0,1},{2,3},{1,0},{3,2},{4,5},{6,7},{5,4},{7,6},{8,9},{10,11},{9,8... | collective-permute-start | bytes 147464 | tf_op jit(solution)/shard_map/ppermute | solution.py:341
  15.2 0.7 %copy-start.3 = (f32[16,16]{1,0:T(8,128)S(1)}, f32[16,16]{1,0:T(8,128)}, u32[]{:S(2)}) copy-start(f32[16,16]{1,0:T(8,128)} %kin_ref.1) | copy-start | bytes 3076
  15.9 0.7 %copy-start.5 = (f32[3,16]{1,0:T(4,128)S(1)}, f32[3,16]{1,0:T(4,128)}, u32[]{:S(2)}) copy-start(f32[3,16]{1,0:T(4,128)} %speed_ref.1) | copy-start | bytes 580
  22.4 17.8 %copy-start.6 = (s32[12]{0:T(128)S(1)}, s32[12]{0:T(128)}, u32[]{:S(2)}) copy-start(s32[12]{0:T(128)} %param.10) | copy-start | bytes 148
  22.4 37.1 %copy-start.2 = (f32[48,96]{1,0:T(8,128)S(1)}, f32[48,96]{1,0:T(8,128)}, u32[]{:S(2)}) copy-start(f32[48,96]{1,0:T(8,128)} %xf_ref) | copy-start | bytes 55300
  22.4 9.3 %collective-permute-start.9 = (f32[16,12,8,128]{3,2,1,0:T(8,128)S(1)}, f32[16,12,8,128]{3,2,1,0:T(8,128)S(1)}, u32[]{:S(2)}, u32[]{:S(2)}) collective-permute-start(f32[16,12,8,128]{3,2,1,0:T(8,128)S(1)} %get-tuple-element.46.s_ref), channel_id=1, source_target_pairs={{0,4},{4,0},{1,5},{5,1},{2,6},{6,2},{3,7},{7,3},{8,12},{12,8},{9,1... | collective-permute-start | bytes 2359304 | tf_op jit(solution)/shard_map/ppermute | solution.py:348
  22.5 9.2 %collective-permute-start.5 = (f32[16,4,8,128]{3,2,1,0:T(8,128)S(1)}, f32[16,4,8,128]{3,2,1,0:T(8,128)S(1)}, u32[]{:S(2)}, u32[]{:S(2)}) collective-permute-start(f32[16,4,8,128]{3,2,1,0:T(8,128)S(1)} %get-tuple-element.47), channel_id=1, source_target_pairs={{0,8},{16,24},{8,0},{24,16},{1,9},{17,25},{9,1},{25,17},{2,10},{18... | collective-permute-start | bytes 786440 | tf_op jit(solution)/shard_map/ppermute | solution.py:341
  22.6 9.2 %collective-permute-start.6 = (f32[16,4,8,128]{3,2,1,0:T(8,128)S(1)}, f32[16,4,8,128]{3,2,1,0:T(8,128)S(1)}, u32[]{:S(2)}, u32[]{:S(2)}) collective-permute-start(f32[16,4,8,128]{3,2,1,0:T(8,128)S(1)} %get-tuple-element.48), channel_id=1, source_target_pairs={{8,16},{16,8},{9,17},{17,9},{10,18},{18,10},{11,19},{19,11},{12,20... | collective-permute-start | bytes 786440 | tf_op jit(solution)/shard_map/ppermute | solution.py:341
  23.2 5.4 %collective-permute-start.8 = (f32[12,8,128]{2,1,0:T(8,128)S(1)}, f32[12,8,128]{2,1,0:T(8,128)S(1)}, u32[]{:S(2)}, u32[]{:S(2)}) collective-permute-start(f32[12,8,128]{2,1,0:T(8,128)S(1)} %get-tuple-element.49), channel_id=1, source_target_pairs={{1,2},{2,1},{5,6},{6,5},{9,10},{10,9},{13,14},{14,13},{17,18},{18,... | collective-permute-start | bytes 147464 | tf_op jit(solution)/shard_map/ppermute | solution.py:341
  23.9 6.5 %collective-permute-start.7 = (f32[12,8,128]{2,1,0:T(8,128)S(1)}, f32[12,8,128]{2,1,0:T(8,128)S(1)}, u32[]{:S(2)}, u32[]{:S(2)}) collective-permute-start(f32[12,8,128]{2,1,0:T(8,128)S(1)} %get-tuple-element.49), channel_id=1, source_target_pairs={{0,1},{2,3},{1,0},{3,2},{4,5},{6,7},{5,4},{7,6},{8,9},{10,11},{9,8... | collective-permute-start | bytes 147464 | tf_op jit(solution)/shard_map/ppermute | solution.py:341
  33.7 17.5 %collective-permute-start.14 = (f32[2,96,128]{2,1,0:T(8,128)S(1)}, f32[2,96,128]{2,1,0:T(8,128)S(1)}, u32[]{:S(2)}, u32[]{:S(2)}) collective-permute-start(f32[2,96,128]{2,1,0:T(8,128)S(1)} %get-tuple-element.67), channel_id=1, source_target_pairs={{0,1},{1,2},{2,3},{3,0},{4,5},{5,6},{6,7},{7,4},{8,9},{9,10},{10,1... | collective-permute-start | bytes 294920 | tf_op jit(solution)/shard_map/ppermute | solution.py:314
  35.4 15.9 %collective-permute-start.15 = (f32[2,96,128]{2,1,0:T(8,128)S(1)}, f32[2,96,128]{2,1,0:T(8,128)S(1)}, u32[]{:S(2)}, u32[]{:S(2)}) collective-permute-start(f32[2,96,128]{2,1,0:T(8,128)S(1)} %get-tuple-element.68), channel_id=1, source_target_pairs={{0,2},{1,3},{2,0},{3,1},{4,6},{5,7},{6,4},{7,5},{8,10},{9,11},{10,... | collective-permute-start | bytes 294920 | tf_op jit(solution)/shard_map/ppermute | solution.py:314
  38.0 13.3 %collective-permute-start.16 = (f32[2,96,128]{2,1,0:T(8,128)S(1)}, f32[2,96,128]{2,1,0:T(8,128)S(1)}, u32[]{:S(2)}, u32[]{:S(2)}) collective-permute-start(f32[2,96,128]{2,1,0:T(8,128)S(1)} %get-tuple-element.69), channel_id=1, source_target_pairs={{0,3},{1,0},{2,1},{3,2},{4,7},{5,4},{6,5},{7,6},{8,11},{9,8},{10,9... | collective-permute-start | bytes 294920 | tf_op jit(solution)/shard_map/ppermute | solution.py:314
  39.3 20.2 %collective-permute-start.13 = (f32[8,64]{1,0:T(8,128)S(1)}, f32[8,64]{1,0:T(8,128)S(1)}, u32[]{:S(2)}, u32[]{:S(2)}) collective-permute-start(f32[8,64]{1,0:T(8,128)S(1)} %copy-done.4), channel_id=1, source_target_pairs={{0,4},{4,0},{1,5},{5,1},{2,6},{6,2},{3,7},{7,3},{8,12},{12,8},{9,1... | collective-permute-start | bytes 6152 | tf_op jit(solution)/shard_map/ppermute | solution.py:314
  40.2 7.9 %collective-permute-start.10 = (s32[1,12]{1,0:T(1,128)S(1)}, s32[1,12]{1,0:T(1,128)S(1)}, u32[]{:S(2)}, u32[]{:S(2)}) collective-permute-start(s32[1,12]{1,0:T(1,128)S(1)} %bitcast.5), channel_id=1, source_target_pairs={{0,8},{4,28},{8,16},{12,4},{16,24},{20,12},{24,0},{28,20},{1,9},{5... | collective-permute-start | bytes 152 | tf_op jit(solution)/shard_map/ppermute | solution.py:330
  48.1 5.4 %collective-permute-start.12 = (s32[1,12]{1,0:T(1,128)S(1)}, s32[1,12]{1,0:T(1,128)S(1)}, u32[]{:S(2)}, u32[]{:S(2)}) collective-permute-start(s32[1,12]{1,0:T(1,128)S(1)} %bitcast.6), channel_id=1, source_target_pairs={{0,16},{8,24},{16,0},{24,8},{1,17},{9,25},{17,1},{25,9},{2,18},{10... | collective-permute-start | bytes 152 | tf_op jit(solution)/shard_map/ppermute | solution.py:314
  51.3 1.2 %collective-permute-start.11 = (s32[1,12]{1,0:T(1,128)S(1)}, s32[1,12]{1,0:T(1,128)S(1)}, u32[]{:S(2)}, u32[]{:S(2)}) collective-permute-start(s32[1,12]{1,0:T(1,128)S(1)} %collective-permute-done.10), channel_id=1, source_target_pairs={{0,4},{4,0},{1,5},{5,1},{2,6},{6,2},{3,7},{7,3},{8,12},{12,8},{9,1... | collective-permute-start | bytes 152 | tf_op jit(solution)/shard_map/ppermute | solution.py:332
  51.3 5.7 %collective-permute-start.22 = (f32[2,96,128]{2,1,0:T(8,128)S(1)}, f32[2,96,128]{2,1,0:T(8,128)S(1)}, u32[]{:S(2)}, u32[]{:S(2)}) collective-permute-start(f32[2,96,128]{2,1,0:T(8,128)S(1)} %shard_map.95.refs_0_), channel_id=1, source_target_pairs={{0,24},{8,0},{16,8},{24,16},{1,25},{9,1},{17,9},{25,17},{2,26},{10... | collective-permute-start | bytes 294920 | tf_op jit(solution)/shard_map/ppermute | solution.py:314
  52.2 6.8 %collective-permute-start.20 = (f32[2,96,128]{2,1,0:T(8,128)S(1)}, f32[2,96,128]{2,1,0:T(8,128)S(1)}, u32[]{:S(2)}, u32[]{:S(2)}) collective-permute-start(f32[2,96,128]{2,1,0:T(8,128)S(1)} %shard_map.95.refs_0_), channel_id=1, source_target_pairs={{0,16},{8,24},{16,0},{24,8},{1,17},{9,25},{17,1},{25,9},{2,18},{10... | collective-permute-start | bytes 294920 | tf_op jit(solution)/shard_map/ppermute | solution.py:314
  52.5 6.5 %collective-permute-start.18 = (f32[2,96,128]{2,1,0:T(8,128)S(1)}, f32[2,96,128]{2,1,0:T(8,128)S(1)}, u32[]{:S(2)}, u32[]{:S(2)}) collective-permute-start(f32[2,96,128]{2,1,0:T(8,128)S(1)} %shard_map.95.refs_0_), channel_id=1, source_target_pairs={{0,8},{8,16},{16,24},{24,0},{1,9},{9,17},{17,25},{25,1},{2,10},{10... | collective-permute-start | bytes 294920 | tf_op jit(solution)/shard_map/ppermute | solution.py:314
  53.4 7.3 %collective-permute-start.17 = (f32[2,96,128]{2,1,0:T(8,128)S(1)}, f32[2,96,128]{2,1,0:T(8,128)S(1)}, u32[]{:S(2)}, u32[]{:S(2)}) collective-permute-start(f32[2,96,128]{2,1,0:T(8,128)S(1)} %shard_map.95.refs_0_), channel_id=1, source_target_pairs={{0,4},{4,0},{1,5},{5,1},{2,6},{6,2},{3,7},{7,3},{8,12},{12,8},{9,1... | collective-permute-start | bytes 294920 | tf_op jit(solution)/shard_map/ppermute | solution.py:314
  57.1 4.8 %collective-permute-start.23 = (f32[2,96,128]{2,1,0:T(8,128)S(1)}, f32[2,96,128]{2,1,0:T(8,128)S(1)}, u32[]{:S(2)}, u32[]{:S(2)}) collective-permute-start(f32[2,96,128]{2,1,0:T(8,128)S(1)} %collective-permute-done.22.refs_0_), channel_id=1, source_target_pairs={{0,4},{4,0},{1,5},{5,1},{2,6},{6,2},{3,7},{7,3},{8,12},{12,8},{9,1... | collective-permute-start | bytes 294920 | tf_op jit(solution)/shard_map/ppermute | solution.py:314
  58.9 1.9 %collective-permute-start.21 = (f32[2,96,128]{2,1,0:T(8,128)S(1)}, f32[2,96,128]{2,1,0:T(8,128)S(1)}, u32[]{:S(2)}, u32[]{:S(2)}) collective-permute-start(f32[2,96,128]{2,1,0:T(8,128)S(1)} %collective-permute-done.20.refs_4_), channel_id=1, source_target_pairs={{0,4},{4,0},{1,5},{5,1},{2,6},{6,2},{3,7},{7,3},{8,12},{12,8},{9,1... | collective-permute-start | bytes 294920 | tf_op jit(solution)/shard_map/ppermute | solution.py:314
  58.9 1.9 %collective-permute-start.19 = (f32[2,96,128]{2,1,0:T(8,128)S(1)}, f32[2,96,128]{2,1,0:T(8,128)S(1)}, u32[]{:S(2)}, u32[]{:S(2)}) collective-permute-start(f32[2,96,128]{2,1,0:T(8,128)S(1)} %collective-permute-done.18.refs_2_), channel_id=1, source_target_pairs={{0,4},{4,0},{1,5},{5,1},{2,6},{6,2},{3,7},{7,3},{8,12},{12,8},{9,1... | collective-permute-start | bytes 294920 | tf_op jit(solution)/shard_map/ppermute | solution.py:314

commit v9 on v8

--- a/solution.py
+++ b/solution.py
@@ -49,12 +49,16 @@
     return lax.rem(lax.axis_index(axis), jnp.int32(2))
 
 
-def rim_kernel(turn, f_ref, out_ref, sem):
+def rim_kernel(f_ref, first_ref, second_ref, sems):
     top, parity = f_ref.shape[1] - REACH, odd("gx")
-    start = top * (parity if turn else 1 - parity)
-    copy = pltpu.make_async_copy(f_ref.at[:, pl.ds(start, REACH)], out_ref, sem)
-    copy.start()
-    copy.wait()
+    copies = [
+        pltpu.make_async_copy(f_ref.at[:, pl.ds(start, REACH)], target, sems.at[i])
+        for i, (start, target) in enumerate(((top * (1 - parity), first_ref), (top * parity, second_ref)))
+    ]
+    for copy in copies:
+        copy.start()
+    for copy in copies:
+        copy.wait()
 
 
 def pack_rim(v, values, rim_ref):
@@ -314,10 +318,14 @@
     return lax.ppermute(x, axis, [(i, (i + k) % count) for i in range(count)])
 
 
+def swapped(x, axis, k):
+    return lax.ppermute(x, axis, [(i, i ^ k) for i in range(lax.axis_size(axis))])
+
+
 def gathered(x, axis):
     count = lax.axis_size(axis)
-    if count <= 4:
-        return [x] + [shifted(x, axis, k) for k in range(1, count)]
+    if count in (2, 4):
+        return [x] + [swapped(x, axis, k) for k in range(1, count)]
     blocks = lax.all_gather(x, axis)
     return [blocks[k] for k in range(count)]
 
@@ -326,12 +334,12 @@
     count = lax.axis_size("gx")
     if count != 4 or lax.axis_size("gy") != 2:
         return gathered(x, "gx")
-    ring = [((i, j), ((i + (1, 3)[j]) % 4, j)) for i in range(4) for j in range(2)]
-    mine = lax.ppermute(x, ("gx", "gy"), [(2 * i + j, 2 * k + l) for (i, j), (k, l) in ring])
-    across = shifted(x, "gx", 2)
+    links = [(2 * i + j, 2 * (i ^ (j + 1)) + j) for i in range(4) for j in range(2)]
+    mine = lax.ppermute(x, ("gx", "gy"), links)
+    across = swapped(x, "gx", 3)
     theirs = lax.ppermute(mine, "gy", [(0, 1), (1, 0)])
     upper = lax.axis_index("gy") == 1
-    return [x, jnp.where(upper, theirs, mine), across, jnp.where(upper, mine, theirs)]
+    return [x, jnp.where(upper, theirs, mine), jnp.where(upper, mine, theirs), across]
 
 
 def paired(first, second, axis):
@@ -363,9 +371,8 @@
     chunk = (pairs, nx * ny, 2 * HALF)
     barrier = lax.optimization_barrier
 
-    first, second = (
-        call(functools.partial(rim_kernel, turn), [(rim, F32)], [HBM], (fields,), [pltpu.SemaphoreType.DMA])[0]
-        for turn in (0, 1)
+    first, second = call(
+        rim_kernel, [(rim, F32), (rim, F32)], [HBM], (fields,), [pltpu.SemaphoreType.DMA((2,))]
     )
     x1, x2 = paired(first, second, "gx")
     packed, same = call(

time: 63.9 us -> 61.1 us (0.956)
  waiting for transfers between devices: 13.2 us -> 8.04 us
  starting transfers between devices: 35.5 us -> 37.8 us
    ppermute x12 -> x3, starting transfers between devices: 11.4 us -> 4.88 us  [shifted(): return lax.ppermute(x, axis, [(i, (i + k) % count) for i in range(count)])]
    ppermute x1 -> x10, starting transfers between devices: 6.56 us -> 12.5 us  [the longest x9 6.59 us: swapped(): lax.ppermute(x, axis, [(i, i ^ k) for i in range(lax.axis_size(axis))])]
    ppermute x12 -> x3, waiting for transfers between devices: 5.51 us -> 0.01 us  [shifted(): return lax.ppermute(x, axis, [(i, (i + k) % count) for i in range(count)])]
    ppermute x1 -> x10, waiting for transfers between devices: 1.3 us -> 6.18 us  [the longest x9 4.63 us: swapped(): lax.ppermute(x, axis, [(i, i ^ k) for i in range(lax.axis_size(axis))])]
    ppermute x8, waiting for transfers between devices: 6.36 us -> 1.85 us  [paired(): out.append(lax.ppermute(x, axis, links + [(j, i) for i, j in links]))]
    ppermute x8, starting transfers between devices: 17 us -> 19.8 us  [paired(): out.append(lax.ppermute(x, axis, links + [(j, i) for i, j in links]))]
    pallas_call x12 -> x11, Pallas kernels: 11.4 us -> 11.4 us  [call(): pl.pallas_call(kernel, out_shape=tuple((jax.ShapeDtypeStruct(s, d) for s,...]
  transfers between devices with their start and end apart: 24 -> 24, of which waited for: 7 -> 5; matrix products, arithmetic and copies ran while one was open for 0% -> 0% of each run, Pallas kernels for 9% -> 10%
where the time goes in v9:
time: 61.1 us; the launch traced here: 60.8 us
  starting transfers between devices  37.8 us (62%)
  Pallas kernels  11.4 us (19%)
  waiting for transfers between devices  8.04 us (13%)
  local copies, waits for them, and re-layouts  2.53 us (4%)
  between operations  0.88 us (1%)
    ppermute x8, starting transfers between devices, paired(): out.append(lax.ppermute(x, axis, links + [(j, i) for i, j in links]))  19.8 us
    pallas_call x11, Pallas kernels, call(): pl.pallas_call(kernel, out_shape=tuple((jax.ShapeDtypeStruct(s, d) for s,...  11.4 us
    ppermute x9, starting transfers between devices, swapped(): lax.ppermute(x, axis, [(i, i ^ k) for i in range(lax.axis_size(axis))])  6.59 us
    ppermute x1, starting transfers between devices, gathered_on_chip(): mine = lax.ppermute(x, ('gx', 'gy'), links)  5.86 us
    ppermute x3, starting transfers between devices, shifted(): return lax.ppermute(x, axis, [(i, (i + k) % count) for i in range(count)])  4.88 us
    ppermute x9, waiting for transfers between devices, swapped(): lax.ppermute(x, axis, [(i, i ^ k) for i in range(lax.axis_size(axis))])  4.63 us
    unnamed x14, local copies, waits for them, and re-layouts  2.53 us
    ppermute x8, waiting for transfers between devices, paired(): out.append(lax.ppermute(x, axis, links + [(j, i) for i, j in links]))  1.85 us
  transfers between devices with their start and end apart: 24, of which 5 were waited for; matrix products, arithmetic and copies ran while one was open for 0% of the time, Pallas kernels for 10%

profile of v9, /device:TPU:0, one launch (start us, length us, event | category | flops | bytes accessed | tf_op | source)
XLA Modules:
  0.0 60.8 jit_solution(12008938986941981708)
XLA Ops:
  0.6 0.6 collective-permute-start.2
  1.2 1.1 %copy-done = f32[16,12,8,128]{3,2,1,0:T(8,128)S(1)} copy-done((f32[16,12,8,128]{3,2,1,0:T(8,128)S(1)}, f32[16,12,8,128]{3,2,1,0:T(8,128)}, u32[]{:S(2)}) %copy-start) | copy-done | bytes 786456
  2.3 0.1 shard_map.87
  2.4 2.6 %collective-permute-start = (f32[16,4,8,128]{3,2,1,0:T(8,128)S(1)}, f32[16,4,8,128]{3,2,1,0:T(8,128)S(1)}, u32[]{:S(2)}, u32[]{:S(2)}) collective-permute-start(f32[16,4,8,128]{3,2,1,0:T(8,128)S(1)} %get-tuple-element.39), channel_id=1, source_target_pairs={{0,8},{16,24},{8,0},{24,16},{1,9},{17,25},{9,1},{25,17},{2,10},{18... | collective-permute-start | bytes 786440 | tf_op jit(solution)/shard_map/ppermute | solution.py:349
  4.9 0.7 %collective-permute-start.1 = (f32[16,4,8,128]{3,2,1,0:T(8,128)S(1)}, f32[16,4,8,128]{3,2,1,0:T(8,128)S(1)}, u32[]{:S(2)}, u32[]{:S(2)}) collective-permute-start(f32[16,4,8,128]{3,2,1,0:T(8,128)S(1)} %get-tuple-element.40), channel_id=1, source_target_pairs={{8,16},{16,8},{9,17},{17,9},{10,18},{18,10},{11,19},{19,11},{12,20... | collective-permute-start | bytes 786440 | tf_op jit(solution)/shard_map/ppermute | solution.py:349
  5.6 0.0 copy-start.4
  5.6 1.7 %shard_map.86 = (f32[12,8,128]{2,1,0:T(8,128)S(1)}, f32[16,12,8,128]{3,2,1,0:T(8,128)S(1)}) custom-call(f32[16,12,8,128]{3,2,1,0:T(8,128)S(1)} %copy-done), custom_call_target="tpu_custom_call" | custom-call | tf_op jit(solution)/shard_map/pallas_call | solution.py:25
  7.4 0.7 %collective-permute-start.4 = (f32[12,8,128]{2,1,0:T(8,128)S(1)}, f32[12,8,128]{2,1,0:T(8,128)S(1)}, u32[]{:S(2)}, u32[]{:S(2)}) collective-permute-start(f32[12,8,128]{2,1,0:T(8,128)S(1)} %get-tuple-element.41), channel_id=1, source_target_pairs={{1,2},{2,1},{5,6},{6,5},{9,10},{10,9},{13,14},{14,13},{17,18},{18,... | collective-permute-start | bytes 147464 | tf_op jit(solution)/shard_map/ppermute | solution.py:349
  8.0 4.5 %collective-permute-start.3 = (f32[12,8,128]{2,1,0:T(8,128)S(1)}, f32[12,8,128]{2,1,0:T(8,128)S(1)}, u32[]{:S(2)}, u32[]{:S(2)}) collective-permute-start(f32[12,8,128]{2,1,0:T(8,128)S(1)} %get-tuple-element.41), channel_id=1, source_target_pairs={{0,1},{2,3},{1,0},{3,2},{4,5},{6,7},{5,4},{7,6},{8,9},{10,11},{9,8... | collective-permute-start | bytes 147464 | tf_op jit(solution)/shard_map/ppermute | solution.py:349
  12.5 0.7 %copy-done.3 = f32[16,16]{1,0:T(8,128)S(1)} copy-done((f32[16,16]{1,0:T(8,128)S(1)}, f32[16,16]{1,0:T(8,128)}, u32[]{:S(2)}) %copy-start.3) | copy-done | bytes 1048
  13.2 0.7 %copy-done.5 = f32[3,16]{1,0:T(4,128)S(1)} copy-done((f32[3,16]{1,0:T(4,128)S(1)}, f32[3,16]{1,0:T(4,128)}, u32[]{:S(2)}) %copy-start.5) | copy-done | bytes 216
  13.9 0.6 %shard_map.88 = (bf16[256,256]{1,0:T(8,128)(2,1)S(1)}, bf16[256,128]{1,0:T(8,128)(2,1)S(1)}, bf16[128,128]{1,0:T(8,128)(2,1)S(1)}, f32[16,2,8,128]{3,2,1,0:T(8,128)S(1)}) custom-call(f32[16,16]{1,0:T(8,128)S(1)} %copy-done.3, f32[3,16]{1,0:T(4,128)S(1)} %copy-done.5), custom_call_target="tpu_custom_call" | custom-call | tf_op jit(solution)/shard_map/pallas_call | solution.py:25
  14.5 0.0 collective-permute-done.4.z2_ref
  14.5 0.1 collective-permute-done.3.z1_ref
  14.6 1.8 %shard_map.89 = (f32[16,12,8,128]{3,2,1,0:T(8,128)S(1)}, f32[16,4,8,128]{3,2,1,0:T(8,128)S(1)}, f32[16,4,8,128]{3,2,1,0:T(8,128)S(1)}, f32[12,8,128]{2,1,0:T(8,128)S(1)}) custom-call(f32[16,12,8,128]{3,2,1,0:T(8,128)S(1)} %get-tuple-element.38.f_ref, f32[16,4,8,128]{3,2,1,0:T(8,128)S(1)} %collective-permute-done.x1_ref, ...), custom_call_target="tpu_custom_call" | custom-call | tf_op jit(solution)/shard_map/pallas_call | solution.py:25
  16.4 0.0 copy-start.6
  16.4 0.0 copy-start.2
  16.4 0.1 collective-permute-start.9
  16.5 5.7 %collective-permute-start.5 = (f32[16,4,8,128]{3,2,1,0:T(8,128)S(1)}, f32[16,4,8,128]{3,2,1,0:T(8,128)S(1)}, u32[]{:S(2)}, u32[]{:S(2)}) collective-permute-start(f32[16,4,8,128]{3,2,1,0:T(8,128)S(1)} %get-tuple-element.51), channel_id=1, source_target_pairs={{0,8},{16,24},{8,0},{24,16},{1,9},{17,25},{9,1},{25,17},{2,10},{18... | collective-permute-start | bytes 786440 | tf_op jit(solution)/shard_map/ppermute | solution.py:349
  22.2 0.7 %collective-permute-start.6 = (f32[16,4,8,128]{3,2,1,0:T(8,128)S(1)}, f32[16,4,8,128]{3,2,1,0:T(8,128)S(1)}, u32[]{:S(2)}, u32[]{:S(2)}) collective-permute-start(f32[16,4,8,128]{3,2,1,0:T(8,128)S(1)} %get-tuple-element.52), channel_id=1, source_target_pairs={{8,16},{16,8},{9,17},{17,9},{10,18},{18,10},{11,19},{19,11},{12,20... | collective-permute-start | bytes 786440 | tf_op jit(solution)/shard_map/ppermute | solution.py:349
  22.9 0.7 %collective-permute-start.8 = (f32[12,8,128]{2,1,0:T(8,128)S(1)}, f32[12,8,128]{2,1,0:T(8,128)S(1)}, u32[]{:S(2)}, u32[]{:S(2)}) collective-permute-start(f32[12,8,128]{2,1,0:T(8,128)S(1)} %get-tuple-element.53), channel_id=1, source_target_pairs={{1,2},{2,1},{5,6},{6,5},{9,10},{10,9},{13,14},{14,13},{17,18},{18,... | collective-permute-start | bytes 147464 | tf_op jit(solution)/shard_map/ppermute | solution.py:349
  23.6 4.5 %collective-permute-start.7 = (f32[12,8,128]{2,1,0:T(8,128)S(1)}, f32[12,8,128]{2,1,0:T(8,128)S(1)}, u32[]{:S(2)}, u32[]{:S(2)}) collective-permute-start(f32[12,8,128]{2,1,0:T(8,128)S(1)} %get-tuple-element.53), channel_id=1, source_target_pairs={{0,1},{2,3},{1,0},{3,2},{4,5},{6,7},{5,4},{7,6},{8,9},{10,11},{9,8... | collective-permute-start | bytes 147464 | tf_op jit(solution)/shard_map/ppermute | solution.py:349
  28.0 0.3 shard_map.90.zf_ref
  28.3 0.0 collective-permute-done.8.z2_ref
  28.3 1.8 %collective-permute-done.7.z1_ref = f32[12,8,128]{2,1,0:T(8,128)S(1)} collective-permute-done((f32[12,8,128]{2,1,0:T(8,128)S(1)}, f32[12,8,128]{2,1,0:T(8,128)S(1)}, u32[]{:S(2)}, u32[]{:S(2)}) %collective-permute-start.7) | collective-permute-done | bytes 49184 | tf_op jit(solution)/shard_map/ppermute | solution.py:349
  30.1 0.0 collective-permute-done.5.x1_ref
  30.1 0.0 collective-permute-done.6.x2_ref
  30.1 0.0 collective-permute-done.9.beside_ref
  30.1 2.0 %shard_map.91 = (f32[16,12,8,128]{3,2,1,0:T(8,128)S(1)}, f32[2,96,128]{2,1,0:T(8,128)S(1)}, f32[2,96,128]{2,1,0:T(8,128)S(1)}, f32[2,96,128]{2,1,0:T(8,128)S(1)}, f32[2,96,128]{2,1,0:T(8,128)S(1)}) custom-call(f32[16,12,8,128]{3,2,1,0:T(8,128)S(1)} %get-tuple-element.38.f_ref, f32[16,12,8,128]{3,2,1,0:T(8,128)S(1)} %get-tuple-element.50.s_ref, ...), custom_call_target="tpu_custom_call" | custom-call | tf_op jit(solution)/shard_map/pallas_call | solution.py:25
  32.1 2.1 %collective-permute-start.14 = (f32[2,96,128]{2,1,0:T(8,128)S(1)}, f32[2,96,128]{2,1,0:T(8,128)S(1)}, u32[]{:S(2)}, u32[]{:S(2)}) collective-permute-start(f32[2,96,128]{2,1,0:T(8,128)S(1)} %get-tuple-element.71), channel_id=1, source_target_pairs={{0,1},{1,2},{2,3},{3,0},{4,5},{5,6},{6,7},{7,4},{8,9},{9,10},{10,1... | collective-permute-start | bytes 294920 | tf_op jit(solution)/shard_map/ppermute | solution.py:318
  34.2 1.4 %collective-permute-start.15 = (f32[2,96,128]{2,1,0:T(8,128)S(1)}, f32[2,96,128]{2,1,0:T(8,128)S(1)}, u32[]{:S(2)}, u32[]{:S(2)}) collective-permute-start(f32[2,96,128]{2,1,0:T(8,128)S(1)} %get-tuple-element.72), channel_id=1, source_target_pairs={{0,2},{1,3},{2,0},{3,1},{4,6},{5,7},{6,4},{7,5},{8,10},{9,11},{10,... | collective-permute-start | bytes 294920 | tf_op jit(solution)/shard_map/ppermute | solution.py:318
  35.6 1.4 %collective-permute-start.16 = (f32[2,96,128]{2,1,0:T(8,128)S(1)}, f32[2,96,128]{2,1,0:T(8,128)S(1)}, u32[]{:S(2)}, u32[]{:S(2)}) collective-permute-start(f32[2,96,128]{2,1,0:T(8,128)S(1)} %get-tuple-element.73), channel_id=1, source_target_pairs={{0,3},{1,0},{2,1},{3,2},{4,7},{5,4},{6,5},{7,6},{8,11},{9,8},{10,9... | collective-permute-start | bytes 294920 | tf_op jit(solution)/shard_map/ppermute | solution.py:318
  37.0 0.9 %shard_map.92 = f32[16,12,8,128]{3,2,1,0:T(8,128)} custom-call(f32[16,12,8,128]{3,2,1,0:T(8,128)S(1)} %get-tuple-element.66.in_ref), custom_call_target="tpu_custom_call" | custom-call | tf_op jit(solution)/shard_map/pallas_call | solution.py:25
  37.9 5.9 %collective-permute-start.10 = (s32[1,12]{1,0:T(1,128)S(1)}, s32[1,12]{1,0:T(1,128)S(1)}, u32[]{:S(2)}, u32[]{:S(2)}) collective-permute-start(s32[1,12]{1,0:T(1,128)S(1)} %bitcast.5), channel_id=1, source_target_pairs={{0,8},{4,20},{8,0},{12,28},{16,24},{20,4},{24,16},{28,12},{1,9},{5... | collective-permute-start | bytes 152 | tf_op jit(solution)/shard_map/ppermute | solution.py:338
  43.8 1.5 %collective-permute-done.10 = s32[1,12]{1,0:T(1,128)S(1)} collective-permute-done((s32[1,12]{1,0:T(1,128)S(1)}, s32[1,12]{1,0:T(1,128)S(1)}, u32[]{:S(2)}, u32[]{:S(2)}) %collective-permute-start.10) | collective-permute-done | bytes 80 | tf_op jit(solution)/shard_map/ppermute | solution.py:338
  45.3 2.5 %collective-permute-start.12 = (s32[1,12]{1,0:T(1,128)S(1)}, s32[1,12]{1,0:T(1,128)S(1)}, u32[]{:S(2)}, u32[]{:S(2)}) collective-permute-start(s32[1,12]{1,0:T(1,128)S(1)} %bitcast.6), channel_id=1, source_target_pairs={{0,24},{8,16},{16,8},{24,0},{1,25},{9,17},{17,9},{25,1},{2,26},{10... | collective-permute-start | bytes 152 | tf_op jit(solution)/shard_map/ppermute | solution.py:322
  47.8 0.9 %collective-permute-start.22 = (f32[2,96,128]{2,1,0:T(8,128)S(1)}, f32[2,96,128]{2,1,0:T(8,128)S(1)}, u32[]{:S(2)}, u32[]{:S(2)}) collective-permute-start(f32[2,96,128]{2,1,0:T(8,128)S(1)} %shard_map.94.refs_0_), channel_id=1, source_target_pairs={{0,24},{8,16},{16,8},{24,0},{1,25},{9,17},{17,9},{25,1},{2,26},{10... | collective-permute-start | bytes 294920 | tf_op jit(solution)/shard_map/ppermute | solution.py:322
  48.7 2.7 %collective-permute-start.20 = (f32[2,96,128]{2,1,0:T(8,128)S(1)}, f32[2,96,128]{2,1,0:T(8,128)S(1)}, u32[]{:S(2)}, u32[]{:S(2)}) collective-permute-start(f32[2,96,128]{2,1,0:T(8,128)S(1)} %shard_map.94.refs_0_), channel_id=1, source_target_pairs={{0,16},{8,24},{16,0},{24,8},{1,17},{9,25},{17,1},{25,9},{2,18},{10... | collective-permute-start | bytes 294920 | tf_op jit(solution)/shard_map/ppermute | solution.py:322
  51.4 0.0 collective-permute-start.18
  51.4 0.1 collective-permute-start.17
  51.5 2.9 %collective-permute-done.22.refs_0_ = f32[2,96,128]{2,1,0:T(8,128)S(1)} collective-permute-done((f32[2,96,128]{2,1,0:T(8,128)S(1)}, f32[2,96,128]{2,1,0:T(8,128)S(1)}, u32[]{:S(2)}, u32[]{:S(2)}) %collective-permute-start.22) | collective-permute-done | bytes 98336 | tf_op jit(solution)/shard_map/ppermute | solution.py:322
  54.4 1.7 %collective-permute-done.20.refs_4_ = f32[2,96,128]{2,1,0:T(8,128)S(1)} collective-permute-done((f32[2,96,128]{2,1,0:T(8,128)S(1)}, f32[2,96,128]{2,1,0:T(8,128)S(1)}, u32[]{:S(2)}, u32[]{:S(2)}) %collective-permute-start.20) | collective-permute-done | bytes 98336 | tf_op jit(solution)/shard_map/ppermute | solution.py:322
  56.1 0.1 collective-permute-start.21
  56.2 0.4 collective-permute-start.19
  56.6 0.1 pad_add_fusion.rank_ref
  56.7 1.2 %shard_map.93.factor_ref = bf16[4,2,768,192]{3,2,1,0:T(8,128)(2,1)S(1)} custom-call(s32[1,48]{1,0:T(1,128)S(1)} %pad_add_fusion.rank_ref, f32[48,96]{1,0:T(8,128)S(1)} %copy-done.2, f32[8,64]{1,0:T(8,128)S(1)} %copy-done.4, f32[8,64]{1,0:T(8,128)S(1)} %collective-permute-done.13.refs_1_), custom_call_target="tpu_custom_call" | custom-call | tf_op jit(solution)/shard_map/pallas_call | solution.py:25
  58.0 1.1 %shard_map.95.total_ref = f32[768,256]{1,0:T(8,128)S(1)} custom-call(bf16[4,2,768,192]{3,2,1,0:T(8,128)(2,1)S(1)} %shard_map.93.factor_ref, f32[2,96,128]{2,1,0:T(8,128)S(1)} %shard_map.94.refs_0_, f32[2,96,128]{2,1,0:T(8,128)S(1)} %collective-permute-done.17.refs_1_, f32[2,96,128]{2,1,0:T(8,128)S(1)} %collective-permute-done.18.refs_2_, ...), custom_call_target="tpu_custom_call" | custom-call | tf_op jit(solution)/shard_map/pallas_call | solution.py:25
  59.1 1.7 %shard_map.96 = f32[4,768,54]{2,1,0:T(8,128)} custom-call(bf16[4,2,768,192]{3,2,1,0:T(8,128)(2,1)S(1)} %shard_map.93.factor_ref, f32[768,256]{1,0:T(8,128)S(1)} %shard_map.95.total_ref, f32[2,96,128]{2,1,0:T(8,128)S(1)} %collective-permute-done.22.refs_0_, f32[2,96,128]{2,1,0:T(8,128)S(1)} %collective-permute-done.23.refs_1_), custom_call_target="tpu_custom_call" | custom-call | tf_op jit(solution)/shard_map/pallas_call | solution.py:25
  (27 shorter events, 0.1 us)
Async XLA Ops:
  0.6 13.9 %collective-permute-start.2 = (f32[16,12,8,128]{3,2,1,0:T(8,128)}, f32[16,12,8,128]{3,2,1,0:T(8,128)S(1)}, u32[]{:S(2)}, u32[]{:S(2)}) collective-permute-start(f32[16,12,8,128]{3,2,1,0:T(8,128)} %f_ref.3), channel_id=1, source_target_pairs={{0,4},{4,0},{1,5},{5,1},{2,6},{6,2},{3,7},{7,3},{8,12},{12,8},{9,1... | collective-permute-start | bytes 2359304 | tf_op jit(solution)/shard_map/ppermute | solution.py:356
  1.2 1.1 %copy-start = (f32[16,12,8,128]{3,2,1,0:T(8,128)S(1)}, f32[16,12,8,128]{3,2,1,0:T(8,128)}, u32[]{:S(2)}) copy-start(f32[16,12,8,128]{3,2,1,0:T(8,128)} %f_ref.3) | copy-start | bytes 2359300
  2.3 25.7 %copy-start.1 = (f32[128,54]{0,1:T(8,128)S(1)}, f32[128,54]{0,1:T(8,128)}, u32[]{:S(2)}) copy-start(f32[128,54]{0,1:T(8,128)} %param.13) | copy-start | bytes 82948
  2.4 12.2 %collective-permute-start = (f32[16,4,8,128]{3,2,1,0:T(8,128)S(1)}, f32[16,4,8,128]{3,2,1,0:T(8,128)S(1)}, u32[]{:S(2)}, u32[]{:S(2)}) collective-permute-start(f32[16,4,8,128]{3,2,1,0:T(8,128)S(1)} %get-tuple-element.39), channel_id=1, source_target_pairs={{0,8},{16,24},{8,0},{24,16},{1,9},{17,25},{9,1},{25,17},{2,10},{18... | collective-permute-start | bytes 786440 | tf_op jit(solution)/shard_map/ppermute | solution.py:349
  4.9 9.6 %collective-permute-start.1 = (f32[16,4,8,128]{3,2,1,0:T(8,128)S(1)}, f32[16,4,8,128]{3,2,1,0:T(8,128)S(1)}, u32[]{:S(2)}, u32[]{:S(2)}) collective-permute-start(f32[16,4,8,128]{3,2,1,0:T(8,128)S(1)} %get-tuple-element.40), channel_id=1, source_target_pairs={{8,16},{16,8},{9,17},{17,9},{10,18},{18,10},{11,19},{19,11},{12,20... | collective-permute-start | bytes 786440 | tf_op jit(solution)/shard_map/ppermute | solution.py:349
  5.6 31.4 %copy-start.4 = (f32[8,64]{1,0:T(8,128)S(1)}, f32[8,64]{1,0:T(8,128)}, u32[]{:S(2)}) copy-start(f32[8,64]{1,0:T(8,128)} %refs_0_) | copy-start | bytes 6148
  7.4 7.1 %collective-permute-start.4 = (f32[12,8,128]{2,1,0:T(8,128)S(1)}, f32[12,8,128]{2,1,0:T(8,128)S(1)}, u32[]{:S(2)}, u32[]{:S(2)}) collective-permute-start(f32[12,8,128]{2,1,0:T(8,128)S(1)} %get-tuple-element.41), channel_id=1, source_target_pairs={{1,2},{2,1},{5,6},{6,5},{9,10},{10,9},{13,14},{14,13},{17,18},{18,... | collective-permute-start | bytes 147464 | tf_op jit(solution)/shard_map/ppermute | solution.py:349
  8.0 6.5 %collective-permute-start.3 = (f32[12,8,128]{2,1,0:T(8,128)S(1)}, f32[12,8,128]{2,1,0:T(8,128)S(1)}, u32[]{:S(2)}, u32[]{:S(2)}) collective-permute-start(f32[12,8,128]{2,1,0:T(8,128)S(1)} %get-tuple-element.41), channel_id=1, source_target_pairs={{0,1},{2,3},{1,0},{3,2},{4,5},{6,7},{5,4},{7,6},{8,9},{10,11},{9,8... | collective-permute-start | bytes 147464 | tf_op jit(solution)/shard_map/ppermute | solution.py:349
  12.5 0.7 %copy-start.3 = (f32[16,16]{1,0:T(8,128)S(1)}, f32[16,16]{1,0:T(8,128)}, u32[]{:S(2)}) copy-start(f32[16,16]{1,0:T(8,128)} %kin_ref.1) | copy-start | bytes 3076
  13.2 0.7 %copy-start.5 = (f32[3,16]{1,0:T(4,128)S(1)}, f32[3,16]{1,0:T(4,128)}, u32[]{:S(2)}) copy-start(f32[3,16]{1,0:T(4,128)} %speed_ref.1) | copy-start | bytes 580
  16.4 21.5 %copy-start.6 = (s32[12]{0:T(128)S(1)}, s32[12]{0:T(128)}, u32[]{:S(2)}) copy-start(s32[12]{0:T(128)} %param.10) | copy-start | bytes 148
  16.4 40.3 %copy-start.2 = (f32[48,96]{1,0:T(8,128)S(1)}, f32[48,96]{1,0:T(8,128)}, u32[]{:S(2)}) copy-start(f32[48,96]{1,0:T(8,128)} %xf_ref) | copy-start | bytes 55300
  16.4 13.7 %collective-permute-start.9 = (f32[16,12,8,128]{3,2,1,0:T(8,128)S(1)}, f32[16,12,8,128]{3,2,1,0:T(8,128)S(1)}, u32[]{:S(2)}, u32[]{:S(2)}) collective-permute-start(f32[16,12,8,128]{3,2,1,0:T(8,128)S(1)} %get-tuple-element.50.s_ref), channel_id=1, source_target_pairs={{0,4},{4,0},{1,5},{5,1},{2,6},{6,2},{3,7},{7,3},{8,12},{12,8},{9,1... | collective-permute-start | bytes 2359304 | tf_op jit(solution)/shard_map/ppermute | solution.py:356
  16.5 13.6 %collective-permute-start.5 = (f32[16,4,8,128]{3,2,1,0:T(8,128)S(1)}, f32[16,4,8,128]{3,2,1,0:T(8,128)S(1)}, u32[]{:S(2)}, u32[]{:S(2)}) collective-permute-start(f32[16,4,8,128]{3,2,1,0:T(8,128)S(1)} %get-tuple-element.51), channel_id=1, source_target_pairs={{0,8},{16,24},{8,0},{24,16},{1,9},{17,25},{9,1},{25,17},{2,10},{18... | collective-permute-start | bytes 786440 | tf_op jit(solution)/shard_map/ppermute | solution.py:349
  22.2 7.9 %collective-permute-start.6 = (f32[16,4,8,128]{3,2,1,0:T(8,128)S(1)}, f32[16,4,8,128]{3,2,1,0:T(8,128)S(1)}, u32[]{:S(2)}, u32[]{:S(2)}) collective-permute-start(f32[16,4,8,128]{3,2,1,0:T(8,128)S(1)} %get-tuple-element.52), channel_id=1, source_target_pairs={{8,16},{16,8},{9,17},{17,9},{10,18},{18,10},{11,19},{19,11},{12,20... | collective-permute-start | bytes 786440 | tf_op jit(solution)/shard_map/ppermute | solution.py:349
  22.9 5.4 %collective-permute-start.8 = (f32[12,8,128]{2,1,0:T(8,128)S(1)}, f32[12,8,128]{2,1,0:T(8,128)S(1)}, u32[]{:S(2)}, u32[]{:S(2)}) collective-permute-start(f32[12,8,128]{2,1,0:T(8,128)S(1)} %get-tuple-element.53), channel_id=1, source_target_pairs={{1,2},{2,1},{5,6},{6,5},{9,10},{10,9},{13,14},{14,13},{17,18},{18,... | collective-permute-start | bytes 147464 | tf_op jit(solution)/shard_map/ppermute | solution.py:349
  23.6 6.5 %collective-permute-start.7 = (f32[12,8,128]{2,1,0:T(8,128)S(1)}, f32[12,8,128]{2,1,0:T(8,128)S(1)}, u32[]{:S(2)}, u32[]{:S(2)}) collective-permute-start(f32[12,8,128]{2,1,0:T(8,128)S(1)} %get-tuple-element.53), channel_id=1, source_target_pairs={{0,1},{2,3},{1,0},{3,2},{4,5},{6,7},{5,4},{7,6},{8,9},{10,11},{9,8... | collective-permute-start | bytes 147464 | tf_op jit(solution)/shard_map/ppermute | solution.py:349
  32.1 15.7 %collective-permute-start.14 = (f32[2,96,128]{2,1,0:T(8,128)S(1)}, f32[2,96,128]{2,1,0:T(8,128)S(1)}, u32[]{:S(2)}, u32[]{:S(2)}) collective-permute-start(f32[2,96,128]{2,1,0:T(8,128)S(1)} %get-tuple-element.71), channel_id=1, source_target_pairs={{0,1},{1,2},{2,3},{3,0},{4,5},{5,6},{6,7},{7,4},{8,9},{9,10},{10,1... | collective-permute-start | bytes 294920 | tf_op jit(solution)/shard_map/ppermute | solution.py:318
  34.2 13.6 %collective-permute-start.15 = (f32[2,96,128]{2,1,0:T(8,128)S(1)}, f32[2,96,128]{2,1,0:T(8,128)S(1)}, u32[]{:S(2)}, u32[]{:S(2)}) collective-permute-start(f32[2,96,128]{2,1,0:T(8,128)S(1)} %get-tuple-element.72), channel_id=1, source_target_pairs={{0,2},{1,3},{2,0},{3,1},{4,6},{5,7},{6,4},{7,5},{8,10},{9,11},{10,... | collective-permute-start | bytes 294920 | tf_op jit(solution)/shard_map/ppermute | solution.py:318
  35.6 12.2 %collective-permute-start.16 = (f32[2,96,128]{2,1,0:T(8,128)S(1)}, f32[2,96,128]{2,1,0:T(8,128)S(1)}, u32[]{:S(2)}, u32[]{:S(2)}) collective-permute-start(f32[2,96,128]{2,1,0:T(8,128)S(1)} %get-tuple-element.73), channel_id=1, source_target_pairs={{0,3},{1,0},{2,1},{3,2},{4,7},{5,4},{6,5},{7,6},{8,11},{9,8},{10,9... | collective-permute-start | bytes 294920 | tf_op jit(solution)/shard_map/ppermute | solution.py:318
  37.0 19.7 %collective-permute-start.13 = (f32[8,64]{1,0:T(8,128)S(1)}, f32[8,64]{1,0:T(8,128)S(1)}, u32[]{:S(2)}, u32[]{:S(2)}) collective-permute-start(f32[8,64]{1,0:T(8,128)S(1)} %copy-done.4), channel_id=1, source_target_pairs={{0,4},{4,0},{1,5},{5,1},{2,6},{6,2},{3,7},{7,3},{8,12},{12,8},{9,1... | collective-permute-start | bytes 6152 | tf_op jit(solution)/shard_map/ppermute | solution.py:322
  37.9 7.4 %collective-permute-start.10 = (s32[1,12]{1,0:T(1,128)S(1)}, s32[1,12]{1,0:T(1,128)S(1)}, u32[]{:S(2)}, u32[]{:S(2)}) collective-permute-start(s32[1,12]{1,0:T(1,128)S(1)} %bitcast.5), channel_id=1, source_target_pairs={{0,8},{4,20},{8,0},{12,28},{16,24},{20,4},{24,16},{28,12},{1,9},{5... | collective-permute-start | bytes 152 | tf_op jit(solution)/shard_map/ppermute | solution.py:338
  45.3 6.1 %collective-permute-start.12 = (s32[1,12]{1,0:T(1,128)S(1)}, s32[1,12]{1,0:T(1,128)S(1)}, u32[]{:S(2)}, u32[]{:S(2)}) collective-permute-start(s32[1,12]{1,0:T(1,128)S(1)} %bitcast.6), channel_id=1, source_target_pairs={{0,24},{8,16},{16,8},{24,0},{1,25},{9,17},{17,9},{25,1},{2,26},{10... | collective-permute-start | bytes 152 | tf_op jit(solution)/shard_map/ppermute | solution.py:322
  47.8 3.6 %collective-permute-start.11 = (s32[1,12]{1,0:T(1,128)S(1)}, s32[1,12]{1,0:T(1,128)S(1)}, u32[]{:S(2)}, u32[]{:S(2)}) collective-permute-start(s32[1,12]{1,0:T(1,128)S(1)} %collective-permute-done.10), channel_id=1, source_target_pairs={{0,4},{4,0},{1,5},{5,1},{2,6},{6,2},{3,7},{7,3},{8,12},{12,8},{9,1... | collective-permute-start | bytes 152 | tf_op jit(solution)/shard_map/ppermute | solution.py:340
  47.8 6.5 %collective-permute-start.22 = (f32[2,96,128]{2,1,0:T(8,128)S(1)}, f32[2,96,128]{2,1,0:T(8,128)S(1)}, u32[]{:S(2)}, u32[]{:S(2)}) collective-permute-start(f32[2,96,128]{2,1,0:T(8,128)S(1)} %shard_map.94.refs_0_), channel_id=1, source_target_pairs={{0,24},{8,16},{16,8},{24,0},{1,25},{9,17},{17,9},{25,1},{2,26},{10... | collective-permute-start | bytes 294920 | tf_op jit(solution)/shard_map/ppermute | solution.py:322
  48.7 7.4 %collective-permute-start.20 = (f32[2,96,128]{2,1,0:T(8,128)S(1)}, f32[2,96,128]{2,1,0:T(8,128)S(1)}, u32[]{:S(2)}, u32[]{:S(2)}) collective-permute-start(f32[2,96,128]{2,1,0:T(8,128)S(1)} %shard_map.94.refs_0_), channel_id=1, source_target_pairs={{0,16},{8,24},{16,0},{24,8},{1,17},{9,25},{17,1},{25,9},{2,18},{10... | collective-permute-start | bytes 294920 | tf_op jit(solution)/shard_map/ppermute | solution.py:322
  51.4 4.8 %collective-permute-start.18 = (f32[2,96,128]{2,1,0:T(8,128)S(1)}, f32[2,96,128]{2,1,0:T(8,128)S(1)}, u32[]{:S(2)}, u32[]{:S(2)}) collective-permute-start(f32[2,96,128]{2,1,0:T(8,128)S(1)} %shard_map.94.refs_0_), channel_id=1, source_target_pairs={{0,8},{8,0},{16,24},{24,16},{1,9},{9,1},{17,25},{25,17},{2,10},{10... | collective-permute-start | bytes 294920 | tf_op jit(solution)/shard_map/ppermute | solution.py:322
  51.4 6.5 %collective-permute-start.17 = (f32[2,96,128]{2,1,0:T(8,128)S(1)}, f32[2,96,128]{2,1,0:T(8,128)S(1)}, u32[]{:S(2)}, u32[]{:S(2)}) collective-permute-start(f32[2,96,128]{2,1,0:T(8,128)S(1)} %shard_map.94.refs_0_), channel_id=1, source_target_pairs={{0,4},{4,0},{1,5},{5,1},{2,6},{6,2},{3,7},{7,3},{8,12},{12,8},{9,1... | collective-permute-start | bytes 294920 | tf_op jit(solution)/shard_map/ppermute | solution.py:322
  54.4 4.7 %collective-permute-start.23 = (f32[2,96,128]{2,1,0:T(8,128)S(1)}, f32[2,96,128]{2,1,0:T(8,128)S(1)}, u32[]{:S(2)}, u32[]{:S(2)}) collective-permute-start(f32[2,96,128]{2,1,0:T(8,128)S(1)} %collective-permute-done.22.refs_0_), channel_id=1, source_target_pairs={{0,4},{4,0},{1,5},{5,1},{2,6},{6,2},{3,7},{7,3},{8,12},{12,8},{9,1... | collective-permute-start | bytes 294920 | tf_op jit(solution)/shard_map/ppermute | solution.py:322
  56.1 1.9 %collective-permute-start.21 = (f32[2,96,128]{2,1,0:T(8,128)S(1)}, f32[2,96,128]{2,1,0:T(8,128)S(1)}, u32[]{:S(2)}, u32[]{:S(2)}) collective-permute-start(f32[2,96,128]{2,1,0:T(8,128)S(1)} %collective-permute-done.20.refs_4_), channel_id=1, source_target_pairs={{0,4},{4,0},{1,5},{5,1},{2,6},{6,2},{3,7},{7,3},{8,12},{12,8},{9,1... | collective-permute-start | bytes 294920 | tf_op jit(solution)/shard_map/ppermute | solution.py:322
  56.2 1.8 %collective-permute-start.19 = (f32[2,96,128]{2,1,0:T(8,128)S(1)}, f32[2,96,128]{2,1,0:T(8,128)S(1)}, u32[]{:S(2)}, u32[]{:S(2)}) collective-permute-start(f32[2,96,128]{2,1,0:T(8,128)S(1)} %collective-permute-done.18.refs_2_), channel_id=1, source_target_pairs={{0,4},{4,0},{1,5},{5,1},{2,6},{6,2},{3,7},{7,3},{8,12},{12,8},{9,1... | collective-permute-start | bytes 294920 | tf_op jit(solution)/shard_map/ppermute | solution.py:322
